TPU v7x, 32 devices: a whole 2x2x4 slice. The times are simulated.
32 devices in a mesh: fsdp: 8 (over z, y), dp: 4 (over x, core).
Axes of the slice: x: 2, y: 2, z: 4, core: 2. Of those that a mesh axis runs over, the one named last changes fastest.
Arguments:
- hidden_in: bfloat16 [128, 128, 768], P(('fsdp', 'dp')), may hold values from -6 to 6
- query_key_value_weight: bfloat16 [768, 2304], P('fsdp'), may hold values from -0.21875 to 0.21875
- attention_output_weight: bfloat16 [768, 768], P('fsdp'), may hold values from -0.625 to 0.625
- gate_up_weight: bfloat16 [768, 6144], P('fsdp'), may hold values from -0.21875 to 0.21875
- down_weight: bfloat16 [3072, 768], P('fsdp'), may hold values from -0.109375 to 0.109375
- gain_attn: bfloat16 [768], P('fsdp'), may hold values from 0.25 to 1.75
- shift_attn: bfloat16 [768], P('fsdp'), may hold values from -3 to 3
- gain_ffn: bfloat16 [768], P('fsdp'), may hold values from 0.25 to 1.75
- shift_ffn: bfloat16 [768], P('fsdp'), may hold values from -3 to 3
- masked_output_gradient: bfloat16 [128, 32, 768], P(('fsdp', 'dp')), may hold values from -6 to 6
- positions: int32 [128, 32], P(('fsdp', 'dp')), may hold values from 0 to 127, as said below
- mask_counts: int32 [128], P(('fsdp', 'dp')), may hold values from 8 to 32
Outputs:
- layer_out: bfloat16 [128, 128, 768], P(('fsdp', 'dp'))
- grad_in: float32 [128, 128, 768], P(('fsdp', 'dp'))
- grad_qkv: float32 [768, 2304], P('fsdp')
- grad_out_proj: float32 [768, 768], P('fsdp')
- grad_up: float32 [768, 6144], P('fsdp')
- grad_down: float32 [3072, 768], P('fsdp')
- grad_gain_attn: float32 [768], P('fsdp')
- grad_shift_attn: float32 [768], P('fsdp')
- grad_gain_ffn: float32 [768], P('fsdp')
- grad_shift_ffn: float32 [768], P('fsdp')
Inputs may be any that keep to these rules, and one draw needn't show every extreme that they name: Within one sequence the listed positions are distinct.
All inputs are finite; a program needn't handle non-finite values.
Results may differ from a plain program's by a relative error of at most 0.015.
Values may be sent and summed in bfloat16 or wider, within the bound.
No kernel may reach another device: no remote copies, remote signals or barrier semaphores. Data moves between devices by JAX's collectives and lax.ppermute only.
A program may use at most 192 MiB of HBM per device.

v0:
```python
import jax
import jax.numpy as jnp
from jax import lax
from jax.sharding import PartitionSpec as P

HEADS = 12
HEAD_DIM = 64
FF = 3072
MICRO = 2


norm_eps = 1e-12


def layer_norm(value, gain, shift):
    center = value - jnp.mean(value, axis=-1, keepdims=True)
    spread = jnp.mean(center * center, axis=-1, keepdims=True)
    return center * lax.rsqrt(spread + norm_eps) * gain + shift


def gated_unit(gate, values):
    return jax.nn.gelu(gate, approximate=False) * values


def alibi_table(length):
    head_index = jnp.arange(HEADS, dtype=jnp.float32)
    slopes = jnp.exp2(-8.0 * (head_index + 1.0) / HEADS)
    places = jnp.arange(length)
    distance = jnp.abs(places[:, None] - places[None, :]).astype(jnp.float32)
    return -slopes[:, None, None] * distance[None, :, :]


def attn_scores(queries, key_rows, length):
    raw = jnp.einsum("sqhc,skhc->shqk", queries, key_rows, preferred_element_type=jnp.float32)
    return raw * HEAD_DIM ** (-0.5) + alibi_table(length)[None]


def forward(rows_in, weights, seqs, length):
    (
        query_key_value_weight,
        attention_output_weight,
        gate_up_weight,
        down_weight,
        gain_attn,
        shift_attn,
        gain_ffn,
        shift_ffn,
    ) = weights
    width = rows_in.shape[1]
    projected = jnp.dot(rows_in, query_key_value_weight, preferred_element_type=jnp.float32).astype(
        jnp.bfloat16
    )
    split = projected.reshape(seqs, length, 3, HEADS, HEAD_DIM)
    queries = split[:, :, 0]
    key_rows = split[:, :, 1]
    value_rows = split[:, :, 2]
    scores = attn_scores(queries, key_rows, length)
    peak = jnp.max(scores, axis=-1, keepdims=True)
    expo = jnp.exp(scores - peak)
    total = jnp.sum(expo, axis=-1, keepdims=True)
    soft_low = (expo / total).astype(jnp.bfloat16)
    log_total = peak + jnp.log(total)
    mixed = jnp.einsum("shqk,skhc->sqhc", soft_low, value_rows, preferred_element_type=jnp.float32)
    context = mixed.astype(jnp.bfloat16).reshape(seqs * length, width)
    resid_one = rows_in.astype(jnp.float32) + jnp.dot(
        context, attention_output_weight, preferred_element_type=jnp.float32
    )
    normed_one = layer_norm(
        resid_one, gain_attn.astype(jnp.float32), shift_attn.astype(jnp.float32)
    )
    normed_low = normed_one.astype(jnp.bfloat16)
    lifted = jnp.dot(normed_low, gate_up_weight, preferred_element_type=jnp.float32)
    gated_hidden = gated_unit(lifted[:, :FF], lifted[:, FF:]).astype(jnp.bfloat16)
    resid_two = normed_one + jnp.dot(gated_hidden, down_weight, preferred_element_type=jnp.float32)
    result = layer_norm(resid_two, gain_ffn.astype(jnp.float32), shift_ffn.astype(jnp.float32))
    kept = (
        queries,
        key_rows,
        value_rows,
        log_total,
        context,
        resid_one,
        normed_low,
        lifted,
        gated_hidden,
        resid_two,
    )
    return (result, kept)


def backward(rows_in, weights, kept, grad_rows, seqs, length):
    (
        query_key_value_weight,
        attention_output_weight,
        gate_up_weight,
        down_weight,
        gain_attn,
        shift_attn,
        gain_ffn,
        shift_ffn,
    ) = weights
    (
        queries,
        key_rows,
        value_rows,
        log_total,
        context,
        resid_one,
        normed_low,
        lifted,
        gated_hidden,
        resid_two,
    ) = kept
    _, pull_two = jax.vjp(
        layer_norm, resid_two, gain_ffn.astype(jnp.float32), shift_ffn.astype(jnp.float32)
    )
    grad_resid_two, grad_gain_ffn, grad_shift_ffn = pull_two(grad_rows)
    grad_down_low = grad_resid_two.astype(jnp.bfloat16)
    grad_w_down = jnp.einsum(
        "nf,nd->fd", gated_hidden, grad_down_low, preferred_element_type=jnp.float32
    )
    grad_gated = jnp.einsum(
        "nd,fd->nf", grad_down_low, down_weight, preferred_element_type=jnp.float32
    )
    _, pull_gate = jax.vjp(gated_unit, lifted[:, :FF], lifted[:, FF:])
    grad_gate, grad_value = pull_gate(grad_gated)
    grad_lifted = jnp.concatenate([grad_gate, grad_value], axis=1).astype(jnp.bfloat16)
    grad_w_up = jnp.einsum("nd,nf->df", normed_low, grad_lifted, preferred_element_type=jnp.float32)
    grad_normed = grad_resid_two + jnp.einsum(
        "nf,df->nd", grad_lifted, gate_up_weight, preferred_element_type=jnp.float32
    )
    _, pull_one = jax.vjp(
        layer_norm, resid_one, gain_attn.astype(jnp.float32), shift_attn.astype(jnp.float32)
    )
    grad_resid_one, grad_gain_attn, grad_shift_attn = pull_one(grad_normed)
    grad_attn_low = grad_resid_one.astype(jnp.bfloat16)
    grad_w_out = jnp.einsum("nd,ne->de", context, grad_attn_low, preferred_element_type=jnp.float32)
    grad_attended = jnp.einsum(
        "ne,de->nd", grad_attn_low, attention_output_weight, preferred_element_type=jnp.float32
    )
    grad_attended = grad_attended.astype(jnp.bfloat16).reshape(seqs, length, HEADS, HEAD_DIM)
    scores = attn_scores(queries, key_rows, length)
    soft = jnp.exp(scores - log_total)
    soft_low = soft.astype(jnp.bfloat16)
    grad_values = jnp.einsum(
        "shqk,sqhc->skhc", soft_low, grad_attended, preferred_element_type=jnp.float32
    )
    grad_soft = jnp.einsum(
        "sqhc,skhc->shqk", grad_attended, value_rows, preferred_element_type=jnp.float32
    )
    grad_scores = soft * (grad_soft - jnp.sum(grad_soft * soft, axis=-1, keepdims=True))
    grad_scores = grad_scores.astype(jnp.bfloat16)
    scale = HEAD_DIM ** (-0.5)
    grad_queries = (
        jnp.einsum("shqk,skhc->sqhc", grad_scores, key_rows, preferred_element_type=jnp.float32)
        * scale
    )
    grad_keys = (
        jnp.einsum("shqk,sqhc->skhc", grad_scores, queries, preferred_element_type=jnp.float32)
        * scale
    )
    width = rows_in.shape[1]
    grad_proj = jnp.stack([grad_queries, grad_keys, grad_values], axis=2).astype(jnp.bfloat16)
    grad_proj = grad_proj.reshape(seqs * length, 3 * width)
    grad_w_qkv = jnp.einsum("nd,ne->de", rows_in, grad_proj, preferred_element_type=jnp.float32)
    grad_input = grad_resid_one + jnp.einsum(
        "ne,de->nd", grad_proj, query_key_value_weight, preferred_element_type=jnp.float32
    )
    grads = (
        grad_w_qkv,
        grad_w_out,
        grad_w_up,
        grad_w_down,
        grad_gain_attn,
        grad_shift_attn,
        grad_gain_ffn,
        grad_shift_ffn,
    )
    return (grad_input, grads)


def add_trees(first, second):
    return jax.tree.map(lambda left_term, right_term: left_term + right_term, first, second)


def on_device(
    hidden_in,
    query_key_value_weight,
    attention_output_weight,
    gate_up_weight,
    down_weight,
    gain_attn,
    shift_attn,
    gain_ffn,
    shift_ffn,
    masked_output_gradient,
    positions,
    mask_counts,
):
    seq_dev, length, width = hidden_in.shape
    seq_micro = seq_dev // MICRO
    slots = jnp.arange(positions.shape[1], dtype=jnp.int32)
    live = slots[None, :] < mask_counts[:, None]
    picks = (positions[:, :, None] == jnp.arange(length, dtype=jnp.int32)[None, None, :]) & live[
        :, :, None
    ]
    grad_full = jnp.einsum(
        "vqj,vqu->vju",
        picks.astype(jnp.bfloat16),
        masked_output_gradient,
        preferred_element_type=jnp.float32,
    )
    outputs = []
    grad_inputs = []
    summed = None
    for micro_step in range(MICRO):
        lower = micro_step * seq_micro
        rows_in = hidden_in[lower : lower + seq_micro].reshape(seq_micro * length, width)
        grad_rows = grad_full[lower : lower + seq_micro].reshape(seq_micro * length, width)
        gathered = (
            lax.all_gather(query_key_value_weight, "fsdp", axis=0, tiled=True),
            lax.all_gather(attention_output_weight, "fsdp", axis=0, tiled=True),
            lax.all_gather(gate_up_weight, "fsdp", axis=0, tiled=True),
            lax.all_gather(down_weight, "fsdp", axis=0, tiled=True),
            lax.all_gather(gain_attn, "fsdp", axis=0, tiled=True),
            lax.all_gather(shift_attn, "fsdp", axis=0, tiled=True),
            lax.all_gather(gain_ffn, "fsdp", axis=0, tiled=True),
            lax.all_gather(shift_ffn, "fsdp", axis=0, tiled=True),
        )
        result, kept = forward(rows_in, gathered, seq_micro, length)
        gathered = (
            lax.all_gather(query_key_value_weight, "fsdp", axis=0, tiled=True),
            lax.all_gather(attention_output_weight, "fsdp", axis=0, tiled=True),
            lax.all_gather(gate_up_weight, "fsdp", axis=0, tiled=True),
            lax.all_gather(down_weight, "fsdp", axis=0, tiled=True),
            lax.all_gather(gain_attn, "fsdp", axis=0, tiled=True),
            lax.all_gather(shift_attn, "fsdp", axis=0, tiled=True),
            lax.all_gather(gain_ffn, "fsdp", axis=0, tiled=True),
            lax.all_gather(shift_ffn, "fsdp", axis=0, tiled=True),
        )
        grad_input, grads = backward(rows_in, gathered, kept, grad_rows, seq_micro, length)
        outputs.append(result.astype(jnp.bfloat16).reshape(seq_micro, length, width))
        grad_inputs.append(grad_input.reshape(seq_micro, length, width))
        owned = (
            lax.psum_scatter(grads[0], "fsdp", scatter_dimension=0, tiled=True),
            lax.psum_scatter(grads[1], "fsdp", scatter_dimension=0, tiled=True),
            lax.psum_scatter(grads[2], "fsdp", scatter_dimension=0, tiled=True),
            lax.psum_scatter(grads[3], "fsdp", scatter_dimension=0, tiled=True),
            lax.psum_scatter(grads[4], "fsdp", scatter_dimension=0, tiled=True),
            lax.psum_scatter(grads[5], "fsdp", scatter_dimension=0, tiled=True),
            lax.psum_scatter(grads[6], "fsdp", scatter_dimension=0, tiled=True),
            lax.psum_scatter(grads[7], "fsdp", scatter_dimension=0, tiled=True),
        )
        shares = (
            lax.psum_scatter(
                owned[0].astype(jnp.bfloat16), "dp", scatter_dimension=1, tiled=True
            ).astype(jnp.float32),
            lax.psum_scatter(
                owned[1].astype(jnp.bfloat16), "dp", scatter_dimension=1, tiled=True
            ).astype(jnp.float32),
            lax.psum_scatter(
                owned[2].astype(jnp.bfloat16), "dp", scatter_dimension=1, tiled=True
            ).astype(jnp.float32),
            lax.psum_scatter(
                owned[3].astype(jnp.bfloat16), "dp", scatter_dimension=1, tiled=True
            ).astype(jnp.float32),
        )
        norms = lax.psum((owned[4], owned[5], owned[6], owned[7]), "dp")
        joined = (
            lax.all_gather(shares[0].astype(jnp.bfloat16), "dp", axis=1, tiled=True).astype(
                jnp.float32
            ),
            lax.all_gather(shares[1].astype(jnp.bfloat16), "dp", axis=1, tiled=True).astype(
                jnp.float32
            ),
            lax.all_gather(shares[2].astype(jnp.bfloat16), "dp", axis=1, tiled=True).astype(
                jnp.float32
            ),
            lax.all_gather(shares[3].astype(jnp.bfloat16), "dp", axis=1, tiled=True).astype(
                jnp.float32
            ),
        )
        owned = (joined[0], joined[1], joined[2], joined[3], norms[0], norms[1], norms[2], norms[3])
        summed = owned if summed is None else add_trees(summed, owned)
    layer_out = jnp.concatenate(outputs, axis=0)
    grad_in = jnp.concatenate(grad_inputs, axis=0)
    return (
        layer_out,
        grad_in,
        summed[0],
        summed[1],
        summed[2],
        summed[3],
        summed[4],
        summed[5],
        summed[6],
        summed[7],
    )


def solution(mesh):
    return jax.shard_map(
        on_device,
        mesh=mesh,
        in_specs=(
            P(("fsdp", "dp"), None, None),
            P("fsdp", None),
            P("fsdp", None),
            P("fsdp", None),
            P("fsdp", None),
            P("fsdp"),
            P("fsdp"),
            P("fsdp"),
            P("fsdp"),
            P(("fsdp", "dp"), None, None),
            P(("fsdp", "dp"), None),
            P(("fsdp", "dp")),
        ),
        out_specs=(
            P(("fsdp", "dp"), None, None),
            P(("fsdp", "dp"), None, None),
            P("fsdp", None),
            P("fsdp", None),
            P("fsdp", None),
            P("fsdp", None),
            P("fsdp"),
            P("fsdp"),
            P("fsdp"),
            P("fsdp"),
        ),
        check_vma=False,
    )
```

profile of v0, /device:TPU:0, one launch (start us, length us, event | category | flops | bytes accessed | tf_op | source)
XLA Modules:
  0.0 1982.9 jit_solution(16681597658885285497)
XLA Ops:
  15.5 24.7 %all-reduce.10 = (bf16[768]{0:T(1024)(128)(2,1)S(1)}, bf16[768]{0:T(1024)(128)(2,1)S(1)}, bf16[768]{0:T(1024)(128)(2,1)S(1)}, bf16[768]{0:T(1024)(128)(2,1)S(1)}) all-reduce(bf16[768]{0:T(1024)(128)(2,1)S(1)} %dynamic-update-slice.1, bf16[768]{0:T(1024)(128)(2,1)S(1)} %dynamic-update-slice, ...), channel_id=1, replica_groups=mesh['fsdp'=8,'dp'=4] {'fsdp'}, use_global_device_ids=true, to_apply=%add.1 | all-reduce | flops 3072 | bytes 12288
  43.4 34.7 %all-gather.9.cloned.1.call-done = bf16[768,2304]{1,0:T(8,128)(2,1)} async-done(((bf16[96,2304]{1,0:T(8,128)(2,1)}), bf16[768,2304]{1,0:T(8,128)(2,1)}) %all-gather.9.cloned.1.call-update) | async-done | bytes 3538960 | tf_op jit(solution)/shard_map/all_gather | solution.py:221
  99.6 20.6 %all-gather.11.cloned.1.call-done = bf16[768,768]{1,0:T(8,128)(2,1)} async-done(((bf16[96,768]{1,0:T(8,128)(2,1)}), bf16[768,768]{1,0:T(8,128)(2,1)}) %all-gather.11.cloned.1.call-update) | async-done | bytes 1179664 | tf_op jit(solution)/shard_map/all_gather | solution.py:222
  126.2 132.1 %all-gather.13.cloned.1.call-done = bf16[768,6144]{1,0:T(8,128)(2,1)} async-done(((bf16[96,6144]{1,0:T(8,128)(2,1)}), bf16[768,6144]{1,0:T(8,128)(2,1)}) %all-gather.13.cloned.1.call-update) | async-done | bytes 9437200 | tf_op jit(solution)/shard_map/all_gather | solution.py:223
  274.6 63.3 %all-gather.15.cloned.1.call-done = bf16[3072,768]{1,0:T(8,128)(2,1)} async-done(((bf16[384,768]{1,0:T(8,128)(2,1)}), bf16[3072,768]{1,0:T(8,128)(2,1)}) %all-gather.15.cloned.1.call-update) | async-done | bytes 4718608 | tf_op jit(solution)/shard_map/all_gather | solution.py:224
  366.4 8.5 fusion.14
  384.4 8.1 fusion.16
  452.1 8.1 copy.145
  475.6 207.5 %reduce-scatter.41.cloned.1.call-done = f32[96,6144]{1,0:T(8,128)} async-done(((f32[768,6144]{1,0:T(8,128)}), f32[96,6144]{1,0:T(8,128)}) %reduce-scatter.41.cloned.1.call-update) | async-done | bytes 2359312 | tf_op jit(solution)/shard_map/reduce_scatter | solution.py:247
  686.0 309.6 %reduce-scatter.37.cloned.1.call-done = f32[96,6144]{1,0:T(8,128)} async-done(((f32[768,6144]{1,0:T(8,128)}), f32[96,6144]{1,0:T(8,128)}) %reduce-scatter.37.cloned.1.call-update) | async-done | bytes 2359312 | tf_op jit(solution)/shard_map/reduce_scatter | solution.py:247
  998.5 69.9 %reduce-scatter.35.cloned.1.call-done = f32[96,768]{1,0:T(8,128)} async-done(((f32[768,768]{1,0:T(8,128)}), f32[96,768]{1,0:T(8,128)}) %reduce-scatter.35.cloned.1.call-update) | async-done | bytes 294928 | tf_op jit(solution)/shard_map/reduce_scatter | solution.py:246
  1070.3 70.7 %reduce-scatter.33.cloned.1.call-done = f32[96,768]{1,0:T(8,128)} async-done(((f32[768,768]{1,0:T(8,128)}), f32[96,768]{1,0:T(8,128)}) %reduce-scatter.33.cloned.1.call-update) | async-done | bytes 294928 | tf_op jit(solution)/shard_map/reduce_scatter | solution.py:246
  1142.9 130.2 %reduce-scatter.51.cloned.1.call-done = f32[96,2304]{1,0:T(8,128)} async-done(((f32[768,2304]{1,0:T(8,128)}), f32[96,2304]{1,0:T(8,128)}) %reduce-scatter.51.cloned.1.call-update) | async-done | bytes 884752
  1275.4 129.5 %reduce-scatter.49.cloned.1.call-done = f32[96,2304]{1,0:T(8,128)} async-done(((f32[768,2304]{1,0:T(8,128)}), f32[96,2304]{1,0:T(8,128)}) %reduce-scatter.49.cloned.1.call-update) | async-done | bytes 884752
  1407.2 162.5 %reduce-scatter.45.cloned.1.call-done = f32[384,768]{1,0:T(8,128)} async-done(((f32[3072,768]{1,0:T(8,128)}), f32[384,768]{1,0:T(8,128)}) %reduce-scatter.45.cloned.1.call-update) | async-done | bytes 1179664 | tf_op jit(solution)/shard_map/reduce_scatter | solution.py:248
  1572.2 162.2 %reduce-scatter.47.cloned.1.call-done = f32[384,768]{1,0:T(8,128)} async-done(((f32[3072,768]{1,0:T(8,128)}), f32[384,768]{1,0:T(8,128)}) %reduce-scatter.47.cloned.1.call-update) | async-done | bytes 1179664 | tf_op jit(solution)/shard_map/reduce_scatter | solution.py:248
  1736.9 25.4 %reduce-scatter.43.cloned.1.call-done = bf16[96,1536]{1,0:T(8,128)(2,1)} async-done(((bf16[96,6144]{1,0:T(8,128)(2,1)}), bf16[96,1536]{1,0:T(8,128)(2,1)}) %reduce-scatter.43.cloned.1.call-update) | async-done | bytes 294928 | tf_op jit(solution)/shard_map/reduce_scatter | solution.py:261
  1763.1 37.1 %all-reduce.8 = (f32[768]{0:T(1024)S(1)}, f32[768]{0:T(1024)S(1)}, f32[768]{0:T(1024)S(1)}, f32[768]{0:T(1024)S(1)}) all-reduce(f32[768]{0:T(1024)S(1)} %add.268, f32[768]{0:T(1024)S(1)} %add.269, f32[768]{0:T(1024)S(1)} %add.270, f32[768]{0:T(1024)S(1)} %add.271), channel_id=22, replica_groups=mesh['fsdp'=8,'dp'=4] {'fsdp'}, use_global_device_ids=true, to_apply=%region_39.0.clone | all-reduce | flops 3072 | bytes 24576
  1819.9 15.3 reduce-scatter.53.cloned.1.call-done
  1841.9 18.3 reduce-scatter.31.cloned.1.call-done
  1861.3 24.0 %reduce-scatter.29.cloned.1.call-done = bf16[96,576]{0,1:T(8,128)(2,1)} async-done(((bf16[96,2304]{0,1:T(8,128)(2,1)}), bf16[96,576]{0,1:T(8,128)(2,1)}) %reduce-scatter.29.cloned.1.call-update) | async-done | bytes 110608 | tf_op jit(solution)/shard_map/reduce_scatter | solution.py:255
  1917.0 17.3 reduce-scatter.59.cloned.1.call-done
  1942.9 10.4 all-gather.19.cloned.1.call-done
  1953.3 19.0 all-gather.17.cloned.1.call-done
  (311 shorter events, 256.6 us)
Async XLA Ops:
  7.2 70.9 %all-gather.9.cloned.1.call-start = ((), (), s32[]{:S(2)}) async-start(), calls=%async_computation.16 | async-start | bytes 3981312 | tf_op jit(solution)/shard_map/all_gather | solution.py:221
  7.9 112.2 %all-gather.11.cloned.1.call-start = ((), (), s32[]{:S(2)}) async-start(), calls=%async_computation.17 | async-start | bytes 1327104 | tf_op jit(solution)/shard_map/all_gather | solution.py:222
  8.7 249.6 %all-gather.13.cloned.1.call-start = ((), (), s32[]{:S(2)}) async-start(), calls=%async_computation.18 | async-start | bytes 10616832 | tf_op jit(solution)/shard_map/all_gather | solution.py:223
  9.4 328.5 %all-gather.15.cloned.1.call-start = ((), (), s32[]{:S(2)}) async-start(), calls=%async_computation.19 | async-start | bytes 5308416 | tf_op jit(solution)/shard_map/all_gather | solution.py:224
  10.0 673.1 %reduce-scatter.41.cloned.1.call-start = ((), (), s32[]{:S(2)}) async-start(), calls=%async_computation.27 | async-start | bytes 21233664 | tf_op jit(solution)/shard_map/reduce_scatter | solution.py:247
  41.5 51.8 %copy-start.18 = (f32[12,128,128]{1,2,0:T(8,128)}, f32[12,128,128]{1,2,0:T(8,128)S(1)}, u32[]{:S(2)}) copy-start(f32[12,128,128]{1,2,0:T(8,128)S(1)} %broadcast_multiply_fusion) | copy-start | bytes 2359300
  374.9 620.7 %reduce-scatter.37.cloned.1.call-start = ((), (), s32[]{:S(2)}) async-start(), calls=%async_computation.24 | async-start | bytes 21233664 | tf_op jit(solution)/shard_map/reduce_scatter | solution.py:247
  392.5 675.9 %reduce-scatter.35.cloned.1.call-start = ((), (), s32[]{:S(2)}) async-start(), calls=%async_computation.23 | async-start | bytes 2654208 | tf_op jit(solution)/shard_map/reduce_scatter | solution.py:246
  411.5 729.5 %reduce-scatter.33.cloned.1.call-start = ((), (), s32[]{:S(2)}) async-start(), calls=%async_computation.22 | async-start | bytes 2654208 | tf_op jit(solution)/shard_map/reduce_scatter | solution.py:246
  414.9 858.2 %reduce-scatter.51.cloned.1.call-start = ((), (), s32[]{:S(2)}) async-start(), calls=%async_computation.33 | async-start | bytes 7962624
  439.9 965.0 %reduce-scatter.49.cloned.1.call-start = ((), (), s32[]{:S(2)}) async-start(), calls=%async_computation.32 | async-start | bytes 7962624
  460.2 1109.5 %reduce-scatter.45.cloned.1.call-start = ((), (), s32[]{:S(2)}) async-start(), calls=%async_computation.30 | async-start | bytes 10616832 | tf_op jit(solution)/shard_map/reduce_scatter | solution.py:248
  467.9 1266.5 %reduce-scatter.47.cloned.1.call-start = ((), (), s32[]{:S(2)}) async-start(), calls=%async_computation.31 | async-start | bytes 10616832 | tf_op jit(solution)/shard_map/reduce_scatter | solution.py:248
  475.6 1286.8 %reduce-scatter.43.cloned.1.call-start = ((), (), s32[]{:S(2)}) async-start(), calls=%async_computation.28 | async-start | bytes 1474560 | tf_op jit(solution)/shard_map/reduce_scatter | solution.py:261
  685.9 1127.2 %reduce-scatter.39.cloned.1.call-start = ((), (), s32[]{:S(2)}) async-start(), calls=%async_computation.25 | async-start | bytes 1474560 | tf_op jit(solution)/shard_map/reduce_scatter | solution.py:261
  998.5 815.6 %reduce-scatter.55.cloned.1.call-start = ((), (), s32[]{:S(2)}) async-start(), calls=%async_computation.35 | async-start | bytes 245760
  1070.3 764.9 %reduce-scatter.53.cloned.1.call-start = ((), (), s32[]{:S(2)}) async-start(), calls=%async_computation.34 | async-start | bytes 245760
  1142.8 717.4 %reduce-scatter.31.cloned.1.call-start = ((), (), s32[]{:S(2)}) async-start(), calls=%async_computation.21 | async-start | bytes 737280 | tf_op jit(solution)/shard_map/reduce_scatter | solution.py:255
  1275.3 609.9 %reduce-scatter.29.cloned.1.call-start = ((), (), s32[]{:S(2)}) async-start(), calls=%async_computation.20 | async-start | bytes 737280 | tf_op jit(solution)/shard_map/reduce_scatter | solution.py:255
  1407.2 502.7 %reduce-scatter.57.cloned.1.call-start = ((), (), s32[]{:S(2)}) async-start(), calls=%async_computation.36 | async-start | bytes 737280
  1571.1 235.9 %copy-start.24 = (f32[256,768]{1,0:T(8,128)S(1)}, f32[256,768]{1,0:T(8,128)}, u32[]{:S(2)}) copy-start(f32[256,768]{1,0:T(8,128)} %get-tuple-element.55) | copy-start | bytes 2359300
  1572.2 362.1 %reduce-scatter.59.cloned.1.call-start = ((), (), s32[]{:S(2)}) async-start(), calls=%async_computation.37 | async-start | bytes 737280
  1736.9 216.4 %all-gather.19.cloned.1.call-start = ((), (), s32[]{:S(2)}) async-start(), calls=%async_computation.29 | async-start | bytes 1474560 | tf_op jit(solution)/shard_map/all_gather | solution.py:276
  1762.4 210.0 %all-gather.17.cloned.1.call-start = ((), (), s32[]{:S(2)}) async-start(), calls=%async_computation.26 | async-start | bytes 1474560 | tf_op jit(solution)/shard_map/all_gather | solution.py:276
  (59 other events, 400.4 us)
Sparse Core Ops, SparseCore 0:
  10.2 67.8 all-gather.8
  80.3 39.8 all-gather.10
  122.4 135.9 all-gather.12
  260.4 77.5 all-gather.14
  375.0 307.9 reduce-scatter.40
  686.8 308.7 reduce-scatter.36
  999.7 68.7 reduce-scatter.34
  1071.9 69.0 reduce-scatter.32
  1144.7 128.3 reduce-scatter.50
  1276.6 128.2 reduce-scatter.48
  1408.5 161.1 reduce-scatter.44
  1573.2 161.1 reduce-scatter.46
  1737.6 24.7 reduce-scatter.42
  1764.7 25.6 reduce-scatter.38
  1793.3 19.7 reduce-scatter.54
  1815.4 19.7 reduce-scatter.52
  1838.1 22.0 reduce-scatter.30
  1863.1 22.0 reduce-scatter.28
  1887.7 22.0 reduce-scatter.56
  1912.2 22.0 reduce-scatter.58
  1935.8 17.4 all-gather.18
  1954.9 17.4 all-gather.16
where the time goes:
time: 1990 us; the launch traced here: 1980 us
  waiting for transfers between devices  1630 us (82%)
  matrix products  114 us (6%)
  blocking collectives  108 us (5%)
  local copies, waits for them, and re-layouts  69.9 us (4%)
  other arithmetic  39.8 us (2%)
    reduce_scatter x2, waiting for transfers between devices, on_device(): lax.psum_scatter(grads[2], 'fsdp', scatter_dimension=0, tiled=True)  517 us
    reduce_scatter x2, waiting for transfers between devices, on_device(): lax.psum_scatter(grads[3], 'fsdp', scatter_dimension=0, tiled=True)  325 us
    unnamed x28, waiting for transfers between devices  303 us
    reduce_scatter x2, waiting for transfers between devices, on_device(): lax.psum_scatter(grads[1], 'fsdp', scatter_dimension=0, tiled=True)  141 us
    all_gather x1, waiting for transfers between devices, on_device(): lax.all_gather(gate_up_weight, 'fsdp', axis=0, tiled=True)  132 us
    all_gather x1, waiting for transfers between devices, on_device(): lax.all_gather(down_weight, 'fsdp', axis=0, tiled=True)  63.3 us
    unnamed x2, blocking collectives  61.8 us
    unnamed x147, local copies, waits for them, and re-layouts  48.4 us
  transfers between devices with their start and end apart: 22, of which 20 were waited for; matrix products, arithmetic and copies ran while one was open for 9% of the time, Pallas kernels for 0%

commit v1 on v0

v1 whole, which is shorter than its diff:
```python
import jax
import jax.numpy as jnp
from jax import lax
from jax.sharding import PartitionSpec as P

HEADS = 12
HEAD_DIM = 64
FF = 3072
EPS = 1e-12
F32 = jnp.float32
LOW = jnp.bfloat16
AXES = ("fsdp", "dp")


def mm(a, b):
    return jnp.dot(a, b, preferred_element_type=F32)


def slopes():
    return jnp.exp2(-8.0 * (jnp.arange(HEADS, dtype=F32) + 1.0) / HEADS)


def norm_parts(value):
    center = value - jnp.mean(value, axis=-1, keepdims=True)
    rstd = lax.rsqrt(jnp.mean(center * center, axis=-1, keepdims=True) + EPS)
    return center * rstd, rstd


def norm_back(grad, unit, rstd, gain):
    scaled = grad * gain
    return rstd * (
        scaled
        - jnp.mean(scaled, axis=-1, keepdims=True)
        - unit * jnp.mean(scaled * unit, axis=-1, keepdims=True)
    )


def pick(onehot, rows):
    if rows.dtype == LOW:
        return jnp.einsum("svj,sjd->svd", onehot.astype(LOW), rows, preferred_element_type=F32).astype(LOW)
    return jnp.einsum("svj,sjd->svd", onehot, rows, precision=lax.Precision.HIGHEST)


def gather_weights(w_qkv, w_out, w_up, w_down):
    fsdp = lax.axis_size("fsdp")
    dp = lax.axis_size("dp")
    rows, width = w_out.shape
    if rows % (8 * dp):
        return (
            lax.all_gather(w_qkv, "fsdp", axis=0, tiled=True),
            lax.all_gather(w_out, "fsdp", axis=0, tiled=True),
            lax.all_gather(w_up, "fsdp", axis=0, tiled=True),
            lax.all_gather(w_down, "fsdp", axis=0, tiled=True),
        )
    mine = lax.axis_index("dp")
    part = rows // dp
    group = w_down.shape[0] // rows
    joined = jnp.concatenate([w_qkv, w_out, w_up], axis=1)
    joined = lax.dynamic_slice_in_dim(joined, mine * part, part, axis=0)
    down = lax.dynamic_slice_in_dim(w_down, mine * part * group, part * group, axis=0)
    down = jnp.concatenate([down[k * part : (k + 1) * part] for k in range(group)], axis=1)
    full = lax.all_gather(jnp.concatenate([joined, down], axis=1), AXES, axis=0, tiled=True)
    a, b = w_qkv.shape[1], w_qkv.shape[1] + w_out.shape[1]
    c = b + w_up.shape[1]
    full_down = full[:, c:].reshape(fsdp * dp, part, group, width)
    full_down = full_down.transpose(0, 2, 1, 3).reshape(fsdp * dp * part * group, width)
    return full[:, :a], full[:, a:b], full[:, b:c], full_down


def scatter_grads(g_qkv, g_out, g_up, g_down):
    fsdp = lax.axis_size("fsdp")
    dp = lax.axis_size("dp")
    width = g_out.shape[1]
    rows = g_out.shape[0] // fsdp
    if rows % (8 * dp):
        return tuple(
            lax.psum(lax.psum_scatter(g, "fsdp", scatter_dimension=0, tiled=True), "dp")
            for g in (g_qkv, g_out, g_up, g_down)
        )
    part = rows // dp
    group = g_down.shape[0] // g_out.shape[0]
    down = g_down.reshape(fsdp * dp, group, part, width).transpose(0, 2, 1, 3)
    down = down.reshape(fsdp * rows, group * width)
    joined = jnp.concatenate([g_qkv, g_out, g_up, down], axis=1).astype(LOW)
    mine = lax.psum_scatter(joined, AXES, scatter_dimension=0, tiled=True)
    full = lax.all_gather(mine, "dp", axis=0, tiled=True).astype(F32)
    a, b = g_qkv.shape[1], g_qkv.shape[1] + width
    c = b + g_up.shape[1]
    full_down = full[:, c:].reshape(dp, part, group, width).transpose(0, 2, 1, 3)
    return full[:, :a], full[:, a:b], full[:, b:c], full_down.reshape(rows * group, width)


def on_device(hidden_in, w_qkv, w_out, w_up, w_down, gain_attn, shift_attn, gain_ffn, shift_ffn, grad_listed, positions, counts):
    seqs, length, width = hidden_in.shape
    tokens = seqs * length
    most = positions.shape[1]
    norms = jnp.stack([gain_attn, shift_attn, gain_ffn, shift_ffn])
    norms = lax.all_gather(norms, "fsdp", axis=1, tiled=True).astype(F32)
    w_qkv, w_out, w_up, w_down = gather_weights(w_qkv, w_out, w_up, w_down)
    live = jnp.arange(most, dtype=jnp.int32)[None, :] < counts[:, None]
    onehot = (positions[:, :, None] == jnp.arange(length, dtype=jnp.int32)).astype(F32)
    rows_in = hidden_in.reshape(tokens, width)
    slope = slopes()
    scale = HEAD_DIM**-0.5
    qkv = mm(rows_in, w_qkv).astype(LOW)
    split = qkv.reshape(seqs, length, 3, HEADS, HEAD_DIM)
    q, k, v = split[:, :, 0], split[:, :, 1], split[:, :, 2]
    place = jnp.arange(length, dtype=F32)
    bias = -slope[:, None, None] * jnp.abs(place[:, None] - place[None, :])
    s = jnp.einsum("sqhc,skhc->shqk", q, k, preferred_element_type=F32) * scale + bias
    p = jax.nn.softmax(s, axis=-1).astype(LOW)
    att = jnp.einsum("shqk,skhc->sqhc", p, v, preferred_element_type=F32).astype(LOW)
    att = att.reshape(tokens, width)
    r1 = rows_in.astype(F32) + mm(att, w_out)
    unit1, _ = norm_parts(r1)
    h1 = unit1 * norms[0] + norms[1]
    h1_low = h1.astype(LOW)
    u = mm(h1_low, w_up)
    act = (jax.nn.gelu(u[:, :FF], approximate=False) * u[:, FF:]).astype(LOW)
    r2 = h1 + mm(act, w_down)
    unit2, _ = norm_parts(r2)
    layer_out = (unit2 * norms[2] + norms[3]).astype(LOW).reshape(seqs, length, width)
    def listed(a):
        return pick(onehot, a.reshape(seqs, length, -1)).reshape(seqs * most, -1)

    dy = jnp.where(live[:, :, None], grad_listed, 0).astype(F32).reshape(seqs * most, width)
    unit2_m, rstd2_m = norm_parts(listed(r2))
    g_gain_ffn = jnp.sum(dy * unit2_m, axis=0)
    g_shift_ffn = jnp.sum(dy, axis=0)
    dr2 = norm_back(dy, unit2_m, rstd2_m, norms[2])
    e2 = dr2.astype(LOW)
    h1_m = listed(h1_low)
    u_m = mm(h1_m, w_up)
    gate, up = u_m[:, :FF], u_m[:, FF:]
    cdf = 0.5 * (1.0 + lax.erf(gate * (0.5**0.5)))
    pdf = jnp.exp(-0.5 * gate * gate) * ((2.0 * jnp.pi) ** -0.5)
    gelu = gate * cdf
    act_m = (gelu * up).astype(LOW)
    g_down = jnp.einsum("nf,nd->fd", act_m, e2, preferred_element_type=F32)
    dact = jnp.einsum("nd,fd->nf", e2, w_down, preferred_element_type=F32)
    du = jnp.concatenate([dact * up * (cdf + gate * pdf), dact * gelu], axis=1).astype(LOW)
    g_up = jnp.einsum("nd,nf->df", h1_m, du, preferred_element_type=F32)
    dh1 = dr2 + jnp.einsum("nf,df->nd", du, w_up, preferred_element_type=F32)
    unit1_m, rstd1_m = norm_parts(listed(r1))
    g_gain_attn = jnp.sum(dh1 * unit1_m, axis=0)
    g_shift_attn = jnp.sum(dh1, axis=0)
    dr1 = norm_back(dh1, unit1_m, rstd1_m, norms[0])
    e1 = dr1.astype(LOW)
    g_out = jnp.einsum("nd,ne->de", listed(att), e1, preferred_element_type=F32)
    datt = jnp.einsum("ne,de->nd", e1, w_out, preferred_element_type=F32).astype(LOW)
    datt = datt.reshape(seqs, most, HEADS, HEAD_DIM)
    q_m = listed(qkv[:, :width]).reshape(seqs, most, HEADS, HEAD_DIM)
    away = jnp.abs(positions[:, :, None].astype(F32) - place[None, None, :])
    s_m = jnp.einsum("sqhc,skhc->shqk", q_m, k, preferred_element_type=F32) * scale
    p_m = jax.nn.softmax(s_m - slope[None, :, None, None] * away[:, None], axis=-1)
    dv = jnp.einsum("shqk,sqhc->skhc", p_m.astype(LOW), datt, preferred_element_type=F32)
    dp = jnp.einsum("sqhc,skhc->shqk", datt, v, preferred_element_type=F32)
    ds = (p_m * (dp - jnp.sum(dp * p_m, axis=-1, keepdims=True))).astype(LOW)
    dq_m = (jnp.einsum("shqk,skhc->sqhc", ds, k, preferred_element_type=F32) * scale).astype(LOW)
    dk = (jnp.einsum("shqk,sqhc->skhc", ds, q_m, preferred_element_type=F32) * scale).astype(LOW)
    put = (onehot * live[:, :, None]).astype(LOW)
    dq = jnp.einsum("svj,svd->sjd", put, dq_m.reshape(seqs, most, width), preferred_element_type=F32)
    dqkv = jnp.concatenate(
        [dq.astype(LOW).reshape(tokens, width), dk.reshape(tokens, width), dv.astype(LOW).reshape(tokens, width)], axis=1
    )
    g_qkv = jnp.einsum("nd,ne->de", rows_in, dqkv, preferred_element_type=F32)
    dr1_all = jnp.einsum("svj,svd->sjd", onehot * live[:, :, None], dr1.reshape(seqs, most, width), precision=lax.Precision.HIGHEST)
    grad_in = dr1_all.reshape(tokens, width) + jnp.einsum("ne,de->nd", dqkv, w_qkv, preferred_element_type=F32)
    owned = scatter_grads(g_qkv, g_out, g_up, g_down)
    small = lax.psum(jnp.stack([g_gain_attn, g_shift_attn, g_gain_ffn, g_shift_ffn]), AXES)
    share = width // lax.axis_size("fsdp")
    small = lax.dynamic_slice_in_dim(small, lax.axis_index("fsdp") * share, share, axis=1)
    return (
        layer_out,
        grad_in.reshape(seqs, length, width),
        *owned,
        small[0],
        small[1],
        small[2],
        small[3],
    )


def solution(mesh):
    rows3 = P(("fsdp", "dp"), None, None)
    rows2 = P("fsdp", None)
    rows1 = P("fsdp")
    return jax.shard_map(
        on_device,
        mesh=mesh,
        in_specs=(rows3, rows2, rows2, rows2, rows2, rows1, rows1, rows1, rows1, rows3, P(("fsdp", "dp"), None), P(("fsdp", "dp"))),
        out_specs=(rows3, rows3, rows2, rows2, rows2, rows2, rows1, rows1, rows1, rows1),
        check_vma=False,
    )
```

time: 1990 us -> 586 us (0.29)
  waiting for transfers between devices: 1630 us -> 304 us
  blocking collectives: 108 us -> 63 us
    reduce_scatter x10 -> x1, waiting for transfers between devices: 1050 us -> 205 us  [scatter_grads(): mine = lax.psum_scatter(joined, AXES, scatter_dimension=0, tiled=True)]
    unnamed x28 -> x3, waiting for transfers between devices: 303 us -> 0.05 us
    all_gather x6 -> x2, waiting for transfers between devices: 280 us -> 99 us  [the longest x1 99 us: gather_weights(): lax.all_gather(jnp.concatenate([joined, down], axis=1), AXES, axis=0, til...]
    unnamed x2 -> x0, blocking collectives: 61.8 us -> none
    unnamed x147 -> x86, local copies, waits for them, and re-layouts: 48.4 us -> 10.1 us
    psum x1, blocking collectives: 6.46 us -> 40.4 us  [on_device(): lax.psum(jnp.stack([g_gain_attn, g_shift_attn, g_gain_ffn, g_shift_ffn]),...]
    convert_element_type x17 -> x7, other arithmetic: 27.1 us -> 4.27 us  [the longest x1 1.19 us: on_device(): (unit2 * norms[2] + norms[3]).astype(LOW).reshape(seqs, length, width)]
    dot_general x37 -> x27, matrix products: 114 us -> 94.3 us  [the longest x5 48.2 us: mm(): return jnp.dot(a, b, preferred_element_type=F32)]
  transfers between devices with their start and end apart: 22 -> 3, of which waited for: 20 -> 2; matrix products, arithmetic and copies ran while one was open for 9% -> 3% of each run, Pallas kernels for 0% -> 0%
where the time goes in v1:
time: 586 us; the launch traced here: 576 us
  waiting for transfers between devices  304 us (52%)
  matrix products  94.3 us (16%)
  local copies, waits for them, and re-layouts  68.5 us (12%)
  blocking collectives  63 us (11%)
  other arithmetic  30.7 us (5%)
  between operations  15 us (3%)
    reduce_scatter x1, waiting for transfers between devices, scatter_grads(): mine = lax.psum_scatter(joined, AXES, scatter_dimension=0, tiled=True)  205 us
    all_gather x1, waiting for transfers between devices, gather_weights(): lax.all_gather(jnp.concatenate([joined, down], axis=1), AXES, axis=0, til...  99 us
    dot_general x5, matrix products, mm(): return jnp.dot(a, b, preferred_element_type=F32)  48.2 us
    psum x1, blocking collectives, on_device(): lax.psum(jnp.stack([g_gain_attn, g_shift_attn, g_gain_ffn, g_shift_ffn]),...  40.4 us
    all_gather x1, blocking collectives, on_device(): norms = lax.all_gather(norms, 'fsdp', axis=1, tiled=True).astype(F32)  22.6 us
    concatenate x1, other arithmetic, scatter_grads(): joined = jnp.concatenate([g_qkv, g_out, g_up, down], axis=1).astype(LOW)  15.7 us
  transfers between devices with their start and end apart: 3, of which 2 were waited for; matrix products, arithmetic and copies ran while one was open for 3% of the time, Pallas kernels for 0%

profile of v1, /device:TPU:0, one launch (start us, length us, event | category | flops | bytes accessed | tf_op | source)
XLA Modules:
  0.0 575.9 jit_solution(14297018178041532854)
XLA Ops:
  13.0 22.6 %all-gather = bf16[8,96,4]{1,2,0:T(4,128)(2,1)S(1)} all-gather(bf16[1,96,4]{1,2,0:T(4,128)(2,1)S(1)} %maximum_bitcast_fusion), channel_id=1, replica_groups=mesh['fsdp'=8,'dp'=4] {'fsdp'}, dimensions={0}, use_global_device_ids=true | all-gather | bytes 6912 | tf_op jit(solution)/shard_map/all_gather | solution.py:98
  40.1 99.0 %all-gather.4.cloned.1.call-done = bf16[768,12288]{1,0:T(8,128)(2,1)} async-done(((bf16[24,12288]{1,0:T(8,128)(2,1)}), bf16[768,12288]{1,0:T(8,128)(2,1)}) %all-gather.4.cloned.1.call-update) | async-done | bytes 18874384 | tf_op jit(solution)/shard_map/all_gather | solution.py:62
  139.1 4.8 slice.124
  144.0 9.7 %reshape.392 = bf16[32,24,4,768]{3,2,1,0:T(4,128)(2,1)} reshape(bf16[768,3072]{1,0:T(8,128)(2,1)} %slice.124) | data formatting | bytes 9437184 | tf_op jit(solution)/shard_map/reshape | solution.py:65
  153.7 5.5 copy.108
  159.2 4.0 fusion.20
  164.7 2.4 copy.101
  167.1 4.2 reshape.390
  179.1 8.3 %fusion.6 = f32[512,6144]{1,0:T(8,128)S(1)} fusion(bf16[512,768]{1,0:T(8,128)(2,1)S(1)} %fusion.49, bf16[768,12288]{1,0:T(8,128)(2,1)} %all-gather.4.cloned.1.call-done), kind=kOutput, calls=%fused_computation.9 | convolution fusion | flops 4831838208 | bytes 22806528 | tf_op jit(solution)/shard_map/dot_general | solution.py:16
  187.5 28.4 %fusion.133 = (f32[512]{0:T(512)}, f32[512,768]{1,0:T(8,128)S(1)}) fusion(bf16[3072,768]{1,0:T(8,128)(2,1)S(1)} %bitcast.158, f32[512,6144]{1,0:T(8,128)S(1)} %fusion.6, f32[768]{0:T(1024)S(1)} %get-tuple-element.20, f32[768]{0:T(1024)S(1)} %get-tuple-element.21, f32[512]{0:T(512)S(1)} %add_rsqrt_fusion.3, f32[512,768]{1,0:T(8,128)S(1)} %get-tuple-element.37, ...), kind=kOutput, calls=%fused_computation.229 | convolution fusion | flops 2522086912 | bytes 20459520 | tf_op jit(solution)/shard_map/dot_general | solution.py:16
  224.7 5.3 fusion.4
  230.0 5.1 fusion.32
  235.4 6.7 %multiply_reduce_fusion.4 = (f32[768]{0:T(1024)}, f32[128]{0:T(128)S(1)}, f32[128]{0:T(128)S(1)}, f32[768]{0:T(1024)}, f32[128,768]{1,0:T(8,128)S(1)}) fusion(f32[4,32,768]{2,1,0:T(8,128)S(1)} %get-tuple-element.43, f32[128]{0:T(128)S(1)} %div.77, f32[128]{0:T(128)S(1)} %rsqrt.42, f32[768]{0:T(1024)S(1)} %get-tuple-element.21, f32[128,768]{1,0:T(8,128)S(1)} %fusion.67, ...), kind=kOutput, calls=%fused_computation.116 | convolution fusion | flops 1212086528 | bytes 12200960 | tf_op jit(solution)/shard_map/nf,df->nd/dot_general | solution.py:143
  248.4 3.9 fusion.43
  255.8 5.3 convolution_convert_fusion
  267.7 2.3 copy.119
  270.0 3.1 copy.132
  275.6 5.2 fusion.19
  280.8 4.3 copy.120
  285.1 15.7 %pad_maximum_fusion = bf16[768,12288]{1,0:T(8,128)(2,1)} fusion(bf16[768,3072]{1,0:T(8,128)(2,1)} %bitcast.149, bf16[768,6144]{1,0:T(8,128)(2,1)} %convolution_convert_fusion, bf16[768,768]{1,0:T(8,128)(2,1)} %copy.121, bf16[768,2304]{1,0:T(8,128)(2,1)S(1)} %copy.120), kind=kLoop, calls=%fused_computation.2 | loop fusion | flops 75497472 | bytes 37748736 | tf_op jit(solution)/shard_map/concatenate | solution.py:84
  300.9 205.2 %reduce-scatter.2.cloned.1.call-done = bf16[24,12288]{1,0:T(8,128)(2,1)} async-done(((bf16[768,12288]{1,0:T(8,128)(2,1)}), bf16[24,12288]{1,0:T(8,128)(2,1)}) %reduce-scatter.2.cloned.1.call-update) | async-done | bytes 589840 | tf_op jit(solution)/shard_map/reduce_scatter | solution.py:85
  509.4 40.4 %psum.7 = f32[4,768]{1,0:T(4,128)} all-reduce(f32[4,768]{1,0:T(4,128)} %pad_maximum_fusion.7), channel_id=1, replica_groups=mesh['fsdp'=8,'dp'=4] {'fsdp','dp'}, use_global_device_ids=true, to_apply=%region_22.23 | all-reduce | flops 3072 | bytes 24576 | tf_op jit(solution)/shard_map/psum | solution.py:170
  555.0 5.2 bitcast_add_fusion
  560.2 2.3 slice.133
  (178 shorter events, 61.8 us)
Async XLA Ops:
  7.2 132.0 %all-gather.4.cloned.1.call-start = ((), (), s32[]{:S(2)}) async-start(), calls=%async_computation.1 | async-start | bytes 19464192 | tf_op jit(solution)/shard_map/all_gather | solution.py:62
  12.2 493.8 %reduce-scatter.2.cloned.1.call-start = ((), (), s32[]{:S(2)}) async-start(), calls=%async_computation.2 | async-start | bytes 19464192 | tf_op jit(solution)/shard_map/reduce_scatter | solution.py:85
  38.4 180.8 %copy-start.28 = (pred[4,32]{1,0:T(4,128)(4,1)}, pred[4,32]{1,0:T(4,128)(4,1)S(1)}, u32[]{:S(2)}) copy-start(pred[4,32]{1,0:T(4,128)(4,1)S(1)} %get-tuple-element.33) | copy-start | bytes 388
  153.7 5.5 copy-start.36
  178.8 8.7 %slice-start = ((s8[4718592]{0:T(1024)(128)(4,1)}), s8[4194304]{0:T(1024)(128)(4,1)S(1)}, s32[]{:S(2)}) async-start(s8[4718592]{0:T(1024)(128)(4,1)} %bitcast.156), calls=%async_computation.4 | async-start | bytes 8388608
  179.1 8.3 %copy-start.10 = (bf16[512,768]{1,0:T(8,128)(2,1)}, bf16[512,768]{1,0:T(8,128)(2,1)S(1)}, u32[]{:S(2)}) copy-start(bf16[512,768]{1,0:T(8,128)(2,1)S(1)} %fusion.49) | copy-start | bytes 2359300
  179.1 8.4 %slice-start.1 = ((s8[4718592]{0:T(1024)(128)(4,1)}), s8[524288]{0:T(1024)(128)(4,1)S(1)}, s32[]{:S(2)}) async-start(s8[4718592]{0:T(1024)(128)(4,1)} %bitcast.156), calls=%async_computation.5 | async-start | bytes 1048576
  187.5 29.6 %copy-start.26 = (s32[4,32]{1,0:T(4,128)S(1)}, s32[4,32]{1,0:T(4,128)}, u32[]{:S(2)}) copy-start(s32[4,32]{1,0:T(4,128)} %param.22) | copy-start | bytes 1540
  187.5 31.7 %copy-start.12 = (bf16[4,32,768]{2,1,0:T(8,128)(2,1)S(1)}, bf16[4,32,768]{2,1,0:T(8,128)(2,1)}, u32[]{:S(2)}) copy-start(bf16[4,32,768]{2,1,0:T(8,128)(2,1)} %param.21) | copy-start | bytes 589828
  222.9 12.4 %copy-start.34 = (f32[128]{0:T(128)}, f32[128]{0:T(128)S(1)}, u32[]{:S(2)}) copy-start(f32[128]{0:T(128)S(1)} %div.77) | copy-start | bytes 1540
  223.2 12.2 %copy-start.35 = (f32[128]{0:T(128)}, f32[128]{0:T(128)S(1)}, u32[]{:S(2)}) copy-start(f32[128]{0:T(128)S(1)} %rsqrt.42) | copy-start | bytes 1540
  224.7 5.3 copy-start.20
  235.2 7.0 %copy-start.22 = (bf16[128,3072]{1,0:T(8,128)(2,1)}, bf16[128,3072]{1,0:T(8,128)(2,1)S(1)}, u32[]{:S(2)}) copy-start(bf16[128,3072]{1,0:T(8,128)(2,1)S(1)} %get-tuple-element.22) | copy-start | bytes 2359300
  235.2 7.0 %copy-start.24 = (bf16[128,3072]{1,0:T(8,128)(2,1)}, bf16[128,3072]{1,0:T(8,128)(2,1)S(1)}, u32[]{:S(2)}) copy-start(bf16[128,3072]{1,0:T(8,128)(2,1)S(1)} %get-tuple-element.23) | copy-start | bytes 2359300
  243.1 30.5 %copy-start.3 = (f32[128,768]{1,0:T(8,128)}, f32[128,768]{1,0:T(8,128)S(1)}, u32[]{:S(2)}) copy-start(f32[128,768]{1,0:T(8,128)S(1)} %subtract_multiply_fusion) | copy-start | bytes 1179652
  261.8 13.7 %copy-start.14 = (bf16[96,8,4,128]{3,1,2,0:T(8,128)(2,1)}, bf16[96,8,4,128]{3,1,2,0:T(8,128)(2,1)S(1)}, u32[]{:S(2)}) copy-start(bf16[96,8,4,128]{3,1,2,0:T(8,128)(2,1)S(1)} %copy.163) | copy-start | bytes 2359300
  262.6 13.0 %copy-start.16 = (bf16[96,8,4,128]{3,1,2,0:T(8,128)(2,1)}, bf16[96,8,4,128]{3,1,2,0:T(8,128)(2,1)S(1)}, u32[]{:S(2)}) copy-start(bf16[96,8,4,128]{3,1,2,0:T(8,128)(2,1)S(1)} %copy.164) | copy-start | bytes 2359300
  300.8 250.6 %copy-start.1 = (f32[512,768]{1,0:T(8,128)S(1)}, f32[512,768]{1,0:T(8,128)}, u32[]{:S(2)}) copy-start(f32[512,768]{1,0:T(8,128)} %copy-done) | copy-start | bytes 4718596
  300.8 251.4 %copy-start.4 = (f32[128,768]{1,0:T(8,128)S(1)}, f32[128,768]{1,0:T(8,128)}, u32[]{:S(2)}) copy-start(f32[128,768]{1,0:T(8,128)} %copy-done.3) | copy-start | bytes 1179652
  300.8 253.0 %copy-start.27 = (f32[768]{0:T(1024)S(1)}, f32[768]{0:T(1024)}, u32[]{:S(2)}) copy-start(f32[768]{0:T(1024)} %get-tuple-element.19) | copy-start | bytes 9220
  300.8 254.2 %copy-start.15 = (bf16[96,8,4,128]{3,1,2,0:T(8,128)(2,1)S(1)}, bf16[96,8,4,128]{3,1,2,0:T(8,128)(2,1)}, u32[]{:S(2)}) copy-start(bf16[96,8,4,128]{3,1,2,0:T(8,128)(2,1)} %copy-done.14) | copy-start | bytes 2359300
  300.8 254.2 %copy-start.17 = (bf16[96,8,4,128]{3,1,2,0:T(8,128)(2,1)S(1)}, bf16[96,8,4,128]{3,1,2,0:T(8,128)(2,1)}, u32[]{:S(2)}) copy-start(bf16[96,8,4,128]{3,1,2,0:T(8,128)(2,1)} %copy-done.16) | copy-start | bytes 2359300
  300.8 259.3 %all-gather.6.cloned.1.call-start = ((), (), s32[]{:S(2)}) async-start(), calls=%async_computation.3 | async-start | bytes 2949120 | tf_op jit(solution)/shard_map/all_gather | solution.py:86
  560.2 5.4 copy-start.2
  (20 other events, 60.8 us)
Sparse Core Ops, SparseCore 0:
  12.4 126.7 all-gather.3
  300.9 205.0 reduce-scatter.1
  507.6 23.6 all-gather.5

commit v2 on v1

--- a/solution.py
+++ b/solution.py
@@ -1,23 +1,48 @@
+import functools
+
 import jax
 import jax.numpy as jnp
 from jax import lax
+from jax.experimental import pallas as pl
+from jax.experimental.pallas import tpu as pltpu
 from jax.sharding import PartitionSpec as P
 
 HEADS = 12
 HEAD_DIM = 64
-FF = 3072
 EPS = 1e-12
 F32 = jnp.float32
 LOW = jnp.bfloat16
 AXES = ("fsdp", "dp")
+D = 768
+ROWS = 96
+LINE = 4
+SHARDS = D // ROWS
+QUARTERS = 4
+EXACT = lax.Precision.HIGHEST
+SCALE = HEAD_DIM**-0.5
+VMEM = pl.BlockSpec(memory_space=pltpu.VMEM)
+SMEM = pl.BlockSpec(memory_space=pltpu.SMEM)
+BIG = pltpu.CompilerParams(vmem_limit_bytes=60 * 1024 * 1024)
+
+
+def out(shape, dtype):
+    return jax.ShapeDtypeStruct(shape, dtype)
+
+
+def cost(flops, size):
+    return pl.CostEstimate(flops=int(flops), bytes_accessed=int(size), transcendentals=0)
 
 
 def mm(a, b):
     return jnp.dot(a, b, preferred_element_type=F32)
 
 
-def slopes():
-    return jnp.exp2(-8.0 * (jnp.arange(HEADS, dtype=F32) + 1.0) / HEADS)
+def mm_nt(a, b):
+    return lax.dot_general(a, b, (((1,), (1,)), ((), ())), preferred_element_type=F32)
+
+
+def mm_tn(a, b):
+    return lax.dot_general(a, b, (((0,), (0,)), ((), ())), preferred_element_type=F32)
 
 
 def norm_parts(value):
@@ -33,6 +58,588 @@
         - jnp.mean(scaled, axis=-1, keepdims=True)
         - unit * jnp.mean(scaled * unit, axis=-1, keepdims=True)
     )
+
+
+def onehot(pos_ref, seq, most, length):
+    spots = lax.broadcasted_iota(jnp.int32, (most, length), 1)
+    return spots == pos_ref[pl.ds(seq * most, most), :]
+
+
+def gelu_parts(gate):
+    cdf = 0.5 * (1.0 + lax.erf(gate * (0.5**0.5)))
+    pdf = jnp.exp(-0.5 * gate * gate) * ((2.0 * jnp.pi) ** -0.5)
+    return gate * cdf, cdf + gate * pdf
+
+
+def slope_of(head):
+    return 2.0 ** (-8.0 * (head + 1.0) / HEADS)
+
+
+def block(ref, *index):
+    value = ref[index] if index else ref[...]
+    return value.reshape(-1, value.shape[-1])
+
+
+def attention_kernel(seqs, most, slope_ref, x_ref, w_ref, norm_ref, pos_ref, qkv_ref, h1_ref, att_m_ref, h1_m_ref, q_m_ref, r1_m_ref, att_ref, r1_ref):
+    length = x_ref.shape[0] // seqs
+    step = 256
+
+    @pl.loop(0, 3 * D // step)
+    def _(n):
+        j = n // (D // step)
+        lane = pl.multiple_of((n - j * (D // step)) * step, step)
+        w = w_ref[:, j, :, pl.ds(lane, step)].reshape(D, step)
+        qkv_ref[:, pl.ds(pl.multiple_of(n * step, step), step)] = mm(x_ref[...], w).astype(LOW)
+
+    first = lax.broadcasted_iota(jnp.int32, (length, 128), 1) < HEAD_DIM
+    row = lax.broadcasted_iota(jnp.int32, (length, length), 0)
+    col = lax.broadcasted_iota(jnp.int32, (length, length), 1)
+    away = jnp.abs(row - col).astype(F32)
+
+    @pl.loop(0, HEADS // 2)
+    def _(t):
+        lane = pl.multiple_of(t * 128, 128)
+        for s in range(seqs):
+            rows = slice(s * length, (s + 1) * length)
+            q = qkv_ref[rows, pl.ds(lane, 128)]
+            k = qkv_ref[rows, pl.ds(D + lane, 128)]
+            v = qkv_ref[rows, pl.ds(2 * D + lane, 128)]
+            mixed = []
+            for h in range(2):
+                mine = jnp.where(first if h == 0 else ~first, q, jnp.zeros_like(q))
+                score = mm_nt(mine, k) * SCALE - slope_ref[2 * t + h] * away
+                e = jnp.exp(score - jnp.max(score, axis=-1, keepdims=True))
+                p = (e / jnp.sum(e, axis=-1, keepdims=True)).astype(LOW)
+                mixed.append(mm(p, v))
+            att_ref[rows, pl.ds(lane, 128)] = jnp.where(first, mixed[0], mixed[1]).astype(LOW)
+
+    @pl.loop(0, D // step)
+    def _(n):
+        lane = pl.multiple_of(n * step, step)
+        w = w_ref[:, 3, :, pl.ds(lane, step)].reshape(D, step)
+        r1_ref[:, pl.ds(lane, step)] = x_ref[:, pl.ds(lane, step)].astype(F32) + mm(att_ref[...], w)
+
+    for s in range(seqs):
+        rows = slice(s * length, (s + 1) * length)
+        listed = slice(s * most, (s + 1) * most)
+        unit, _ = norm_parts(r1_ref[rows, :])
+        h1 = unit * norm_ref[0:1, :] + norm_ref[1:2, :]
+        h1_ref[rows, :] = h1
+        hot = onehot(pos_ref, s, most, length)
+        hot_low = hot.astype(LOW)
+        r1_m_ref[listed, :] = jnp.dot(hot.astype(F32), r1_ref[rows, :], precision=EXACT, preferred_element_type=F32)
+        h1_m_ref[listed, :] = mm(hot_low, h1.astype(LOW)).astype(LOW)
+        att_m_ref[listed, :] = mm(hot_low, att_ref[rows, :]).astype(LOW)
+        q_m_ref[listed, :] = mm(hot_low, qkv_ref[rows, 0:D]).astype(LOW)
+
+
+def attention_forward(x, w_attn, norms, pos, slopes, seqs):
+    tokens = x.shape[0]
+    listed = pos.shape[0]
+    return pl.pallas_call(
+        functools.partial(attention_kernel, seqs, listed // seqs),
+        out_shape=(
+            out((tokens, 3 * D), LOW),
+            out((tokens, D), F32),
+            out((listed, D), LOW),
+            out((listed, D), LOW),
+            out((listed, D), LOW),
+            out((listed, D), F32),
+        ),
+        in_specs=[SMEM, VMEM, VMEM, VMEM, VMEM],
+        out_specs=(VMEM,) * 6,
+        scratch_shapes=[pltpu.VMEM((tokens, D), LOW), pltpu.VMEM((tokens, D), F32)],
+        compiler_params=BIG,
+        cost_estimate=cost(2 * tokens * D * 4 * D, 8e6),
+        name="attention_forward",
+    )(slopes, x, w_attn, norms, pos)
+
+
+def ffn_kernel(seqs, most, h1_ref, gate_ref, up_ref, down_ref, norm_ref, pos_ref, dy_ref, y_ref, dr2_ref, e2_ref, small_ref, low_ref, act_ref, acc_ref):
+    j = pl.program_id(0)
+    tokens = h1_ref.shape[0]
+    length = tokens // seqs
+    step = 256
+
+    @pl.when(j == 0)
+    def _():
+        low_ref[...] = h1_ref[...].astype(LOW)
+        acc_ref[...] = h1_ref[...]
+
+    @pl.loop(0, D // step)
+    def _(n):
+        lane = pl.multiple_of(n * step, step)
+        gate = mm(low_ref[...], gate_ref[:, :, pl.ds(lane, step)].reshape(D, step))
+        up = mm(low_ref[...], up_ref[:, :, pl.ds(lane, step)].reshape(D, step))
+        cdf = 0.5 * (1.0 + lax.erf(gate * (0.5**0.5)))
+        act_ref[:, pl.ds(lane, step)] = (gate * cdf * up).astype(LOW)
+
+    @pl.loop(0, D // step)
+    def _(n):
+        lane = pl.multiple_of(n * step, step)
+        acc_ref[:, pl.ds(lane, step)] += mm(act_ref[...], down_ref[:, :, :, pl.ds(lane, step)].reshape(D, step))
+
+    @pl.when(j == QUARTERS - 1)
+    def _():
+        gain = norm_ref[2:3, :]
+        small = [jnp.zeros((1, D), F32)] * 2
+        for s in range(seqs):
+            rows = slice(s * length, (s + 1) * length)
+            listed = slice(s * most, (s + 1) * most)
+            unit, _ = norm_parts(acc_ref[rows, :])
+            y_ref[rows, :] = (unit * gain + norm_ref[3:4, :]).astype(LOW)
+            hot = onehot(pos_ref, s, most, length).astype(F32)
+            picked = jnp.dot(hot, acc_ref[rows, :], precision=EXACT, preferred_element_type=F32)
+            unit_m, rstd_m = norm_parts(picked)
+            dy = dy_ref[listed, :].astype(F32)
+            small = [small[0] + jnp.sum(dy * unit_m, axis=0, keepdims=True), small[1] + jnp.sum(dy, axis=0, keepdims=True)]
+            dr2 = norm_back(dy, unit_m, rstd_m, gain)
+            dr2_ref[listed, :] = dr2
+            e2_ref[listed, :] = dr2.astype(LOW)
+        small_ref[...] = jnp.concatenate(small, axis=0)
+
+
+def ffn_forward(h1, w_ffn, norms, pos, dy, seqs):
+    tokens = h1.shape[0]
+    listed = pos.shape[0]
+    whole = lambda shape: pl.BlockSpec(shape, lambda j: (0,) * len(shape), pipeline_mode=pl.Buffered(1))
+    return pl.pallas_call(
+        functools.partial(ffn_kernel, seqs, listed // seqs),
+        out_shape=(out((tokens, D), LOW), out((listed, D), F32), out((listed, D), LOW), out((2, D), F32)),
+        grid=(QUARTERS,),
+        in_specs=[
+            whole((tokens, D)),
+            pl.BlockSpec((SHARDS, None, None, ROWS, D), lambda j: (0, j, 0, 0, 0)),
+            pl.BlockSpec((SHARDS, None, None, ROWS, D), lambda j: (0, j, 1, 0, 0)),
+            pl.BlockSpec((SHARDS // QUARTERS, QUARTERS, None, ROWS, D), lambda j: (j, 0, 2, 0, 0)),
+            whole(norms.shape),
+            whole(pos.shape),
+            whole(dy.shape),
+        ],
+        out_specs=(
+            pl.BlockSpec((tokens, D), lambda j: (0, 0)),
+            pl.BlockSpec((listed, D), lambda j: (0, 0)),
+            pl.BlockSpec((listed, D), lambda j: (0, 0)),
+            pl.BlockSpec((2, D), lambda j: (0, 0)),
+        ),
+        scratch_shapes=[pltpu.VMEM((tokens, D), LOW), pltpu.VMEM((tokens, D), LOW), pltpu.VMEM((tokens, D), F32)],
+        compiler_params=BIG,
+        cost_estimate=cost(2 * tokens * D * 12 * D, 18e6),
+        name="ffn_forward",
+    )(h1, w_ffn, w_ffn, w_ffn, norms, pos, dy)
+
+
+def ffn_again_kernel(where_ref, h_ref, gate_ref, up_ref, act_ref, to_gate_ref, to_up_ref):
+    step = 256
+
+    @pl.loop(0, D // step)
+    def _(n):
+        lane = pl.multiple_of(n * step, step)
+        rows = block(h_ref)
+        gate = mm(rows, gate_ref[:, :, pl.ds(lane, step)].reshape(D, step))
+        up = mm(rows, up_ref[:, :, pl.ds(lane, step)].reshape(D, step))
+        value, slope = gelu_parts(gate)
+        act_ref[:, pl.ds(lane, step)] = (value * up).astype(LOW)
+        to_gate_ref[:, pl.ds(lane, step)] = slope * up
+        to_up_ref[:, pl.ds(lane, step)] = value
+
+
+def quarter_specs(which):
+    specs = {
+        "gate": pl.BlockSpec((SHARDS, None, None, ROWS, D), lambda g, w: (0, w[4], 0, 0, 0)),
+        "up": pl.BlockSpec((SHARDS, None, None, ROWS, D), lambda g, w: (0, w[4], 1, 0, 0)),
+        "down": pl.BlockSpec((SHARDS // QUARTERS, QUARTERS, None, ROWS, D), lambda g, w: (w[4], 0, 2, 0, 0)),
+    }
+    return [specs[name] for name in which]
+
+
+def at_once(shape):
+    return pl.BlockSpec(shape, lambda g, w: (0,) * len(shape))
+
+
+def ffn_again(where, h_all, w_ffn):
+    rows = h_all.shape[0] * h_all.shape[1]
+    return pl.pallas_call(
+        ffn_again_kernel,
+        out_shape=(out((rows, D), LOW), out((rows, D), F32), out((rows, D), F32)),
+        grid_spec=pltpu.PrefetchScalarGridSpec(
+            num_scalar_prefetch=1,
+            grid=(1,),
+            in_specs=[at_once(h_all.shape), *quarter_specs(["gate", "up"])],
+            out_specs=(at_once((rows, D)),) * 3,
+        ),
+        compiler_params=BIG,
+        cost_estimate=cost(4 * rows * D * D, 8e6),
+        name="ffn_again",
+    )(where, h_all, w_ffn, w_ffn)
+
+
+def ffn_back_kernel(where_ref, e_ref, to_gate_ref, to_up_ref, gate_ref, up_ref, down_ref, dgate_ref, dup_ref, keep_ref, send_ref):
+    listed = e_ref.shape[1]
+    half = QUARTERS // 2
+    for n in range(SHARDS // QUARTERS):
+        lanes = slice(n * QUARTERS * ROWS, (n + 1) * QUARTERS * ROWS)
+        dact = mm_nt(block(e_ref), block(down_ref, n))
+        dgate_ref[:, lanes] = (dact * to_gate_ref[:, lanes]).astype(LOW)
+        dup_ref[:, lanes] = (dact * to_up_ref[:, lanes]).astype(LOW)
+    for n in range(2):
+        shards = slice(n * SHARDS // 2, (n + 1) * SHARDS // 2)
+        lanes = slice(n * D // 2, (n + 1) * D // 2)
+        part = mm_nt(dgate_ref[...], block(gate_ref, shards)) + mm_nt(dup_ref[...], block(up_ref, shards))
+        for r in range(half):
+            keep_ref[r, :, lanes] = part[2 * r * listed : (2 * r + 1) * listed]
+            send_ref[r, :, lanes] = part[(2 * r + 1) * listed : (2 * r + 2) * listed].astype(LOW)
+
+
+def ffn_back(where, e_all, to_gate, to_up, w_ffn):
+    count, listed, _ = e_all.shape
+    rows = count * listed
+    return pl.pallas_call(
+        ffn_back_kernel,
+        out_shape=(out((rows, D), LOW), out((rows, D), LOW), out((count // 2, listed, D), F32), out((count // 2, listed, D), LOW)),
+        grid_spec=pltpu.PrefetchScalarGridSpec(
+            num_scalar_prefetch=1,
+            grid=(1,),
+            in_specs=[at_once(e_all.shape), at_once((rows, D)), at_once((rows, D)), *quarter_specs(["gate", "up", "down"])],
+            out_specs=(at_once((rows, D)), at_once((rows, D)), at_once((count // 2, listed, D)), at_once((count // 2, listed, D))),
+        ),
+        compiler_params=BIG,
+        cost_estimate=cost(6 * rows * D * D, 12e6),
+        name="ffn_back",
+    )(where, e_all, to_gate, to_up, w_ffn, w_ffn, w_ffn)
+
+
+def weight_grad_kernel(where_ref, a_ref, b_ref, keep_ref, send_ref, full_ref):
+    z, y = where_ref[0], where_ref[1]
+    a = block(a_ref)
+    step = 256
+
+    @pl.loop(0, D // step)
+    def _(n):
+        lane = pl.multiple_of(n * step, step)
+        full_ref[:, pl.ds(lane, step)] = mm_tn(a, block(b_ref, *([slice(None)] * (len(b_ref.shape) - 1)), pl.ds(lane, step)))
+
+    for r in range(LINE):
+        base = 2 * lax.rem(z + r, LINE)
+        for other, ref in ((0, keep_ref), (1, send_ref)):
+            start = (base + (y if other == 0 else 1 - y)) * ROWS
+            ref[r] = full_ref[pl.ds(pl.multiple_of(start, 8), ROWS), :].astype(LOW)
+
+
+def weight_grad(where, a, b):
+    shape = (LINE, ROWS, D)
+    rows = a.size // D
+    return pl.pallas_call(
+        weight_grad_kernel,
+        out_shape=(out(shape, LOW), out(shape, LOW)),
+        in_specs=[SMEM, VMEM, VMEM],
+        out_specs=(VMEM, VMEM),
+        scratch_shapes=[pltpu.VMEM((D, D), F32)],
+        compiler_params=BIG,
+        cost_estimate=cost(2 * rows * D * D, 4e6),
+        name="weight_grad",
+    )(where, a, b)
+
+
+def attention_back_kernel(seqs, most, slope_ref, dr2_ref, part_ref, came_ref, r1_ref, q_ref, qkv_ref, att_ref, w_ref, norm_ref, pos_ref, dr1_ref, rhs_ref, lhs_ref, small_ref, datt_ref):
+    length = qkv_ref.shape[0] // seqs
+    listed = seqs * most
+    dh1 = dr2_ref[...] + part_ref[...] + came_ref[...].astype(F32)
+    unit, rstd = norm_parts(r1_ref[...])
+    small_ref[0:1, :] = jnp.sum(dh1 * unit, axis=0, keepdims=True)
+    small_ref[1:2, :] = jnp.sum(dh1, axis=0, keepdims=True)
+    dr1 = norm_back(dh1, unit, rstd, norm_ref[0:1, :])
+    dr1_ref[...] = dr1
+    low = dr1.astype(LOW)
+    rhs_ref[0:listed, 3 * D : 4 * D] = low
+    rhs_ref[listed:, 3 * D : 4 * D] = jnp.zeros((seqs * length - listed, D), LOW)
+    lhs_ref[0:listed, :] = att_ref[...]
+    lhs_ref[listed:, :] = jnp.zeros((seqs * length - listed, D), LOW)
+    for n in range(2):
+        lanes = slice(n * D // 2, (n + 1) * D // 2)
+        datt_ref[:, lanes] = mm_nt(low, block(w_ref, slice(n * SHARDS // 2, (n + 1) * SHARDS // 2), 3)).astype(LOW)
+    first = lax.broadcasted_iota(jnp.int32, (length, 128), 1) < HEAD_DIM
+    first_m = lax.broadcasted_iota(jnp.int32, (most, 128), 1) < HEAD_DIM
+    spots = lax.broadcasted_iota(jnp.int32, (most, length), 1)
+
+    @pl.loop(0, HEADS // 2)
+    def _(t):
+        lane = pl.multiple_of(t * 128, 128)
+        for s in range(seqs):
+            rows = slice(s * length, (s + 1) * length)
+            mine = slice(s * most, (s + 1) * most)
+            at = pos_ref[mine, :]
+            away = jnp.abs(at - spots).astype(F32)
+            hot = (spots == at).astype(LOW)
+            q = q_ref[mine, pl.ds(lane, 128)]
+            da = datt_ref[mine, pl.ds(lane, 128)]
+            k = qkv_ref[rows, pl.ds(D + lane, 128)]
+            v = qkv_ref[rows, pl.ds(2 * D + lane, 128)]
+            dq, dk, dv = [], [], []
+            for h in range(2):
+                pick = first_m if h == 0 else ~first_m
+                score = mm_nt(jnp.where(pick, q, jnp.zeros_like(q)), k) * SCALE - slope_ref[2 * t + h] * away
+                e = jnp.exp(score - jnp.max(score, axis=-1, keepdims=True))
+                p = e / jnp.sum(e, axis=-1, keepdims=True)
+                dp = mm_nt(jnp.where(pick, da, jnp.zeros_like(da)), v)
+                ds = (p * (dp - jnp.sum(dp * p, axis=-1, keepdims=True))).astype(LOW)
+                dv.append(mm_tn(p.astype(LOW), da))
+                dq.append(mm(ds, k))
+                dk.append(mm_tn(ds, q))
+            dq = (jnp.where(first_m, dq[0], dq[1]) * SCALE).astype(LOW)
+            rhs_ref[rows, pl.ds(lane, 128)] = mm_tn(hot, dq).astype(LOW)
+            rhs_ref[rows, pl.ds(D + lane, 128)] = (jnp.where(first, dk[0], dk[1]) * SCALE).astype(LOW)
+            rhs_ref[rows, pl.ds(2 * D + lane, 128)] = jnp.where(first, dv[0], dv[1]).astype(LOW)
+
+
+def attention_back(dr2, part, came, r1_m, q_m, qkv, att_m, w_attn, norms, pos, slopes, seqs):
+    tokens = qkv.shape[0]
+    listed = pos.shape[0]
+    return pl.pallas_call(
+        functools.partial(attention_back_kernel, seqs, listed // seqs),
+        out_shape=(out((listed, D), F32), out((tokens, 4 * D), LOW), out((tokens, D), LOW), out((2, D), F32)),
+        in_specs=[SMEM] + [VMEM] * 10,
+        out_specs=(VMEM,) * 4,
+        scratch_shapes=[pltpu.VMEM((listed, D), LOW)],
+        compiler_params=BIG,
+        cost_estimate=cost(2 * listed * D * D * 2, 12e6),
+        name="attention_back",
+    )(slopes, dr2, part, came, r1_m, q_m, qkv, att_m, w_attn, norms, pos)
+
+
+def attention_grads_kernel(where_ref, x_ref, lhs_ref, rhs_ref, keep0_ref, keep1_ref, send0_ref, send1_ref, full_ref):
+    z, y, mine = where_ref[0], where_ref[1], where_ref[4]
+    half = ROWS // 2
+    step = 256
+    for rc in (1, 0):
+        for rx in (0, 1):
+            r = 2 * rx + rc
+            j = (mine + r) if False else jnp.bitwise_xor(mine, r)
+            is_out = j == 3
+
+            def fill(a_ref):
+                @pl.loop(0, D // step)
+                def _(n):
+                    lane = pl.multiple_of(n * step, step)
+                    cols = pl.ds(pl.multiple_of(j * D + n * step, step), step)
+                    full_ref[:, pl.ds(lane, step)] = mm_tn(a_ref[...], rhs_ref[:, cols])
+
+            @pl.when(is_out)
+            def _():
+                fill(lhs_ref)
+
+            @pl.when(jnp.logical_not(is_out))
+            def _():
+                fill(x_ref)
+
+            refs = (keep0_ref, keep1_ref) if rc == 0 else (send0_ref, send1_ref)
+            for rz in range(LINE):
+                base = 2 * lax.rem(z + rz, LINE)
+                for ry in (0, 1):
+                    start = (base + (y if ry == 0 else 1 - y)) * ROWS
+                    for part in (0, 1):
+                        rows = pl.ds(pl.multiple_of(start + part * half, 8), half)
+                        value = full_ref[rows, :].astype(LOW)
+                        if part == 0:
+                            refs[0][rx, ry, rz] = value
+                        else:
+                            refs[1][ry, rx, rz] = value
+
+
+def attention_grads(where, x, lhs, rhs):
+    shape = (2, 2, LINE, ROWS // 2, D)
+    return pl.pallas_call(
+        attention_grads_kernel,
+        out_shape=(out(shape, LOW),) * 4,
+        in_specs=[SMEM, VMEM, VMEM, VMEM],
+        out_specs=(VMEM,) * 4,
+        scratch_shapes=[pltpu.VMEM((D, D), F32)],
+        compiler_params=BIG,
+        cost_estimate=cost(2 * x.shape[0] * D * 4 * D, 10e6),
+        name="attention_grads",
+    )(where, x, lhs, rhs)
+
+
+def input_grad_kernel(seqs, rhs_ref, w_ref, dr1_ref, pos_ref, out_ref):
+    length = out_ref.shape[0] // seqs
+    most = dr1_ref.shape[0] // seqs
+    for n in range(2):
+        lanes = slice(n * D // 2, (n + 1) * D // 2)
+        shards = slice(n * SHARDS // 2, (n + 1) * SHARDS // 2)
+        total = mm_nt(rhs_ref[:, 0:D], block(w_ref, shards, 0))
+        total += mm_nt(rhs_ref[:, D : 2 * D], block(w_ref, shards, 1))
+        total += mm_nt(rhs_ref[:, 2 * D : 3 * D], block(w_ref, shards, 2))
+        for s in range(seqs):
+            rows = slice(s * length, (s + 1) * length)
+            hot = (lax.broadcasted_iota(jnp.int32, (length, most), 0) == pos_ref[s : s + 1, :]).astype(F32)
+            spread = jnp.dot(hot, dr1_ref[s * most : (s + 1) * most, lanes], precision=EXACT, preferred_element_type=F32)
+            out_ref[rows, lanes] = total[rows] + spread
+
+
+def input_grad(rhs, w_attn, dr1, positions):
+    tokens = rhs.shape[0]
+    return pl.pallas_call(
+        functools.partial(input_grad_kernel, positions.shape[0]),
+        out_shape=out((tokens, D), F32),
+        in_specs=[VMEM] * 4,
+        out_specs=VMEM,
+        compiler_params=BIG,
+        cost_estimate=cost(2 * tokens * D * 3 * D, 10e6),
+        name="input_grad",
+    )(rhs, w_attn, dr1, positions)
+
+
+def place(z, y, x, c):
+    return (2 * z + y) * 4 + 2 * x + c
+
+
+def grid_perm(move):
+    return [
+        (place(z, y, x, c), place(*move(z, y, x, c)))
+        for z in range(4)
+        for y in range(2)
+        for x in range(2)
+        for c in range(2)
+    ]
+
+
+MOVES = {
+    "x": grid_perm(lambda z, y, x, c: (z, y, 1 - x, c)),
+    "y": grid_perm(lambda z, y, x, c: (z, 1 - y, x, c)),
+    "c": grid_perm(lambda z, y, x, c: (z, y, x, 1 - c)),
+    1: grid_perm(lambda z, y, x, c: ((z + 1) % 4, y, x, c)),
+    2: grid_perm(lambda z, y, x, c: ((z + 2) % 4, y, x, c)),
+    3: grid_perm(lambda z, y, x, c: ((z + 3) % 4, y, x, c)),
+    "down": [(m * 4 + q, (2 * q + m // 4) * 4 + m % 4) for m in range(8) for q in range(4)],
+}
+
+
+def send(value, move):
+    return lax.ppermute(value, AXES, MOVES[move])
+
+
+def share_dp(value):
+    core = send(value, "c")
+    return value, core, send(value, "x"), send(core, "x")
+
+
+def line_sum(block_list, kept):
+    total = kept.astype(F32)
+    for r, value in block_list:
+        total = total + send(value, r).astype(F32)
+    return total
+
+
+def reduce_quarter(keep, away):
+    got = send(away, "y")
+    total = keep.astype(F32) + got.astype(F32)
+    return line_sum([(r, total[r].astype(LOW)) for r in (1, 2, 3)], total[0]).astype(LOW)
+
+
+def reduce_attention(keep, away, first, second):
+    total = keep.astype(F32) + send(away, "c").astype(F32)
+    total = total[0] + send(total[1].astype(LOW), first).astype(F32)
+    total = total[0] + send(total[1].astype(LOW), second).astype(F32)
+    return line_sum([(r, total[r].astype(LOW)) for r in (1, 2, 3)], total[0]).astype(LOW)
+
+
+def finish_kernel(rows_out, where_ref, a_ref, b_ref, c_ref, d_ref, *rest):
+    outs, held = rest[:-1], rest[-1]
+    mine = where_ref[4]
+    for r, ref in enumerate((a_ref, b_ref, c_ref, d_ref)):
+        held[jnp.bitwise_xor(mine, r)] = ref[...].astype(F32)
+    if rows_out:
+        for j in range(QUARTERS):
+            outs[0][j * ROWS : (j + 1) * ROWS, :] = held[j]
+    else:
+        at = 0
+        for ref in outs:
+            for j in range(ref.shape[1] // D):
+                ref[:, j * D : (j + 1) * D] = held[at]
+                at += 1
+
+
+def finish(where, pieces, widths, rows_out=False):
+    shapes = [out((QUARTERS * ROWS, D), F32)] if rows_out else [out((ROWS, n * D), F32) for n in widths]
+    return pl.pallas_call(
+        functools.partial(finish_kernel, rows_out),
+        out_shape=tuple(shapes),
+        in_specs=[SMEM] + [VMEM] * 4,
+        out_specs=(VMEM,) * len(shapes),
+        scratch_shapes=[pltpu.VMEM((QUARTERS, ROWS, D), F32)],
+        compiler_params=BIG,
+        cost_estimate=cost(1e5, 2e6),
+        name="finish",
+    )(where, *pieces)
+
+
+def on_block(hidden_in, w_qkv, w_out, w_up, w_down, gain_attn, shift_attn, gain_ffn, shift_ffn, grad_listed, positions, counts):
+    seqs, length, width = hidden_in.shape
+    tokens = seqs * length
+    most = positions.shape[1]
+    i, j = lax.axis_index("fsdp"), lax.axis_index("dp")
+    where = jnp.stack([i // 2, i % 2, j // 2, j % 2, j]).astype(jnp.int32)
+    ff = w_down.shape[0] * SHARDS
+    attn_piece = lax.dynamic_slice_in_dim(jnp.concatenate([w_qkv, w_out], axis=1), j * D, D, axis=1)
+    w_attn = lax.all_gather(attn_piece, AXES, axis=0, tiled=False).reshape(SHARDS, QUARTERS, ROWS, D)
+    ffn_piece = jnp.stack(
+        [
+            lax.dynamic_slice_in_dim(w_up, j * D, D, axis=1),
+            lax.dynamic_slice_in_dim(w_up, ff + j * D, D, axis=1),
+            lax.dynamic_slice_in_dim(w_down, j * ROWS, ROWS, axis=0),
+        ]
+    )
+    w_ffn = lax.all_gather(ffn_piece, AXES, axis=0, tiled=False).reshape(SHARDS, QUARTERS, 3, ROWS, D)
+    norms = jnp.stack([gain_attn, shift_attn, gain_ffn, shift_ffn])
+    norms = lax.all_gather(norms, "fsdp", axis=1, tiled=True).astype(F32)
+    slopes = jnp.exp2(-8.0 * (jnp.arange(HEADS, dtype=F32) + 1.0) / HEADS)
+    x = hidden_in.reshape(tokens, width)
+    pos = positions.reshape(seqs * most, 1)
+    live = jnp.arange(most, dtype=jnp.int32)[None, :] < counts[:, None]
+    dy = jnp.where(live[:, :, None], grad_listed, jnp.zeros_like(grad_listed)).reshape(seqs * most, width)
+
+    qkv, h1, att_m, h1_m, q_m, r1_m = attention_forward(x, w_attn, norms, pos, slopes, seqs)
+    h_all = jnp.stack(share_dp(h1_m))
+    layer_out, dr2, e2, small_ffn = ffn_forward(h1, w_ffn, norms, pos, dy, seqs)
+    act, to_gate, to_up = ffn_again(where, h_all, w_ffn)
+    e_all = jnp.stack(share_dp(e2))
+    dgate, dup, keep, away = ffn_back(where, e_all, to_gate, to_up, w_ffn)
+    total = keep + send(away, "c").astype(F32)
+    came = send(total[1].astype(LOW), "x")
+    g_down = reduce_quarter(*weight_grad(where, act, e_all))
+    g_gate = reduce_quarter(*weight_grad(where, h_all, dgate))
+    g_up = reduce_quarter(*weight_grad(where, h_all, dup))
+    dr1, rhs, lhs, small_attn = attention_back(dr2, total[0], came, r1_m, q_m, qkv, att_m, w_attn, norms, pos, slopes, seqs)
+    keep0, keep1, away0, away1 = attention_grads(where, x, lhs, rhs)
+    g_attn = jnp.concatenate(
+        [reduce_attention(keep0, away0, "x", "y"), reduce_attention(keep1, away1, "y", "x")], axis=0
+    )
+    grad_in = input_grad(rhs, w_attn, dr1, positions)
+    (grad_down,) = finish(where, share_dp(send(g_down, "down")), (), rows_out=True)
+    (grad_gate,) = finish(where, share_dp(g_gate), (QUARTERS,))
+    (grad_up,) = finish(where, share_dp(g_up), (QUARTERS,))
+    grad_qkv, grad_out = finish(where, share_dp(g_attn), (3, 1))
+    small = lax.psum(jnp.concatenate([small_attn, small_ffn]), AXES)
+    small = lax.dynamic_slice_in_dim(small, i * ROWS, ROWS, axis=1)
+    return (
+        layer_out.reshape(seqs, length, width),
+        grad_in.reshape(seqs, length, width),
+        grad_qkv,
+        grad_out,
+        jnp.concatenate([grad_gate, grad_up], axis=1),
+        grad_down,
+        small[0],
+        small[1],
+        small[2],
+        small[3],
+    )
+
+
+FF = 3072
+
+
+def slopes():
+    return jnp.exp2(-8.0 * (jnp.arange(HEADS, dtype=F32) + 1.0) / HEADS)
 
 
 def pick(onehot, rows):
@@ -185,8 +792,10 @@
     rows3 = P(("fsdp", "dp"), None, None)
     rows2 = P("fsdp", None)
     rows1 = P("fsdp")
+    shape = dict(mesh.shape)
+    step = on_block if shape == {"fsdp": SHARDS, "dp": QUARTERS} else on_device
     return jax.shard_map(
-        on_device,
+        step,
         mesh=mesh,
         in_specs=(rows3, rows2, rows2, rows2, rows2, rows1, rows1, rows1, rows1, rows3, P(("fsdp", "dp"), None), P(("fsdp", "dp"))),
         out_specs=(rows3, rows3, rows2, rows2, rows2, rows2, rows1, rows1, rows1, rows1),

time: 586 us -> 441 us (0.75); the launches traced: 576 us -> 440 us
  waiting for transfers between devices: 304 us -> 165 us
  Pallas kernels: 0 us -> 124 us
  matrix products: 94.3 us -> 0 us
  local copies, waits for them, and re-layouts: 68.5 us -> 11.1 us
  starting transfers between devices: 0.12 us -> 52.1 us
  other arithmetic: 30.7 us -> 11.2 us
    reduce_scatter x1 -> x0, waiting for transfers between devices: 205 us -> none  [scatter_grads(): mine = lax.psum_scatter(joined, AXES, scatter_dimension=0, tiled=True)]
    pallas_call x0 -> x14, Pallas kernels: none -> 124 us  [the longest x1 28 us: attention_back(): pl.pallas_call(functools.partial(attention_back_kernel, seqs, listed // s...]
    dot_general x27 -> x0, matrix products: 94.3 us -> none  [the longest x5 48.2 us: mm(): return jnp.dot(a, b, preferred_element_type=F32)]
    ppermute x0 -> x45, starting transfers between devices: none -> 52 us  [send(): return lax.ppermute(value, AXES, MOVES[move])]
    ppermute x0 -> x45, waiting for transfers between devices: none -> 45.3 us  [send(): return lax.ppermute(value, AXES, MOVES[move])]
    all_gather x2, waiting for transfers between devices: 99 us -> 120 us  [the longest x1 78.3 us: on_block(): lax.all_gather(ffn_piece, AXES, axis=0, tiled=False)]
    reshape x6 -> x1, local copies, waits for them, and re-layouts: 17.6 us -> 0.72 us  [on_block(): pos = positions.reshape(seqs * most, 1)]
    slice x9 -> x0, local copies, waits for them, and re-layouts: 12.3 us -> none  [the longest x1 4.81 us: gather_weights(): full_down = full[:, c:].reshape(fsdp * dp, part, group, width)]
  transfers between devices with their start and end apart: 3 -> 47, of which waited for: 2 -> 14; matrix products, arithmetic and copies ran while one was open for 3% -> 3% of each run, Pallas kernels for 0% -> 26%
where the time goes in v2:
time: 441 us; the launch traced here: 440 us
  waiting for transfers between devices  165 us (37%)
  Pallas kernels  124 us (28%)
  blocking collectives  61.6 us (14%)
  starting transfers between devices  52.1 us (12%)
  between operations  14.7 us (3%)
  other arithmetic  11.2 us (3%)
  local copies, waits for them, and re-layouts  11.1 us (3%)
    all_gather x1, waiting for transfers between devices, on_block(): lax.all_gather(ffn_piece, AXES, axis=0, tiled=False)  78.3 us
    ppermute x45, starting transfers between devices, send(): return lax.ppermute(value, AXES, MOVES[move])  52 us
    ppermute x45, waiting for transfers between devices, send(): return lax.ppermute(value, AXES, MOVES[move])  45.3 us
    all_gather x1, waiting for transfers between devices, on_block(): lax.all_gather(attn_piece, AXES, axis=0, tiled=False)  41.7 us
    psum x1, blocking collectives, on_block(): small = lax.psum(jnp.concatenate([small_attn, small_ffn]), AXES)  39.3 us
    pallas_call x1, Pallas kernels, attention_back(): pl.pallas_call(functools.partial(attention_back_kernel, seqs, listed // s...  28 us
    pallas_call x1, Pallas kernels, attention_forward(): pl.pallas_call(functools.partial(attention_kernel, seqs, listed // seqs),...  25.9 us
    all_gather x1, blocking collectives, on_block(): norms = lax.all_gather(norms, 'fsdp', axis=1, tiled=True).astype(F32)  22.3 us
  transfers between devices with their start and end apart: 47, of which 14 were waited for; matrix products, arithmetic and copies ran while one was open for 3% of the time, Pallas kernels for 26%

profile of v2, /device:TPU:0, one launch (start us, length us, event | category | flops | bytes accessed | tf_op | source)
XLA Modules:
  0.0 440.4 jit_solution(5486992897506449036)
XLA Ops:
  11.1 22.3 %all-gather.2 = bf16[8,96,4]{1,2,0:T(4,128)(2,1)S(1)} all-gather(bf16[1,96,4]{1,2,0:T(4,128)(2,1)S(1)} %maximum_bitcast_fusion), channel_id=1, replica_groups=mesh['fsdp'=8,'dp'=4] {'fsdp'}, dimensions={0}, use_global_device_ids=true | all-gather | bytes 6912 | tf_op jit(solution)/shard_map/all_gather | solution.py:594
  36.2 41.7 %all-gather.6.cloned.1.call-done = bf16[3072,768]{1,0:T(8,128)(2,1)} async-done(((bf16[96,768]{1,0:T(8,128)(2,1)}), bf16[3072,768]{1,0:T(8,128)(2,1)}) %all-gather.6.cloned.1.call-update) | async-done | bytes 4718608 | tf_op jit(solution)/shard_map/all_gather | solution.py:584
  77.9 25.9 %attention_forward.1 = (bf16[512,2304]{1,0:T(8,128)(2,1)}, f32[512,768]{1,0:T(8,128)}, bf16[128,768]{1,0:T(8,128)(2,1)}, bf16[128,768]{1,0:T(8,128)(2,1)}, bf16[128,768]{1,0:T(8,128)(2,1)}, /*index=5*/f32[128,768]{1,0:T(8,128)}) custom-call(f32[12]{0:T(128)} %multiply_exponential_fusion.slope_ref, bf16[512,768]{1,0:T(8,128)(2,1)} %bitcast.182, ...), custom_call_target="tpu_custom_call" | custom-call | flops 2415919104 | bytes 8000000 | tf_op jit(solution)/shard_map/attention_forward/pallas_call | solution.py:139
  104.0 78.3 %all-gather.8.cloned.1.call-done = bf16[96,96,768]{2,1,0:T(8,128)(2,1)} async-done(((bf16[3,96,768]{2,1,0:T(8,128)(2,1)}), bf16[96,96,768]{2,1,0:T(8,128)(2,1)}) %all-gather.8.cloned.1.call-update) | async-done | bytes 14155792 | tf_op jit(solution)/shard_map/all_gather | solution.py:592
  182.3 17.0 %ffn_forward.1 = (bf16[512,768]{1,0:T(8,128)(2,1)}, f32[128,768]{1,0:T(8,128)}, bf16[128,768]{1,0:T(8,128)(2,1)}, f32[2,768]{1,0:T(2,128)}) custom-call(f32[512,768]{1,0:T(8,128)} %get-tuple-element.43.h1_ref, bf16[8,4,3,96,768]{4,3,2,1,0:T(8,128)(2,1)} %bitcast.154, bf16[8,4,3,96,768]{4,3,2,1,0:T(8,128)(2,1)} %bitcast.155, ...), custom_call_target="tpu_custom_call" | custom-call | flops 7247757312 | bytes 18000000 | tf_op jit(solution)/shard_map/ffn_forward/pallas_call | solution.py:206
  207.4 4.2 collective-permute-done.5
  212.6 6.7 %ffn_again.1 = (bf16[512,768]{1,0:T(8,128)(2,1)}, f32[512,768]{1,0:T(8,128)}, f32[512,768]{1,0:T(8,128)}) custom-call(s32[5]{0:T(128)} %stack.89.where_ref, bf16[4,128,768]{2,1,0:T(8,128)(2,1)} %pad_maximum_fusion.2.h_ref.a_ref, bf16[8,4,3,96,768]{4,3,2,1,0:T(8,128)(2,1)} %bitcast.157, bf16[8,4,3,96,768]{4,3,2,1,0:T(8,128)(2,1)} %bitcast.158), custom_call_target="tpu_custom_call" | custom-call | flops 1207959552 | bytes 8000000 | tf_op jit(solution)/shard_map/ffn_again/pallas_call | solution.py:262
  220.3 7.4 %ffn_back.1 = (bf16[512,768]{1,0:T(8,128)(2,1)}, bf16[512,768]{1,0:T(8,128)(2,1)}, f32[2,128,768]{2,1,0:T(8,128)}, bf16[2,128,768]{2,1,0:T(8,128)(2,1)}) custom-call(s32[5]{0:T(128)} %stack.89.where_ref, bf16[4,128,768]{2,1,0:T(8,128)(2,1)} %pad_maximum_fusion.1.e_ref.b_ref, f32[512,768]{1,0:T(8,128)} %get-tuple-element.48.to_gate_ref, ...), custom_call_target="tpu_custom_call" | custom-call | flops 1811939328 | bytes 12000000 | tf_op jit(solution)/shard_map/ffn_back/pallas_call | solution.py:297
  227.7 3.9 weight_grad.5
  233.0 3.9 weight_grad.3
  237.4 3.8 weight_grad.4
  244.3 3.7 collective-permute-done.37
  253.4 28.0 %attention_back.1 = (f32[128,768]{1,0:T(8,128)}, bf16[512,3072]{1,0:T(8,128)(2,1)}, bf16[512,768]{1,0:T(8,128)(2,1)}, f32[2,768]{1,0:T(2,128)}) custom-call(f32[12]{0:T(128)} %multiply_exponential_fusion.slope_ref, f32[128,768]{1,0:T(8,128)} %get-tuple-element.45.dr2_ref, f32[128,768]{1,0:T(8,128)} %slice_bitcast_fusion.4.part_ref, ...), custom_call_target="tpu_custom_call" | custom-call | flops 301989888 | bytes 12000000 | tf_op jit(solution)/shard_map/attention_back/pallas_call | solution.py:398
  282.1 39.3 %psum.7 = f32[4,768]{1,0:T(4,128)S(1)} all-reduce(f32[4,768]{1,0:T(4,128)S(1)} %pad_maximum_fusion.5), channel_id=1, replica_groups=mesh['fsdp'=8,'dp'=4] {'fsdp','dp'}, use_global_device_ids=true, to_apply=%region_0.1 | all-reduce | flops 3072 | bytes 24576 | tf_op jit(solution)/shard_map/psum | solution.py:622
  321.5 10.2 %attention_grads.1 = (bf16[2,2,4,48,768]{4,3,2,1,0:T(8,128)(2,1)}, bf16[2,2,4,48,768]{4,3,2,1,0:T(8,128)(2,1)}, bf16[2,2,4,48,768]{4,3,2,1,0:T(8,128)(2,1)}, bf16[2,2,4,48,768]{4,3,2,1,0:T(8,128)(2,1)}) custom-call(s32[5]{0:T(128)} %stack.89.where_ref, bf16[512,768]{1,0:T(8,128)(2,1)} %bitcast.183, bf16[512,768]{1,0:T(8,128)(2,1)} %get-tuple-element.58.lhs_ref, ...), custom_call_target="tpu_custom_call" | custom-call | flops 2415919104 | bytes 10000000 | tf_op jit(solution)/shard_map/attention_grads/pallas_call | solution.py:451
  338.2 4.7 %collective-permute-done.24 = bf16[96,768]{1,0:T(8,128)(2,1)S(1)} collective-permute-done((bf16[96,768]{1,0:T(8,128)(2,1)S(1)}, bf16[96,768]{1,0:T(8,128)(2,1)S(1)}, u32[]{:S(2)}, u32[]{:S(2)}) %collective-permute-start.24) | collective-permute-done | bytes 147488 | tf_op jit(solution)/shard_map/ppermute | solution.py:518
  347.0 8.1 %collective-permute-done.25 = bf16[96,768]{1,0:T(8,128)(2,1)S(1)} collective-permute-done((bf16[96,768]{1,0:T(8,128)(2,1)S(1)}, bf16[96,768]{1,0:T(8,128)(2,1)S(1)}, u32[]{:S(2)}, u32[]{:S(2)}) %collective-permute-start.25) | collective-permute-done | bytes 147488 | tf_op jit(solution)/shard_map/ppermute | solution.py:518
  356.3 5.7 %collective-permute-start.9 = (bf16[2,4,48,768]{3,2,1,0:T(8,128)(2,1)S(1)}, bf16[2,4,48,768]{3,2,1,0:T(8,128)(2,1)S(1)}, u32[]{:S(2)}, u32[]{:S(2)}) collective-permute-start(bf16[2,4,48,768]{3,2,1,0:T(8,128)(2,1)S(1)} %fusion.2), channel_id=1, source_target_pairs={{0,2},{1,3},{2,0},{3,1},{4,6},{5,7},{6,4},{7,5},{8,10},{9,11},{10,... | collective-permute-start | bytes 1769480 | tf_op jit(solution)/shard_map/ppermute | solution.py:518
  362.5 4.6 %collective-permute-done.32 = bf16[96,768]{1,0:T(8,128)(2,1)S(1)} collective-permute-done((bf16[96,768]{1,0:T(8,128)(2,1)S(1)}, bf16[96,768]{1,0:T(8,128)(2,1)S(1)}, u32[]{:S(2)}, u32[]{:S(2)}) %collective-permute-start.32) | collective-permute-done | bytes 147488 | tf_op jit(solution)/shard_map/ppermute | solution.py:518
  367.2 6.4 %collective-permute-done.9 = bf16[2,4,48,768]{3,2,1,0:T(8,128)(2,1)S(1)} collective-permute-done((bf16[2,4,48,768]{3,2,1,0:T(8,128)(2,1)S(1)}, bf16[2,4,48,768]{3,2,1,0:T(8,128)(2,1)S(1)}, u32[]{:S(2)}, u32[]{:S(2)}) %collective-permute-start.9) | collective-permute-done | bytes 589856 | tf_op jit(solution)/shard_map/ppermute | solution.py:518
  380.0 4.4 %collective-permute-done.10 = bf16[4,48,768]{2,1,0:T(8,128)(2,1)S(1)} collective-permute-done((bf16[4,48,768]{2,1,0:T(8,128)(2,1)S(1)}, bf16[4,48,768]{2,1,0:T(8,128)(2,1)S(1)}, u32[]{:S(2)}, u32[]{:S(2)}) %collective-permute-start.10) | collective-permute-done | bytes 294944 | tf_op jit(solution)/shard_map/ppermute | solution.py:518
  391.9 3.6 collective-permute-start.19
  396.1 3.6 collective-permute-start.28
  404.9 8.3 %input_grad.1 = f32[512,768]{1,0:T(8,128)} custom-call(bf16[512,3072]{1,0:T(8,128)(2,1)} %get-tuple-element.56.rhs_ref, bf16[8,4,96,768]{3,2,1,0:T(8,128)(2,1)} %bitcast.164, f32[128,768]{1,0:T(8,128)} %get-tuple-element.57.dr1_ref, s32[4,32]{1,0:T(4,128)} %pos_ref.1), custom_call_target="tpu_custom_call" | custom-call | flops 1811939328 | bytes 10000000 | tf_op jit(solution)/shard_map/input_grad/pallas_call | solution.py:481
  (207 shorter events, 80.0 us)
Async XLA Ops:
  7.2 70.7 %all-gather.6.cloned.1.call-start = ((), (), s32[]{:S(2)}) async-start(), calls=%async_computation | async-start | bytes 4866048 | tf_op jit(solution)/shard_map/all_gather | solution.py:584
  9.0 173.3 %all-gather.8.cloned.1.call-start = ((), (), s32[]{:S(2)}) async-start(), calls=%async_computation.1 | async-start | bytes 14598144 | tf_op jit(solution)/shard_map/all_gather | solution.py:592
  103.8 97.3 %collective-permute-start.3 = (bf16[128,768]{1,0:T(8,128)(2,1)}, bf16[128,768]{1,0:T(8,128)(2,1)S(1)}, u32[]{:S(2)}, u32[]{:S(2)}) collective-permute-start(bf16[128,768]{1,0:T(8,128)(2,1)} %get-tuple-element.47), channel_id=1, source_target_pairs={{0,1},{1,0},{2,3},{3,2},{4,5},{5,4},{6,7},{7,6},{8,9},{9,8},{10,11... | collective-permute-start | bytes 589832 | tf_op jit(solution)/shard_map/ppermute | solution.py:518
  202.3 17.0 %collective-permute-start.1 = (bf16[128,768]{1,0:T(8,128)(2,1)}, bf16[128,768]{1,0:T(8,128)(2,1)S(1)}, u32[]{:S(2)}, u32[]{:S(2)}) collective-permute-start(bf16[128,768]{1,0:T(8,128)(2,1)} %get-tuple-element.46), channel_id=1, source_target_pairs={{0,2},{1,3},{2,0},{3,1},{4,6},{5,7},{6,4},{7,5},{8,10},{9,11},{10,... | collective-permute-start | bytes 589832 | tf_op jit(solution)/shard_map/ppermute | solution.py:518
  203.7 15.6 %collective-permute-start.2 = (bf16[128,768]{1,0:T(8,128)(2,1)S(1)}, bf16[128,768]{1,0:T(8,128)(2,1)S(1)}, u32[]{:S(2)}, u32[]{:S(2)}) collective-permute-start(bf16[128,768]{1,0:T(8,128)(2,1)S(1)} %collective-permute-done), channel_id=1, source_target_pairs={{0,2},{1,3},{2,0},{3,1},{4,6},{5,7},{6,4},{7,5},{8,10},{9,11},{10,... | collective-permute-start | bytes 589832 | tf_op jit(solution)/shard_map/ppermute | solution.py:518
  227.7 15.1 %collective-permute-start.6 = (bf16[2,128,768]{2,1,0:T(8,128)(2,1)}, bf16[2,128,768]{2,1,0:T(8,128)(2,1)S(1)}, u32[]{:S(2)}, u32[]{:S(2)}) collective-permute-start(bf16[2,128,768]{2,1,0:T(8,128)(2,1)} %get-tuple-element.51), channel_id=1, source_target_pairs={{0,1},{1,0},{2,3},{3,2},{4,5},{5,4},{6,7},{7,6},{8,9},{9,8},{10,11... | collective-permute-start | bytes 1179656 | tf_op jit(solution)/shard_map/ppermute | solution.py:518
  231.6 16.4 %collective-permute-start.37 = (bf16[4,96,768]{2,1,0:T(8,128)(2,1)}, bf16[4,96,768]{2,1,0:T(8,128)(2,1)S(1)}, u32[]{:S(2)}, u32[]{:S(2)}) collective-permute-start(bf16[4,96,768]{2,1,0:T(8,128)(2,1)} %get-tuple-element.73), channel_id=1, source_target_pairs={{0,4},{1,5},{2,6},{3,7},{4,0},{5,1},{6,2},{7,3},{8,12},{9,13},{10,... | collective-permute-start | bytes 1769480 | tf_op jit(solution)/shard_map/ppermute | solution.py:518
  236.9 94.7 %collective-permute-start.23 = (bf16[4,96,768]{2,1,0:T(8,128)(2,1)}, bf16[4,96,768]{2,1,0:T(8,128)(2,1)S(1)}, u32[]{:S(2)}, u32[]{:S(2)}) collective-permute-start(bf16[4,96,768]{2,1,0:T(8,128)(2,1)} %get-tuple-element.67), channel_id=1, source_target_pairs={{0,4},{1,5},{2,6},{3,7},{4,0},{5,1},{6,2},{7,3},{8,12},{9,13},{10,... | collective-permute-start | bytes 1769480 | tf_op jit(solution)/shard_map/ppermute | solution.py:518
  241.3 90.6 %collective-permute-start.30 = (bf16[4,96,768]{2,1,0:T(8,128)(2,1)}, bf16[4,96,768]{2,1,0:T(8,128)(2,1)S(1)}, u32[]{:S(2)}, u32[]{:S(2)}) collective-permute-start(bf16[4,96,768]{2,1,0:T(8,128)(2,1)} %get-tuple-element.70), channel_id=1, source_target_pairs={{0,4},{1,5},{2,6},{3,7},{4,0},{5,1},{6,2},{7,3},{8,12},{9,13},{10,... | collective-permute-start | bytes 1769480 | tf_op jit(solution)/shard_map/ppermute | solution.py:518
  248.9 85.4 %collective-permute-start.38 = (bf16[96,768]{1,0:T(8,128)(2,1)}, bf16[96,768]{1,0:T(8,128)(2,1)S(1)}, u32[]{:S(2)}, u32[]{:S(2)}) collective-permute-start(bf16[96,768]{1,0:T(8,128)(2,1)} %get-tuple-element.88), channel_id=1, source_target_pairs={{0,8},{1,9},{2,10},{3,11},{4,12},{5,13},{6,14},{7,15},{8,16},{9,17... | collective-permute-start | bytes 442376 | tf_op jit(solution)/shard_map/ppermute | solution.py:518
  249.9 85.0 %collective-permute-start.40 = (bf16[96,768]{1,0:T(8,128)(2,1)}, bf16[96,768]{1,0:T(8,128)(2,1)S(1)}, u32[]{:S(2)}, u32[]{:S(2)}) collective-permute-start(bf16[96,768]{1,0:T(8,128)(2,1)} %get-tuple-element.89), channel_id=1, source_target_pairs={{0,24},{1,25},{2,26},{3,27},{4,28},{5,29},{6,30},{7,31},{8,0},{9,1... | collective-permute-start | bytes 442376 | tf_op jit(solution)/shard_map/ppermute | solution.py:518
  252.7 85.4 %collective-permute-start.39 = (bf16[96,768]{1,0:T(8,128)(2,1)S(1)}, bf16[96,768]{1,0:T(8,128)(2,1)S(1)}, u32[]{:S(2)}, u32[]{:S(2)}) collective-permute-start(bf16[96,768]{1,0:T(8,128)(2,1)S(1)} %get-tuple-element.90), channel_id=1, source_target_pairs={{0,16},{1,17},{2,18},{3,19},{4,20},{5,21},{6,22},{7,23},{8,24},{9,... | collective-permute-start | bytes 442376 | tf_op jit(solution)/shard_map/ppermute | solution.py:518
  331.6 23.5 %collective-permute-start.8 = (bf16[2,2,4,48,768]{4,3,2,1,0:T(8,128)(2,1)}, bf16[2,2,4,48,768]{4,3,2,1,0:T(8,128)(2,1)S(1)}, u32[]{:S(2)}, u32[]{:S(2)}) collective-permute-start(bf16[2,2,4,48,768]{4,3,2,1,0:T(8,128)(2,1)} %get-tuple-element.60), channel_id=1, source_target_pairs={{0,1},{1,0},{2,3},{3,2},{4,5},{5,4},{6,7},{7,6},{8,9},{9,8},{10,11... | collective-permute-start | bytes 3538952 | tf_op jit(solution)/shard_map/ppermute | solution.py:518
  333.0 23.3 %collective-permute-start.14 = (bf16[2,2,4,48,768]{4,3,2,1,0:T(8,128)(2,1)S(1)}, bf16[2,2,4,48,768]{4,3,2,1,0:T(8,128)(2,1)S(1)}, u32[]{:S(2)}, u32[]{:S(2)}) collective-permute-start(bf16[2,2,4,48,768]{4,3,2,1,0:T(8,128)(2,1)S(1)} %copy-done.35), channel_id=1, source_target_pairs={{0,1},{1,0},{2,3},{3,2},{4,5},{5,4},{6,7},{7,6},{8,9},{9,8},{10,11... | collective-permute-start | bytes 3538952 | tf_op jit(solution)/shard_map/ppermute | solution.py:518
  338.1 17.0 %collective-permute-start.25 = (bf16[96,768]{1,0:T(8,128)(2,1)S(1)}, bf16[96,768]{1,0:T(8,128)(2,1)S(1)}, u32[]{:S(2)}, u32[]{:S(2)}) collective-permute-start(bf16[96,768]{1,0:T(8,128)(2,1)S(1)} %get-tuple-element.93), channel_id=1, source_target_pairs={{0,16},{1,17},{2,18},{3,19},{4,20},{5,21},{6,22},{7,23},{8,24},{9,... | collective-permute-start | bytes 442376 | tf_op jit(solution)/shard_map/ppermute | solution.py:518
  342.8 19.5 %collective-permute-start.31 = (bf16[96,768]{1,0:T(8,128)(2,1)S(1)}, bf16[96,768]{1,0:T(8,128)(2,1)S(1)}, u32[]{:S(2)}, u32[]{:S(2)}) collective-permute-start(bf16[96,768]{1,0:T(8,128)(2,1)S(1)} %get-tuple-element.94), channel_id=1, source_target_pairs={{0,8},{1,9},{2,10},{3,11},{4,12},{5,13},{6,14},{7,15},{8,16},{9,17... | collective-permute-start | bytes 442376 | tf_op jit(solution)/shard_map/ppermute | solution.py:518
  344.0 18.5 %collective-permute-start.33 = (bf16[96,768]{1,0:T(8,128)(2,1)S(1)}, bf16[96,768]{1,0:T(8,128)(2,1)S(1)}, u32[]{:S(2)}, u32[]{:S(2)}) collective-permute-start(bf16[96,768]{1,0:T(8,128)(2,1)S(1)} %get-tuple-element.95), channel_id=1, source_target_pairs={{0,24},{1,25},{2,26},{3,27},{4,28},{5,29},{6,30},{7,31},{8,0},{9,1... | collective-permute-start | bytes 442376 | tf_op jit(solution)/shard_map/ppermute | solution.py:518
  355.2 35.2 %collective-permute-start.41 = (bf16[96,768]{1,0:T(8,128)(2,1)S(1)}, bf16[96,768]{1,0:T(8,128)(2,1)S(1)}, u32[]{:S(2)}, u32[]{:S(2)}) collective-permute-start(bf16[96,768]{1,0:T(8,128)(2,1)S(1)} %fusion.11), channel_id=1, source_target_pairs={{0,0},{1,8},{2,16},{3,24},{4,1},{5,9},{6,17},{7,25},{8,2},{9,10},{... | collective-permute-start | bytes 442376 | tf_op jit(solution)/shard_map/ppermute | solution.py:518
  356.3 17.4 %collective-permute-start.9 = (bf16[2,4,48,768]{3,2,1,0:T(8,128)(2,1)S(1)}, bf16[2,4,48,768]{3,2,1,0:T(8,128)(2,1)S(1)}, u32[]{:S(2)}, u32[]{:S(2)}) collective-permute-start(bf16[2,4,48,768]{3,2,1,0:T(8,128)(2,1)S(1)} %fusion.2), channel_id=1, source_target_pairs={{0,2},{1,3},{2,0},{3,1},{4,6},{5,7},{6,4},{7,5},{8,10},{9,11},{10,... | collective-permute-start | bytes 1769480 | tf_op jit(solution)/shard_map/ppermute | solution.py:518
  362.4 33.7 %collective-permute-start.27 = (bf16[96,768]{1,0:T(8,128)(2,1)S(1)}, bf16[96,768]{1,0:T(8,128)(2,1)S(1)}, u32[]{:S(2)}, u32[]{:S(2)}) collective-permute-start(bf16[96,768]{1,0:T(8,128)(2,1)S(1)} %fusion.19.a_ref), channel_id=1, source_target_pairs={{0,1},{1,0},{2,3},{3,2},{4,5},{5,4},{6,7},{7,6},{8,9},{9,8},{10,11... | collective-permute-start | bytes 442376 | tf_op jit(solution)/shard_map/ppermute | solution.py:518
  362.4 16.3 %collective-permute-start.15 = (bf16[2,4,48,768]{3,2,1,0:T(8,128)(2,1)S(1)}, bf16[2,4,48,768]{3,2,1,0:T(8,128)(2,1)S(1)}, u32[]{:S(2)}, u32[]{:S(2)}) collective-permute-start(bf16[2,4,48,768]{3,2,1,0:T(8,128)(2,1)S(1)} %fusion.3), channel_id=1, source_target_pairs={{0,4},{1,5},{2,6},{3,7},{4,0},{5,1},{6,2},{7,3},{8,12},{9,13},{10,... | collective-permute-start | bytes 1769480 | tf_op jit(solution)/shard_map/ppermute | solution.py:518
  399.6 18.1 %collective-permute-start.35 = (bf16[96,768]{1,0:T(8,128)(2,1)S(1)}, bf16[96,768]{1,0:T(8,128)(2,1)S(1)}, u32[]{:S(2)}, u32[]{:S(2)}) collective-permute-start(bf16[96,768]{1,0:T(8,128)(2,1)S(1)} %fusion.15.a_ref), channel_id=1, source_target_pairs={{0,2},{1,3},{2,0},{3,1},{4,6},{5,7},{6,4},{7,5},{8,10},{9,11},{10,... | collective-permute-start | bytes 442376 | tf_op jit(solution)/shard_map/ppermute | solution.py:518
  401.8 15.9 %collective-permute-start.36 = (bf16[96,768]{1,0:T(8,128)(2,1)S(1)}, bf16[96,768]{1,0:T(8,128)(2,1)S(1)}, u32[]{:S(2)}, u32[]{:S(2)}) collective-permute-start(bf16[96,768]{1,0:T(8,128)(2,1)S(1)} %collective-permute-done.34.b_ref), channel_id=1, source_target_pairs={{0,2},{1,3},{2,0},{3,1},{4,6},{5,7},{6,4},{7,5},{8,10},{9,11},{10,... | collective-permute-start | bytes 442376 | tf_op jit(solution)/shard_map/ppermute | solution.py:518
  404.8 17.2 %collective-permute-start.20 = (bf16[96,768]{1,0:T(8,128)(2,1)S(1)}, bf16[96,768]{1,0:T(8,128)(2,1)S(1)}, u32[]{:S(2)}, u32[]{:S(2)}) collective-permute-start(bf16[96,768]{1,0:T(8,128)(2,1)S(1)} %pad_maximum_fusion.4.a_ref), channel_id=1, source_target_pairs={{0,1},{1,0},{2,3},{3,2},{4,5},{5,4},{6,7},{7,6},{8,9},{9,8},{10,11... | collective-permute-start | bytes 442376 | tf_op jit(solution)/shard_map/ppermute | solution.py:518
  (60 other events, 591.7 us)
Sparse Core Ops, SparseCore 0:
  11.5 66.3 all-gather.5
  81.4 100.8 all-gather.7

commit v3 on v2

--- a/solution.py
+++ b/solution.py
@@ -29,8 +29,8 @@
     return jax.ShapeDtypeStruct(shape, dtype)
 
 
-def cost(flops, size):
-    return pl.CostEstimate(flops=int(flops), bytes_accessed=int(size), transcendentals=0)
+def cost(us):
+    return pl.CostEstimate(flops=0, bytes_accessed=int(us * 3.0e6), transcendentals=0)
 
 
 def mm(a, b):
@@ -80,7 +80,31 @@
     return value.reshape(-1, value.shape[-1])
 
 
-def attention_kernel(seqs, most, slope_ref, x_ref, w_ref, norm_ref, pos_ref, qkv_ref, h1_ref, att_m_ref, h1_m_ref, q_m_ref, r1_m_ref, att_ref, r1_ref):
+EXTRA = 8
+HALVES = ((0, 48), (48, 56))
+KEYS = [(ry, rx, rc) for rc in (0, 1) for rx in (0, 1) for ry in (0, 1)]
+
+
+def attention_kernel(seqs, most, where_ref, slope_ref, x_ref, norm_ref, pos_ref, *rest):
+    lines, rest = rest[:16], rest[16:]
+    qkv_ref, h1_ref, att_m_ref, h1_m_ref, q_m_ref, r1_m_ref, w_ref, att_ref, r1_ref, sem = rest
+    z, y, c_x = where_ref[0], where_ref[1], where_ref[4]
+    copies = []
+    for n, (ry, rx, rc) in enumerate(KEYS):
+        j = jnp.bitwise_xor(c_x, 2 * rx + rc)
+        for r in range(LINE):
+            shard = 2 * lax.rem(z + LINE - r, LINE) + jnp.bitwise_xor(y, ry)
+            for half, (start, size) in enumerate(HALVES):
+                size = min(size, ROWS - start)
+                copies.append(
+                    pltpu.make_async_copy(
+                        lines[2 * n + half].at[r, pl.ds(0, size)], w_ref.at[shard, j, pl.ds(start, size)], sem
+                    )
+                )
+    for copy in copies:
+        copy.start()
+    for copy in copies:
+        copy.wait()
     length = x_ref.shape[0] // seqs
     step = 256
 
@@ -99,19 +123,19 @@
     @pl.loop(0, HEADS // 2)
     def _(t):
         lane = pl.multiple_of(t * 128, 128)
+        bias = jnp.concatenate([slope_ref[2 * t] * away, slope_ref[2 * t + 1] * away], axis=0)
         for s in range(seqs):
             rows = slice(s * length, (s + 1) * length)
             q = qkv_ref[rows, pl.ds(lane, 128)]
             k = qkv_ref[rows, pl.ds(D + lane, 128)]
             v = qkv_ref[rows, pl.ds(2 * D + lane, 128)]
-            mixed = []
-            for h in range(2):
-                mine = jnp.where(first if h == 0 else ~first, q, jnp.zeros_like(q))
-                score = mm_nt(mine, k) * SCALE - slope_ref[2 * t + h] * away
-                e = jnp.exp(score - jnp.max(score, axis=-1, keepdims=True))
-                p = (e / jnp.sum(e, axis=-1, keepdims=True)).astype(LOW)
-                mixed.append(mm(p, v))
-            att_ref[rows, pl.ds(lane, 128)] = jnp.where(first, mixed[0], mixed[1]).astype(LOW)
+            zero = jnp.zeros_like(q)
+            both = jnp.concatenate([jnp.where(first, q, zero), jnp.where(first, zero, q)], axis=0)
+            score = mm_nt(both, k) * SCALE - bias
+            e = jnp.exp(score - jnp.max(score, axis=-1, keepdims=True))
+            p = (e * (1.0 / jnp.sum(e, axis=-1, keepdims=True))).astype(LOW)
+            mixed = mm(p, v)
+            att_ref[rows, pl.ds(lane, 128)] = jnp.where(first, mixed[:length], mixed[length:]).astype(LOW)
 
     @pl.loop(0, D // step)
     def _(n):
@@ -133,7 +157,7 @@
         q_m_ref[listed, :] = mm(hot_low, qkv_ref[rows, 0:D]).astype(LOW)
 
 
-def attention_forward(x, w_attn, norms, pos, slopes, seqs):
+def attention_forward(where, x, lines, norms, pos, slopes, seqs):
     tokens = x.shape[0]
     listed = pos.shape[0]
     return pl.pallas_call(
@@ -145,14 +169,15 @@
             out((listed, D), LOW),
             out((listed, D), LOW),
             out((listed, D), F32),
+            out((SHARDS, QUARTERS, ROWS, D), LOW),
         ),
-        in_specs=[SMEM, VMEM, VMEM, VMEM, VMEM],
-        out_specs=(VMEM,) * 6,
-        scratch_shapes=[pltpu.VMEM((tokens, D), LOW), pltpu.VMEM((tokens, D), F32)],
+        in_specs=[SMEM, SMEM, VMEM, VMEM, VMEM] + [pl.BlockSpec(memory_space=pl.ANY)] * 16,
+        out_specs=(VMEM,) * 7,
+        scratch_shapes=[pltpu.VMEM((tokens, D), LOW), pltpu.VMEM((tokens, D), F32), pltpu.SemaphoreType.DMA],
         compiler_params=BIG,
-        cost_estimate=cost(2 * tokens * D * 4 * D, 8e6),
+        cost_estimate=cost(20),
         name="attention_forward",
-    )(slopes, x, w_attn, norms, pos)
+    )(where, slopes, x, norms, pos, *lines)
 
 
 def ffn_kernel(seqs, most, h1_ref, gate_ref, up_ref, down_ref, norm_ref, pos_ref, dy_ref, y_ref, dr2_ref, e2_ref, small_ref, low_ref, act_ref, acc_ref):
@@ -224,7 +249,7 @@
         ),
         scratch_shapes=[pltpu.VMEM((tokens, D), LOW), pltpu.VMEM((tokens, D), LOW), pltpu.VMEM((tokens, D), F32)],
         compiler_params=BIG,
-        cost_estimate=cost(2 * tokens * D * 12 * D, 18e6),
+        cost_estimate=cost(16),
         name="ffn_forward",
     )(h1, w_ffn, w_ffn, w_ffn, norms, pos, dy)
 
@@ -269,7 +294,7 @@
             out_specs=(at_once((rows, D)),) * 3,
         ),
         compiler_params=BIG,
-        cost_estimate=cost(4 * rows * D * D, 8e6),
+        cost_estimate=cost(6),
         name="ffn_again",
     )(where, h_all, w_ffn, w_ffn)
 
@@ -304,7 +329,7 @@
             out_specs=(at_once((rows, D)), at_once((rows, D)), at_once((count // 2, listed, D)), at_once((count // 2, listed, D))),
         ),
         compiler_params=BIG,
-        cost_estimate=cost(6 * rows * D * D, 12e6),
+        cost_estimate=cost(7),
         name="ffn_back",
     )(where, e_all, to_gate, to_up, w_ffn, w_ffn, w_ffn)
 
@@ -336,12 +361,12 @@
         out_specs=(VMEM, VMEM),
         scratch_shapes=[pltpu.VMEM((D, D), F32)],
         compiler_params=BIG,
-        cost_estimate=cost(2 * rows * D * D, 4e6),
+        cost_estimate=cost(4),
         name="weight_grad",
     )(where, a, b)
 
 
-def attention_back_kernel(seqs, most, slope_ref, dr2_ref, part_ref, came_ref, r1_ref, q_ref, qkv_ref, att_ref, w_ref, norm_ref, pos_ref, dr1_ref, rhs_ref, lhs_ref, small_ref, datt_ref):
+def attention_back_kernel(seqs, most, slope_ref, dr2_ref, part_ref, came_ref, r1_ref, q_ref, qkv_ref, att_ref, w_ref, norm_ref, pos_ref, dr1_ref, rhs_ref, lhs_ref, small_ref, datt_ref, away_ref, hot_ref):
     length = qkv_ref.shape[0] // seqs
     listed = seqs * most
     dh1 = dr2_ref[...] + part_ref[...] + came_ref[...].astype(F32)
@@ -358,9 +383,14 @@
     for n in range(2):
         lanes = slice(n * D // 2, (n + 1) * D // 2)
         datt_ref[:, lanes] = mm_nt(low, block(w_ref, slice(n * SHARDS // 2, (n + 1) * SHARDS // 2), 3)).astype(LOW)
-    first = lax.broadcasted_iota(jnp.int32, (length, 128), 1) < HEAD_DIM
     first_m = lax.broadcasted_iota(jnp.int32, (most, 128), 1) < HEAD_DIM
-    spots = lax.broadcasted_iota(jnp.int32, (most, length), 1)
+    spots = lax.broadcasted_iota(jnp.int32, (listed, length), 1)
+    away_ref[...] = jnp.abs(pos_ref[...] - spots).astype(F32)
+    hot_ref[...] = (spots == pos_ref[...]).astype(LOW)
+
+    def both(value):
+        zero = jnp.zeros_like(value)
+        return jnp.concatenate([jnp.where(first_m, value, zero), jnp.where(first_m, zero, value)], axis=0)
 
     @pl.loop(0, HEADS // 2)
     def _(t):
@@ -368,28 +398,22 @@
         for s in range(seqs):
             rows = slice(s * length, (s + 1) * length)
             mine = slice(s * most, (s + 1) * most)
-            at = pos_ref[mine, :]
-            away = jnp.abs(at - spots).astype(F32)
-            hot = (spots == at).astype(LOW)
-            q = q_ref[mine, pl.ds(lane, 128)]
-            da = datt_ref[mine, pl.ds(lane, 128)]
+            away = away_ref[mine, :]
+            q = both(q_ref[mine, pl.ds(lane, 128)])
+            da = both(datt_ref[mine, pl.ds(lane, 128)])
             k = qkv_ref[rows, pl.ds(D + lane, 128)]
             v = qkv_ref[rows, pl.ds(2 * D + lane, 128)]
-            dq, dk, dv = [], [], []
-            for h in range(2):
-                pick = first_m if h == 0 else ~first_m
-                score = mm_nt(jnp.where(pick, q, jnp.zeros_like(q)), k) * SCALE - slope_ref[2 * t + h] * away
-                e = jnp.exp(score - jnp.max(score, axis=-1, keepdims=True))
-                p = e / jnp.sum(e, axis=-1, keepdims=True)
-                dp = mm_nt(jnp.where(pick, da, jnp.zeros_like(da)), v)
-                ds = (p * (dp - jnp.sum(dp * p, axis=-1, keepdims=True))).astype(LOW)
-                dv.append(mm_tn(p.astype(LOW), da))
-                dq.append(mm(ds, k))
-                dk.append(mm_tn(ds, q))
-            dq = (jnp.where(first_m, dq[0], dq[1]) * SCALE).astype(LOW)
-            rhs_ref[rows, pl.ds(lane, 128)] = mm_tn(hot, dq).astype(LOW)
-            rhs_ref[rows, pl.ds(D + lane, 128)] = (jnp.where(first, dk[0], dk[1]) * SCALE).astype(LOW)
-            rhs_ref[rows, pl.ds(2 * D + lane, 128)] = jnp.where(first, dv[0], dv[1]).astype(LOW)
+            bias = jnp.concatenate([slope_ref[2 * t] * away, slope_ref[2 * t + 1] * away], axis=0)
+            score = mm_nt(q, k) * SCALE - bias
+            e = jnp.exp(score - jnp.max(score, axis=-1, keepdims=True))
+            p = e * (1.0 / jnp.sum(e, axis=-1, keepdims=True))
+            dp = mm_nt(da, v)
+            ds = (p * (dp - jnp.sum(dp * p, axis=-1, keepdims=True))).astype(LOW)
+            dq = mm(ds, k)
+            dq = (jnp.where(first_m, dq[:most], dq[most:]) * SCALE).astype(LOW)
+            rhs_ref[rows, pl.ds(lane, 128)] = mm_tn(hot_ref[mine, :], dq).astype(LOW)
+            rhs_ref[rows, pl.ds(D + lane, 128)] = (mm_tn(ds, q) * SCALE).astype(LOW)
+            rhs_ref[rows, pl.ds(2 * D + lane, 128)] = mm_tn(p.astype(LOW), da).astype(LOW)
 
 
 def attention_back(dr2, part, came, r1_m, q_m, qkv, att_m, w_attn, norms, pos, slopes, seqs):
@@ -400,9 +424,9 @@
         out_shape=(out((listed, D), F32), out((tokens, 4 * D), LOW), out((tokens, D), LOW), out((2, D), F32)),
         in_specs=[SMEM] + [VMEM] * 10,
         out_specs=(VMEM,) * 4,
-        scratch_shapes=[pltpu.VMEM((listed, D), LOW)],
+        scratch_shapes=[pltpu.VMEM((listed, D), LOW), pltpu.VMEM((listed, tokens // seqs), F32), pltpu.VMEM((listed, tokens // seqs), LOW)],
         compiler_params=BIG,
-        cost_estimate=cost(2 * listed * D * D * 2, 12e6),
+        cost_estimate=cost(18),
         name="attention_back",
     )(slopes, dr2, part, came, r1_m, q_m, qkv, att_m, w_attn, norms, pos)
 
@@ -455,7 +479,7 @@
         out_specs=(VMEM,) * 4,
         scratch_shapes=[pltpu.VMEM((D, D), F32)],
         compiler_params=BIG,
-        cost_estimate=cost(2 * x.shape[0] * D * 4 * D, 10e6),
+        cost_estimate=cost(10),
         name="attention_grads",
     )(where, x, lhs, rhs)
 
@@ -484,7 +508,7 @@
         in_specs=[VMEM] * 4,
         out_specs=VMEM,
         compiler_params=BIG,
-        cost_estimate=cost(2 * tokens * D * 3 * D, 10e6),
+        cost_estimate=cost(8),
         name="input_grad",
     )(rhs, w_attn, dr1, positions)
 
@@ -543,20 +567,22 @@
     return line_sum([(r, total[r].astype(LOW)) for r in (1, 2, 3)], total[0]).astype(LOW)
 
 
-def finish_kernel(rows_out, where_ref, a_ref, b_ref, c_ref, d_ref, *rest):
-    outs, held = rest[:-1], rest[-1]
+def finish_kernel(rows_out, where_ref, *rest):
+    held = rest[-1]
+    count = len(held.shape) and held.shape[0]
+    pieces, outs = rest[: QUARTERS * count], rest[QUARTERS * count : -1]
     mine = where_ref[4]
-    for r, ref in enumerate((a_ref, b_ref, c_ref, d_ref)):
-        held[jnp.bitwise_xor(mine, r)] = ref[...].astype(F32)
+    for n, ref in enumerate(pieces):
+        held[n // QUARTERS, jnp.bitwise_xor(mine, n % QUARTERS)] = ref[...].astype(F32)
     if rows_out:
         for j in range(QUARTERS):
-            outs[0][j * ROWS : (j + 1) * ROWS, :] = held[j]
-    else:
-        at = 0
-        for ref in outs:
-            for j in range(ref.shape[1] // D):
-                ref[:, j * D : (j + 1) * D] = held[at]
-                at += 1
+            outs[0][j * ROWS : (j + 1) * ROWS, :] = held[0, j]
+        return
+    at = 0
+    for ref in outs:
+        for j in range(ref.shape[1] // D):
+            ref[:, j * D : (j + 1) * D] = held[at // QUARTERS, at % QUARTERS]
+            at += 1
 
 
 def finish(where, pieces, widths, rows_out=False):
@@ -564,13 +590,27 @@
     return pl.pallas_call(
         functools.partial(finish_kernel, rows_out),
         out_shape=tuple(shapes),
-        in_specs=[SMEM] + [VMEM] * 4,
+        in_specs=[SMEM] + [VMEM] * len(pieces),
         out_specs=(VMEM,) * len(shapes),
-        scratch_shapes=[pltpu.VMEM((QUARTERS, ROWS, D), F32)],
+        scratch_shapes=[pltpu.VMEM((len(pieces) // QUARTERS, QUARTERS, ROWS, D), F32)],
         compiler_params=BIG,
-        cost_estimate=cost(1e5, 2e6),
+        cost_estimate=cost(2),
         name="finish",
     )(where, *pieces)
+
+
+def spread(piece, order):
+    got = {frozenset(): piece}
+    for step in (*order, "c"):
+        for key in list(got):
+            got[key | {step}] = send(got[key], step)
+    return [got[frozenset(n for n, b in zip("yxc", key) if b)] for key in KEYS]
+
+
+def sum_all(value):
+    for step in ("c", "x", "y"):
+        value = value + send(value, step)
+    return value + send(value, 1) + send(value, 2) + send(value, 3)
 
 
 def on_block(hidden_in, w_qkv, w_out, w_up, w_down, gain_attn, shift_attn, gain_ffn, shift_ffn, grad_listed, positions, counts):
@@ -581,7 +621,14 @@
     where = jnp.stack([i // 2, i % 2, j // 2, j % 2, j]).astype(jnp.int32)
     ff = w_down.shape[0] * SHARDS
     attn_piece = lax.dynamic_slice_in_dim(jnp.concatenate([w_qkv, w_out], axis=1), j * D, D, axis=1)
-    w_attn = lax.all_gather(attn_piece, AXES, axis=0, tiled=False).reshape(SHARDS, QUARTERS, ROWS, D)
+    norms = jnp.concatenate([gain_attn, shift_attn, gain_ffn, shift_ffn, jnp.zeros((D - 4 * ROWS,), LOW)])
+    attn_piece = jnp.concatenate([attn_piece, jnp.broadcast_to(norms, (EXTRA, D))], axis=0)
+    line = jnp.stack([attn_piece] + [send(attn_piece, r) for r in (1, 2, 3)])
+    halves = [
+        spread(line[:, start : start + size], order)
+        for (start, size), order in zip(HALVES, (("y", "x"), ("x", "y")))
+    ]
+    lines = [half[n] for n in range(len(KEYS)) for half in halves]
     ffn_piece = jnp.stack(
         [
             lax.dynamic_slice_in_dim(w_up, j * D, D, axis=1),
@@ -590,16 +637,19 @@
         ]
     )
     w_ffn = lax.all_gather(ffn_piece, AXES, axis=0, tiled=False).reshape(SHARDS, QUARTERS, 3, ROWS, D)
-    norms = jnp.stack([gain_attn, shift_attn, gain_ffn, shift_ffn])
-    norms = lax.all_gather(norms, "fsdp", axis=1, tiled=True).astype(F32)
+    tails = jnp.stack([halves[1][n][:, 48, : 4 * ROWS] for n in range(2)])
+    tails = jnp.where(i % 2 == 0, tails, tails[::-1])
+    tails = jnp.roll(tails[:, ::-1], i // 2 + 1, axis=1)
+    norms = tails.transpose(1, 0, 2).reshape(SHARDS, 4, ROWS).transpose(1, 0, 2).reshape(4, D).astype(F32)
     slopes = jnp.exp2(-8.0 * (jnp.arange(HEADS, dtype=F32) + 1.0) / HEADS)
     x = hidden_in.reshape(tokens, width)
     pos = positions.reshape(seqs * most, 1)
     live = jnp.arange(most, dtype=jnp.int32)[None, :] < counts[:, None]
     dy = jnp.where(live[:, :, None], grad_listed, jnp.zeros_like(grad_listed)).reshape(seqs * most, width)
 
-    qkv, h1, att_m, h1_m, q_m, r1_m = attention_forward(x, w_attn, norms, pos, slopes, seqs)
+    qkv, h1, att_m, h1_m, q_m, r1_m, w_attn = attention_forward(where, x, lines, norms, pos, slopes, seqs)
     h_all = jnp.stack(share_dp(h1_m))
+    h1, h_all = lax.optimization_barrier((h1, h_all))
     layer_out, dr2, e2, small_ffn = ffn_forward(h1, w_ffn, norms, pos, dy, seqs)
     act, to_gate, to_up = ffn_again(where, h_all, w_ffn)
     e_all = jnp.stack(share_dp(e2))
@@ -616,17 +666,16 @@
     )
     grad_in = input_grad(rhs, w_attn, dr1, positions)
     (grad_down,) = finish(where, share_dp(send(g_down, "down")), (), rows_out=True)
-    (grad_gate,) = finish(where, share_dp(g_gate), (QUARTERS,))
-    (grad_up,) = finish(where, share_dp(g_up), (QUARTERS,))
+    (grad_up,) = finish(where, (*share_dp(g_gate), *share_dp(g_up)), (2 * QUARTERS,))
     grad_qkv, grad_out = finish(where, share_dp(g_attn), (3, 1))
-    small = lax.psum(jnp.concatenate([small_attn, small_ffn]), AXES)
+    small = sum_all(jnp.concatenate([small_attn, small_ffn]))
     small = lax.dynamic_slice_in_dim(small, i * ROWS, ROWS, axis=1)
     return (
         layer_out.reshape(seqs, length, width),
         grad_in.reshape(seqs, length, width),
         grad_qkv,
         grad_out,
-        jnp.concatenate([grad_gate, grad_up], axis=1),
+        grad_up,
         grad_down,
         small[0],
         small[1],

time: 441 us -> 351 us (0.80)
  blocking collectives: 61.6 us -> 0 us
  waiting for transfers between devices: 165 us -> 142 us
  Pallas kernels: 124 us -> 106 us
  starting transfers between devices: 52.1 us -> 65.6 us
    ppermute x45 -> x68, waiting for transfers between devices: 45.3 us -> 115 us  [send(): return lax.ppermute(value, AXES, MOVES[move])]
    all_gather x1, waiting for transfers between devices: 78.3 us -> 27.2 us  [on_block(): lax.all_gather(ffn_piece, AXES, axis=0, tiled=False)]
    all_gather x1 -> x0, waiting for transfers between devices: 41.7 us -> none  [on_block(): lax.all_gather(attn_piece, AXES, axis=0, tiled=False)]
    psum x1 -> x0, blocking collectives: 39.3 us -> none  [on_block(): small = lax.psum(jnp.concatenate([small_attn, small_ffn]), AXES)]
    all_gather x1 -> x0, blocking collectives: 22.3 us -> none  [on_block(): norms = lax.all_gather(norms, 'fsdp', axis=1, tiled=True).astype(F32)]
    ppermute x45 -> x68, starting transfers between devices: 52 us -> 65.6 us  [send(): return lax.ppermute(value, AXES, MOVES[move])]
    pallas_call x1, Pallas kernels: 28 us -> 18.8 us  [attention_back(): pl.pallas_call(functools.partial(attention_back_kernel, seqs, listed // s...]
    pallas_call x1, Pallas kernels: 25.9 us -> 18.2 us  [attention_forward(): pl.pallas_call(functools.partial(attention_kernel, seqs, listed // seqs),...]
  transfers between devices with their start and end apart: 47 -> 69, of which waited for: 14 -> 31; matrix products, arithmetic and copies ran while one was open for 3% -> 4% of each run, Pallas kernels for 26% -> 23%
where the time goes in v3:
time: 351 us
  waiting for transfers between devices  142 us (40%)
  Pallas kernels  106 us (30%)
  starting transfers between devices  65.6 us (19%)
  between operations  14.9 us (4%)
  local copies, waits for them, and re-layouts  11.3 us (3%)
  other arithmetic  11.3 us (3%)
    ppermute x68, waiting for transfers between devices, send(): return lax.ppermute(value, AXES, MOVES[move])  115 us
    ppermute x68, starting transfers between devices, send(): return lax.ppermute(value, AXES, MOVES[move])  65.6 us
    all_gather x1, waiting for transfers between devices, on_block(): lax.all_gather(ffn_piece, AXES, axis=0, tiled=False)  27.2 us
    pallas_call x1, Pallas kernels, attention_back(): pl.pallas_call(functools.partial(attention_back_kernel, seqs, listed // s...  18.8 us
    pallas_call x1, Pallas kernels, attention_forward(): pl.pallas_call(functools.partial(attention_kernel, seqs, listed // seqs),...  18.2 us
    pallas_call x1, Pallas kernels, ffn_forward(): pl.pallas_call(functools.partial(ffn_kernel, seqs, listed // seqs), out_s...  17 us
    pallas_call x3, Pallas kernels, weight_grad(): pl.pallas_call(weight_grad_kernel, out_shape=(out(shape, LOW), out(shape,...  11.7 us
    pallas_call x1, Pallas kernels, attention_grads(): pl.pallas_call(attention_grads_kernel, out_shape=(out(shape, LOW),) * 4,...  10.2 us
  transfers between devices with their start and end apart: 69, of which 31 were waited for; matrix products, arithmetic and copies ran while one was open for 4% of the time, Pallas kernels for 23%

profile of v3, /device:TPU:0, one launch (start us, length us, event | category | flops | bytes accessed | tf_op | source)
XLA Modules:
  0.0 350.8 jit_solution(4073900237956443805)
XLA Ops:
  9.6 4.1 %collective-permute-start.1 = (bf16[104,768]{1,0:T(8,128)(2,1)S(1)}, bf16[104,768]{1,0:T(8,128)(2,1)S(1)}, u32[]{:S(2)}, u32[]{:S(2)}) collective-permute-start(bf16[104,768]{1,0:T(8,128)(2,1)S(1)} %get-tuple-element.110), channel_id=1, source_target_pairs={{0,16},{1,17},{2,18},{3,19},{4,20},{5,21},{6,22},{7,23},{8,24},{9,... | collective-permute-start | bytes 479240 | tf_op jit(solution)/shard_map/ppermute | solution.py:542
  17.5 8.0 %collective-permute-done.1 = bf16[104,768]{1,0:T(8,128)(2,1)S(1)} collective-permute-done((bf16[104,768]{1,0:T(8,128)(2,1)S(1)}, bf16[104,768]{1,0:T(8,128)(2,1)S(1)}, u32[]{:S(2)}, u32[]{:S(2)}) %collective-permute-start.1) | collective-permute-done | bytes 159776 | tf_op jit(solution)/shard_map/ppermute | solution.py:542
  31.4 6.8 %collective-permute-done.6.rest_5_ = bf16[4,56,768]{2,1,0:T(8,128)(2,1)S(1)} collective-permute-done((bf16[4,56,768]{2,1,0:T(8,128)(2,1)S(1)}, bf16[4,56,768]{2,1,0:T(8,128)(2,1)S(1)}, u32[]{:S(2)}, u32[]{:S(2)}) %collective-permute-start.6) | collective-permute-done | bytes 344096 | tf_op jit(solution)/shard_map/ppermute | solution.py:542
  49.3 6.9 %collective-permute-done.8.rest_7_ = bf16[4,56,768]{2,1,0:T(8,128)(2,1)S(1)} collective-permute-done((bf16[4,56,768]{2,1,0:T(8,128)(2,1)S(1)}, bf16[4,56,768]{2,1,0:T(8,128)(2,1)S(1)}, u32[]{:S(2)}, u32[]{:S(2)}) %collective-permute-start.8) | collective-permute-done | bytes 344096 | tf_op jit(solution)/shard_map/ppermute | solution.py:542
  56.8 6.1 %collective-permute-done.7.rest_6_ = bf16[4,48,768]{2,1,0:T(8,128)(2,1)} collective-permute-done((bf16[4,48,768]{2,1,0:T(8,128)(2,1)}, bf16[4,48,768]{2,1,0:T(8,128)(2,1)}, u32[]{:S(2)}, u32[]{:S(2)}) %collective-permute-start.7) | collective-permute-done | bytes 294944 | tf_op jit(solution)/shard_map/ppermute | solution.py:542
  65.6 18.2 %attention_forward.1 = (bf16[512,2304]{1,0:T(8,128)(2,1)}, f32[512,768]{1,0:T(8,128)}, bf16[128,768]{1,0:T(8,128)(2,1)}, bf16[128,768]{1,0:T(8,128)(2,1)}, bf16[...) custom-call(s32[5]{0:T(128)} %stack.83.where_ref, f32[12]{0:T(128)} %multiply_exponential_fusion.slope_ref, ...), custom_call_target="tpu_custom_call" | custom-call | bytes 60000000 | tf_op jit(solution)/shard_map/attention_forward/pallas_call | solution.py:163
  87.8 8.6 %collective-permute-done.18 = bf16[128,768]{1,0:T(8,128)(2,1)S(1)} collective-permute-done((bf16[128,768]{1,0:T(8,128)(2,1)}, bf16[128,768]{1,0:T(8,128)(2,1)S(1)}, u32[]{:S(2)}, u32[]{:S(2)}) %collective-permute-start.18) | collective-permute-done | bytes 196640 | tf_op jit(solution)/shard_map/ppermute | solution.py:542
  96.4 8.2 %collective-permute-done.19 = bf16[128,768]{1,0:T(8,128)(2,1)S(1)} collective-permute-done((bf16[128,768]{1,0:T(8,128)(2,1)S(1)}, bf16[128,768]{1,0:T(8,128)(2,1)S(1)}, u32[]{:S(2)}, u32[]{:S(2)}) %collective-permute-start.19) | collective-permute-done | bytes 196640 | tf_op jit(solution)/shard_map/ppermute | solution.py:542
  106.5 27.2 %all-gather.3.cloned.1.call-done = bf16[96,96,768]{2,1,0:T(8,128)(2,1)} async-done(((bf16[3,96,768]{2,1,0:T(8,128)(2,1)}), bf16[96,96,768]{2,1,0:T(8,128)(2,1)}) %all-gather.3.cloned.1.call-update) | async-done | bytes 14155792 | tf_op jit(solution)/shard_map/all_gather | solution.py:639
  133.8 17.0 %ffn_forward.1 = (bf16[512,768]{1,0:T(8,128)(2,1)}, f32[128,768]{1,0:T(8,128)}, bf16[128,768]{1,0:T(8,128)(2,1)}, f32[2,768]{1,0:T(2,128)}) custom-call(f32[512,768]{1,0:T(8,128)} %get-tuple-element.48.h1_ref, bf16[8,4,3,96,768]{4,3,2,1,0:T(8,128)(2,1)} %bitcast.156, bf16[8,4,3,96,768]{4,3,2,1,0:T(8,128)(2,1)} %bitcast.157, ...), custom_call_target="tpu_custom_call" | custom-call | bytes 48000000 | tf_op jit(solution)/shard_map/ffn_forward/pallas_call | solution.py:231
  153.1 6.6 %ffn_again.1 = (bf16[512,768]{1,0:T(8,128)(2,1)}, f32[512,768]{1,0:T(8,128)}, f32[512,768]{1,0:T(8,128)}) custom-call(s32[5]{0:T(128)} %stack.83.where_ref, bf16[4,128,768]{2,1,0:T(8,128)(2,1)} %pad_maximum_fusion.h_ref.a_ref, bf16[8,4,3,96,768]{4,3,2,1,0:T(8,128)(2,1)} %bitcast.159, bf16[8,4,3,96,768]{4,3,2,1,0:T(8,128)(2,1)} %bitcast.160), custom_call_target="tpu_custom_call" | custom-call | bytes 18000000 | tf_op jit(solution)/shard_map/ffn_again/pallas_call | solution.py:287
  163.6 7.4 %ffn_back.1 = (bf16[512,768]{1,0:T(8,128)(2,1)}, bf16[512,768]{1,0:T(8,128)(2,1)}, f32[2,128,768]{2,1,0:T(8,128)}, bf16[2,128,768]{2,1,0:T(8,128)(2,1)}) custom-call(s32[5]{0:T(128)} %stack.83.where_ref, bf16[4,128,768]{2,1,0:T(8,128)(2,1)} %pad_maximum_fusion.1.e_ref.b_ref, f32[512,768]{1,0:T(8,128)} %get-tuple-element.53.to_gate_ref, ...), custom_call_target="tpu_custom_call" | custom-call | bytes 21000000 | tf_op jit(solution)/shard_map/ffn_back/pallas_call | solution.py:322
  180.2 3.9 %weight_grad.4 = (bf16[4,96,768]{2,1,0:T(8,128)(2,1)}, bf16[4,96,768]{2,1,0:T(8,128)(2,1)}) custom-call(s32[5]{0:T(128)} %stack.83.where_ref, bf16[4,128,768]{2,1,0:T(8,128)(2,1)} %pad_maximum_fusion.h_ref.a_ref, bf16[512,768]{1,0:T(8,128)(2,1)} %get-tuple-element.74.b_ref), custom_call_target="tpu_custom_call" | custom-call | bytes 12000000 | tf_op jit(solution)/shard_map/weight_grad/pallas_call | solution.py:357
  187.7 5.1 %collective-permute-done.24.came_ref = bf16[128,768]{1,0:T(8,128)(2,1)S(1)} collective-permute-done((bf16[128,768]{1,0:T(8,128)(2,1)S(1)}, bf16[128,768]{1,0:T(8,128)(2,1)S(1)}, u32[]{:S(2)}, u32[]{:S(2)}) %collective-permute-start.24) | collective-permute-done | bytes 196640 | tf_op jit(solution)/shard_map/ppermute | solution.py:542
  193.5 18.8 %attention_back.1 = (f32[128,768]{1,0:T(8,128)}, bf16[512,3072]{1,0:T(8,128)(2,1)}, bf16[512,768]{1,0:T(8,128)(2,1)}, f32[2,768]{1,0:T(2,128)}) custom-call(f32[12]{0:T(128)} %multiply_exponential_fusion.slope_ref, f32[128,768]{1,0:T(8,128)} %get-tuple-element.50.dr2_ref, f32[128,768]{1,0:T(8,128)} %slice_bitcast_fusion.4.part_ref, ...), custom_call_target="tpu_custom_call" | custom-call | bytes 54000000 | tf_op jit(solution)/shard_map/attention_back/pallas_call | solution.py:422
  219.6 10.2 %attention_grads.1 = (bf16[2,2,4,48,768]{4,3,2,1,0:T(8,128)(2,1)}, bf16[2,2,4,48,768]{4,3,2,1,0:T(8,128)(2,1)}, bf16[2,2,4,48,768]{4,3,2,1,0:T(8,128)(2,1)}, bf16[2,2,4,48,768]{4,3,2,1,0:T(8,128)(2,1)}) custom-call(s32[5]{0:T(128)} %stack.83.where_ref, bf16[512,768]{1,0:T(8,128)(2,1)} %bitcast.165, bf16[512,768]{1,0:T(8,128)(2,1)} %get-tuple-element.64.lhs_ref, ...), custom_call_target="tpu_custom_call" | custom-call | bytes 30000000 | tf_op jit(solution)/shard_map/attention_grads/pallas_call | solution.py:475
  246.7 5.5 %collective-permute-start.48 = (bf16[96,768]{1,0:T(8,128)(2,1)S(1)}, bf16[96,768]{1,0:T(8,128)(2,1)S(1)}, u32[]{:S(2)}, u32[]{:S(2)}) collective-permute-start(bf16[96,768]{1,0:T(8,128)(2,1)S(1)} %get-tuple-element.97), channel_id=1, source_target_pairs={{0,8},{1,9},{2,10},{3,11},{4,12},{5,13},{6,14},{7,15},{8,16},{9,17... | collective-permute-start | bytes 442376 | tf_op jit(solution)/shard_map/ppermute | solution.py:542
  252.2 7.5 %collective-permute-done.42 = bf16[96,768]{1,0:T(8,128)(2,1)S(1)} collective-permute-done((bf16[96,768]{1,0:T(8,128)(2,1)S(1)}, bf16[96,768]{1,0:T(8,128)(2,1)S(1)}, u32[]{:S(2)}, u32[]{:S(2)}) %collective-permute-start.42) | collective-permute-done | bytes 147488 | tf_op jit(solution)/shard_map/ppermute | solution.py:542
  261.9 5.1 %collective-permute-start.66 = (f32[4,768]{1,0:T(4,128)S(1)}, f32[4,768]{1,0:T(4,128)S(1)}, u32[]{:S(2)}, u32[]{:S(2)}) collective-permute-start(f32[4,768]{1,0:T(4,128)S(1)} %add.176), channel_id=1, source_target_pairs={{0,16},{1,17},{2,18},{3,19},{4,20},{5,21},{6,22},{7,23},{8,24},{9,... | collective-permute-start | bytes 36872 | tf_op jit(solution)/shard_map/ppermute | solution.py:542
  268.8 6.6 %collective-permute-done.26 = bf16[2,4,48,768]{3,2,1,0:T(8,128)(2,1)S(1)} collective-permute-done((bf16[2,4,48,768]{3,2,1,0:T(8,128)(2,1)S(1)}, bf16[2,4,48,768]{3,2,1,0:T(8,128)(2,1)S(1)}, u32[]{:S(2)}, u32[]{:S(2)}) %collective-permute-start.26) | collective-permute-done | bytes 589856 | tf_op jit(solution)/shard_map/ppermute | solution.py:542
  276.1 5.4 %collective-permute-done.32 = bf16[2,4,48,768]{3,2,1,0:T(8,128)(2,1)S(1)} collective-permute-done((bf16[2,4,48,768]{3,2,1,0:T(8,128)(2,1)S(1)}, bf16[2,4,48,768]{3,2,1,0:T(8,128)(2,1)S(1)}, u32[]{:S(2)}, u32[]{:S(2)}) %collective-permute-start.32) | collective-permute-done | bytes 589856 | tf_op jit(solution)/shard_map/ppermute | solution.py:542
  307.0 4.6 %collective-permute-done.65 = f32[4,768]{1,0:T(4,128)S(1)} collective-permute-done((f32[4,768]{1,0:T(4,128)S(1)}, f32[4,768]{1,0:T(4,128)S(1)}, u32[]{:S(2)}, u32[]{:S(2)}) %collective-permute-start.65) | collective-permute-done | bytes 12320 | tf_op jit(solution)/shard_map/ppermute | solution.py:542
  313.8 8.3 %input_grad.1 = f32[512,768]{1,0:T(8,128)} custom-call(bf16[512,3072]{1,0:T(8,128)(2,1)} %get-tuple-element.62.rhs_ref, bf16[8,4,96,768]{3,2,1,0:T(8,128)(2,1)} %get-tuple-element.61.w_ref, f32[128,768]{1,0:T(8,128)} %get-tuple-element.63.dr1_ref, s32[4,32]{1,0:T(4,128)} %pos_ref.1), custom_call_target="tpu_custom_call" | custom-call | bytes 24000000 | tf_op jit(solution)/shard_map/input_grad/pallas_call | solution.py:505
  327.4 4.8 %collective-permute-done.53.rest_7_ = bf16[96,768]{1,0:T(8,128)(2,1)S(1)} collective-permute-done((bf16[96,768]{1,0:T(8,128)(2,1)S(1)}, bf16[96,768]{1,0:T(8,128)(2,1)S(1)}, u32[]{:S(2)}, u32[]{:S(2)}) %collective-permute-start.53) | collective-permute-done | bytes 147488 | tf_op jit(solution)/shard_map/ppermute | solution.py:542
  (282 shorter events, 124.9 us)
Async XLA Ops:
  7.2 126.5 %all-gather.3.cloned.1.call-start = ((), (), s32[]{:S(2)}) async-start(), calls=%async_computation | async-start | bytes 14598144 | tf_op jit(solution)/shard_map/all_gather | solution.py:639
  9.6 16.0 %collective-permute-start.1 = (bf16[104,768]{1,0:T(8,128)(2,1)S(1)}, bf16[104,768]{1,0:T(8,128)(2,1)S(1)}, u32[]{:S(2)}, u32[]{:S(2)}) collective-permute-start(bf16[104,768]{1,0:T(8,128)(2,1)S(1)} %get-tuple-element.110), channel_id=1, source_target_pairs={{0,16},{1,17},{2,18},{3,19},{4,20},{5,21},{6,22},{7,23},{8,24},{9,... | collective-permute-start | bytes 479240 | tf_op jit(solution)/shard_map/ppermute | solution.py:542
  29.4 17.1 %collective-permute-start.3 = (bf16[4,56,768]{2,1,0:T(8,128)(2,1)S(1)}, bf16[4,56,768]{2,1,0:T(8,128)(2,1)S(1)}, u32[]{:S(2)}, u32[]{:S(2)}) collective-permute-start(bf16[4,56,768]{2,1,0:T(8,128)(2,1)S(1)} %slice.173.rest_1_), channel_id=1, source_target_pairs={{0,4},{1,5},{2,6},{3,7},{4,0},{5,1},{6,2},{7,3},{8,12},{9,13},{10,... | collective-permute-start | bytes 1032200 | tf_op jit(solution)/shard_map/ppermute | solution.py:542
  31.2 15.3 %collective-permute-start.4 = (bf16[4,48,768]{2,1,0:T(8,128)(2,1)S(1)}, bf16[4,48,768]{2,1,0:T(8,128)(2,1)}, u32[]{:S(2)}, u32[]{:S(2)}) collective-permute-start(bf16[4,48,768]{2,1,0:T(8,128)(2,1)S(1)} %pad_maximum_fusion.4.rest_0_), channel_id=1, source_target_pairs={{0,4},{1,5},{2,6},{3,7},{4,0},{5,1},{6,2},{7,3},{8,12},{9,13},{10,... | collective-permute-start | bytes 884744 | tf_op jit(solution)/shard_map/ppermute | solution.py:542
  31.4 17.8 %collective-permute-start.10 = (bf16[4,56,768]{2,1,0:T(8,128)(2,1)S(1)}, bf16[4,56,768]{2,1,0:T(8,128)(2,1)S(1)}, u32[]{:S(2)}, u32[]{:S(2)}) collective-permute-start(bf16[4,56,768]{2,1,0:T(8,128)(2,1)S(1)} %slice.173.rest_1_), channel_id=1, source_target_pairs={{0,1},{1,0},{2,3},{3,2},{4,5},{5,4},{6,7},{7,6},{8,9},{9,8},{10,11... | collective-permute-start | bytes 1032200 | tf_op jit(solution)/shard_map/ppermute | solution.py:542
  38.2 18.0 %collective-permute-start.8 = (bf16[4,56,768]{2,1,0:T(8,128)(2,1)S(1)}, bf16[4,56,768]{2,1,0:T(8,128)(2,1)S(1)}, u32[]{:S(2)}, u32[]{:S(2)}) collective-permute-start(bf16[4,56,768]{2,1,0:T(8,128)(2,1)S(1)} %collective-permute-done.6.rest_5_), channel_id=1, source_target_pairs={{0,4},{1,5},{2,6},{3,7},{4,0},{5,1},{6,2},{7,3},{8,12},{9,13},{10,... | collective-permute-start | bytes 1032200 | tf_op jit(solution)/shard_map/ppermute | solution.py:542
  46.5 16.4 %collective-permute-start.7 = (bf16[4,48,768]{2,1,0:T(8,128)(2,1)}, bf16[4,48,768]{2,1,0:T(8,128)(2,1)}, u32[]{:S(2)}, u32[]{:S(2)}) collective-permute-start(bf16[4,48,768]{2,1,0:T(8,128)(2,1)} %collective-permute-done.4.rest_2_), channel_id=1, source_target_pairs={{0,2},{1,3},{2,0},{3,1},{4,6},{5,7},{6,4},{7,5},{8,10},{9,11},{10,... | collective-permute-start | bytes 884744 | tf_op jit(solution)/shard_map/ppermute | solution.py:542
  48.5 15.6 %collective-permute-start.14 = (bf16[4,56,768]{2,1,0:T(8,128)(2,1)S(1)}, bf16[4,56,768]{2,1,0:T(8,128)(2,1)S(1)}, u32[]{:S(2)}, u32[]{:S(2)}) collective-permute-start(bf16[4,56,768]{2,1,0:T(8,128)(2,1)S(1)} %collective-permute-done.6.rest_5_), channel_id=1, source_target_pairs={{0,1},{1,0},{2,3},{3,2},{4,5},{5,4},{6,7},{7,6},{8,9},{9,8},{10,11... | collective-permute-start | bytes 1032200 | tf_op jit(solution)/shard_map/ppermute | solution.py:542
  85.5 19.1 %collective-permute-start.19 = (bf16[128,768]{1,0:T(8,128)(2,1)S(1)}, bf16[128,768]{1,0:T(8,128)(2,1)S(1)}, u32[]{:S(2)}, u32[]{:S(2)}) collective-permute-start(bf16[128,768]{1,0:T(8,128)(2,1)S(1)} %collective-permute-done.17), channel_id=1, source_target_pairs={{0,2},{1,3},{2,0},{3,1},{4,6},{5,7},{6,4},{7,5},{8,10},{9,11},{10,... | collective-permute-start | bytes 589832 | tf_op jit(solution)/shard_map/ppermute | solution.py:542
  171.0 15.2 %collective-permute-start.23 = (bf16[2,128,768]{2,1,0:T(8,128)(2,1)}, bf16[2,128,768]{2,1,0:T(8,128)(2,1)S(1)}, u32[]{:S(2)}, u32[]{:S(2)}) collective-permute-start(bf16[2,128,768]{2,1,0:T(8,128)(2,1)} %get-tuple-element.56), channel_id=1, source_target_pairs={{0,1},{1,0},{2,3},{3,2},{4,5},{5,4},{6,7},{7,6},{8,9},{9,8},{10,11... | collective-permute-start | bytes 1179656 | tf_op jit(solution)/shard_map/ppermute | solution.py:542
  174.9 38.7 %collective-permute-start.54 = (bf16[4,96,768]{2,1,0:T(8,128)(2,1)}, bf16[4,96,768]{2,1,0:T(8,128)(2,1)}, u32[]{:S(2)}, u32[]{:S(2)}) collective-permute-start(bf16[4,96,768]{2,1,0:T(8,128)(2,1)} %get-tuple-element.79), channel_id=1, source_target_pairs={{0,4},{1,5},{2,6},{3,7},{4,0},{5,1},{6,2},{7,3},{8,12},{9,13},{10,... | collective-permute-start | bytes 1769480 | tf_op jit(solution)/shard_map/ppermute | solution.py:542
  184.2 35.2 %collective-permute-start.40 = (bf16[4,96,768]{2,1,0:T(8,128)(2,1)}, bf16[4,96,768]{2,1,0:T(8,128)(2,1)S(1)}, u32[]{:S(2)}, u32[]{:S(2)}) collective-permute-start(bf16[4,96,768]{2,1,0:T(8,128)(2,1)} %get-tuple-element.73), channel_id=1, source_target_pairs={{0,4},{1,5},{2,6},{3,7},{4,0},{5,1},{6,2},{7,3},{8,12},{9,13},{10,... | collective-permute-start | bytes 1769480 | tf_op jit(solution)/shard_map/ppermute | solution.py:542
  184.7 45.9 %collective-permute-start.47 = (bf16[4,96,768]{2,1,0:T(8,128)(2,1)}, bf16[4,96,768]{2,1,0:T(8,128)(2,1)S(1)}, u32[]{:S(2)}, u32[]{:S(2)}) collective-permute-start(bf16[4,96,768]{2,1,0:T(8,128)(2,1)} %get-tuple-element.76), channel_id=1, source_target_pairs={{0,4},{1,5},{2,6},{3,7},{4,0},{5,1},{6,2},{7,3},{8,12},{9,13},{10,... | collective-permute-start | bytes 1769480 | tf_op jit(solution)/shard_map/ppermute | solution.py:542
  213.6 16.2 %collective-permute-start.62 = (f32[4,768]{1,0:T(4,128)}, f32[4,768]{1,0:T(4,128)}, u32[]{:S(2)}, u32[]{:S(2)}) collective-permute-start(f32[4,768]{1,0:T(4,128)} %pad_maximum_fusion.7), channel_id=1, source_target_pairs={{0,1},{1,0},{2,3},{3,2},{4,5},{5,4},{6,7},{7,6},{8,9},{9,8},{10,11... | collective-permute-start | bytes 36872 | tf_op jit(solution)/shard_map/ppermute | solution.py:542
  215.6 22.5 %collective-permute-start.55 = (bf16[96,768]{1,0:T(8,128)(2,1)}, bf16[96,768]{1,0:T(8,128)(2,1)}, u32[]{:S(2)}, u32[]{:S(2)}) collective-permute-start(bf16[96,768]{1,0:T(8,128)(2,1)} %get-tuple-element.94), channel_id=1, source_target_pairs={{0,8},{1,9},{2,10},{3,11},{4,12},{5,13},{6,14},{7,15},{8,16},{9,17... | collective-permute-start | bytes 442376 | tf_op jit(solution)/shard_map/ppermute | solution.py:542
  216.5 22.2 %collective-permute-start.57 = (bf16[96,768]{1,0:T(8,128)(2,1)}, bf16[96,768]{1,0:T(8,128)(2,1)}, u32[]{:S(2)}, u32[]{:S(2)}) collective-permute-start(bf16[96,768]{1,0:T(8,128)(2,1)} %get-tuple-element.95), channel_id=1, source_target_pairs={{0,24},{1,25},{2,26},{3,27},{4,28},{5,29},{6,30},{7,31},{8,0},{9,1... | collective-permute-start | bytes 442376 | tf_op jit(solution)/shard_map/ppermute | solution.py:542
  219.4 22.6 %collective-permute-start.56 = (bf16[96,768]{1,0:T(8,128)(2,1)}, bf16[96,768]{1,0:T(8,128)(2,1)}, u32[]{:S(2)}, u32[]{:S(2)}) collective-permute-start(bf16[96,768]{1,0:T(8,128)(2,1)} %get-tuple-element.96), channel_id=1, source_target_pairs={{0,16},{1,17},{2,18},{3,19},{4,20},{5,21},{6,22},{7,23},{8,24},{9,... | collective-permute-start | bytes 442376 | tf_op jit(solution)/shard_map/ppermute | solution.py:542
  229.7 30.1 %collective-permute-start.25 = (bf16[2,2,4,48,768]{4,3,2,1,0:T(8,128)(2,1)}, bf16[2,2,4,48,768]{4,3,2,1,0:T(8,128)(2,1)S(1)}, u32[]{:S(2)}, u32[]{:S(2)}) collective-permute-start(bf16[2,2,4,48,768]{4,3,2,1,0:T(8,128)(2,1)} %get-tuple-element.66), channel_id=1, source_target_pairs={{0,1},{1,0},{2,3},{3,2},{4,5},{5,4},{6,7},{7,6},{8,9},{9,8},{10,11... | collective-permute-start | bytes 3538952 | tf_op jit(solution)/shard_map/ppermute | solution.py:542
  238.0 22.3 %collective-permute-start.31 = (bf16[2,2,4,48,768]{4,3,2,1,0:T(8,128)(2,1)S(1)}, bf16[2,2,4,48,768]{4,3,2,1,0:T(8,128)(2,1)S(1)}, u32[]{:S(2)}, u32[]{:S(2)}) collective-permute-start(bf16[2,2,4,48,768]{4,3,2,1,0:T(8,128)(2,1)S(1)} %copy-done.44), channel_id=1, source_target_pairs={{0,1},{1,0},{2,3},{3,2},{4,5},{5,4},{6,7},{7,6},{8,9},{9,8},{10,11... | collective-permute-start | bytes 3538952 | tf_op jit(solution)/shard_map/ppermute | solution.py:542
  242.0 17.7 %collective-permute-start.42 = (bf16[96,768]{1,0:T(8,128)(2,1)S(1)}, bf16[96,768]{1,0:T(8,128)(2,1)S(1)}, u32[]{:S(2)}, u32[]{:S(2)}) collective-permute-start(bf16[96,768]{1,0:T(8,128)(2,1)S(1)} %get-tuple-element.102), channel_id=1, source_target_pairs={{0,16},{1,17},{2,18},{3,19},{4,20},{5,21},{6,22},{7,23},{8,24},{9,... | collective-permute-start | bytes 442376 | tf_op jit(solution)/shard_map/ppermute | solution.py:542
  259.8 43.4 %collective-permute-start.67 = (f32[4,768]{1,0:T(4,128)S(1)}, f32[4,768]{1,0:T(4,128)S(1)}, u32[]{:S(2)}, u32[]{:S(2)}) collective-permute-start(f32[4,768]{1,0:T(4,128)S(1)} %add.176), channel_id=1, source_target_pairs={{0,24},{1,25},{2,26},{3,27},{4,28},{5,29},{6,30},{7,31},{8,0},{9,1... | collective-permute-start | bytes 36872 | tf_op jit(solution)/shard_map/ppermute | solution.py:542
  261.9 45.0 %collective-permute-start.66 = (f32[4,768]{1,0:T(4,128)S(1)}, f32[4,768]{1,0:T(4,128)S(1)}, u32[]{:S(2)}, u32[]{:S(2)}) collective-permute-start(f32[4,768]{1,0:T(4,128)S(1)} %add.176), channel_id=1, source_target_pairs={{0,16},{1,17},{2,18},{3,19},{4,20},{5,21},{6,22},{7,23},{8,24},{9,... | collective-permute-start | bytes 36872 | tf_op jit(solution)/shard_map/ppermute | solution.py:542
  298.3 15.3 %collective-permute-start.45 = (bf16[96,768]{1,0:T(8,128)(2,1)S(1)}, bf16[96,768]{1,0:T(8,128)(2,1)S(1)}, u32[]{:S(2)}, u32[]{:S(2)}) collective-permute-start(bf16[96,768]{1,0:T(8,128)(2,1)S(1)} %fusion.19.rest_0_), channel_id=1, source_target_pairs={{0,2},{1,3},{2,0},{3,1},{4,6},{5,7},{6,4},{7,5},{8,10},{9,11},{10,... | collective-permute-start | bytes 442376 | tf_op jit(solution)/shard_map/ppermute | solution.py:542
  306.9 15.3 %collective-permute-start.52 = (bf16[96,768]{1,0:T(8,128)(2,1)S(1)}, bf16[96,768]{1,0:T(8,128)(2,1)S(1)}, u32[]{:S(2)}, u32[]{:S(2)}) collective-permute-start(bf16[96,768]{1,0:T(8,128)(2,1)S(1)} %fusion.15.rest_4_), channel_id=1, source_target_pairs={{0,2},{1,3},{2,0},{3,1},{4,6},{5,7},{6,4},{7,5},{8,10},{9,11},{10,... | collective-permute-start | bytes 442376 | tf_op jit(solution)/shard_map/ppermute | solution.py:542
  (91 other events, 935.7 us)
Sparse Core Ops, SparseCore 0:
  11.5 122.1 all-gather.2

commit v4 on v3

--- a/solution.py
+++ b/solution.py
@@ -336,13 +336,14 @@
 
 def weight_grad_kernel(where_ref, a_ref, b_ref, keep_ref, send_ref, full_ref):
     z, y = where_ref[0], where_ref[1]
-    a = block(a_ref)
+    b = block(b_ref)
     step = 256
 
     @pl.loop(0, D // step)
     def _(n):
         lane = pl.multiple_of(n * step, step)
-        full_ref[:, pl.ds(lane, step)] = mm_tn(a, block(b_ref, *([slice(None)] * (len(b_ref.shape) - 1)), pl.ds(lane, step)))
+        a = block(a_ref, *([slice(None)] * (len(a_ref.shape) - 1)), pl.ds(lane, step))
+        full_ref[pl.ds(lane, step), :] = mm_tn(a, b)
 
     for r in range(LINE):
         base = 2 * lax.rem(z + r, LINE)
@@ -366,9 +367,7 @@
     )(where, a, b)
 
 
-def attention_back_kernel(seqs, most, slope_ref, dr2_ref, part_ref, came_ref, r1_ref, q_ref, qkv_ref, att_ref, w_ref, norm_ref, pos_ref, dr1_ref, rhs_ref, lhs_ref, small_ref, datt_ref, away_ref, hot_ref):
-    length = qkv_ref.shape[0] // seqs
-    listed = seqs * most
+def norm_back_kernel(dr2_ref, part_ref, came_ref, r1_ref, w_ref, norm_ref, dr1_ref, low_ref, datt_ref, small_ref):
     dh1 = dr2_ref[...] + part_ref[...] + came_ref[...].astype(F32)
     unit, rstd = norm_parts(r1_ref[...])
     small_ref[0:1, :] = jnp.sum(dh1 * unit, axis=0, keepdims=True)
@@ -376,13 +375,31 @@
     dr1 = norm_back(dh1, unit, rstd, norm_ref[0:1, :])
     dr1_ref[...] = dr1
     low = dr1.astype(LOW)
-    rhs_ref[0:listed, 3 * D : 4 * D] = low
-    rhs_ref[listed:, 3 * D : 4 * D] = jnp.zeros((seqs * length - listed, D), LOW)
-    lhs_ref[0:listed, :] = att_ref[...]
-    lhs_ref[listed:, :] = jnp.zeros((seqs * length - listed, D), LOW)
+    low_ref[...] = low
     for n in range(2):
         lanes = slice(n * D // 2, (n + 1) * D // 2)
-        datt_ref[:, lanes] = mm_nt(low, block(w_ref, slice(n * SHARDS // 2, (n + 1) * SHARDS // 2), 3)).astype(LOW)
+        datt_ref[:, lanes] = mm_nt(low, block(w_ref, slice(n * SHARDS // 2, (n + 1) * SHARDS // 2))).astype(LOW)
+
+
+def norm_back_call(dr2, part, came, r1_m, w_attn, norms):
+    listed = dr2.shape[0]
+    same = lambda shape: pl.BlockSpec(shape, lambda g: (0,) * len(shape))
+    rows = same((listed, D))
+    return pl.pallas_call(
+        norm_back_kernel,
+        out_shape=(out((listed, D), F32), out((listed, D), LOW), out((listed, D), LOW), out((2, D), F32)),
+        grid=(1,),
+        in_specs=[rows, rows, rows, rows, pl.BlockSpec((SHARDS, None, ROWS, D), lambda g: (0, 3, 0, 0)), same((4, D))],
+        out_specs=(rows, rows, rows, same((2, D))),
+        compiler_params=BIG,
+        cost_estimate=cost(4),
+        name="norm_back",
+    )(dr2, part, came, r1_m, w_attn, norms)
+
+
+def attention_back_kernel(seqs, most, slope_ref, datt_ref, q_ref, qkv_ref, pos_ref, rhs_ref, away_ref, hot_ref):
+    length = qkv_ref.shape[0] // seqs
+    listed = seqs * most
     first_m = lax.broadcasted_iota(jnp.int32, (most, 128), 1) < HEAD_DIM
     spots = lax.broadcasted_iota(jnp.int32, (listed, length), 1)
     away_ref[...] = jnp.abs(pos_ref[...] - spots).astype(F32)
@@ -416,72 +433,66 @@
             rhs_ref[rows, pl.ds(2 * D + lane, 128)] = mm_tn(p.astype(LOW), da).astype(LOW)
 
 
-def attention_back(dr2, part, came, r1_m, q_m, qkv, att_m, w_attn, norms, pos, slopes, seqs):
+def attention_back(datt, q_m, qkv, pos, slopes, seqs):
     tokens = qkv.shape[0]
     listed = pos.shape[0]
     return pl.pallas_call(
         functools.partial(attention_back_kernel, seqs, listed // seqs),
-        out_shape=(out((listed, D), F32), out((tokens, 4 * D), LOW), out((tokens, D), LOW), out((2, D), F32)),
-        in_specs=[SMEM] + [VMEM] * 10,
-        out_specs=(VMEM,) * 4,
-        scratch_shapes=[pltpu.VMEM((listed, D), LOW), pltpu.VMEM((listed, tokens // seqs), F32), pltpu.VMEM((listed, tokens // seqs), LOW)],
-        compiler_params=BIG,
-        cost_estimate=cost(18),
+        out_shape=out((tokens, 3 * D), LOW),
+        in_specs=[SMEM] + [VMEM] * 4,
+        out_specs=VMEM,
+        scratch_shapes=[pltpu.VMEM((listed, tokens // seqs), F32), pltpu.VMEM((listed, tokens // seqs), LOW)],
+        compiler_params=BIG,
+        cost_estimate=cost(15),
         name="attention_back",
-    )(slopes, dr2, part, came, r1_m, q_m, qkv, att_m, w_attn, norms, pos)
-
-
-def attention_grads_kernel(where_ref, x_ref, lhs_ref, rhs_ref, keep0_ref, keep1_ref, send0_ref, send1_ref, full_ref):
+    )(slopes, datt, q_m, qkv, pos)
+
+
+def attention_grads_kernel(rc, where_ref, flip_ref, rhs_ref, att_ref, low_ref, cut_ref, full_ref):
     z, y, mine = where_ref[0], where_ref[1], where_ref[4]
     half = ROWS // 2
     step = 256
-    for rc in (1, 0):
-        for rx in (0, 1):
-            r = 2 * rx + rc
-            j = (mine + r) if False else jnp.bitwise_xor(mine, r)
-            is_out = j == 3
-
-            def fill(a_ref):
-                @pl.loop(0, D // step)
-                def _(n):
-                    lane = pl.multiple_of(n * step, step)
-                    cols = pl.ds(pl.multiple_of(j * D + n * step, step), step)
-                    full_ref[:, pl.ds(lane, step)] = mm_tn(a_ref[...], rhs_ref[:, cols])
-
-            @pl.when(is_out)
-            def _():
-                fill(lhs_ref)
-
-            @pl.when(jnp.logical_not(is_out))
-            def _():
-                fill(x_ref)
-
-            refs = (keep0_ref, keep1_ref) if rc == 0 else (send0_ref, send1_ref)
-            for rz in range(LINE):
-                base = 2 * lax.rem(z + rz, LINE)
-                for ry in (0, 1):
-                    start = (base + (y if ry == 0 else 1 - y)) * ROWS
-                    for part in (0, 1):
-                        rows = pl.ds(pl.multiple_of(start + part * half, 8), half)
-                        value = full_ref[rows, :].astype(LOW)
-                        if part == 0:
-                            refs[0][rx, ry, rz] = value
-                        else:
-                            refs[1][ry, rx, rz] = value
-
-
-def attention_grads(where, x, lhs, rhs):
-    shape = (2, 2, LINE, ROWS // 2, D)
-    return pl.pallas_call(
-        attention_grads_kernel,
-        out_shape=(out(shape, LOW),) * 4,
-        in_specs=[SMEM, VMEM, VMEM, VMEM],
-        out_specs=(VMEM,) * 4,
+    for rx in (0, 1):
+        j = jnp.bitwise_xor(mine, 2 * rx + rc)
+
+        @pl.when(j == 3)
+        def _():
+            for n in range(D // step):
+                rows = slice(n * step, (n + 1) * step)
+                full_ref[rows, :] = mm_tn(att_ref[:, rows], low_ref[...])
+
+        @pl.when(j != 3)
+        def _():
+            @pl.loop(0, D // step)
+            def _(n):
+                lane = pl.multiple_of(n * step, step)
+                cols = pl.ds(pl.multiple_of(j * D + n * step, step), step)
+                full_ref[:, pl.ds(lane, step)] = mm(flip_ref[...], rhs_ref[:, cols])
+
+        for rz in range(LINE):
+            base = 2 * lax.rem(z + rz, LINE)
+            for ry in (0, 1):
+                start = (base + (y if ry == 0 else 1 - y)) * ROWS
+                for part in (0, 1):
+                    rows = pl.ds(pl.multiple_of(start + part * half, 8), half)
+                    value = full_ref[rows, :].astype(LOW)
+                    if part == 0:
+                        cut_ref[0, rx, ry, rz] = value
+                    else:
+                        cut_ref[1, ry, rx, rz] = value
+
+
+def attention_grads(where, rc, x_flip, rhs, att_m, low):
+    return pl.pallas_call(
+        functools.partial(attention_grads_kernel, rc),
+        out_shape=out((2, 2, 2, LINE, ROWS // 2, D), LOW),
+        in_specs=[SMEM] + [VMEM] * 4,
+        out_specs=VMEM,
         scratch_shapes=[pltpu.VMEM((D, D), F32)],
         compiler_params=BIG,
-        cost_estimate=cost(10),
+        cost_estimate=cost(5),
         name="attention_grads",
-    )(where, x, lhs, rhs)
+    )(where, x_flip, rhs, att_m, low)
 
 
 def input_grad_kernel(seqs, rhs_ref, w_ref, dr1_ref, pos_ref, out_ref):
@@ -543,59 +554,68 @@
 
 
 def share_dp(value):
-    core = send(value, "c")
-    return value, core, send(value, "x"), send(core, "x")
-
-
-def line_sum(block_list, kept):
-    total = kept.astype(F32)
-    for r, value in block_list:
-        total = total + send(value, r).astype(F32)
-    return total
-
-
-def reduce_quarter(keep, away):
-    got = send(away, "y")
-    total = keep.astype(F32) + got.astype(F32)
-    return line_sum([(r, total[r].astype(LOW)) for r in (1, 2, 3)], total[0]).astype(LOW)
-
-
-def reduce_attention(keep, away, first, second):
-    total = keep.astype(F32) + send(away, "c").astype(F32)
-    total = total[0] + send(total[1].astype(LOW), first).astype(F32)
-    total = total[0] + send(total[1].astype(LOW), second).astype(F32)
-    return line_sum([(r, total[r].astype(LOW)) for r in (1, 2, 3)], total[0]).astype(LOW)
-
-
-def finish_kernel(rows_out, where_ref, *rest):
-    held = rest[-1]
-    count = len(held.shape) and held.shape[0]
-    pieces, outs = rest[: QUARTERS * count], rest[QUARTERS * count : -1]
+    other = send(value, "x")
+    return value, send(value, "c"), other, send(other, "c")
+
+
+def after(value, *earlier):
+    return lax.optimization_barrier((value, *earlier))[0]
+
+
+def add(kept, got):
+    return kept.astype(F32) + got.astype(F32)
+
+
+def line_send(total):
+    return [send(total[r].astype(LOW), r) for r in (1, 2, 3)]
+
+
+def line_add(total, got):
+    return (total[0] + got[0].astype(F32) + got[1].astype(F32) + got[2].astype(F32)).astype(LOW)
+
+
+def finish_ffn_kernel(where_ref, *rest):
+    pieces, (down_ref, up_ref) = rest[:QUARTERS], rest[QUARTERS:]
     mine = where_ref[4]
     for n, ref in enumerate(pieces):
-        held[n // QUARTERS, jnp.bitwise_xor(mine, n % QUARTERS)] = ref[...].astype(F32)
-    if rows_out:
-        for j in range(QUARTERS):
-            outs[0][j * ROWS : (j + 1) * ROWS, :] = held[0, j]
-        return
-    at = 0
-    for ref in outs:
-        for j in range(ref.shape[1] // D):
-            ref[:, j * D : (j + 1) * D] = held[at // QUARTERS, at % QUARTERS]
-            at += 1
-
-
-def finish(where, pieces, widths, rows_out=False):
-    shapes = [out((QUARTERS * ROWS, D), F32)] if rows_out else [out((ROWS, n * D), F32) for n in widths]
-    return pl.pallas_call(
-        functools.partial(finish_kernel, rows_out),
-        out_shape=tuple(shapes),
-        in_specs=[SMEM] + [VMEM] * len(pieces),
-        out_specs=(VMEM,) * len(shapes),
-        scratch_shapes=[pltpu.VMEM((len(pieces) // QUARTERS, QUARTERS, ROWS, D), F32)],
+        j = jnp.bitwise_xor(mine, n)
+        down_ref[pl.ds(pl.multiple_of(j * ROWS, 8), ROWS), :] = ref[0].astype(F32)
+        for half in (0, 1):
+            up_ref[:, pl.ds(pl.multiple_of((half * QUARTERS + j) * D, D), D)] = ref[1 + half].astype(F32)
+
+
+def finish_attention_kernel(where_ref, *rest):
+    pieces, (qkv_ref, out_ref, held_ref) = rest[:QUARTERS], rest[QUARTERS:]
+    mine = where_ref[4]
+    for n, ref in enumerate(pieces):
+        held_ref[jnp.bitwise_xor(mine, n)] = ref[...].astype(F32)
+    for j in range(3):
+        qkv_ref[:, j * D : (j + 1) * D] = held_ref[j]
+    out_ref[...] = held_ref[3]
+
+
+def finish_ffn(where, pieces):
+    return pl.pallas_call(
+        finish_ffn_kernel,
+        out_shape=(out((QUARTERS * ROWS, D), F32), out((ROWS, 2 * QUARTERS * D), F32)),
+        in_specs=[SMEM] + [VMEM] * QUARTERS,
+        out_specs=(VMEM, VMEM),
+        compiler_params=BIG,
+        cost_estimate=cost(4),
+        name="finish_ffn",
+    )(where, *pieces)
+
+
+def finish_attention(where, pieces):
+    return pl.pallas_call(
+        finish_attention_kernel,
+        out_shape=(out((ROWS, 3 * D), F32), out((ROWS, D), F32)),
+        in_specs=[SMEM] + [VMEM] * QUARTERS,
+        out_specs=(VMEM, VMEM),
+        scratch_shapes=[pltpu.VMEM((QUARTERS, ROWS, D), F32)],
         compiler_params=BIG,
         cost_estimate=cost(2),
-        name="finish",
+        name="finish_attention",
     )(where, *pieces)
 
 
@@ -605,12 +625,6 @@
         for key in list(got):
             got[key | {step}] = send(got[key], step)
     return [got[frozenset(n for n, b in zip("yxc", key) if b)] for key in KEYS]
-
-
-def sum_all(value):
-    for step in ("c", "x", "y"):
-        value = value + send(value, step)
-    return value + send(value, 1) + send(value, 2) + send(value, 3)
 
 
 def on_block(hidden_in, w_qkv, w_out, w_up, w_down, gain_attn, shift_attn, gain_ffn, shift_ffn, grad_listed, positions, counts):
@@ -624,6 +638,8 @@
     norms = jnp.concatenate([gain_attn, shift_attn, gain_ffn, shift_ffn, jnp.zeros((D - 4 * ROWS,), LOW)])
     attn_piece = jnp.concatenate([attn_piece, jnp.broadcast_to(norms, (EXTRA, D))], axis=0)
     line = jnp.stack([attn_piece] + [send(attn_piece, r) for r in (1, 2, 3)])
+    x = hidden_in.reshape(tokens, width)
+    line, x_flip = lax.optimization_barrier((line, x.T))
     halves = [
         spread(line[:, start : start + size], order)
         for (start, size), order in zip(HALVES, (("y", "x"), ("x", "y")))
@@ -642,7 +658,6 @@
     tails = jnp.roll(tails[:, ::-1], i // 2 + 1, axis=1)
     norms = tails.transpose(1, 0, 2).reshape(SHARDS, 4, ROWS).transpose(1, 0, 2).reshape(4, D).astype(F32)
     slopes = jnp.exp2(-8.0 * (jnp.arange(HEADS, dtype=F32) + 1.0) / HEADS)
-    x = hidden_in.reshape(tokens, width)
     pos = positions.reshape(seqs * most, 1)
     live = jnp.arange(most, dtype=jnp.int32)[None, :] < counts[:, None]
     dy = jnp.where(live[:, :, None], grad_listed, jnp.zeros_like(grad_listed)).reshape(seqs * most, width)
@@ -654,22 +669,46 @@
     act, to_gate, to_up = ffn_again(where, h_all, w_ffn)
     e_all = jnp.stack(share_dp(e2))
     dgate, dup, keep, away = ffn_back(where, e_all, to_gate, to_up, w_ffn)
-    total = keep + send(away, "c").astype(F32)
-    came = send(total[1].astype(LOW), "x")
-    g_down = reduce_quarter(*weight_grad(where, act, e_all))
-    g_gate = reduce_quarter(*weight_grad(where, h_all, dgate))
-    g_up = reduce_quarter(*weight_grad(where, h_all, dup))
-    dr1, rhs, lhs, small_attn = attention_back(dr2, total[0], came, r1_m, q_m, qkv, att_m, w_attn, norms, pos, slopes, seqs)
-    keep0, keep1, away0, away1 = attention_grads(where, x, lhs, rhs)
-    g_attn = jnp.concatenate(
-        [reduce_attention(keep0, away0, "x", "y"), reduce_attention(keep1, away1, "y", "x")], axis=0
-    )
-    grad_in = input_grad(rhs, w_attn, dr1, positions)
-    (grad_down,) = finish(where, share_dp(send(g_down, "down")), (), rows_out=True)
-    (grad_up,) = finish(where, (*share_dp(g_gate), *share_dp(g_up)), (2 * QUARTERS,))
-    grad_qkv, grad_out = finish(where, share_dp(g_attn), (3, 1))
-    small = sum_all(jnp.concatenate([small_attn, small_ffn]))
-    small = lax.dynamic_slice_in_dim(small, i * ROWS, ROWS, axis=1)
+    part = add(keep, send(away, "c"))
+    keep_d, away_d = weight_grad(where, act, e_all)
+    got_d = send(away_d, "y")
+    keep_g, away_g = weight_grad(where, after(h_all, away_d), dgate)
+    came = send(part[1].astype(LOW), "x")
+    got_g = send(away_g, "y")
+    keep_u, away_u = weight_grad(where, after(h_all, away_g), dup)
+    got_u = send(away_u, "y")
+    dr1, low, datt, small_attn = norm_back_call(dr2, part[0], after(came, away_u), r1_m, w_attn, norms)
+    small = lax.all_gather(jnp.concatenate([small_attn, small_ffn]), AXES)
+    sum_d = add(keep_d, got_d)
+    line_d = line_send(sum_d)
+    rhs = attention_back(after(datt, sum_d), q_m, qkv, pos, slopes, seqs)
+    got_g, got_u, rhs = lax.optimization_barrier((got_g, got_u, rhs))
+    sum_gu = jnp.concatenate([add(keep_g, got_g), add(keep_u, got_u)], axis=1)
+    line_gu = line_send(sum_gu)
+    away = attention_grads(where, 1, x_flip, after(rhs, sum_gu), att_m, low)
+    came = send(away, "c")
+    g_down = line_add(sum_d, after(line_d, away))
+    g_down = send(g_down, "down")
+    keep = attention_grads(where, 0, x_flip, after(rhs, away), att_m, low)
+    came, keep = lax.optimization_barrier((came, keep))
+    total = add(keep, came)
+    got0 = send(total[0, 1].astype(LOW), "x")
+    got1 = send(total[1, 1].astype(LOW), "y")
+    grad_in = input_grad(after(rhs, total), w_attn, dr1, positions)
+    g_ffn = jnp.concatenate([g_down, line_add(sum_gu, after(line_gu, grad_in))]).reshape(3, ROWS, D)
+    got0, got1 = after((got0, got1), g_ffn)
+    shared = share_dp(g_ffn)
+    total0 = add(total[0, 0], got0)
+    total1 = add(total[1, 0], got1)
+    got0 = send(total0[1].astype(LOW), "y")
+    got1 = send(total1[1].astype(LOW), "x")
+    got0, got1, shared = lax.optimization_barrier((got0, got1, shared))
+    total = jnp.concatenate([add(total0[0], got0), add(total1[0], got1)], axis=1)
+    line_a = line_send(total)
+    grad_down, grad_up = finish_ffn(where, after(shared, total))
+    g_attn = line_add(total, after(line_a, grad_down))
+    grad_qkv, grad_out = finish_attention(where, share_dp(g_attn))
+    small = jnp.sum(lax.dynamic_slice_in_dim(small, i * ROWS, ROWS, axis=2), axis=0)
     return (
         layer_out.reshape(seqs, length, width),
         grad_in.reshape(seqs, length, width),

time: 351 us -> 382 us (1.088)
  blocking collectives: 0 us -> 39.7 us
  starting transfers between devices: 65.6 us -> 46.5 us
  other arithmetic: 11.3 us -> 15.6 us
  waiting for transfers between devices: 142 us -> 146 us
    all_gather x0 -> x1, blocking collectives: none -> 39.7 us  [on_block(): small = lax.all_gather(jnp.concatenate([small_attn, small_ffn]), AXES)]
    ppermute x68 -> x49, starting transfers between devices: 65.6 us -> 46.5 us  [send(): return lax.ppermute(value, AXES, MOVES[move])]
    another operation x5 -> x4, other arithmetic: 1.61 us -> 6.49 us
    pallas_call x4 -> x5, Pallas kernels: 17.8 us -> 20.2 us  [the longest x2 11.3 us: attention_grads(): pl.pallas_call(functools.partial(attention_grads_kernel, rc), out_shape=o...]
    ppermute x68 -> x49, waiting for transfers between devices: 115 us -> 115 us  [send(): return lax.ppermute(value, AXES, MOVES[move])]
  transfers between devices with their start and end apart: 69 -> 50, of which waited for: 31 -> 22; matrix products, arithmetic and copies ran while one was open for 4% -> 6% of each run, Pallas kernels for 23% -> 19%
where the time goes in v4:
time: 382 us; the launch traced here: 381 us
  waiting for transfers between devices  146 us (38%)
  Pallas kernels  105 us (27%)
  starting transfers between devices  46.5 us (12%)
  blocking collectives  39.7 us (10%)
  other arithmetic  15.6 us (4%)
  between operations  14.7 us (4%)
  local copies, waits for them, and re-layouts  14.2 us (4%)
    ppermute x49, waiting for transfers between devices, send(): return lax.ppermute(value, AXES, MOVES[move])  115 us
    ppermute x49, starting transfers between devices, send(): return lax.ppermute(value, AXES, MOVES[move])  46.5 us
    all_gather x1, blocking collectives, on_block(): small = lax.all_gather(jnp.concatenate([small_attn, small_ffn]), AXES)  39.7 us
    all_gather x1, waiting for transfers between devices, on_block(): lax.all_gather(ffn_piece, AXES, axis=0, tiled=False)  30.3 us
    pallas_call x1, Pallas kernels, attention_forward(): pl.pallas_call(functools.partial(attention_kernel, seqs, listed // seqs),...  18 us
    pallas_call x1, Pallas kernels, ffn_forward(): pl.pallas_call(functools.partial(ffn_kernel, seqs, listed // seqs), out_s...  17 us
    pallas_call x1, Pallas kernels, attention_back(): pl.pallas_call(functools.partial(attention_back_kernel, seqs, listed // s...  15.8 us
    pallas_call x3, Pallas kernels, weight_grad(): pl.pallas_call(weight_grad_kernel, out_shape=(out(shape, LOW), out(shape,...  11.6 us
  transfers between devices with their start and end apart: 50, of which 22 were waited for; matrix products, arithmetic and copies ran while one was open for 6% of the time, Pallas kernels for 19%

profile of v4, /device:TPU:0, one launch (start us, length us, event | category | flops | bytes accessed | tf_op | source)
XLA Modules:
  0.0 381.0 jit_solution(7260752517176017980)
XLA Ops:
  18.8 6.8 %collective-permute-done.1 = bf16[104,768]{1,0:T(8,128)(2,1)S(1)} collective-permute-done((bf16[104,768]{1,0:T(8,128)(2,1)S(1)}, bf16[104,768]{1,0:T(8,128)(2,1)S(1)}, u32[]{:S(2)}, u32[]{:S(2)}) %collective-permute-start.1) | collective-permute-done | bytes 159776 | tf_op jit(solution)/shard_map/ppermute | solution.py:553
  31.4 6.8 %collective-permute-done.6.rest_5_ = bf16[4,56,768]{2,1,0:T(8,128)(2,1)S(1)} collective-permute-done((bf16[4,56,768]{2,1,0:T(8,128)(2,1)S(1)}, bf16[4,56,768]{2,1,0:T(8,128)(2,1)S(1)}, u32[]{:S(2)}, u32[]{:S(2)}) %collective-permute-start.6) | collective-permute-done | bytes 344096 | tf_op jit(solution)/shard_map/ppermute | solution.py:553
  50.8 5.4 %collective-permute-done.8.rest_7_ = bf16[4,56,768]{2,1,0:T(8,128)(2,1)S(1)} collective-permute-done((bf16[4,56,768]{2,1,0:T(8,128)(2,1)S(1)}, bf16[4,56,768]{2,1,0:T(8,128)(2,1)S(1)}, u32[]{:S(2)}, u32[]{:S(2)}) %collective-permute-start.8) | collective-permute-done | bytes 344096 | tf_op jit(solution)/shard_map/ppermute | solution.py:553
  56.8 6.1 %collective-permute-done.7.rest_6_ = bf16[4,48,768]{2,1,0:T(8,128)(2,1)} collective-permute-done((bf16[4,48,768]{2,1,0:T(8,128)(2,1)}, bf16[4,48,768]{2,1,0:T(8,128)(2,1)}, u32[]{:S(2)}, u32[]{:S(2)}) %collective-permute-start.7) | collective-permute-done | bytes 294944 | tf_op jit(solution)/shard_map/ppermute | solution.py:553
  65.9 18.0 %attention_forward.1 = (bf16[512,2304]{1,0:T(8,128)(2,1)}, f32[512,768]{1,0:T(8,128)}, bf16[128,768]{1,0:T(8,128)(2,1)}, bf16[128,768]{1,0:T(8,128)(2,1)}, bf16[...) custom-call(s32[5]{0:T(128)} %stack.83.where_ref, f32[12]{0:T(128)} %multiply_exponential_fusion.slope_ref, ...), custom_call_target="tpu_custom_call" | custom-call | bytes 60000000 | tf_op jit(solution)/shard_map/attention_forward/pallas_call | solution.py:163
  85.6 10.3 %collective-permute-done.18 = bf16[128,768]{1,0:T(8,128)(2,1)S(1)} collective-permute-done((bf16[128,768]{1,0:T(8,128)(2,1)}, bf16[128,768]{1,0:T(8,128)(2,1)S(1)}, u32[]{:S(2)}, u32[]{:S(2)}) %collective-permute-start.18) | collective-permute-done | bytes 196640 | tf_op jit(solution)/shard_map/ppermute | solution.py:553
  99.3 30.3 %all-gather.5.cloned.1.call-done = bf16[96,96,768]{2,1,0:T(8,128)(2,1)} async-done(((bf16[3,96,768]{2,1,0:T(8,128)(2,1)}), bf16[96,96,768]{2,1,0:T(8,128)(2,1)}) %all-gather.5.cloned.1.call-update) | async-done | bytes 14155792 | tf_op jit(solution)/shard_map/all_gather | solution.py:655
  129.6 17.0 %ffn_forward.1 = (bf16[512,768]{1,0:T(8,128)(2,1)}, f32[128,768]{1,0:T(8,128)}, bf16[128,768]{1,0:T(8,128)(2,1)}, f32[2,768]{1,0:T(2,128)}) custom-call(f32[512,768]{1,0:T(8,128)} %get-tuple-element.82.h1_ref, bf16[8,4,3,96,768]{4,3,2,1,0:T(8,128)(2,1)} %bitcast.126, bf16[8,4,3,96,768]{4,3,2,1,0:T(8,128)(2,1)} %bitcast.127, ...), custom_call_target="tpu_custom_call" | custom-call | bytes 48000000 | tf_op jit(solution)/shard_map/ffn_forward/pallas_call | solution.py:231
  147.2 6.7 %collective-permute-done.21 = bf16[128,768]{1,0:T(8,128)(2,1)S(1)} collective-permute-done((bf16[128,768]{1,0:T(8,128)(2,1)}, bf16[128,768]{1,0:T(8,128)(2,1)S(1)}, u32[]{:S(2)}, u32[]{:S(2)}) %collective-permute-start.21) | collective-permute-done | bytes 196640 | tf_op jit(solution)/shard_map/ppermute | solution.py:553
  153.9 6.6 %ffn_again.1 = (bf16[512,768]{1,0:T(8,128)(2,1)}, f32[512,768]{1,0:T(8,128)}, f32[512,768]{1,0:T(8,128)}) custom-call(s32[5]{0:T(128)} %stack.83.where_ref, bf16[4,128,768]{2,1,0:T(8,128)(2,1)} %pad_maximum_fusion.2.h_ref.a_ref, bf16[8,4,3,96,768]{4,3,2,1,0:T(8,128)(2,1)} %bitcast.129, bf16[8,4,3,96,768]{4,3,2,1,0:T(8,128)(2,1)} %bitcast.130), custom_call_target="tpu_custom_call" | custom-call | bytes 18000000 | tf_op jit(solution)/shard_map/ffn_again/pallas_call | solution.py:287
  161.5 7.4 %ffn_back.1 = (bf16[512,768]{1,0:T(8,128)(2,1)}, bf16[512,768]{1,0:T(8,128)(2,1)}, f32[2,128,768]{2,1,0:T(8,128)}, bf16[2,128,768]{2,1,0:T(8,128)(2,1)}) custom-call(s32[5]{0:T(128)} %stack.83.where_ref, bf16[4,128,768]{2,1,0:T(8,128)(2,1)} %pad_maximum_fusion.3.b_ref.e_ref, f32[512,768]{1,0:T(8,128)} %get-tuple-element.89.to_gate_ref, ...), custom_call_target="tpu_custom_call" | custom-call | bytes 21000000 | tf_op jit(solution)/shard_map/ffn_back/pallas_call | solution.py:322
  186.0 4.7 %collective-permute-done.26.came_ref = bf16[128,768]{1,0:T(8,128)(2,1)S(1)} collective-permute-done((bf16[128,768]{1,0:T(8,128)(2,1)S(1)}, bf16[128,768]{1,0:T(8,128)(2,1)S(1)}, u32[]{:S(2)}, u32[]{:S(2)}) %collective-permute-start.26) | collective-permute-done | bytes 196640 | tf_op jit(solution)/shard_map/ppermute | solution.py:553
  194.5 11.7 %collective-permute-done.27 = bf16[4,96,768]{2,1,0:T(8,128)(2,1)S(1)} collective-permute-done((bf16[4,96,768]{2,1,0:T(8,128)(2,1)S(1)}, bf16[4,96,768]{2,1,0:T(8,128)(2,1)S(1)}, u32[]{:S(2)}, u32[]{:S(2)}) %collective-permute-start.27) | collective-permute-done | bytes 589856 | tf_op jit(solution)/shard_map/ppermute | solution.py:553
  206.3 15.8 %attention_back.1.rhs_ref = bf16[512,2304]{1,0:T(8,128)(2,1)} custom-call(f32[12]{0:T(128)} %multiply_exponential_fusion.slope_ref, bf16[128,768]{1,0:T(8,128)(2,1)} %get-tuple-element.104.datt_ref, bf16[128,768]{1,0:T(8,128)(2,1)} %get-tuple-element.105.q_ref, bf16[512,2304]{1,0:T(8,128)(2,1)} %get-tuple-element.106.qkv_ref, s32[128,1]{1,0:T(8,128)} %reshape.98.pos_ref), custom_call_target="tpu_custom_call" | custom-call | bytes 45000000 | tf_op jit(solution)/shard_map/attention_back/pallas_call | solution.py:439
  222.1 5.4 %attention_grads.2 = bf16[2,2,2,4,48,768]{5,4,3,2,1,0:T(8,128)(2,1)} custom-call(s32[5]{0:T(128)} %stack.83.where_ref, bf16[768,512]{1,0:T(8,128)(2,1)} %bitcast.134, bf16[512,2304]{1,0:T(8,128)(2,1)} %attention_back.1.rhs_ref, bf16[128,768]{1,0:T(8,128)(2,1)} %get-tuple-element.114.att_ref, bf16[128,768]{1,0:T(8,128)(2,1)} %get-tuple-element.115.low_ref), custom_call_target="tpu_custom_call" | custom-call | bytes 15000000 | tf_op jit(solution)/shard_map/attention_grads/pallas_call | solution.py:486
  236.8 5.9 %attention_grads.3 = bf16[2,2,2,4,48,768]{5,4,3,2,1,0:T(8,128)(2,1)} custom-call(s32[5]{0:T(128)} %stack.83.where_ref, bf16[768,512]{1,0:T(8,128)(2,1)} %bitcast.135, bf16[512,2304]{1,0:T(8,128)(2,1)} %attention_back.1.rhs_ref, bf16[128,768]{1,0:T(8,128)(2,1)} %get-tuple-element.114.att_ref, bf16[128,768]{1,0:T(8,128)(2,1)} %get-tuple-element.115.low_ref), custom_call_target="tpu_custom_call" | custom-call | bytes 15000000 | tf_op jit(solution)/shard_map/attention_grads/pallas_call | solution.py:486
  248.6 6.2 %fusion.28 = (bf16[2,2,2,4,48,768]{5,4,3,2,1,0:T(8,128)(2,1)}, f32[2,2,2,4,48,768]{5,4,3,2,1,0:T(8,128)}) fusion(bf16[2,2,2,4,48,768]{5,4,3,2,1,0:T(8,128)(2,1)} %collective-permute-done.28, bf16[2,2,2,4,48,768]{5,4,3,2,1,0:T(8,128)(2,1)} %attention_grads.3), kind=kLoop, calls=%fused_computation.86 | loop fusion | flops 4718592 | bytes 11796480 | tf_op jit(solution)/shard_map/convert.16
  254.7 8.1 %input_grad.1 = f32[512,768]{1,0:T(8,128)} custom-call(bf16[512,2304]{1,0:T(8,128)(2,1)} %attention_back.1.rhs_ref, bf16[8,4,96,768]{3,2,1,0:T(8,128)(2,1)} %get-tuple-element.101.w_ref, f32[128,768]{1,0:T(8,128)} %get-tuple-element.120.dr1_ref, s32[4,32]{1,0:T(4,128)} %pos_ref.1), custom_call_target="tpu_custom_call" | custom-call | bytes 24000000 | tf_op jit(solution)/shard_map/input_grad/pallas_call | solution.py:516
  264.3 9.2 %collective-permute-done.36 = bf16[192,768]{1,0:T(8,128)(2,1)S(1)} collective-permute-done((bf16[192,768]{1,0:T(8,128)(2,1)}, bf16[192,768]{1,0:T(8,128)(2,1)S(1)}, u32[]{:S(2)}, u32[]{:S(2)}) %collective-permute-start.36) | collective-permute-done | bytes 294944 | tf_op jit(solution)/shard_map/ppermute | solution.py:553
  275.1 6.7 %collective-permute-start.29 = (bf16[2,4,48,768]{3,2,1,0:T(8,128)(2,1)S(1)}, bf16[2,4,48,768]{3,2,1,0:T(8,128)(2,1)S(1)}, u32[]{:S(2)}, u32[]{:S(2)}) collective-permute-start(bf16[2,4,48,768]{3,2,1,0:T(8,128)(2,1)S(1)} %get-tuple-element.153), channel_id=1, source_target_pairs={{0,2},{1,3},{2,0},{3,1},{4,6},{5,7},{6,4},{7,5},{8,10},{9,11},{10,... | collective-permute-start | bytes 1769480 | tf_op jit(solution)/shard_map/ppermute | solution.py:553
  283.1 19.9 %collective-permute-done.41.rest_2_ = bf16[3,96,768]{2,1,0:T(8,128)(2,1)S(1)} collective-permute-done((bf16[3,96,768]{2,1,0:T(8,128)(2,1)S(1)}, bf16[3,96,768]{2,1,0:T(8,128)(2,1)S(1)}, u32[]{:S(2)}, u32[]{:S(2)}) %collective-permute-start.41) | collective-permute-done | bytes 442400 | tf_op jit(solution)/shard_map/ppermute | solution.py:553
  305.1 7.7 %collective-permute-done.38 = bf16[4,48,768]{2,1,0:T(8,128)(2,1)S(1)} collective-permute-done((bf16[4,48,768]{2,1,0:T(8,128)(2,1)S(1)}, bf16[4,48,768]{2,1,0:T(8,128)(2,1)S(1)}, u32[]{:S(2)}, u32[]{:S(2)}) %collective-permute-start.38) | collective-permute-done | bytes 294944 | tf_op jit(solution)/shard_map/ppermute | solution.py:553
  321.7 7.1 %collective-permute-done.44 = bf16[96,768]{1,0:T(8,128)(2,1)S(1)} collective-permute-done((bf16[96,768]{1,0:T(8,128)(2,1)S(1)}, bf16[96,768]{1,0:T(8,128)(2,1)S(1)}, u32[]{:S(2)}, u32[]{:S(2)}) %collective-permute-start.44) | collective-permute-done | bytes 147488 | tf_op jit(solution)/shard_map/ppermute | solution.py:553
  329.3 39.7 %all-gather.2 = f32[32,4,768]{2,1,0:T(4,128)S(1)} all-gather(f32[1,4,768]{2,1,0:T(4,128)S(1)} %maximum_bitcast_fusion), channel_id=3, replica_groups=mesh['fsdp'=8,'dp'=4] {'fsdp','dp'}, dimensions={0}, use_global_device_ids=true | all-gather | bytes 405504 | tf_op jit(solution)/shard_map/all_gather | solution.py:681
  (225 shorter events, 96.9 us)
Async XLA Ops:
  7.2 122.3 %all-gather.5.cloned.1.call-start = ((), (), s32[]{:S(2)}) async-start(), calls=%async_computation | async-start | bytes 14598144 | tf_op jit(solution)/shard_map/all_gather | solution.py:655
  9.6 16.0 %collective-permute-start.1 = (bf16[104,768]{1,0:T(8,128)(2,1)S(1)}, bf16[104,768]{1,0:T(8,128)(2,1)S(1)}, u32[]{:S(2)}, u32[]{:S(2)}) collective-permute-start(bf16[104,768]{1,0:T(8,128)(2,1)S(1)} %get-tuple-element.168), channel_id=1, source_target_pairs={{0,16},{1,17},{2,18},{3,19},{4,20},{5,21},{6,22},{7,23},{8,24},{9,... | collective-permute-start | bytes 479240 | tf_op jit(solution)/shard_map/ppermute | solution.py:553
  29.4 17.1 %collective-permute-start.3 = (bf16[4,56,768]{2,1,0:T(8,128)(2,1)S(1)}, bf16[4,56,768]{2,1,0:T(8,128)(2,1)S(1)}, u32[]{:S(2)}, u32[]{:S(2)}) collective-permute-start(bf16[4,56,768]{2,1,0:T(8,128)(2,1)S(1)} %slice.106.rest_1_), channel_id=1, source_target_pairs={{0,4},{1,5},{2,6},{3,7},{4,0},{5,1},{6,2},{7,3},{8,12},{9,13},{10,... | collective-permute-start | bytes 1032200 | tf_op jit(solution)/shard_map/ppermute | solution.py:553
  31.2 15.3 %collective-permute-start.4 = (bf16[4,48,768]{2,1,0:T(8,128)(2,1)S(1)}, bf16[4,48,768]{2,1,0:T(8,128)(2,1)}, u32[]{:S(2)}, u32[]{:S(2)}) collective-permute-start(bf16[4,48,768]{2,1,0:T(8,128)(2,1)S(1)} %slice.108.rest_0_), channel_id=1, source_target_pairs={{0,4},{1,5},{2,6},{3,7},{4,0},{5,1},{6,2},{7,3},{8,12},{9,13},{10,... | collective-permute-start | bytes 884744 | tf_op jit(solution)/shard_map/ppermute | solution.py:553
  31.4 19.1 %collective-permute-start.10 = (bf16[4,56,768]{2,1,0:T(8,128)(2,1)S(1)}, bf16[4,56,768]{2,1,0:T(8,128)(2,1)S(1)}, u32[]{:S(2)}, u32[]{:S(2)}) collective-permute-start(bf16[4,56,768]{2,1,0:T(8,128)(2,1)S(1)} %slice.106.rest_1_), channel_id=1, source_target_pairs={{0,1},{1,0},{2,3},{3,2},{4,5},{5,4},{6,7},{7,6},{8,9},{9,8},{10,11... | collective-permute-start | bytes 1032200 | tf_op jit(solution)/shard_map/ppermute | solution.py:553
  38.2 18.0 %collective-permute-start.8 = (bf16[4,56,768]{2,1,0:T(8,128)(2,1)S(1)}, bf16[4,56,768]{2,1,0:T(8,128)(2,1)S(1)}, u32[]{:S(2)}, u32[]{:S(2)}) collective-permute-start(bf16[4,56,768]{2,1,0:T(8,128)(2,1)S(1)} %collective-permute-done.6.rest_5_), channel_id=1, source_target_pairs={{0,4},{1,5},{2,6},{3,7},{4,0},{5,1},{6,2},{7,3},{8,12},{9,13},{10,... | collective-permute-start | bytes 1032200 | tf_op jit(solution)/shard_map/ppermute | solution.py:553
  46.5 16.4 %collective-permute-start.7 = (bf16[4,48,768]{2,1,0:T(8,128)(2,1)}, bf16[4,48,768]{2,1,0:T(8,128)(2,1)}, u32[]{:S(2)}, u32[]{:S(2)}) collective-permute-start(bf16[4,48,768]{2,1,0:T(8,128)(2,1)} %collective-permute-done.4.rest_2_), channel_id=1, source_target_pairs={{0,2},{1,3},{2,0},{3,1},{4,6},{5,7},{6,4},{7,5},{8,10},{9,11},{10,... | collective-permute-start | bytes 884744 | tf_op jit(solution)/shard_map/ppermute | solution.py:553
  168.9 15.6 %collective-permute-start.25 = (bf16[2,128,768]{2,1,0:T(8,128)(2,1)}, bf16[2,128,768]{2,1,0:T(8,128)(2,1)S(1)}, u32[]{:S(2)}, u32[]{:S(2)}) collective-permute-start(bf16[2,128,768]{2,1,0:T(8,128)(2,1)} %get-tuple-element.98), channel_id=1, source_target_pairs={{0,1},{1,0},{2,3},{3,2},{4,5},{5,4},{6,7},{7,6},{8,9},{9,8},{10,11... | collective-permute-start | bytes 1179656 | tf_op jit(solution)/shard_map/ppermute | solution.py:553
  177.1 45.0 %collective-permute-start.23 = (bf16[4,96,768]{2,1,0:T(8,128)(2,1)}, bf16[4,96,768]{2,1,0:T(8,128)(2,1)S(1)}, u32[]{:S(2)}, u32[]{:S(2)}) collective-permute-start(bf16[4,96,768]{2,1,0:T(8,128)(2,1)} %get-tuple-element.92), channel_id=1, source_target_pairs={{0,4},{1,5},{2,6},{3,7},{4,0},{5,1},{6,2},{7,3},{8,12},{9,13},{10,... | collective-permute-start | bytes 1769480 | tf_op jit(solution)/shard_map/ppermute | solution.py:553
  178.6 27.6 %collective-permute-start.27 = (bf16[4,96,768]{2,1,0:T(8,128)(2,1)S(1)}, bf16[4,96,768]{2,1,0:T(8,128)(2,1)S(1)}, u32[]{:S(2)}, u32[]{:S(2)}) collective-permute-start(bf16[4,96,768]{2,1,0:T(8,128)(2,1)S(1)} %copy-done.37), channel_id=1, source_target_pairs={{0,4},{1,5},{2,6},{3,7},{4,0},{5,1},{6,2},{7,3},{8,12},{9,13},{10,... | collective-permute-start | bytes 1769480 | tf_op jit(solution)/shard_map/ppermute | solution.py:553
  183.0 39.1 %collective-permute-start.24 = (bf16[4,96,768]{2,1,0:T(8,128)(2,1)}, bf16[4,96,768]{2,1,0:T(8,128)(2,1)S(1)}, u32[]{:S(2)}, u32[]{:S(2)}) collective-permute-start(bf16[4,96,768]{2,1,0:T(8,128)(2,1)} %get-tuple-element.95), channel_id=1, source_target_pairs={{0,4},{1,5},{2,6},{3,7},{4,0},{5,1},{6,2},{7,3},{8,12},{9,13},{10,... | collective-permute-start | bytes 1769480 | tf_op jit(solution)/shard_map/ppermute | solution.py:553
  227.5 21.1 %collective-permute-start.28 = (bf16[2,2,2,4,48,768]{5,4,3,2,1,0:T(8,128)(2,1)}, bf16[2,2,2,4,48,768]{5,4,3,2,1,0:T(8,128)(2,1)}, u32[]{:S(2)}, u32[]{:S(2)}) collective-permute-start(bf16[2,2,2,4,48,768]{5,4,3,2,1,0:T(8,128)(2,1)} %attention_grads.2), channel_id=1, source_target_pairs={{0,1},{1,0},{2,3},{3,2},{4,5},{5,4},{6,7},{7,6},{8,9},{9,8},{10,11... | collective-permute-start | bytes 7077896 | tf_op jit(solution)/shard_map/ppermute | solution.py:553
  228.3 14.4 %collective-permute-start.33 = (bf16[96,768]{1,0:T(8,128)(2,1)}, bf16[96,768]{1,0:T(8,128)(2,1)}, u32[]{:S(2)}, u32[]{:S(2)}) collective-permute-start(bf16[96,768]{1,0:T(8,128)(2,1)} %get-tuple-element.164), channel_id=1, source_target_pairs={{0,24},{1,25},{2,26},{3,27},{4,28},{5,29},{6,30},{7,31},{8,0},{9,1... | collective-permute-start | bytes 442376 | tf_op jit(solution)/shard_map/ppermute | solution.py:553
  230.0 15.2 %collective-permute-start.32 = (bf16[96,768]{1,0:T(8,128)(2,1)}, bf16[96,768]{1,0:T(8,128)(2,1)}, u32[]{:S(2)}, u32[]{:S(2)}) collective-permute-start(bf16[96,768]{1,0:T(8,128)(2,1)} %get-tuple-element.165), channel_id=1, source_target_pairs={{0,16},{1,17},{2,18},{3,19},{4,20},{5,21},{6,22},{7,23},{8,24},{9,... | collective-permute-start | bytes 442376 | tf_op jit(solution)/shard_map/ppermute | solution.py:553
  230.7 14.5 %collective-permute-start.31 = (bf16[96,768]{1,0:T(8,128)(2,1)}, bf16[96,768]{1,0:T(8,128)(2,1)}, u32[]{:S(2)}, u32[]{:S(2)}) collective-permute-start(bf16[96,768]{1,0:T(8,128)(2,1)} %get-tuple-element.166), channel_id=1, source_target_pairs={{0,8},{1,9},{2,10},{3,11},{4,12},{5,13},{6,14},{7,15},{8,16},{9,17... | collective-permute-start | bytes 442376 | tf_op jit(solution)/shard_map/ppermute | solution.py:553
  234.2 30.1 %collective-permute-start.37 = (bf16[192,768]{1,0:T(8,128)(2,1)}, bf16[192,768]{1,0:T(8,128)(2,1)S(1)}, u32[]{:S(2)}, u32[]{:S(2)}) collective-permute-start(bf16[192,768]{1,0:T(8,128)(2,1)} %get-tuple-element.156), channel_id=1, source_target_pairs={{0,24},{1,25},{2,26},{3,27},{4,28},{5,29},{6,30},{7,31},{8,0},{9,1... | collective-permute-start | bytes 884744 | tf_op jit(solution)/shard_map/ppermute | solution.py:553
  242.7 30.9 %collective-permute-start.36 = (bf16[192,768]{1,0:T(8,128)(2,1)}, bf16[192,768]{1,0:T(8,128)(2,1)S(1)}, u32[]{:S(2)}, u32[]{:S(2)}) collective-permute-start(bf16[192,768]{1,0:T(8,128)(2,1)} %get-tuple-element.157), channel_id=1, source_target_pairs={{0,16},{1,17},{2,18},{3,19},{4,20},{5,21},{6,22},{7,23},{8,24},{9,... | collective-permute-start | bytes 884744 | tf_op jit(solution)/shard_map/ppermute | solution.py:553
  245.2 28.3 %collective-permute-start.35 = (bf16[192,768]{1,0:T(8,128)(2,1)}, bf16[192,768]{1,0:T(8,128)(2,1)}, u32[]{:S(2)}, u32[]{:S(2)}) collective-permute-start(bf16[192,768]{1,0:T(8,128)(2,1)} %get-tuple-element.158), channel_id=1, source_target_pairs={{0,8},{1,9},{2,10},{3,11},{4,12},{5,13},{6,14},{7,15},{8,16},{9,17... | collective-permute-start | bytes 884744 | tf_op jit(solution)/shard_map/ppermute | solution.py:553
  247.0 35.8 %collective-permute-start.34 = (bf16[96,768]{1,0:T(8,128)(2,1)}, bf16[96,768]{1,0:T(8,128)(2,1)S(1)}, u32[]{:S(2)}, u32[]{:S(2)}) collective-permute-start(bf16[96,768]{1,0:T(8,128)(2,1)} %fusion.21), channel_id=1, source_target_pairs={{0,0},{1,8},{2,16},{3,24},{4,1},{5,9},{6,17},{7,25},{8,2},{9,10},{... | collective-permute-start | bytes 442376 | tf_op jit(solution)/shard_map/ppermute | solution.py:553
  273.6 29.3 %collective-permute-start.30 = (bf16[2,4,48,768]{3,2,1,0:T(8,128)(2,1)S(1)}, bf16[2,4,48,768]{3,2,1,0:T(8,128)(2,1)S(1)}, u32[]{:S(2)}, u32[]{:S(2)}) collective-permute-start(bf16[2,4,48,768]{3,2,1,0:T(8,128)(2,1)S(1)} %get-tuple-element.152), channel_id=1, source_target_pairs={{0,4},{1,5},{2,6},{3,7},{4,0},{5,1},{6,2},{7,3},{8,12},{9,13},{10,... | collective-permute-start | bytes 1769480 | tf_op jit(solution)/shard_map/ppermute | solution.py:553
  275.1 27.9 %collective-permute-start.29 = (bf16[2,4,48,768]{3,2,1,0:T(8,128)(2,1)S(1)}, bf16[2,4,48,768]{3,2,1,0:T(8,128)(2,1)S(1)}, u32[]{:S(2)}, u32[]{:S(2)}) collective-permute-start(bf16[2,4,48,768]{3,2,1,0:T(8,128)(2,1)S(1)} %get-tuple-element.153), channel_id=1, source_target_pairs={{0,2},{1,3},{2,0},{3,1},{4,6},{5,7},{6,4},{7,5},{8,10},{9,11},{10,... | collective-permute-start | bytes 1769480 | tf_op jit(solution)/shard_map/ppermute | solution.py:553
  282.9 20.0 %collective-permute-start.41 = (bf16[3,96,768]{2,1,0:T(8,128)(2,1)S(1)}, bf16[3,96,768]{2,1,0:T(8,128)(2,1)S(1)}, u32[]{:S(2)}, u32[]{:S(2)}) collective-permute-start(bf16[3,96,768]{2,1,0:T(8,128)(2,1)S(1)} %bitcast.138), channel_id=1, source_target_pairs={{0,2},{1,3},{2,0},{3,1},{4,6},{5,7},{6,4},{7,5},{8,10},{9,11},{10,... | collective-permute-start | bytes 1327112 | tf_op jit(solution)/shard_map/ppermute | solution.py:553
  283.0 22.1 %collective-permute-start.40 = (bf16[3,96,768]{2,1,0:T(8,128)(2,1)S(1)}, bf16[3,96,768]{2,1,0:T(8,128)(2,1)S(1)}, u32[]{:S(2)}, u32[]{:S(2)}) collective-permute-start(bf16[3,96,768]{2,1,0:T(8,128)(2,1)S(1)} %bitcast.139), channel_id=1, source_target_pairs={{0,1},{1,0},{2,3},{3,2},{4,5},{5,4},{6,7},{7,6},{8,9},{9,8},{10,11... | collective-permute-start | bytes 1327112 | tf_op jit(solution)/shard_map/ppermute | solution.py:553
  328.9 40.6 %collective-permute-start.47 = (bf16[96,768]{1,0:T(8,128)(2,1)S(1)}, bf16[96,768]{1,0:T(8,128)(2,1)S(1)}, u32[]{:S(2)}, u32[]{:S(2)}) collective-permute-start(bf16[96,768]{1,0:T(8,128)(2,1)S(1)} %fusion.17.rest_0_), channel_id=1, source_target_pairs={{0,2},{1,3},{2,0},{3,1},{4,6},{5,7},{6,4},{7,5},{8,10},{9,11},{10,... | collective-permute-start | bytes 442376 | tf_op jit(solution)/shard_map/ppermute | solution.py:553
  (65 other events, 645.2 us)
Sparse Core Ops, SparseCore 0:
  11.5 117.9 all-gather.4

commit v5 on v4

--- a/solution.py
+++ b/solution.py
@@ -30,7 +30,7 @@
 
 
 def cost(us):
-    return pl.CostEstimate(flops=0, bytes_accessed=int(us * 3.0e6), transcendentals=0)
+    return pl.CostEstimate(flops=0, bytes_accessed=int(us * 3.0e3), transcendentals=0)
 
 
 def mm(a, b):
@@ -81,6 +81,7 @@
 
 
 EXTRA = 8
+TAIL = 16
 HALVES = ((0, 48), (48, 56))
 KEYS = [(ry, rx, rc) for rc in (0, 1) for rx in (0, 1) for ry in (0, 1)]
 
@@ -448,10 +449,14 @@
     )(slopes, datt, q_m, qkv, pos)
 
 
-def attention_grads_kernel(rc, where_ref, flip_ref, rhs_ref, att_ref, low_ref, cut_ref, full_ref):
+def attention_grads_kernel(rc, where_ref, flip_ref, rhs_ref, att_ref, low_ref, small_attn_ref, small_ffn_ref, cut0_ref, cut1_ref, full_ref, tail_ref):
     z, y, mine = where_ref[0], where_ref[1], where_ref[4]
     half = ROWS // 2
     step = 256
+    tail_ref[...] = jnp.zeros(tail_ref.shape, LOW)
+    small = jnp.concatenate([small_attn_ref[...], small_ffn_ref[...]], axis=0).astype(LOW)
+    for n in range(SHARDS):
+        tail_ref[n, 0:4, 0:ROWS] = small[:, n * ROWS : (n + 1) * ROWS]
     for rx in (0, 1):
         j = jnp.bitwise_xor(mine, 2 * rx + rc)
 
@@ -472,27 +477,25 @@
         for rz in range(LINE):
             base = 2 * lax.rem(z + rz, LINE)
             for ry in (0, 1):
-                start = (base + (y if ry == 0 else 1 - y)) * ROWS
-                for part in (0, 1):
-                    rows = pl.ds(pl.multiple_of(start + part * half, 8), half)
-                    value = full_ref[rows, :].astype(LOW)
-                    if part == 0:
-                        cut_ref[0, rx, ry, rz] = value
-                    else:
-                        cut_ref[1, ry, rx, rz] = value
-
-
-def attention_grads(where, rc, x_flip, rhs, att_m, low):
+                shard = base + (y if ry == 0 else 1 - y)
+                start = shard * ROWS
+                cut0_ref[rx, ry, rz] = full_ref[pl.ds(pl.multiple_of(start, 8), half), :].astype(LOW)
+                cut1_ref[ry, rx, rz, 0:half] = full_ref[pl.ds(pl.multiple_of(start + half, 8), half), :].astype(LOW)
+                cut1_ref[ry, rx, rz, half:] = tail_ref[shard]
+
+
+def attention_grads(where, rc, x_flip, rhs, att_m, low, small_attn, small_ffn):
+    half = ROWS // 2
     return pl.pallas_call(
         functools.partial(attention_grads_kernel, rc),
-        out_shape=out((2, 2, 2, LINE, ROWS // 2, D), LOW),
-        in_specs=[SMEM] + [VMEM] * 4,
-        out_specs=VMEM,
-        scratch_shapes=[pltpu.VMEM((D, D), F32)],
+        out_shape=(out((2, 2, LINE, half, D), LOW), out((2, 2, LINE, half + TAIL, D), LOW)),
+        in_specs=[SMEM] + [VMEM] * 6,
+        out_specs=(VMEM, VMEM),
+        scratch_shapes=[pltpu.VMEM((D, D), F32), pltpu.VMEM((SHARDS, TAIL, D), LOW)],
         compiler_params=BIG,
         cost_estimate=cost(5),
         name="attention_grads",
-    )(where, x_flip, rhs, att_m, low)
+    )(where, x_flip, rhs, att_m, low, small_attn, small_ffn)
 
 
 def input_grad_kernel(seqs, rhs_ref, w_ref, dr1_ref, pos_ref, out_ref):
@@ -566,12 +569,16 @@
     return kept.astype(F32) + got.astype(F32)
 
 
-def line_send(total):
-    return [send(total[r].astype(LOW), r) for r in (1, 2, 3)]
-
-
-def line_add(total, got):
-    return (total[0] + got[0].astype(F32) + got[1].astype(F32) + got[2].astype(F32)).astype(LOW)
+def line_parts(keep, got):
+    return [add(keep[r], got[r]).astype(LOW) for r in (1, 2, 3)]
+
+
+def line_send(parts):
+    return [send(value, r) for r, value in zip((1, 2, 3), parts)]
+
+
+def line_add(keep, got, came):
+    return (add(keep[0], got[0]) + came[0].astype(F32) + came[1].astype(F32) + came[2].astype(F32)).astype(LOW)
 
 
 def finish_ffn_kernel(where_ref, *rest):
@@ -678,37 +685,37 @@
     keep_u, away_u = weight_grad(where, after(h_all, away_g), dup)
     got_u = send(away_u, "y")
     dr1, low, datt, small_attn = norm_back_call(dr2, part[0], after(came, away_u), r1_m, w_attn, norms)
-    small = lax.all_gather(jnp.concatenate([small_attn, small_ffn]), AXES)
-    sum_d = add(keep_d, got_d)
-    line_d = line_send(sum_d)
-    rhs = attention_back(after(datt, sum_d), q_m, qkv, pos, slopes, seqs)
-    got_g, got_u, rhs = lax.optimization_barrier((got_g, got_u, rhs))
-    sum_gu = jnp.concatenate([add(keep_g, got_g), add(keep_u, got_u)], axis=1)
-    line_gu = line_send(sum_gu)
-    away = attention_grads(where, 1, x_flip, after(rhs, sum_gu), att_m, low)
-    came = send(away, "c")
-    g_down = line_add(sum_d, after(line_d, away))
+    parts_d = line_parts(keep_d, got_d)
+    rhs = attention_back(after(datt, parts_d), q_m, qkv, pos, slopes, seqs)
+    got_d, got_g, got_u, rhs = lax.optimization_barrier((got_d, got_g, got_u, rhs))
+    keep_gu, got_gu = jnp.concatenate([keep_g, keep_u], axis=1), jnp.concatenate([got_g, got_u], axis=1)
+    parts_gu = line_parts(keep_gu, got_gu)
+    away0, away1 = attention_grads(where, 1, x_flip, after(rhs, parts_gu), att_m, low, small_attn, small_ffn)
+    came0, came1 = send(away0, "c"), send(away1, "c")
+    g_down = line_add(keep_d, got_d, after(line_send(parts_d), away0))
     g_down = send(g_down, "down")
-    keep = attention_grads(where, 0, x_flip, after(rhs, away), att_m, low)
-    came, keep = lax.optimization_barrier((came, keep))
-    total = add(keep, came)
-    got0 = send(total[0, 1].astype(LOW), "x")
-    got1 = send(total[1, 1].astype(LOW), "y")
-    grad_in = input_grad(after(rhs, total), w_attn, dr1, positions)
-    g_ffn = jnp.concatenate([g_down, line_add(sum_gu, after(line_gu, grad_in))]).reshape(3, ROWS, D)
+    keep0, keep1 = attention_grads(where, 0, x_flip, after(rhs, away0), att_m, low, small_attn, small_ffn)
+    came0, came1, keep0, keep1 = lax.optimization_barrier((came0, came1, keep0, keep1))
+    away0, away1 = add(keep0[1], came0[1]).astype(LOW), add(keep1[1], came1[1]).astype(LOW)
+    got0, got1 = send(away0, "x"), send(away1, "y")
+    grad_in = input_grad(after(rhs, (away0, away1)), w_attn, dr1, positions)
+    g_gu = line_add(keep_gu, got_gu, after(line_send(parts_gu), grad_in))
+    g_ffn = jnp.concatenate([g_down, g_gu]).reshape(3, ROWS, D)
     got0, got1 = after((got0, got1), g_ffn)
     shared = share_dp(g_ffn)
-    total0 = add(total[0, 0], got0)
-    total1 = add(total[1, 0], got1)
+    total0 = add(keep0[0], came0[0]) + got0.astype(F32)
+    total1 = add(keep1[0], came1[0]) + got1.astype(F32)
     got0 = send(total0[1].astype(LOW), "y")
     got1 = send(total1[1].astype(LOW), "x")
     got0, got1, shared = lax.optimization_barrier((got0, got1, shared))
     total = jnp.concatenate([add(total0[0], got0), add(total1[0], got1)], axis=1)
-    line_a = line_send(total)
-    grad_down, grad_up = finish_ffn(where, after(shared, total))
-    g_attn = line_add(total, after(line_a, grad_down))
-    grad_qkv, grad_out = finish_attention(where, share_dp(g_attn))
-    small = jnp.sum(lax.dynamic_slice_in_dim(small, i * ROWS, ROWS, axis=2), axis=0)
+    parts = [total[r].astype(LOW) for r in (1, 2, 3)]
+    line_a = line_send(parts)
+    grad_down, grad_up = finish_ffn(where, after(shared, parts))
+    line_a = after(line_a, grad_down)
+    g_attn = (total[0] + line_a[0].astype(F32) + line_a[1].astype(F32) + line_a[2].astype(F32))
+    small = g_attn[ROWS : ROWS + 4, :ROWS]
+    grad_qkv, grad_out = finish_attention(where, share_dp(g_attn[:ROWS].astype(LOW)))
     return (
         layer_out.reshape(seqs, length, width),
         grad_in.reshape(seqs, length, width),

time: 382 us -> 344 us (0.901)
  blocking collectives: 39.7 us -> 0 us
  starting transfers between devices: 46.5 us -> 57.3 us
  waiting for transfers between devices: 146 us -> 138 us
    all_gather x1 -> x0, blocking collectives: 39.7 us -> none  [on_block(): small = lax.all_gather(jnp.concatenate([small_attn, small_ffn]), AXES)]
    ppermute x49 -> x50, starting transfers between devices: 46.5 us -> 57.3 us  [send(): return lax.ppermute(value, AXES, MOVES[move])]
    ppermute x49 -> x50, waiting for transfers between devices: 115 us -> 108 us  [send(): return lax.ppermute(value, AXES, MOVES[move])]
    another operation x4 -> x1, other arithmetic: 6.49 us -> 0.07 us
    convert_element_type x3 -> x6, other arithmetic: 2.92 us -> 7.85 us  [the longest x2 2.62 us: line_add(): (add(keep[0], got[0]) + came[0].astype(F32) + came[1].astype(F32) + came[...]
  transfers between devices with their start and end apart: 50 -> 51, of which waited for: 22 -> 23; matrix products, arithmetic and copies ran while one was open for 6% -> 6% of each run, Pallas kernels for 19% -> 21%
where the time goes in v5:
time: 344 us; the launch traced here: 343 us
  waiting for transfers between devices  138 us (40%)
  Pallas kernels  105 us (31%)
  starting transfers between devices  57.3 us (17%)
  other arithmetic  17.1 us (5%)
  between operations  14.7 us (4%)
  local copies, waits for them, and re-layouts  10.5 us (3%)
    ppermute x50, waiting for transfers between devices, send(): return lax.ppermute(value, AXES, MOVES[move])  108 us
    ppermute x50, starting transfers between devices, send(): return lax.ppermute(value, AXES, MOVES[move])  57.3 us
    all_gather x1, waiting for transfers between devices, on_block(): lax.all_gather(ffn_piece, AXES, axis=0, tiled=False)  30.3 us
    pallas_call x1, Pallas kernels, attention_forward(): pl.pallas_call(functools.partial(attention_kernel, seqs, listed // seqs),...  18 us
    pallas_call x1, Pallas kernels, ffn_forward(): pl.pallas_call(functools.partial(ffn_kernel, seqs, listed // seqs), out_s...  17 us
    pallas_call x1, Pallas kernels, attention_back(): pl.pallas_call(functools.partial(attention_back_kernel, seqs, listed // s...  15.9 us
    pallas_call x3, Pallas kernels, weight_grad(): pl.pallas_call(weight_grad_kernel, out_shape=(out(shape, LOW), out(shape,...  11.5 us
    pallas_call x2, Pallas kernels, attention_grads(): pl.pallas_call(functools.partial(attention_grads_kernel, rc), out_shape=(...  11.4 us
  transfers between devices with their start and end apart: 51, of which 23 were waited for; matrix products, arithmetic and copies ran while one was open for 6% of the time, Pallas kernels for 21%

profile of v5, /device:TPU:0, one launch (start us, length us, event | category | flops | bytes accessed | tf_op | source)
XLA Modules:
  0.0 342.9 jit_solution(4373290280853114502)
XLA Ops:
  9.6 4.1 %collective-permute-start.1 = (bf16[104,768]{1,0:T(8,128)(2,1)S(1)}, bf16[104,768]{1,0:T(8,128)(2,1)S(1)}, u32[]{:S(2)}, u32[]{:S(2)}) collective-permute-start(bf16[104,768]{1,0:T(8,128)(2,1)S(1)} %get-tuple-element.178), channel_id=1, source_target_pairs={{0,16},{1,17},{2,18},{3,19},{4,20},{5,21},{6,22},{7,23},{8,24},{9,... | collective-permute-start | bytes 479240 | tf_op jit(solution)/shard_map/ppermute | solution.py:556
  18.8 6.8 %collective-permute-done.1 = bf16[104,768]{1,0:T(8,128)(2,1)S(1)} collective-permute-done((bf16[104,768]{1,0:T(8,128)(2,1)S(1)}, bf16[104,768]{1,0:T(8,128)(2,1)S(1)}, u32[]{:S(2)}, u32[]{:S(2)}) %collective-permute-start.1) | collective-permute-done | bytes 159776 | tf_op jit(solution)/shard_map/ppermute | solution.py:556
  31.4 6.8 %collective-permute-done.6.rest_5_ = bf16[4,56,768]{2,1,0:T(8,128)(2,1)S(1)} collective-permute-done((bf16[4,56,768]{2,1,0:T(8,128)(2,1)S(1)}, bf16[4,56,768]{2,1,0:T(8,128)(2,1)S(1)}, u32[]{:S(2)}, u32[]{:S(2)}) %collective-permute-start.6) | collective-permute-done | bytes 344096 | tf_op jit(solution)/shard_map/ppermute | solution.py:556
  50.7 5.5 %collective-permute-done.8.rest_7_ = bf16[4,56,768]{2,1,0:T(8,128)(2,1)S(1)} collective-permute-done((bf16[4,56,768]{2,1,0:T(8,128)(2,1)S(1)}, bf16[4,56,768]{2,1,0:T(8,128)(2,1)S(1)}, u32[]{:S(2)}, u32[]{:S(2)}) %collective-permute-start.8) | collective-permute-done | bytes 344096 | tf_op jit(solution)/shard_map/ppermute | solution.py:556
  56.8 6.1 %collective-permute-done.7.rest_6_ = bf16[4,48,768]{2,1,0:T(8,128)(2,1)} collective-permute-done((bf16[4,48,768]{2,1,0:T(8,128)(2,1)}, bf16[4,48,768]{2,1,0:T(8,128)(2,1)}, u32[]{:S(2)}, u32[]{:S(2)}) %collective-permute-start.7) | collective-permute-done | bytes 294944 | tf_op jit(solution)/shard_map/ppermute | solution.py:556
  65.8 18.0 %attention_forward.1 = (bf16[512,2304]{1,0:T(8,128)(2,1)}, f32[512,768]{1,0:T(8,128)}, bf16[128,768]{1,0:T(8,128)(2,1)}, bf16[128,768]{1,0:T(8,128)(2,1)}, bf16[...) custom-call(s32[5]{0:T(128)} %stack.83.where_ref, f32[12]{0:T(128)} %multiply_exponential_fusion.slope_ref, ...), custom_call_target="tpu_custom_call" | custom-call | bytes 60000 | tf_op jit(solution)/shard_map/attention_forward/pallas_call | solution.py:164
  85.6 10.4 %collective-permute-done.18 = bf16[128,768]{1,0:T(8,128)(2,1)S(1)} collective-permute-done((bf16[128,768]{1,0:T(8,128)(2,1)}, bf16[128,768]{1,0:T(8,128)(2,1)S(1)}, u32[]{:S(2)}, u32[]{:S(2)}) %collective-permute-start.18) | collective-permute-done | bytes 196640 | tf_op jit(solution)/shard_map/ppermute | solution.py:556
  99.3 30.3 %all-gather.3.cloned.1.call-done = bf16[96,96,768]{2,1,0:T(8,128)(2,1)} async-done(((bf16[3,96,768]{2,1,0:T(8,128)(2,1)}), bf16[96,96,768]{2,1,0:T(8,128)(2,1)}) %all-gather.3.cloned.1.call-update) | async-done | bytes 14155792 | tf_op jit(solution)/shard_map/all_gather | solution.py:662
  129.6 17.0 %ffn_forward.1 = (bf16[512,768]{1,0:T(8,128)(2,1)}, f32[128,768]{1,0:T(8,128)}, bf16[128,768]{1,0:T(8,128)(2,1)}, f32[2,768]{1,0:T(2,128)}) custom-call(f32[512,768]{1,0:T(8,128)} %get-tuple-element.89.h1_ref, bf16[8,4,3,96,768]{4,3,2,1,0:T(8,128)(2,1)} %bitcast.114, bf16[8,4,3,96,768]{4,3,2,1,0:T(8,128)(2,1)} %bitcast.115, ...), custom_call_target="tpu_custom_call" | custom-call | bytes 48000 | tf_op jit(solution)/shard_map/ffn_forward/pallas_call | solution.py:232
  147.2 6.7 %collective-permute-done.21 = bf16[128,768]{1,0:T(8,128)(2,1)S(1)} collective-permute-done((bf16[128,768]{1,0:T(8,128)(2,1)}, bf16[128,768]{1,0:T(8,128)(2,1)S(1)}, u32[]{:S(2)}, u32[]{:S(2)}) %collective-permute-start.21) | collective-permute-done | bytes 196640 | tf_op jit(solution)/shard_map/ppermute | solution.py:556
  153.9 6.6 %ffn_again.1 = (bf16[512,768]{1,0:T(8,128)(2,1)}, f32[512,768]{1,0:T(8,128)}, f32[512,768]{1,0:T(8,128)}) custom-call(s32[5]{0:T(128)} %stack.83.where_ref, bf16[4,128,768]{2,1,0:T(8,128)(2,1)} %pad_maximum_fusion.1.h_ref.a_ref, bf16[8,4,3,96,768]{4,3,2,1,0:T(8,128)(2,1)} %bitcast.117, bf16[8,4,3,96,768]{4,3,2,1,0:T(8,128)(2,1)} %bitcast.118), custom_call_target="tpu_custom_call" | custom-call | bytes 18000 | tf_op jit(solution)/shard_map/ffn_again/pallas_call | solution.py:288
  161.5 7.4 %ffn_back.1 = (bf16[512,768]{1,0:T(8,128)(2,1)}, bf16[512,768]{1,0:T(8,128)(2,1)}, f32[2,128,768]{2,1,0:T(8,128)}, bf16[2,128,768]{2,1,0:T(8,128)(2,1)}) custom-call(s32[5]{0:T(128)} %stack.83.where_ref, bf16[4,128,768]{2,1,0:T(8,128)(2,1)} %pad_maximum_fusion.2.b_ref.e_ref, f32[512,768]{1,0:T(8,128)} %get-tuple-element.96.to_gate_ref, ...), custom_call_target="tpu_custom_call" | custom-call | bytes 21000 | tf_op jit(solution)/shard_map/ffn_back/pallas_call | solution.py:323
  188.1 4.6 %collective-permute-done.27.came_ref = bf16[128,768]{1,0:T(8,128)(2,1)S(1)} collective-permute-done((bf16[128,768]{1,0:T(8,128)(2,1)S(1)}, bf16[128,768]{1,0:T(8,128)(2,1)S(1)}, u32[]{:S(2)}, u32[]{:S(2)}) %collective-permute-start.27) | collective-permute-done | bytes 196640 | tf_op jit(solution)/shard_map/ppermute | solution.py:556
  196.6 9.5 %collective-permute-done.23 = bf16[4,96,768]{2,1,0:T(8,128)(2,1)S(1)} collective-permute-done((bf16[4,96,768]{2,1,0:T(8,128)(2,1)}, bf16[4,96,768]{2,1,0:T(8,128)(2,1)S(1)}, u32[]{:S(2)}, u32[]{:S(2)}) %collective-permute-start.23) | collective-permute-done | bytes 589856 | tf_op jit(solution)/shard_map/ppermute | solution.py:556
  207.1 15.9 %attention_back.1.rhs_ref = bf16[512,2304]{1,0:T(8,128)(2,1)} custom-call(f32[12]{0:T(128)} %multiply_exponential_fusion.slope_ref, bf16[128,768]{1,0:T(8,128)(2,1)} %get-tuple-element.111.datt_ref, bf16[128,768]{1,0:T(8,128)(2,1)} %get-tuple-element.112.q_ref, bf16[512,2304]{1,0:T(8,128)(2,1)} %get-tuple-element.113.qkv_ref, s32[128,1]{1,0:T(8,128)} %reshape.129.pos_ref), custom_call_target="tpu_custom_call" | custom-call | bytes 45000 | tf_op jit(solution)/shard_map/attention_back/pallas_call | solution.py:440
  224.1 5.4 %attention_grads.2 = (bf16[2,2,4,48,768]{4,3,2,1,0:T(8,128)(2,1)}, bf16[2,2,4,64,768]{4,3,2,1,0:T(8,128)(2,1)}) custom-call(s32[5]{0:T(128)} %stack.83.where_ref, bf16[768,512]{1,0:T(8,128)(2,1)} %bitcast.122, bf16[512,2304]{1,0:T(8,128)(2,1)} %attention_back.1.rhs_ref, bf16[128,768]{1,0:T(8,128)(2,1)} %get-tuple-element.121.att_ref, ...), custom_call_target="tpu_custom_call" | custom-call | bytes 15000 | tf_op jit(solution)/shard_map/attention_grads/pallas_call | solution.py:489
  233.7 6.0 %attention_grads.3 = (bf16[2,2,4,48,768]{4,3,2,1,0:T(8,128)(2,1)}, bf16[2,2,4,64,768]{4,3,2,1,0:T(8,128)(2,1)}) custom-call(s32[5]{0:T(128)} %stack.83.where_ref, bf16[768,512]{1,0:T(8,128)(2,1)} %bitcast.123, bf16[512,2304]{1,0:T(8,128)(2,1)} %attention_back.1.rhs_ref, bf16[128,768]{1,0:T(8,128)(2,1)} %get-tuple-element.121.att_ref, ...), custom_call_target="tpu_custom_call" | custom-call | bytes 15000 | tf_op jit(solution)/shard_map/attention_grads/pallas_call | solution.py:489
  242.3 4.6 %collective-permute-done.33 = bf16[96,768]{1,0:T(8,128)(2,1)} collective-permute-done((bf16[96,768]{1,0:T(8,128)(2,1)}, bf16[96,768]{1,0:T(8,128)(2,1)}, u32[]{:S(2)}, u32[]{:S(2)}) %collective-permute-start.33) | collective-permute-done | bytes 147488 | tf_op jit(solution)/shard_map/ppermute | solution.py:556
  246.9 12.1 %collective-permute-start.36 = (bf16[192,768]{1,0:T(8,128)(2,1)}, bf16[192,768]{1,0:T(8,128)(2,1)}, u32[]{:S(2)}, u32[]{:S(2)}) collective-permute-start(bf16[192,768]{1,0:T(8,128)(2,1)} %get-tuple-element.164), channel_id=1, source_target_pairs={{0,8},{1,9},{2,10},{3,11},{4,12},{5,13},{6,14},{7,15},{8,16},{9,17... | collective-permute-start | bytes 884744 | tf_op jit(solution)/shard_map/ppermute | solution.py:556
  263.8 4.0 %collective-permute-start.30 = (bf16[2,4,48,768]{3,2,1,0:T(8,128)(2,1)}, bf16[2,4,48,768]{3,2,1,0:T(8,128)(2,1)}, u32[]{:S(2)}, u32[]{:S(2)}) collective-permute-start(bf16[2,4,48,768]{3,2,1,0:T(8,128)(2,1)} %fusion.3), channel_id=1, source_target_pairs={{0,2},{1,3},{2,0},{3,1},{4,6},{5,7},{6,4},{7,5},{8,10},{9,11},{10,... | collective-permute-start | bytes 1769480 | tf_op jit(solution)/shard_map/ppermute | solution.py:556
  268.9 8.1 %input_grad.1 = f32[512,768]{1,0:T(8,128)} custom-call(bf16[512,2304]{1,0:T(8,128)(2,1)} %attention_back.1.rhs_ref, bf16[8,4,96,768]{3,2,1,0:T(8,128)(2,1)} %get-tuple-element.108.w_ref, f32[128,768]{1,0:T(8,128)} %get-tuple-element.135.dr1_ref, s32[4,32]{1,0:T(4,128)} %pos_ref.1), custom_call_target="tpu_custom_call" | custom-call | bytes 24000 | tf_op jit(solution)/shard_map/input_grad/pallas_call | solution.py:519
  280.5 12.3 %collective-permute-done.42.rest_2_ = bf16[3,96,768]{2,1,0:T(8,128)(2,1)S(1)} collective-permute-done((bf16[3,96,768]{2,1,0:T(8,128)(2,1)S(1)}, bf16[3,96,768]{2,1,0:T(8,128)(2,1)S(1)}, u32[]{:S(2)}, u32[]{:S(2)}) %collective-permute-start.42) | collective-permute-done | bytes 442400 | tf_op jit(solution)/shard_map/ppermute | solution.py:556
  300.3 8.0 %collective-permute-done.39 = bf16[4,48,768]{2,1,0:T(8,128)(2,1)S(1)} collective-permute-done((bf16[4,48,768]{2,1,0:T(8,128)(2,1)S(1)}, bf16[4,48,768]{2,1,0:T(8,128)(2,1)S(1)}, u32[]{:S(2)}, u32[]{:S(2)}) %collective-permute-start.39) | collective-permute-done | bytes 294944 | tf_op jit(solution)/shard_map/ppermute | solution.py:556
  317.2 9.0 %collective-permute-done.45 = bf16[112,768]{1,0:T(8,128)(2,1)S(1)} collective-permute-done((bf16[112,768]{1,0:T(8,128)(2,1)S(1)}, bf16[112,768]{1,0:T(8,128)(2,1)S(1)}, u32[]{:S(2)}, u32[]{:S(2)}) %collective-permute-start.45) | collective-permute-done | bytes 172064 | tf_op jit(solution)/shard_map/ppermute | solution.py:556
  (228 shorter events, 102.9 us)
Async XLA Ops:
  7.2 122.3 %all-gather.3.cloned.1.call-start = ((), (), s32[]{:S(2)}) async-start(), calls=%async_computation | async-start | bytes 14598144 | tf_op jit(solution)/shard_map/all_gather | solution.py:662
  9.6 16.0 %collective-permute-start.1 = (bf16[104,768]{1,0:T(8,128)(2,1)S(1)}, bf16[104,768]{1,0:T(8,128)(2,1)S(1)}, u32[]{:S(2)}, u32[]{:S(2)}) collective-permute-start(bf16[104,768]{1,0:T(8,128)(2,1)S(1)} %get-tuple-element.178), channel_id=1, source_target_pairs={{0,16},{1,17},{2,18},{3,19},{4,20},{5,21},{6,22},{7,23},{8,24},{9,... | collective-permute-start | bytes 479240 | tf_op jit(solution)/shard_map/ppermute | solution.py:556
  29.4 17.1 %collective-permute-start.3 = (bf16[4,56,768]{2,1,0:T(8,128)(2,1)S(1)}, bf16[4,56,768]{2,1,0:T(8,128)(2,1)S(1)}, u32[]{:S(2)}, u32[]{:S(2)}) collective-permute-start(bf16[4,56,768]{2,1,0:T(8,128)(2,1)S(1)} %slice.143.rest_1_), channel_id=1, source_target_pairs={{0,4},{1,5},{2,6},{3,7},{4,0},{5,1},{6,2},{7,3},{8,12},{9,13},{10,... | collective-permute-start | bytes 1032200 | tf_op jit(solution)/shard_map/ppermute | solution.py:556
  31.2 15.3 %collective-permute-start.4 = (bf16[4,48,768]{2,1,0:T(8,128)(2,1)S(1)}, bf16[4,48,768]{2,1,0:T(8,128)(2,1)}, u32[]{:S(2)}, u32[]{:S(2)}) collective-permute-start(bf16[4,48,768]{2,1,0:T(8,128)(2,1)S(1)} %slice.145.rest_0_), channel_id=1, source_target_pairs={{0,4},{1,5},{2,6},{3,7},{4,0},{5,1},{6,2},{7,3},{8,12},{9,13},{10,... | collective-permute-start | bytes 884744 | tf_op jit(solution)/shard_map/ppermute | solution.py:556
  31.4 19.1 %collective-permute-start.10 = (bf16[4,56,768]{2,1,0:T(8,128)(2,1)S(1)}, bf16[4,56,768]{2,1,0:T(8,128)(2,1)S(1)}, u32[]{:S(2)}, u32[]{:S(2)}) collective-permute-start(bf16[4,56,768]{2,1,0:T(8,128)(2,1)S(1)} %slice.143.rest_1_), channel_id=1, source_target_pairs={{0,1},{1,0},{2,3},{3,2},{4,5},{5,4},{6,7},{7,6},{8,9},{9,8},{10,11... | collective-permute-start | bytes 1032200 | tf_op jit(solution)/shard_map/ppermute | solution.py:556
  38.2 18.0 %collective-permute-start.8 = (bf16[4,56,768]{2,1,0:T(8,128)(2,1)S(1)}, bf16[4,56,768]{2,1,0:T(8,128)(2,1)S(1)}, u32[]{:S(2)}, u32[]{:S(2)}) collective-permute-start(bf16[4,56,768]{2,1,0:T(8,128)(2,1)S(1)} %collective-permute-done.6.rest_5_), channel_id=1, source_target_pairs={{0,4},{1,5},{2,6},{3,7},{4,0},{5,1},{6,2},{7,3},{8,12},{9,13},{10,... | collective-permute-start | bytes 1032200 | tf_op jit(solution)/shard_map/ppermute | solution.py:556
  46.5 16.4 %collective-permute-start.7 = (bf16[4,48,768]{2,1,0:T(8,128)(2,1)}, bf16[4,48,768]{2,1,0:T(8,128)(2,1)}, u32[]{:S(2)}, u32[]{:S(2)}) collective-permute-start(bf16[4,48,768]{2,1,0:T(8,128)(2,1)} %collective-permute-done.4.rest_2_), channel_id=1, source_target_pairs={{0,2},{1,3},{2,0},{3,1},{4,6},{5,7},{6,4},{7,5},{8,10},{9,11},{10,... | collective-permute-start | bytes 884744 | tf_op jit(solution)/shard_map/ppermute | solution.py:556
  49.8 14.3 %collective-permute-start.14 = (bf16[4,56,768]{2,1,0:T(8,128)(2,1)S(1)}, bf16[4,56,768]{2,1,0:T(8,128)(2,1)S(1)}, u32[]{:S(2)}, u32[]{:S(2)}) collective-permute-start(bf16[4,56,768]{2,1,0:T(8,128)(2,1)S(1)} %collective-permute-done.6.rest_5_), channel_id=1, source_target_pairs={{0,1},{1,0},{2,3},{3,2},{4,5},{5,4},{6,7},{7,6},{8,9},{9,8},{10,11... | collective-permute-start | bytes 1032200 | tf_op jit(solution)/shard_map/ppermute | solution.py:556
  168.9 15.6 %collective-permute-start.26 = (bf16[2,128,768]{2,1,0:T(8,128)(2,1)}, bf16[2,128,768]{2,1,0:T(8,128)(2,1)}, u32[]{:S(2)}, u32[]{:S(2)}) collective-permute-start(bf16[2,128,768]{2,1,0:T(8,128)(2,1)} %get-tuple-element.105), channel_id=1, source_target_pairs={{0,1},{1,0},{2,3},{3,2},{4,5},{5,4},{6,7},{7,6},{8,9},{9,8},{10,11... | collective-permute-start | bytes 1179656 | tf_op jit(solution)/shard_map/ppermute | solution.py:556
  177.1 45.9 %collective-permute-start.24 = (bf16[4,96,768]{2,1,0:T(8,128)(2,1)}, bf16[4,96,768]{2,1,0:T(8,128)(2,1)S(1)}, u32[]{:S(2)}, u32[]{:S(2)}) collective-permute-start(bf16[4,96,768]{2,1,0:T(8,128)(2,1)} %get-tuple-element.99), channel_id=1, source_target_pairs={{0,4},{1,5},{2,6},{3,7},{4,0},{5,1},{6,2},{7,3},{8,12},{9,13},{10,... | collective-permute-start | bytes 1769480 | tf_op jit(solution)/shard_map/ppermute | solution.py:556
  178.6 27.6 %collective-permute-start.23 = (bf16[4,96,768]{2,1,0:T(8,128)(2,1)}, bf16[4,96,768]{2,1,0:T(8,128)(2,1)S(1)}, u32[]{:S(2)}, u32[]{:S(2)}) collective-permute-start(bf16[4,96,768]{2,1,0:T(8,128)(2,1)} %get-tuple-element.94), channel_id=1, source_target_pairs={{0,4},{1,5},{2,6},{3,7},{4,0},{5,1},{6,2},{7,3},{8,12},{9,13},{10,... | collective-permute-start | bytes 1769480 | tf_op jit(solution)/shard_map/ppermute | solution.py:556
  183.0 40.0 %collective-permute-start.25 = (bf16[4,96,768]{2,1,0:T(8,128)(2,1)}, bf16[4,96,768]{2,1,0:T(8,128)(2,1)S(1)}, u32[]{:S(2)}, u32[]{:S(2)}) collective-permute-start(bf16[4,96,768]{2,1,0:T(8,128)(2,1)} %get-tuple-element.102), channel_id=1, source_target_pairs={{0,4},{1,5},{2,6},{3,7},{4,0},{5,1},{6,2},{7,3},{8,12},{9,13},{10,... | collective-permute-start | bytes 1769480 | tf_op jit(solution)/shard_map/ppermute | solution.py:556
  229.5 32.2 %collective-permute-start.29 = (bf16[2,2,4,64,768]{4,3,2,1,0:T(8,128)(2,1)}, bf16[2,2,4,64,768]{4,3,2,1,0:T(8,128)(2,1)S(1)}, u32[]{:S(2)}, u32[]{:S(2)}) collective-permute-start(bf16[2,2,4,64,768]{4,3,2,1,0:T(8,128)(2,1)} %get-tuple-element.126), channel_id=1, source_target_pairs={{0,1},{1,0},{2,3},{3,2},{4,5},{5,4},{6,7},{7,6},{8,9},{9,8},{10,11... | collective-permute-start | bytes 4718600 | tf_op jit(solution)/shard_map/ppermute | solution.py:556
  229.5 30.9 %collective-permute-start.28 = (bf16[2,2,4,48,768]{4,3,2,1,0:T(8,128)(2,1)}, bf16[2,2,4,48,768]{4,3,2,1,0:T(8,128)(2,1)}, u32[]{:S(2)}, u32[]{:S(2)}) collective-permute-start(bf16[2,2,4,48,768]{4,3,2,1,0:T(8,128)(2,1)} %get-tuple-element.125), channel_id=1, source_target_pairs={{0,1},{1,0},{2,3},{3,2},{4,5},{5,4},{6,7},{7,6},{8,9},{9,8},{10,11... | collective-permute-start | bytes 3538952 | tf_op jit(solution)/shard_map/ppermute | solution.py:556
  231.7 15.2 %collective-permute-start.33 = (bf16[96,768]{1,0:T(8,128)(2,1)}, bf16[96,768]{1,0:T(8,128)(2,1)}, u32[]{:S(2)}, u32[]{:S(2)}) collective-permute-start(bf16[96,768]{1,0:T(8,128)(2,1)} %get-tuple-element.166), channel_id=1, source_target_pairs={{0,16},{1,17},{2,18},{3,19},{4,20},{5,21},{6,22},{7,23},{8,24},{9,... | collective-permute-start | bytes 442376 | tf_op jit(solution)/shard_map/ppermute | solution.py:556
  232.4 14.5 %collective-permute-start.32 = (bf16[96,768]{1,0:T(8,128)(2,1)}, bf16[96,768]{1,0:T(8,128)(2,1)}, u32[]{:S(2)}, u32[]{:S(2)}) collective-permute-start(bf16[96,768]{1,0:T(8,128)(2,1)} %get-tuple-element.167), channel_id=1, source_target_pairs={{0,8},{1,9},{2,10},{3,11},{4,12},{5,13},{6,14},{7,15},{8,16},{9,17... | collective-permute-start | bytes 442376 | tf_op jit(solution)/shard_map/ppermute | solution.py:556
  239.7 37.3 %collective-permute-start.38 = (bf16[192,768]{1,0:T(8,128)(2,1)}, bf16[192,768]{1,0:T(8,128)(2,1)}, u32[]{:S(2)}, u32[]{:S(2)}) collective-permute-start(bf16[192,768]{1,0:T(8,128)(2,1)} %get-tuple-element.162), channel_id=1, source_target_pairs={{0,24},{1,25},{2,26},{3,27},{4,28},{5,29},{6,30},{7,31},{8,0},{9,1... | collective-permute-start | bytes 884744 | tf_op jit(solution)/shard_map/ppermute | solution.py:556
  246.9 31.1 %collective-permute-start.37 = (bf16[192,768]{1,0:T(8,128)(2,1)}, bf16[192,768]{1,0:T(8,128)(2,1)}, u32[]{:S(2)}, u32[]{:S(2)}) collective-permute-start(bf16[192,768]{1,0:T(8,128)(2,1)} %get-tuple-element.163), channel_id=1, source_target_pairs={{0,16},{1,17},{2,18},{3,19},{4,20},{5,21},{6,22},{7,23},{8,24},{9,... | collective-permute-start | bytes 884744 | tf_op jit(solution)/shard_map/ppermute | solution.py:556
  246.9 31.1 %collective-permute-start.36 = (bf16[192,768]{1,0:T(8,128)(2,1)}, bf16[192,768]{1,0:T(8,128)(2,1)}, u32[]{:S(2)}, u32[]{:S(2)}) collective-permute-start(bf16[192,768]{1,0:T(8,128)(2,1)} %get-tuple-element.164), channel_id=1, source_target_pairs={{0,8},{1,9},{2,10},{3,11},{4,12},{5,13},{6,14},{7,15},{8,16},{9,17... | collective-permute-start | bytes 884744 | tf_op jit(solution)/shard_map/ppermute | solution.py:556
  260.3 19.0 %collective-permute-start.35 = (bf16[96,768]{1,0:T(8,128)(2,1)S(1)}, bf16[96,768]{1,0:T(8,128)(2,1)}, u32[]{:S(2)}, u32[]{:S(2)}) collective-permute-start(bf16[96,768]{1,0:T(8,128)(2,1)S(1)} %fusion.20), channel_id=1, source_target_pairs={{0,0},{1,8},{2,16},{3,24},{4,1},{5,9},{6,17},{7,25},{8,2},{9,10},{... | collective-permute-start | bytes 442376 | tf_op jit(solution)/shard_map/ppermute | solution.py:556
  263.8 29.0 %collective-permute-start.30 = (bf16[2,4,48,768]{3,2,1,0:T(8,128)(2,1)}, bf16[2,4,48,768]{3,2,1,0:T(8,128)(2,1)}, u32[]{:S(2)}, u32[]{:S(2)}) collective-permute-start(bf16[2,4,48,768]{3,2,1,0:T(8,128)(2,1)} %fusion.3), channel_id=1, source_target_pairs={{0,2},{1,3},{2,0},{3,1},{4,6},{5,7},{6,4},{7,5},{8,10},{9,11},{10,... | collective-permute-start | bytes 1769480 | tf_op jit(solution)/shard_map/ppermute | solution.py:556
  277.0 18.9 %collective-permute-start.31 = (bf16[2,4,64,768]{3,2,1,0:T(8,128)(2,1)}, bf16[2,4,64,768]{3,2,1,0:T(8,128)(2,1)S(1)}, u32[]{:S(2)}, u32[]{:S(2)}) collective-permute-start(bf16[2,4,64,768]{3,2,1,0:T(8,128)(2,1)} %fusion.1), channel_id=1, source_target_pairs={{0,4},{1,5},{2,6},{3,7},{4,0},{5,1},{6,2},{7,3},{8,12},{9,13},{10,... | collective-permute-start | bytes 2359304 | tf_op jit(solution)/shard_map/ppermute | solution.py:556
  280.4 19.9 %collective-permute-start.41 = (bf16[3,96,768]{2,1,0:T(8,128)(2,1)S(1)}, bf16[3,96,768]{2,1,0:T(8,128)(2,1)S(1)}, u32[]{:S(2)}, u32[]{:S(2)}) collective-permute-start(bf16[3,96,768]{2,1,0:T(8,128)(2,1)S(1)} %bitcast.127), channel_id=1, source_target_pairs={{0,1},{1,0},{2,3},{3,2},{4,5},{5,4},{6,7},{7,6},{8,9},{9,8},{10,11... | collective-permute-start | bytes 1327112 | tf_op jit(solution)/shard_map/ppermute | solution.py:556
  312.4 13.8 %collective-permute-start.45 = (bf16[112,768]{1,0:T(8,128)(2,1)S(1)}, bf16[112,768]{1,0:T(8,128)(2,1)S(1)}, u32[]{:S(2)}, u32[]{:S(2)}) collective-permute-start(bf16[112,768]{1,0:T(8,128)(2,1)S(1)} %get-tuple-element.171), channel_id=1, source_target_pairs={{0,16},{1,17},{2,18},{3,19},{4,20},{5,21},{6,22},{7,23},{8,24},{9,... | collective-permute-start | bytes 516104 | tf_op jit(solution)/shard_map/ppermute | solution.py:556
  (67 other events, 650.4 us)
Sparse Core Ops, SparseCore 0:
  11.5 117.9 all-gather.2

commit v6 on v5

--- a/solution.py
+++ b/solution.py
@@ -30,7 +30,7 @@
 
 
 def cost(us):
-    return pl.CostEstimate(flops=0, bytes_accessed=int(us * 3.0e3), transcendentals=0)
+    return pl.CostEstimate(flops=0, bytes_accessed=int(us * 3.0e6), transcendentals=0)
 
 
 def mm(a, b):
@@ -449,7 +449,7 @@
     )(slopes, datt, q_m, qkv, pos)
 
 
-def attention_grads_kernel(rc, where_ref, flip_ref, rhs_ref, att_ref, low_ref, small_attn_ref, small_ffn_ref, cut0_ref, cut1_ref, full_ref, tail_ref):
+def attention_grads_kernel(where_ref, flip_ref, rhs_ref, att_ref, low_ref, small_attn_ref, small_ffn_ref, keep0_ref, keep1_ref, away0_ref, away1_ref, full_ref, tail_ref):
     z, y, mine = where_ref[0], where_ref[1], where_ref[4]
     half = ROWS // 2
     step = 256
@@ -457,43 +457,45 @@
     small = jnp.concatenate([small_attn_ref[...], small_ffn_ref[...]], axis=0).astype(LOW)
     for n in range(SHARDS):
         tail_ref[n, 0:4, 0:ROWS] = small[:, n * ROWS : (n + 1) * ROWS]
-    for rx in (0, 1):
-        j = jnp.bitwise_xor(mine, 2 * rx + rc)
-
-        @pl.when(j == 3)
-        def _():
-            for n in range(D // step):
-                rows = slice(n * step, (n + 1) * step)
-                full_ref[rows, :] = mm_tn(att_ref[:, rows], low_ref[...])
-
-        @pl.when(j != 3)
-        def _():
-            @pl.loop(0, D // step)
-            def _(n):
-                lane = pl.multiple_of(n * step, step)
-                cols = pl.ds(pl.multiple_of(j * D + n * step, step), step)
-                full_ref[:, pl.ds(lane, step)] = mm(flip_ref[...], rhs_ref[:, cols])
-
-        for rz in range(LINE):
-            base = 2 * lax.rem(z + rz, LINE)
-            for ry in (0, 1):
-                shard = base + (y if ry == 0 else 1 - y)
-                start = shard * ROWS
-                cut0_ref[rx, ry, rz] = full_ref[pl.ds(pl.multiple_of(start, 8), half), :].astype(LOW)
-                cut1_ref[ry, rx, rz, 0:half] = full_ref[pl.ds(pl.multiple_of(start + half, 8), half), :].astype(LOW)
-                cut1_ref[ry, rx, rz, half:] = tail_ref[shard]
-
-
-def attention_grads(where, rc, x_flip, rhs, att_m, low, small_attn, small_ffn):
+    for rc in (1, 0):
+        cut0_ref, cut1_ref = (keep0_ref, keep1_ref) if rc == 0 else (away0_ref, away1_ref)
+        for rx in (0, 1):
+            j = jnp.bitwise_xor(mine, 2 * rx + rc)
+
+            @pl.when(j == 3)
+            def _():
+                for n in range(D // step):
+                    rows = slice(n * step, (n + 1) * step)
+                    full_ref[rows, :] = mm_tn(att_ref[:, rows], low_ref[...])
+
+            @pl.when(j != 3)
+            def _():
+                @pl.loop(0, D // step)
+                def _(n):
+                    lane = pl.multiple_of(n * step, step)
+                    cols = pl.ds(pl.multiple_of(j * D + n * step, step), step)
+                    full_ref[:, pl.ds(lane, step)] = mm(flip_ref[...], rhs_ref[:, cols])
+
+            for rz in range(LINE):
+                base = 2 * lax.rem(z + rz, LINE)
+                for ry in (0, 1):
+                    shard = base + (y if ry == 0 else 1 - y)
+                    start = shard * ROWS
+                    cut0_ref[rx, ry, rz] = full_ref[pl.ds(pl.multiple_of(start, 8), half), :].astype(LOW)
+                    cut1_ref[ry, rx, rz, 0:half] = full_ref[pl.ds(pl.multiple_of(start + half, 8), half), :].astype(LOW)
+                    cut1_ref[ry, rx, rz, half:] = tail_ref[shard]
+
+
+def attention_grads(where, x_flip, rhs, att_m, low, small_attn, small_ffn):
     half = ROWS // 2
     return pl.pallas_call(
-        functools.partial(attention_grads_kernel, rc),
-        out_shape=(out((2, 2, LINE, half, D), LOW), out((2, 2, LINE, half + TAIL, D), LOW)),
+        attention_grads_kernel,
+        out_shape=(out((2, 2, LINE, half, D), LOW), out((2, 2, LINE, half + TAIL, D), LOW)) * 2,
         in_specs=[SMEM] + [VMEM] * 6,
-        out_specs=(VMEM, VMEM),
+        out_specs=(VMEM,) * 4,
         scratch_shapes=[pltpu.VMEM((D, D), F32), pltpu.VMEM((SHARDS, TAIL, D), LOW)],
         compiler_params=BIG,
-        cost_estimate=cost(5),
+        cost_estimate=cost(10),
         name="attention_grads",
     )(where, x_flip, rhs, att_m, low, small_attn, small_ffn)
 
@@ -674,33 +676,35 @@
     h1, h_all = lax.optimization_barrier((h1, h_all))
     layer_out, dr2, e2, small_ffn = ffn_forward(h1, w_ffn, norms, pos, dy, seqs)
     act, to_gate, to_up = ffn_again(where, h_all, w_ffn)
-    e_all = jnp.stack(share_dp(e2))
+    other = after(send(e2, "x"), act)
+    e_all = jnp.stack([e2, send(e2, "c"), other, send(other, "c")])
     dgate, dup, keep, away = ffn_back(where, e_all, to_gate, to_up, w_ffn)
     part = add(keep, send(away, "c"))
+    part, part_away = part[0], part[1].astype(LOW)
     keep_d, away_d = weight_grad(where, act, e_all)
+    came = send(part_away, "x")
     got_d = send(away_d, "y")
-    keep_g, away_g = weight_grad(where, after(h_all, away_d), dgate)
-    came = send(part[1].astype(LOW), "x")
+    keep_g, away_g = weight_grad(where, after(h_all, (away_d, part_away)), dgate)
     got_g = send(away_g, "y")
-    keep_u, away_u = weight_grad(where, after(h_all, away_g), dup)
+    keep_u, away_u = weight_grad(where, after(h_all, (away_g, came)), dup)
     got_u = send(away_u, "y")
-    dr1, low, datt, small_attn = norm_back_call(dr2, part[0], after(came, away_u), r1_m, w_attn, norms)
+    dr1, low, datt, small_attn = norm_back_call(dr2, part, after(came, away_u), r1_m, w_attn, norms)
+    rhs = attention_back(datt, q_m, qkv, pos, slopes, seqs)
+    got_d, got_g, got_u, rhs = lax.optimization_barrier((got_d, got_g, got_u, rhs))
     parts_d = line_parts(keep_d, got_d)
-    rhs = attention_back(after(datt, parts_d), q_m, qkv, pos, slopes, seqs)
-    got_d, got_g, got_u, rhs = lax.optimization_barrier((got_d, got_g, got_u, rhs))
+    line_d = line_send(parts_d)
+    keep0, keep1, away0, away1 = attention_grads(where, x_flip, after(rhs, parts_d), att_m, low, small_attn, small_ffn)
+    away0, away1, line_d = lax.optimization_barrier((away0, away1, line_d))
+    came0, came1 = send(away0, "c"), send(away1, "c")
     keep_gu, got_gu = jnp.concatenate([keep_g, keep_u], axis=1), jnp.concatenate([got_g, got_u], axis=1)
-    parts_gu = line_parts(keep_gu, got_gu)
-    away0, away1 = attention_grads(where, 1, x_flip, after(rhs, parts_gu), att_m, low, small_attn, small_ffn)
-    came0, came1 = send(away0, "c"), send(away1, "c")
-    g_down = line_add(keep_d, got_d, after(line_send(parts_d), away0))
-    g_down = send(g_down, "down")
-    keep0, keep1 = attention_grads(where, 0, x_flip, after(rhs, away0), att_m, low, small_attn, small_ffn)
-    came0, came1, keep0, keep1 = lax.optimization_barrier((came0, came1, keep0, keep1))
+    parts_gu = line_parts(keep_gu, after(got_gu, away0))
+    line_gu = line_send(parts_gu)
+    g_down = send(line_add(keep_d, got_d, line_d), "down")
     away0, away1 = add(keep0[1], came0[1]).astype(LOW), add(keep1[1], came1[1]).astype(LOW)
     got0, got1 = send(away0, "x"), send(away1, "y")
     grad_in = input_grad(after(rhs, (away0, away1)), w_attn, dr1, positions)
-    g_gu = line_add(keep_gu, got_gu, after(line_send(parts_gu), grad_in))
-    g_ffn = jnp.concatenate([g_down, g_gu]).reshape(3, ROWS, D)
+    g_down, line_gu, grad_in = lax.optimization_barrier((g_down, line_gu, grad_in))
+    g_ffn = jnp.concatenate([g_down, line_add(keep_gu, got_gu, line_gu)]).reshape(3, ROWS, D)
     got0, got1 = after((got0, got1), g_ffn)
     shared = share_dp(g_ffn)
     total0 = add(keep0[0], came0[0]) + got0.astype(F32)

time: 344 us -> 327 us (0.951)
  starting transfers between devices: 57.3 us -> 42.5 us
    ppermute x50, starting transfers between devices: 57.3 us -> 42.4 us  [send(): return lax.ppermute(value, AXES, MOVES[move])]
    pallas_call x2 -> x1, Pallas kernels: 11.4 us -> 8.84 us  [attention_grads(): pl.pallas_call(attention_grads_kernel, out_shape=(out((2, 2, LINE, half,...]
  transfers between devices with their start and end apart: 51 -> 51, of which waited for: 23 -> 23; matrix products, arithmetic and copies ran while one was open for 6% -> 5% of each run, Pallas kernels for 21% -> 23%
where the time goes in v6:
time: 327 us; the launch traced here: 326 us
  waiting for transfers between devices  141 us (43%)
  Pallas kernels  102 us (31%)
  starting transfers between devices  42.5 us (13%)
  between operations  14.8 us (5%)
  other arithmetic  14.6 us (4%)
  local copies, waits for them, and re-layouts  11 us (3%)
    ppermute x50, waiting for transfers between devices, send(): return lax.ppermute(value, AXES, MOVES[move])  111 us
    ppermute x50, starting transfers between devices, send(): return lax.ppermute(value, AXES, MOVES[move])  42.4 us
    all_gather x1, waiting for transfers between devices, on_block(): lax.all_gather(ffn_piece, AXES, axis=0, tiled=False)  30.3 us
    pallas_call x1, Pallas kernels, attention_forward(): pl.pallas_call(functools.partial(attention_kernel, seqs, listed // seqs),...  18.1 us
    pallas_call x1, Pallas kernels, ffn_forward(): pl.pallas_call(functools.partial(ffn_kernel, seqs, listed // seqs), out_s...  17 us
    pallas_call x1, Pallas kernels, attention_back(): pl.pallas_call(functools.partial(attention_back_kernel, seqs, listed // s...  15.7 us
    pallas_call x3, Pallas kernels, weight_grad(): pl.pallas_call(weight_grad_kernel, out_shape=(out(shape, LOW), out(shape,...  11.6 us
    pallas_call x1, Pallas kernels, attention_grads(): pl.pallas_call(attention_grads_kernel, out_shape=(out((2, 2, LINE, half,...  8.84 us
  transfers between devices with their start and end apart: 51, of which 23 were waited for; matrix products, arithmetic and copies ran while one was open for 5% of the time, Pallas kernels for 23%

profile of v6, /device:TPU:0, one launch (start us, length us, event | category | flops | bytes accessed | tf_op | source)
XLA Modules:
  0.0 325.9 jit_solution(7207688228000882733)
XLA Ops:
  9.6 4.1 %collective-permute-start.1 = (bf16[104,768]{1,0:T(8,128)(2,1)S(1)}, bf16[104,768]{1,0:T(8,128)(2,1)S(1)}, u32[]{:S(2)}, u32[]{:S(2)}) collective-permute-start(bf16[104,768]{1,0:T(8,128)(2,1)S(1)} %get-tuple-element.178), channel_id=1, source_target_pairs={{0,16},{1,17},{2,18},{3,19},{4,20},{5,21},{6,22},{7,23},{8,24},{9,... | collective-permute-start | bytes 479240 | tf_op jit(solution)/shard_map/ppermute | solution.py:558
  18.7 6.9 %collective-permute-done.1 = bf16[104,768]{1,0:T(8,128)(2,1)S(1)} collective-permute-done((bf16[104,768]{1,0:T(8,128)(2,1)S(1)}, bf16[104,768]{1,0:T(8,128)(2,1)S(1)}, u32[]{:S(2)}, u32[]{:S(2)}) %collective-permute-start.1) | collective-permute-done | bytes 159776 | tf_op jit(solution)/shard_map/ppermute | solution.py:558
  31.4 6.8 %collective-permute-done.6.rest_5_ = bf16[4,56,768]{2,1,0:T(8,128)(2,1)S(1)} collective-permute-done((bf16[4,56,768]{2,1,0:T(8,128)(2,1)S(1)}, bf16[4,56,768]{2,1,0:T(8,128)(2,1)S(1)}, u32[]{:S(2)}, u32[]{:S(2)}) %collective-permute-start.6) | collective-permute-done | bytes 344096 | tf_op jit(solution)/shard_map/ppermute | solution.py:558
  42.5 4.0 %collective-permute-done.4.rest_2_ = bf16[4,48,768]{2,1,0:T(8,128)(2,1)} collective-permute-done((bf16[4,48,768]{2,1,0:T(8,128)(2,1)S(1)}, bf16[4,48,768]{2,1,0:T(8,128)(2,1)}, u32[]{:S(2)}, u32[]{:S(2)}) %collective-permute-start.4) | collective-permute-done | bytes 294944 | tf_op jit(solution)/shard_map/ppermute | solution.py:558
  50.7 5.5 %collective-permute-done.8.rest_7_ = bf16[4,56,768]{2,1,0:T(8,128)(2,1)S(1)} collective-permute-done((bf16[4,56,768]{2,1,0:T(8,128)(2,1)S(1)}, bf16[4,56,768]{2,1,0:T(8,128)(2,1)S(1)}, u32[]{:S(2)}, u32[]{:S(2)}) %collective-permute-start.8) | collective-permute-done | bytes 344096 | tf_op jit(solution)/shard_map/ppermute | solution.py:558
  56.8 6.1 %collective-permute-done.7.rest_6_ = bf16[4,48,768]{2,1,0:T(8,128)(2,1)} collective-permute-done((bf16[4,48,768]{2,1,0:T(8,128)(2,1)}, bf16[4,48,768]{2,1,0:T(8,128)(2,1)}, u32[]{:S(2)}, u32[]{:S(2)}) %collective-permute-start.7) | collective-permute-done | bytes 294944 | tf_op jit(solution)/shard_map/ppermute | solution.py:558
  65.8 18.1 %attention_forward.1 = (bf16[512,2304]{1,0:T(8,128)(2,1)}, f32[512,768]{1,0:T(8,128)}, bf16[128,768]{1,0:T(8,128)(2,1)}, bf16[128,768]{1,0:T(8,128)(2,1)}, bf16[...) custom-call(s32[5]{0:T(128)} %stack.83.where_ref, f32[12]{0:T(128)} %multiply_exponential_fusion.slope_ref, ...), custom_call_target="tpu_custom_call" | custom-call | bytes 60000000 | tf_op jit(solution)/shard_map/attention_forward/pallas_call | solution.py:164
  85.6 10.4 %collective-permute-done.18 = bf16[128,768]{1,0:T(8,128)(2,1)S(1)} collective-permute-done((bf16[128,768]{1,0:T(8,128)(2,1)}, bf16[128,768]{1,0:T(8,128)(2,1)S(1)}, u32[]{:S(2)}, u32[]{:S(2)}) %collective-permute-start.18) | collective-permute-done | bytes 196640 | tf_op jit(solution)/shard_map/ppermute | solution.py:558
  99.3 30.3 %all-gather.3.cloned.1.call-done = bf16[96,96,768]{2,1,0:T(8,128)(2,1)} async-done(((bf16[3,96,768]{2,1,0:T(8,128)(2,1)}), bf16[96,96,768]{2,1,0:T(8,128)(2,1)}) %all-gather.3.cloned.1.call-update) | async-done | bytes 14155792 | tf_op jit(solution)/shard_map/all_gather | solution.py:664
  129.6 17.0 %ffn_forward.1 = (bf16[512,768]{1,0:T(8,128)(2,1)}, f32[128,768]{1,0:T(8,128)}, bf16[128,768]{1,0:T(8,128)(2,1)}, f32[2,768]{1,0:T(2,128)}) custom-call(f32[512,768]{1,0:T(8,128)} %get-tuple-element.89.h1_ref, bf16[8,4,3,96,768]{4,3,2,1,0:T(8,128)(2,1)} %bitcast.114, bf16[8,4,3,96,768]{4,3,2,1,0:T(8,128)(2,1)} %bitcast.115, ...), custom_call_target="tpu_custom_call" | custom-call | bytes 48000000 | tf_op jit(solution)/shard_map/ffn_forward/pallas_call | solution.py:232
  147.2 6.6 %ffn_again.1 = (bf16[512,768]{1,0:T(8,128)(2,1)}, f32[512,768]{1,0:T(8,128)}, f32[512,768]{1,0:T(8,128)}) custom-call(s32[5]{0:T(128)} %stack.83.where_ref, bf16[4,128,768]{2,1,0:T(8,128)(2,1)} %pad_maximum_fusion.1.h_ref.a_ref, bf16[8,4,3,96,768]{4,3,2,1,0:T(8,128)(2,1)} %bitcast.117, bf16[8,4,3,96,768]{4,3,2,1,0:T(8,128)(2,1)} %bitcast.118), custom_call_target="tpu_custom_call" | custom-call | bytes 18000000 | tf_op jit(solution)/shard_map/ffn_again/pallas_call | solution.py:288
  156.3 7.5 %ffn_back.1 = (bf16[512,768]{1,0:T(8,128)(2,1)}, bf16[512,768]{1,0:T(8,128)(2,1)}, f32[2,128,768]{2,1,0:T(8,128)}, bf16[2,128,768]{2,1,0:T(8,128)(2,1)}) custom-call(s32[5]{0:T(128)} %stack.83.where_ref, bf16[4,128,768]{2,1,0:T(8,128)(2,1)} %pad_maximum_fusion.2.b_ref.e_ref, f32[512,768]{1,0:T(8,128)} %get-tuple-element.97.to_gate_ref, ...), custom_call_target="tpu_custom_call" | custom-call | bytes 21000000 | tf_op jit(solution)/shard_map/ffn_back/pallas_call | solution.py:323
  168.5 3.8 %weight_grad.3 = (bf16[4,96,768]{2,1,0:T(8,128)(2,1)}, bf16[4,96,768]{2,1,0:T(8,128)(2,1)}) custom-call(s32[5]{0:T(128)} %stack.83.where_ref, bf16[512,768]{1,0:T(8,128)(2,1)} %get-tuple-element.92.a_ref, bf16[4,128,768]{2,1,0:T(8,128)(2,1)} %pad_maximum_fusion.2.b_ref.e_ref), custom_call_target="tpu_custom_call" | custom-call | bytes 12000000 | tf_op jit(solution)/shard_map/weight_grad/pallas_call | solution.py:359
  178.2 3.9 %weight_grad.5 = (bf16[4,96,768]{2,1,0:T(8,128)(2,1)}, bf16[4,96,768]{2,1,0:T(8,128)(2,1)}) custom-call(s32[5]{0:T(128)} %stack.83.where_ref, bf16[4,128,768]{2,1,0:T(8,128)(2,1)} %pad_maximum_fusion.1.h_ref.a_ref, bf16[512,768]{1,0:T(8,128)(2,1)} %get-tuple-element.105.b_ref), custom_call_target="tpu_custom_call" | custom-call | bytes 12000000 | tf_op jit(solution)/shard_map/weight_grad/pallas_call | solution.py:359
  187.5 15.7 %attention_back.1.rhs_ref = bf16[512,2304]{1,0:T(8,128)(2,1)} custom-call(f32[12]{0:T(128)} %multiply_exponential_fusion.slope_ref, bf16[128,768]{1,0:T(8,128)(2,1)} %get-tuple-element.111.datt_ref, bf16[128,768]{1,0:T(8,128)(2,1)} %get-tuple-element.112.q_ref, bf16[512,2304]{1,0:T(8,128)(2,1)} %get-tuple-element.113.qkv_ref, s32[128,1]{1,0:T(8,128)} %reshape.129.pos_ref), custom_call_target="tpu_custom_call" | custom-call | bytes 45000000 | tf_op jit(solution)/shard_map/attention_back/pallas_call | solution.py:440
  203.2 9.9 %collective-permute-done.27 = bf16[4,96,768]{2,1,0:T(8,128)(2,1)S(1)} collective-permute-done((bf16[4,96,768]{2,1,0:T(8,128)(2,1)}, bf16[4,96,768]{2,1,0:T(8,128)(2,1)S(1)}, u32[]{:S(2)}, u32[]{:S(2)}) %collective-permute-start.27) | collective-permute-done | bytes 589856 | tf_op jit(solution)/shard_map/ppermute | solution.py:558
  217.0 8.8 %attention_grads.1 = (bf16[2,2,4,48,768]{4,3,2,1,0:T(8,128)(2,1)}, bf16[2,2,4,64,768]{4,3,2,1,0:T(8,128)(2,1)}, bf16[2,2,4,48,768]{4,3,2,1,0:T(8,128)(2,1)}, bf16[2,2,4,64,768]{4,3,2,1,0:T(8,128)(2,1)}) custom-call(s32[5]{0:T(128)} %stack.83.where_ref, bf16[768,512]{1,0:T(8,128)(2,1)} %bitcast.122, bf16[512,2304]{1,0:T(8,128)(2,1)} %attention_back.1.rhs_ref, ...), custom_call_target="tpu_custom_call" | custom-call | bytes 30000000 | tf_op jit(solution)/shard_map/attention_grads/pallas_call | solution.py:491
  234.6 5.1 %collective-permute-start.34 = (bf16[192,768]{1,0:T(8,128)(2,1)}, bf16[192,768]{1,0:T(8,128)(2,1)}, u32[]{:S(2)}, u32[]{:S(2)}) collective-permute-start(bf16[192,768]{1,0:T(8,128)(2,1)} %get-tuple-element.162), channel_id=1, source_target_pairs={{0,24},{1,25},{2,26},{3,27},{4,28},{5,29},{6,30},{7,31},{8,0},{9,1... | collective-permute-start | bytes 884744 | tf_op jit(solution)/shard_map/ppermute | solution.py:558
  244.1 8.1 %input_grad.1 = f32[512,768]{1,0:T(8,128)} custom-call(bf16[512,2304]{1,0:T(8,128)(2,1)} %attention_back.1.rhs_ref, bf16[8,4,96,768]{3,2,1,0:T(8,128)(2,1)} %get-tuple-element.110.w_ref, f32[128,768]{1,0:T(8,128)} %get-tuple-element.137.dr1_ref, s32[4,32]{1,0:T(4,128)} %pos_ref.1), custom_call_target="tpu_custom_call" | custom-call | bytes 24000000 | tf_op jit(solution)/shard_map/input_grad/pallas_call | solution.py:521
  252.4 17.0 %collective-permute-done.33 = bf16[192,768]{1,0:T(8,128)(2,1)} collective-permute-done((bf16[192,768]{1,0:T(8,128)(2,1)}, bf16[192,768]{1,0:T(8,128)(2,1)}, u32[]{:S(2)}, u32[]{:S(2)}) %collective-permute-start.33) | collective-permute-done | bytes 294944 | tf_op jit(solution)/shard_map/ppermute | solution.py:558
  270.9 11.1 %collective-permute-done.42.rest_2_ = bf16[3,96,768]{2,1,0:T(8,128)(2,1)S(1)} collective-permute-done((bf16[3,96,768]{2,1,0:T(8,128)(2,1)S(1)}, bf16[3,96,768]{2,1,0:T(8,128)(2,1)S(1)}, u32[]{:S(2)}, u32[]{:S(2)}) %collective-permute-start.42) | collective-permute-done | bytes 442400 | tf_op jit(solution)/shard_map/ppermute | solution.py:558
  286.9 7.6 %collective-permute-done.39 = bf16[4,48,768]{2,1,0:T(8,128)(2,1)S(1)} collective-permute-done((bf16[4,48,768]{2,1,0:T(8,128)(2,1)S(1)}, bf16[4,48,768]{2,1,0:T(8,128)(2,1)S(1)}, u32[]{:S(2)}, u32[]{:S(2)}) %collective-permute-start.39) | collective-permute-done | bytes 294944 | tf_op jit(solution)/shard_map/ppermute | solution.py:558
  301.8 7.6 %collective-permute-done.45 = bf16[112,768]{1,0:T(8,128)(2,1)S(1)} collective-permute-done((bf16[112,768]{1,0:T(8,128)(2,1)S(1)}, bf16[112,768]{1,0:T(8,128)(2,1)S(1)}, u32[]{:S(2)}, u32[]{:S(2)}) %collective-permute-start.45) | collective-permute-done | bytes 172064 | tf_op jit(solution)/shard_map/ppermute | solution.py:558
  309.9 4.8 %collective-permute-done.48.rest_2_ = bf16[96,768]{1,0:T(8,128)(2,1)S(1)} collective-permute-done((bf16[96,768]{1,0:T(8,128)(2,1)S(1)}, bf16[96,768]{1,0:T(8,128)(2,1)S(1)}, u32[]{:S(2)}, u32[]{:S(2)}) %collective-permute-start.48) | collective-permute-done | bytes 147488 | tf_op jit(solution)/shard_map/ppermute | solution.py:558
  (239 shorter events, 84.6 us)
Async XLA Ops:
  7.2 122.3 %all-gather.3.cloned.1.call-start = ((), (), s32[]{:S(2)}) async-start(), calls=%async_computation | async-start | bytes 14598144 | tf_op jit(solution)/shard_map/all_gather | solution.py:664
  9.6 16.0 %collective-permute-start.1 = (bf16[104,768]{1,0:T(8,128)(2,1)S(1)}, bf16[104,768]{1,0:T(8,128)(2,1)S(1)}, u32[]{:S(2)}, u32[]{:S(2)}) collective-permute-start(bf16[104,768]{1,0:T(8,128)(2,1)S(1)} %get-tuple-element.178), channel_id=1, source_target_pairs={{0,16},{1,17},{2,18},{3,19},{4,20},{5,21},{6,22},{7,23},{8,24},{9,... | collective-permute-start | bytes 479240 | tf_op jit(solution)/shard_map/ppermute | solution.py:558
  29.0 13.5 %collective-permute-start.5 = (bf16[4,48,768]{2,1,0:T(8,128)(2,1)S(1)}, bf16[4,48,768]{2,1,0:T(8,128)(2,1)}, u32[]{:S(2)}, u32[]{:S(2)}) collective-permute-start(bf16[4,48,768]{2,1,0:T(8,128)(2,1)S(1)} %slice.145.rest_0_), channel_id=1, source_target_pairs={{0,2},{1,3},{2,0},{3,1},{4,6},{5,7},{6,4},{7,5},{8,10},{9,11},{10,... | collective-permute-start | bytes 884744 | tf_op jit(solution)/shard_map/ppermute | solution.py:558
  29.4 17.1 %collective-permute-start.3 = (bf16[4,56,768]{2,1,0:T(8,128)(2,1)S(1)}, bf16[4,56,768]{2,1,0:T(8,128)(2,1)S(1)}, u32[]{:S(2)}, u32[]{:S(2)}) collective-permute-start(bf16[4,56,768]{2,1,0:T(8,128)(2,1)S(1)} %slice.143.rest_1_), channel_id=1, source_target_pairs={{0,4},{1,5},{2,6},{3,7},{4,0},{5,1},{6,2},{7,3},{8,12},{9,13},{10,... | collective-permute-start | bytes 1032200 | tf_op jit(solution)/shard_map/ppermute | solution.py:558
  31.2 15.3 %collective-permute-start.4 = (bf16[4,48,768]{2,1,0:T(8,128)(2,1)S(1)}, bf16[4,48,768]{2,1,0:T(8,128)(2,1)}, u32[]{:S(2)}, u32[]{:S(2)}) collective-permute-start(bf16[4,48,768]{2,1,0:T(8,128)(2,1)S(1)} %slice.145.rest_0_), channel_id=1, source_target_pairs={{0,4},{1,5},{2,6},{3,7},{4,0},{5,1},{6,2},{7,3},{8,12},{9,13},{10,... | collective-permute-start | bytes 884744 | tf_op jit(solution)/shard_map/ppermute | solution.py:558
  31.4 19.1 %collective-permute-start.10 = (bf16[4,56,768]{2,1,0:T(8,128)(2,1)S(1)}, bf16[4,56,768]{2,1,0:T(8,128)(2,1)S(1)}, u32[]{:S(2)}, u32[]{:S(2)}) collective-permute-start(bf16[4,56,768]{2,1,0:T(8,128)(2,1)S(1)} %slice.143.rest_1_), channel_id=1, source_target_pairs={{0,1},{1,0},{2,3},{3,2},{4,5},{5,4},{6,7},{7,6},{8,9},{9,8},{10,11... | collective-permute-start | bytes 1032200 | tf_op jit(solution)/shard_map/ppermute | solution.py:558
  38.2 18.0 %collective-permute-start.8 = (bf16[4,56,768]{2,1,0:T(8,128)(2,1)S(1)}, bf16[4,56,768]{2,1,0:T(8,128)(2,1)S(1)}, u32[]{:S(2)}, u32[]{:S(2)}) collective-permute-start(bf16[4,56,768]{2,1,0:T(8,128)(2,1)S(1)} %collective-permute-done.6.rest_5_), channel_id=1, source_target_pairs={{0,4},{1,5},{2,6},{3,7},{4,0},{5,1},{6,2},{7,3},{8,12},{9,13},{10,... | collective-permute-start | bytes 1032200 | tf_op jit(solution)/shard_map/ppermute | solution.py:558
  46.5 16.4 %collective-permute-start.7 = (bf16[4,48,768]{2,1,0:T(8,128)(2,1)}, bf16[4,48,768]{2,1,0:T(8,128)(2,1)}, u32[]{:S(2)}, u32[]{:S(2)}) collective-permute-start(bf16[4,48,768]{2,1,0:T(8,128)(2,1)} %collective-permute-done.4.rest_2_), channel_id=1, source_target_pairs={{0,2},{1,3},{2,0},{3,1},{4,6},{5,7},{6,4},{7,5},{8,10},{9,11},{10,... | collective-permute-start | bytes 884744 | tf_op jit(solution)/shard_map/ppermute | solution.py:558
  49.8 14.3 %collective-permute-start.14 = (bf16[4,56,768]{2,1,0:T(8,128)(2,1)S(1)}, bf16[4,56,768]{2,1,0:T(8,128)(2,1)S(1)}, u32[]{:S(2)}, u32[]{:S(2)}) collective-permute-start(bf16[4,56,768]{2,1,0:T(8,128)(2,1)S(1)} %collective-permute-done.6.rest_5_), channel_id=1, source_target_pairs={{0,1},{1,0},{2,3},{3,2},{4,5},{5,4},{6,7},{7,6},{8,9},{9,8},{10,11... | collective-permute-start | bytes 1032200 | tf_op jit(solution)/shard_map/ppermute | solution.py:558
  50.6 13.6 %collective-permute-start.12 = (bf16[4,56,768]{2,1,0:T(8,128)(2,1)S(1)}, bf16[4,56,768]{2,1,0:T(8,128)(2,1)S(1)}, u32[]{:S(2)}, u32[]{:S(2)}) collective-permute-start(bf16[4,56,768]{2,1,0:T(8,128)(2,1)S(1)} %collective-permute-done.3.rest_3_), channel_id=1, source_target_pairs={{0,1},{1,0},{2,3},{3,2},{4,5},{5,4},{6,7},{7,6},{8,9},{9,8},{10,11... | collective-permute-start | bytes 1032200 | tf_op jit(solution)/shard_map/ppermute | solution.py:558
  172.3 30.9 %collective-permute-start.23 = (bf16[4,96,768]{2,1,0:T(8,128)(2,1)}, bf16[4,96,768]{2,1,0:T(8,128)(2,1)S(1)}, u32[]{:S(2)}, u32[]{:S(2)}) collective-permute-start(bf16[4,96,768]{2,1,0:T(8,128)(2,1)} %get-tuple-element.96), channel_id=1, source_target_pairs={{0,4},{1,5},{2,6},{3,7},{4,0},{5,1},{6,2},{7,3},{8,12},{9,13},{10,... | collective-permute-start | bytes 1769480 | tf_op jit(solution)/shard_map/ppermute | solution.py:558
  177.6 25.6 %collective-permute-start.25 = (bf16[4,96,768]{2,1,0:T(8,128)(2,1)}, bf16[4,96,768]{2,1,0:T(8,128)(2,1)S(1)}, u32[]{:S(2)}, u32[]{:S(2)}) collective-permute-start(bf16[4,96,768]{2,1,0:T(8,128)(2,1)} %get-tuple-element.103), channel_id=1, source_target_pairs={{0,4},{1,5},{2,6},{3,7},{4,0},{5,1},{6,2},{7,3},{8,12},{9,13},{10,... | collective-permute-start | bytes 1769480 | tf_op jit(solution)/shard_map/ppermute | solution.py:558
  182.1 31.1 %collective-permute-start.27 = (bf16[4,96,768]{2,1,0:T(8,128)(2,1)}, bf16[4,96,768]{2,1,0:T(8,128)(2,1)S(1)}, u32[]{:S(2)}, u32[]{:S(2)}) collective-permute-start(bf16[4,96,768]{2,1,0:T(8,128)(2,1)} %get-tuple-element.106), channel_id=1, source_target_pairs={{0,4},{1,5},{2,6},{3,7},{4,0},{5,1},{6,2},{7,3},{8,12},{9,13},{10,... | collective-permute-start | bytes 1769480 | tf_op jit(solution)/shard_map/ppermute | solution.py:558
  215.0 13.3 %collective-permute-start.29 = (bf16[96,768]{1,0:T(8,128)(2,1)S(1)}, bf16[96,768]{1,0:T(8,128)(2,1)S(1)}, u32[]{:S(2)}, u32[]{:S(2)}) collective-permute-start(bf16[96,768]{1,0:T(8,128)(2,1)S(1)} %get-tuple-element.166), channel_id=1, source_target_pairs={{0,16},{1,17},{2,18},{3,19},{4,20},{5,21},{6,22},{7,23},{8,24},{9,... | collective-permute-start | bytes 442376 | tf_op jit(solution)/shard_map/ppermute | solution.py:558
  228.3 13.5 %collective-permute-start.36 = (bf16[2,2,4,64,768]{4,3,2,1,0:T(8,128)(2,1)}, bf16[2,2,4,64,768]{4,3,2,1,0:T(8,128)(2,1)S(1)}, u32[]{:S(2)}, u32[]{:S(2)}) collective-permute-start(bf16[2,2,4,64,768]{4,3,2,1,0:T(8,128)(2,1)} %get-tuple-element.135), channel_id=1, source_target_pairs={{0,1},{1,0},{2,3},{3,2},{4,5},{5,4},{6,7},{7,6},{8,9},{9,8},{10,11... | collective-permute-start | bytes 4718600 | tf_op jit(solution)/shard_map/ppermute | solution.py:558
  231.9 20.2 %collective-permute-start.31 = (bf16[96,768]{1,0:T(8,128)(2,1)}, bf16[96,768]{1,0:T(8,128)(2,1)S(1)}, u32[]{:S(2)}, u32[]{:S(2)}) collective-permute-start(bf16[96,768]{1,0:T(8,128)(2,1)} %fusion.20), channel_id=1, source_target_pairs={{0,0},{1,8},{2,16},{3,24},{4,1},{5,9},{6,17},{7,25},{8,2},{9,10},{... | collective-permute-start | bytes 442376 | tf_op jit(solution)/shard_map/ppermute | solution.py:558
  234.6 17.7 %collective-permute-start.34 = (bf16[192,768]{1,0:T(8,128)(2,1)}, bf16[192,768]{1,0:T(8,128)(2,1)}, u32[]{:S(2)}, u32[]{:S(2)}) collective-permute-start(bf16[192,768]{1,0:T(8,128)(2,1)} %get-tuple-element.162), channel_id=1, source_target_pairs={{0,24},{1,25},{2,26},{3,27},{4,28},{5,29},{6,30},{7,31},{8,0},{9,1... | collective-permute-start | bytes 884744 | tf_op jit(solution)/shard_map/ppermute | solution.py:558
  239.7 29.6 %collective-permute-start.33 = (bf16[192,768]{1,0:T(8,128)(2,1)}, bf16[192,768]{1,0:T(8,128)(2,1)}, u32[]{:S(2)}, u32[]{:S(2)}) collective-permute-start(bf16[192,768]{1,0:T(8,128)(2,1)} %get-tuple-element.163), channel_id=1, source_target_pairs={{0,16},{1,17},{2,18},{3,19},{4,20},{5,21},{6,22},{7,23},{8,24},{9,... | collective-permute-start | bytes 884744 | tf_op jit(solution)/shard_map/ppermute | solution.py:558
  239.7 29.6 %collective-permute-start.32 = (bf16[192,768]{1,0:T(8,128)(2,1)}, bf16[192,768]{1,0:T(8,128)(2,1)}, u32[]{:S(2)}, u32[]{:S(2)}) collective-permute-start(bf16[192,768]{1,0:T(8,128)(2,1)} %get-tuple-element.164), channel_id=1, source_target_pairs={{0,8},{1,9},{2,10},{3,11},{4,12},{5,13},{6,14},{7,15},{8,16},{9,17... | collective-permute-start | bytes 884744 | tf_op jit(solution)/shard_map/ppermute | solution.py:558
  241.8 40.2 %collective-permute-start.37 = (bf16[2,4,48,768]{3,2,1,0:T(8,128)(2,1)}, bf16[2,4,48,768]{3,2,1,0:T(8,128)(2,1)}, u32[]{:S(2)}, u32[]{:S(2)}) collective-permute-start(bf16[2,4,48,768]{3,2,1,0:T(8,128)(2,1)} %fusion.3), channel_id=1, source_target_pairs={{0,2},{1,3},{2,0},{3,1},{4,6},{5,7},{6,4},{7,5},{8,10},{9,11},{10,... | collective-permute-start | bytes 1769480 | tf_op jit(solution)/shard_map/ppermute | solution.py:558
  252.2 29.8 %collective-permute-start.38 = (bf16[2,4,64,768]{3,2,1,0:T(8,128)(2,1)}, bf16[2,4,64,768]{3,2,1,0:T(8,128)(2,1)S(1)}, u32[]{:S(2)}, u32[]{:S(2)}) collective-permute-start(bf16[2,4,64,768]{3,2,1,0:T(8,128)(2,1)} %fusion.1), channel_id=1, source_target_pairs={{0,4},{1,5},{2,6},{3,7},{4,0},{5,1},{6,2},{7,3},{8,12},{9,13},{10,... | collective-permute-start | bytes 2359304 | tf_op jit(solution)/shard_map/ppermute | solution.py:558
  270.8 16.1 %collective-permute-start.41 = (bf16[3,96,768]{2,1,0:T(8,128)(2,1)S(1)}, bf16[3,96,768]{2,1,0:T(8,128)(2,1)S(1)}, u32[]{:S(2)}, u32[]{:S(2)}) collective-permute-start(bf16[3,96,768]{2,1,0:T(8,128)(2,1)S(1)} %bitcast.126), channel_id=1, source_target_pairs={{0,1},{1,0},{2,3},{3,2},{4,5},{5,4},{6,7},{7,6},{8,9},{9,8},{10,11... | collective-permute-start | bytes 1327112 | tf_op jit(solution)/shard_map/ppermute | solution.py:558
  294.8 14.6 %collective-permute-start.45 = (bf16[112,768]{1,0:T(8,128)(2,1)S(1)}, bf16[112,768]{1,0:T(8,128)(2,1)S(1)}, u32[]{:S(2)}, u32[]{:S(2)}) collective-permute-start(bf16[112,768]{1,0:T(8,128)(2,1)S(1)} %get-tuple-element.171), channel_id=1, source_target_pairs={{0,16},{1,17},{2,18},{3,19},{4,20},{5,21},{6,22},{7,23},{8,24},{9,... | collective-permute-start | bytes 516104 | tf_op jit(solution)/shard_map/ppermute | solution.py:558
  294.9 14.5 %collective-permute-start.44 = (bf16[112,768]{1,0:T(8,128)(2,1)S(1)}, bf16[112,768]{1,0:T(8,128)(2,1)S(1)}, u32[]{:S(2)}, u32[]{:S(2)}) collective-permute-start(bf16[112,768]{1,0:T(8,128)(2,1)S(1)} %get-tuple-element.172), channel_id=1, source_target_pairs={{0,8},{1,9},{2,10},{3,11},{4,12},{5,13},{6,14},{7,15},{8,16},{9,17... | collective-permute-start | bytes 516104 | tf_op jit(solution)/shard_map/ppermute | solution.py:558
  (73 other events, 646.6 us)
Sparse Core Ops, SparseCore 0:
  11.5 117.9 all-gather.2

commit v7 on v6

--- a/solution.py
+++ b/solution.py
@@ -690,28 +690,28 @@
     got_u = send(away_u, "y")
     dr1, low, datt, small_attn = norm_back_call(dr2, part, after(came, away_u), r1_m, w_attn, norms)
     rhs = attention_back(datt, q_m, qkv, pos, slopes, seqs)
-    got_d, got_g, got_u, rhs = lax.optimization_barrier((got_d, got_g, got_u, rhs))
+    got_d, rhs = lax.optimization_barrier((got_d, rhs))
     parts_d = line_parts(keep_d, got_d)
     line_d = line_send(parts_d)
     keep0, keep1, away0, away1 = attention_grads(where, x_flip, after(rhs, parts_d), att_m, low, small_attn, small_ffn)
-    away0, away1, line_d = lax.optimization_barrier((away0, away1, line_d))
+    away0, away1, line_d, got_g, got_u = lax.optimization_barrier((away0, away1, line_d, got_g, got_u))
     came0, came1 = send(away0, "c"), send(away1, "c")
     keep_gu, got_gu = jnp.concatenate([keep_g, keep_u], axis=1), jnp.concatenate([got_g, got_u], axis=1)
-    parts_gu = line_parts(keep_gu, after(got_gu, away0))
+    parts_gu = line_parts(keep_gu, got_gu)
     line_gu = line_send(parts_gu)
     g_down = send(line_add(keep_d, got_d, line_d), "down")
     away0, away1 = add(keep0[1], came0[1]).astype(LOW), add(keep1[1], came1[1]).astype(LOW)
     got0, got1 = send(away0, "x"), send(away1, "y")
     grad_in = input_grad(after(rhs, (away0, away1)), w_attn, dr1, positions)
-    g_down, line_gu, grad_in = lax.optimization_barrier((g_down, line_gu, grad_in))
-    g_ffn = jnp.concatenate([g_down, line_add(keep_gu, got_gu, line_gu)]).reshape(3, ROWS, D)
-    got0, got1 = after((got0, got1), g_ffn)
-    shared = share_dp(g_ffn)
+    got0, got1, grad_in = lax.optimization_barrier((got0, got1, grad_in))
     total0 = add(keep0[0], came0[0]) + got0.astype(F32)
     total1 = add(keep1[0], came1[0]) + got1.astype(F32)
-    got0 = send(total0[1].astype(LOW), "y")
-    got1 = send(total1[1].astype(LOW), "x")
-    got0, got1, shared = lax.optimization_barrier((got0, got1, shared))
+    away0, away1 = total0[1].astype(LOW), total1[1].astype(LOW)
+    got0, got1 = send(away0, "y"), send(away1, "x")
+    g_down, line_gu = after((g_down, line_gu), (away0, away1))
+    g_ffn = jnp.concatenate([g_down, line_add(keep_gu, got_gu, line_gu)]).reshape(3, ROWS, D)
+    shared = share_dp(g_ffn)
+    got0, got1 = after((got0, got1), g_ffn)
     total = jnp.concatenate([add(total0[0], got0), add(total1[0], got1)], axis=1)
     parts = [total[r].astype(LOW) for r in (1, 2, 3)]
     line_a = line_send(parts)

time: 327 us -> 308 us (0.942)
  waiting for transfers between devices: 141 us -> 120 us
    ppermute x50, waiting for transfers between devices: 111 us -> 89.3 us  [send(): return lax.ppermute(value, AXES, MOVES[move])]
  transfers between devices with their start and end apart: 51 -> 51, of which waited for: 23 -> 22; matrix products, arithmetic and copies ran while one was open for 5% -> 6% of each run, Pallas kernels for 23% -> 25%
where the time goes in v7:
time: 308 us
  waiting for transfers between devices  120 us (39%)
  Pallas kernels  102 us (33%)
  starting transfers between devices  43.9 us (14%)
  other arithmetic  14.8 us (5%)
  between operations  14.7 us (5%)
  local copies, waits for them, and re-layouts  12.3 us (4%)
    ppermute x50, waiting for transfers between devices, send(): return lax.ppermute(value, AXES, MOVES[move])  89.3 us
    ppermute x50, starting transfers between devices, send(): return lax.ppermute(value, AXES, MOVES[move])  43.9 us
    all_gather x1, waiting for transfers between devices, on_block(): lax.all_gather(ffn_piece, AXES, axis=0, tiled=False)  30.3 us
    pallas_call x1, Pallas kernels, attention_forward(): pl.pallas_call(functools.partial(attention_kernel, seqs, listed // seqs),...  18.1 us
    pallas_call x1, Pallas kernels, ffn_forward(): pl.pallas_call(functools.partial(ffn_kernel, seqs, listed // seqs), out_s...  17 us
    pallas_call x1, Pallas kernels, attention_back(): pl.pallas_call(functools.partial(attention_back_kernel, seqs, listed // s...  15.7 us
    pallas_call x3, Pallas kernels, weight_grad(): pl.pallas_call(weight_grad_kernel, out_shape=(out(shape, LOW), out(shape,...  11.6 us
    pallas_call x1, Pallas kernels, attention_grads(): pl.pallas_call(attention_grads_kernel, out_shape=(out((2, 2, LINE, half,...  8.83 us
  transfers between devices with their start and end apart: 51, of which 22 were waited for; matrix products, arithmetic and copies ran while one was open for 6% of the time, Pallas kernels for 25%

profile of v7, /device:TPU:0, one launch (start us, length us, event | category | flops | bytes accessed | tf_op | source)
XLA Modules:
  0.0 307.5 jit_solution(12927921749022665095)
XLA Ops:
  9.6 4.1 %collective-permute-start.1 = (bf16[104,768]{1,0:T(8,128)(2,1)S(1)}, bf16[104,768]{1,0:T(8,128)(2,1)S(1)}, u32[]{:S(2)}, u32[]{:S(2)}) collective-permute-start(bf16[104,768]{1,0:T(8,128)(2,1)S(1)} %get-tuple-element.168), channel_id=1, source_target_pairs={{0,16},{1,17},{2,18},{3,19},{4,20},{5,21},{6,22},{7,23},{8,24},{9,... | collective-permute-start | bytes 479240 | tf_op jit(solution)/shard_map/ppermute | solution.py:558
  18.7 6.9 %collective-permute-done.1 = bf16[104,768]{1,0:T(8,128)(2,1)S(1)} collective-permute-done((bf16[104,768]{1,0:T(8,128)(2,1)S(1)}, bf16[104,768]{1,0:T(8,128)(2,1)S(1)}, u32[]{:S(2)}, u32[]{:S(2)}) %collective-permute-start.1) | collective-permute-done | bytes 159776 | tf_op jit(solution)/shard_map/ppermute | solution.py:558
  31.4 6.8 %collective-permute-done.6.rest_5_ = bf16[4,56,768]{2,1,0:T(8,128)(2,1)S(1)} collective-permute-done((bf16[4,56,768]{2,1,0:T(8,128)(2,1)S(1)}, bf16[4,56,768]{2,1,0:T(8,128)(2,1)S(1)}, u32[]{:S(2)}, u32[]{:S(2)}) %collective-permute-start.6) | collective-permute-done | bytes 344096 | tf_op jit(solution)/shard_map/ppermute | solution.py:558
  42.5 4.0 %collective-permute-done.4.rest_2_ = bf16[4,48,768]{2,1,0:T(8,128)(2,1)} collective-permute-done((bf16[4,48,768]{2,1,0:T(8,128)(2,1)S(1)}, bf16[4,48,768]{2,1,0:T(8,128)(2,1)}, u32[]{:S(2)}, u32[]{:S(2)}) %collective-permute-start.4) | collective-permute-done | bytes 294944 | tf_op jit(solution)/shard_map/ppermute | solution.py:558
  50.8 5.4 %collective-permute-done.8.rest_7_ = bf16[4,56,768]{2,1,0:T(8,128)(2,1)S(1)} collective-permute-done((bf16[4,56,768]{2,1,0:T(8,128)(2,1)S(1)}, bf16[4,56,768]{2,1,0:T(8,128)(2,1)S(1)}, u32[]{:S(2)}, u32[]{:S(2)}) %collective-permute-start.8) | collective-permute-done | bytes 344096 | tf_op jit(solution)/shard_map/ppermute | solution.py:558
  56.8 6.1 %collective-permute-done.7.rest_6_ = bf16[4,48,768]{2,1,0:T(8,128)(2,1)} collective-permute-done((bf16[4,48,768]{2,1,0:T(8,128)(2,1)}, bf16[4,48,768]{2,1,0:T(8,128)(2,1)}, u32[]{:S(2)}, u32[]{:S(2)}) %collective-permute-start.7) | collective-permute-done | bytes 294944 | tf_op jit(solution)/shard_map/ppermute | solution.py:558
  65.8 18.1 %attention_forward.1 = (bf16[512,2304]{1,0:T(8,128)(2,1)}, f32[512,768]{1,0:T(8,128)}, bf16[128,768]{1,0:T(8,128)(2,1)}, bf16[128,768]{1,0:T(8,128)(2,1)}, bf16[...) custom-call(s32[5]{0:T(128)} %stack.83.where_ref, f32[12]{0:T(128)} %multiply_exponential_fusion.slope_ref, ...), custom_call_target="tpu_custom_call" | custom-call | bytes 60000000 | tf_op jit(solution)/shard_map/attention_forward/pallas_call | solution.py:164
  85.6 10.4 %collective-permute-done.18 = bf16[128,768]{1,0:T(8,128)(2,1)S(1)} collective-permute-done((bf16[128,768]{1,0:T(8,128)(2,1)}, bf16[128,768]{1,0:T(8,128)(2,1)S(1)}, u32[]{:S(2)}, u32[]{:S(2)}) %collective-permute-start.18) | collective-permute-done | bytes 196640 | tf_op jit(solution)/shard_map/ppermute | solution.py:558
  99.3 30.3 %all-gather.3.cloned.1.call-done = bf16[96,96,768]{2,1,0:T(8,128)(2,1)} async-done(((bf16[3,96,768]{2,1,0:T(8,128)(2,1)}), bf16[96,96,768]{2,1,0:T(8,128)(2,1)}) %all-gather.3.cloned.1.call-update) | async-done | bytes 14155792 | tf_op jit(solution)/shard_map/all_gather | solution.py:664
  129.6 17.0 %ffn_forward.1 = (bf16[512,768]{1,0:T(8,128)(2,1)}, f32[128,768]{1,0:T(8,128)}, bf16[128,768]{1,0:T(8,128)(2,1)}, f32[2,768]{1,0:T(2,128)}) custom-call(f32[512,768]{1,0:T(8,128)} %get-tuple-element.84.h1_ref, bf16[8,4,3,96,768]{4,3,2,1,0:T(8,128)(2,1)} %bitcast.114, bf16[8,4,3,96,768]{4,3,2,1,0:T(8,128)(2,1)} %bitcast.115, ...), custom_call_target="tpu_custom_call" | custom-call | bytes 48000000 | tf_op jit(solution)/shard_map/ffn_forward/pallas_call | solution.py:232
  147.2 6.6 %ffn_again.1 = (bf16[512,768]{1,0:T(8,128)(2,1)}, f32[512,768]{1,0:T(8,128)}, f32[512,768]{1,0:T(8,128)}) custom-call(s32[5]{0:T(128)} %stack.83.where_ref, bf16[4,128,768]{2,1,0:T(8,128)(2,1)} %pad_maximum_fusion.1.h_ref.a_ref, bf16[8,4,3,96,768]{4,3,2,1,0:T(8,128)(2,1)} %bitcast.117, bf16[8,4,3,96,768]{4,3,2,1,0:T(8,128)(2,1)} %bitcast.118), custom_call_target="tpu_custom_call" | custom-call | bytes 18000000 | tf_op jit(solution)/shard_map/ffn_again/pallas_call | solution.py:288
  156.4 7.5 %ffn_back.1 = (bf16[512,768]{1,0:T(8,128)(2,1)}, bf16[512,768]{1,0:T(8,128)(2,1)}, f32[2,128,768]{2,1,0:T(8,128)}, bf16[2,128,768]{2,1,0:T(8,128)(2,1)}) custom-call(s32[5]{0:T(128)} %stack.83.where_ref, bf16[4,128,768]{2,1,0:T(8,128)(2,1)} %pad_maximum_fusion.2.b_ref.e_ref, f32[512,768]{1,0:T(8,128)} %get-tuple-element.93.to_gate_ref, ...), custom_call_target="tpu_custom_call" | custom-call | bytes 21000000 | tf_op jit(solution)/shard_map/ffn_back/pallas_call | solution.py:323
  164.2 3.8 %weight_grad.3 = (bf16[4,96,768]{2,1,0:T(8,128)(2,1)}, bf16[4,96,768]{2,1,0:T(8,128)(2,1)}) custom-call(s32[5]{0:T(128)} %stack.83.where_ref, bf16[512,768]{1,0:T(8,128)(2,1)} %get-tuple-element.88.a_ref, bf16[4,128,768]{2,1,0:T(8,128)(2,1)} %pad_maximum_fusion.2.b_ref.e_ref), custom_call_target="tpu_custom_call" | custom-call | bytes 12000000 | tf_op jit(solution)/shard_map/weight_grad/pallas_call | solution.py:359
  171.1 3.8 %weight_grad.4 = (bf16[4,96,768]{2,1,0:T(8,128)(2,1)}, bf16[4,96,768]{2,1,0:T(8,128)(2,1)}) custom-call(s32[5]{0:T(128)} %stack.83.where_ref, bf16[4,128,768]{2,1,0:T(8,128)(2,1)} %pad_maximum_fusion.1.h_ref.a_ref, bf16[512,768]{1,0:T(8,128)(2,1)} %get-tuple-element.98.b_ref), custom_call_target="tpu_custom_call" | custom-call | bytes 12000000 | tf_op jit(solution)/shard_map/weight_grad/pallas_call | solution.py:359
  176.4 3.9 %weight_grad.5 = (bf16[4,96,768]{2,1,0:T(8,128)(2,1)}, bf16[4,96,768]{2,1,0:T(8,128)(2,1)}) custom-call(s32[5]{0:T(128)} %stack.83.where_ref, bf16[4,128,768]{2,1,0:T(8,128)(2,1)} %pad_maximum_fusion.1.h_ref.a_ref, bf16[512,768]{1,0:T(8,128)(2,1)} %get-tuple-element.101.b_ref), custom_call_target="tpu_custom_call" | custom-call | bytes 12000000 | tf_op jit(solution)/shard_map/weight_grad/pallas_call | solution.py:359
  184.9 15.7 %attention_back.1.rhs_ref = bf16[512,2304]{1,0:T(8,128)(2,1)} custom-call(f32[12]{0:T(128)} %multiply_exponential_fusion.slope_ref, bf16[128,768]{1,0:T(8,128)(2,1)} %get-tuple-element.106.datt_ref, bf16[128,768]{1,0:T(8,128)(2,1)} %get-tuple-element.107.q_ref, bf16[512,2304]{1,0:T(8,128)(2,1)} %get-tuple-element.108.qkv_ref, s32[128,1]{1,0:T(8,128)} %reshape.129.pos_ref), custom_call_target="tpu_custom_call" | custom-call | bytes 45000000 | tf_op jit(solution)/shard_map/attention_back/pallas_call | solution.py:440
  204.4 8.8 %attention_grads.1 = (bf16[2,2,4,48,768]{4,3,2,1,0:T(8,128)(2,1)}, bf16[2,2,4,64,768]{4,3,2,1,0:T(8,128)(2,1)}, bf16[2,2,4,48,768]{4,3,2,1,0:T(8,128)(2,1)}, bf16[2,2,4,64,768]{4,3,2,1,0:T(8,128)(2,1)}) custom-call(s32[5]{0:T(128)} %stack.83.where_ref, bf16[768,512]{1,0:T(8,128)(2,1)} %bitcast.122, bf16[512,2304]{1,0:T(8,128)(2,1)} %attention_back.1.rhs_ref, ...), custom_call_target="tpu_custom_call" | custom-call | bytes 30000000 | tf_op jit(solution)/shard_map/attention_grads/pallas_call | solution.py:491
  228.9 4.5 %collective-permute-start.40 = (bf16[192,768]{1,0:T(8,128)(2,1)}, bf16[192,768]{1,0:T(8,128)(2,1)}, u32[]{:S(2)}, u32[]{:S(2)}) collective-permute-start(bf16[192,768]{1,0:T(8,128)(2,1)} %get-tuple-element.152), channel_id=1, source_target_pairs={{0,24},{1,25},{2,26},{3,27},{4,28},{5,29},{6,30},{7,31},{8,0},{9,1... | collective-permute-start | bytes 884744 | tf_op jit(solution)/shard_map/ppermute | solution.py:558
  233.4 8.1 %input_grad.1 = f32[512,768]{1,0:T(8,128)} custom-call(bf16[512,2304]{1,0:T(8,128)(2,1)} %attention_back.1.rhs_ref, bf16[8,4,96,768]{3,2,1,0:T(8,128)(2,1)} %get-tuple-element.105.w_ref, f32[128,768]{1,0:T(8,128)} %get-tuple-element.124.dr1_ref, s32[4,32]{1,0:T(4,128)} %pos_ref.1), custom_call_target="tpu_custom_call" | custom-call | bytes 24000000 | tf_op jit(solution)/shard_map/input_grad/pallas_call | solution.py:521
  248.3 14.2 %collective-permute-done.39 = bf16[192,768]{1,0:T(8,128)(2,1)} collective-permute-done((bf16[192,768]{1,0:T(8,128)(2,1)}, bf16[192,768]{1,0:T(8,128)(2,1)}, u32[]{:S(2)}, u32[]{:S(2)}) %collective-permute-start.39) | collective-permute-done | bytes 294944 | tf_op jit(solution)/shard_map/ppermute | solution.py:558
  264.6 10.4 %collective-permute-done.45.rest_2_ = bf16[3,96,768]{2,1,0:T(8,128)(2,1)S(1)} collective-permute-done((bf16[3,96,768]{2,1,0:T(8,128)(2,1)S(1)}, bf16[3,96,768]{2,1,0:T(8,128)(2,1)S(1)}, u32[]{:S(2)}, u32[]{:S(2)}) %collective-permute-start.45) | collective-permute-done | bytes 442400 | tf_op jit(solution)/shard_map/ppermute | solution.py:558
  279.4 3.4 %finish_ffn.1 = (f32[384,768]{1,0:T(8,128)}, f32[96,6144]{1,0:T(8,128)}) custom-call(s32[5]{0:T(128)} %stack.83.where_ref, bf16[3,96,768]{2,1,0:T(8,128)(2,1)} %bitcast.127, bf16[3,96,768]{2,1,0:T(8,128)(2,1)} %copy-done.22, bf16[3,96,768]{2,1,0:T(8,128)(2,1)} %copy-done.21, bf16[3,96,768]{2,1,0:T(8,128)(2,1)} %copy-done.23), custom_call_target="tpu_custom_call" | custom-call | bytes 12000000 | tf_op jit(solution)/shard_map/finish_ffn/pallas_call | solution.py:607
  283.3 7.6 %collective-permute-done.42 = bf16[112,768]{1,0:T(8,128)(2,1)S(1)} collective-permute-done((bf16[112,768]{1,0:T(8,128)(2,1)S(1)}, bf16[112,768]{1,0:T(8,128)(2,1)S(1)}, u32[]{:S(2)}, u32[]{:S(2)}) %collective-permute-start.42) | collective-permute-done | bytes 172064 | tf_op jit(solution)/shard_map/ppermute | solution.py:558
  292.6 3.8 %collective-permute-done.48.rest_2_ = bf16[96,768]{1,0:T(8,128)(2,1)S(1)} collective-permute-done((bf16[96,768]{1,0:T(8,128)(2,1)S(1)}, bf16[96,768]{1,0:T(8,128)(2,1)S(1)}, u32[]{:S(2)}, u32[]{:S(2)}) %collective-permute-start.48) | collective-permute-done | bytes 147488 | tf_op jit(solution)/shard_map/ppermute | solution.py:558
  (247 shorter events, 81.6 us)
Async XLA Ops:
  7.2 122.3 %all-gather.3.cloned.1.call-start = ((), (), s32[]{:S(2)}) async-start(), calls=%async_computation | async-start | bytes 14598144 | tf_op jit(solution)/shard_map/all_gather | solution.py:664
  9.6 16.0 %collective-permute-start.1 = (bf16[104,768]{1,0:T(8,128)(2,1)S(1)}, bf16[104,768]{1,0:T(8,128)(2,1)S(1)}, u32[]{:S(2)}, u32[]{:S(2)}) collective-permute-start(bf16[104,768]{1,0:T(8,128)(2,1)S(1)} %get-tuple-element.168), channel_id=1, source_target_pairs={{0,16},{1,17},{2,18},{3,19},{4,20},{5,21},{6,22},{7,23},{8,24},{9,... | collective-permute-start | bytes 479240 | tf_op jit(solution)/shard_map/ppermute | solution.py:558
  29.0 13.5 %collective-permute-start.5 = (bf16[4,48,768]{2,1,0:T(8,128)(2,1)S(1)}, bf16[4,48,768]{2,1,0:T(8,128)(2,1)}, u32[]{:S(2)}, u32[]{:S(2)}) collective-permute-start(bf16[4,48,768]{2,1,0:T(8,128)(2,1)S(1)} %slice.145.rest_0_), channel_id=1, source_target_pairs={{0,2},{1,3},{2,0},{3,1},{4,6},{5,7},{6,4},{7,5},{8,10},{9,11},{10,... | collective-permute-start | bytes 884744 | tf_op jit(solution)/shard_map/ppermute | solution.py:558
  29.4 17.1 %collective-permute-start.3 = (bf16[4,56,768]{2,1,0:T(8,128)(2,1)S(1)}, bf16[4,56,768]{2,1,0:T(8,128)(2,1)S(1)}, u32[]{:S(2)}, u32[]{:S(2)}) collective-permute-start(bf16[4,56,768]{2,1,0:T(8,128)(2,1)S(1)} %slice.143.rest_1_), channel_id=1, source_target_pairs={{0,4},{1,5},{2,6},{3,7},{4,0},{5,1},{6,2},{7,3},{8,12},{9,13},{10,... | collective-permute-start | bytes 1032200 | tf_op jit(solution)/shard_map/ppermute | solution.py:558
  31.2 15.3 %collective-permute-start.4 = (bf16[4,48,768]{2,1,0:T(8,128)(2,1)S(1)}, bf16[4,48,768]{2,1,0:T(8,128)(2,1)}, u32[]{:S(2)}, u32[]{:S(2)}) collective-permute-start(bf16[4,48,768]{2,1,0:T(8,128)(2,1)S(1)} %slice.145.rest_0_), channel_id=1, source_target_pairs={{0,4},{1,5},{2,6},{3,7},{4,0},{5,1},{6,2},{7,3},{8,12},{9,13},{10,... | collective-permute-start | bytes 884744 | tf_op jit(solution)/shard_map/ppermute | solution.py:558
  31.4 19.2 %collective-permute-start.10 = (bf16[4,56,768]{2,1,0:T(8,128)(2,1)S(1)}, bf16[4,56,768]{2,1,0:T(8,128)(2,1)S(1)}, u32[]{:S(2)}, u32[]{:S(2)}) collective-permute-start(bf16[4,56,768]{2,1,0:T(8,128)(2,1)S(1)} %slice.143.rest_1_), channel_id=1, source_target_pairs={{0,1},{1,0},{2,3},{3,2},{4,5},{5,4},{6,7},{7,6},{8,9},{9,8},{10,11... | collective-permute-start | bytes 1032200 | tf_op jit(solution)/shard_map/ppermute | solution.py:558
  38.2 18.0 %collective-permute-start.8 = (bf16[4,56,768]{2,1,0:T(8,128)(2,1)S(1)}, bf16[4,56,768]{2,1,0:T(8,128)(2,1)S(1)}, u32[]{:S(2)}, u32[]{:S(2)}) collective-permute-start(bf16[4,56,768]{2,1,0:T(8,128)(2,1)S(1)} %collective-permute-done.6.rest_5_), channel_id=1, source_target_pairs={{0,4},{1,5},{2,6},{3,7},{4,0},{5,1},{6,2},{7,3},{8,12},{9,13},{10,... | collective-permute-start | bytes 1032200 | tf_op jit(solution)/shard_map/ppermute | solution.py:558
  46.5 16.4 %collective-permute-start.7 = (bf16[4,48,768]{2,1,0:T(8,128)(2,1)}, bf16[4,48,768]{2,1,0:T(8,128)(2,1)}, u32[]{:S(2)}, u32[]{:S(2)}) collective-permute-start(bf16[4,48,768]{2,1,0:T(8,128)(2,1)} %collective-permute-done.4.rest_2_), channel_id=1, source_target_pairs={{0,2},{1,3},{2,0},{3,1},{4,6},{5,7},{6,4},{7,5},{8,10},{9,11},{10,... | collective-permute-start | bytes 884744 | tf_op jit(solution)/shard_map/ppermute | solution.py:558
  49.8 14.3 %collective-permute-start.14 = (bf16[4,56,768]{2,1,0:T(8,128)(2,1)S(1)}, bf16[4,56,768]{2,1,0:T(8,128)(2,1)S(1)}, u32[]{:S(2)}, u32[]{:S(2)}) collective-permute-start(bf16[4,56,768]{2,1,0:T(8,128)(2,1)S(1)} %collective-permute-done.6.rest_5_), channel_id=1, source_target_pairs={{0,1},{1,0},{2,3},{3,2},{4,5},{5,4},{6,7},{7,6},{8,9},{9,8},{10,11... | collective-permute-start | bytes 1032200 | tf_op jit(solution)/shard_map/ppermute | solution.py:558
  50.6 13.5 %collective-permute-start.12 = (bf16[4,56,768]{2,1,0:T(8,128)(2,1)S(1)}, bf16[4,56,768]{2,1,0:T(8,128)(2,1)S(1)}, u32[]{:S(2)}, u32[]{:S(2)}) collective-permute-start(bf16[4,56,768]{2,1,0:T(8,128)(2,1)S(1)} %collective-permute-done.3.rest_3_), channel_id=1, source_target_pairs={{0,1},{1,0},{2,3},{3,2},{4,5},{5,4},{6,7},{7,6},{8,9},{9,8},{10,11... | collective-permute-start | bytes 1032200 | tf_op jit(solution)/shard_map/ppermute | solution.py:558
  168.0 32.5 %collective-permute-start.23 = (bf16[4,96,768]{2,1,0:T(8,128)(2,1)}, bf16[4,96,768]{2,1,0:T(8,128)(2,1)S(1)}, u32[]{:S(2)}, u32[]{:S(2)}) collective-permute-start(bf16[4,96,768]{2,1,0:T(8,128)(2,1)} %get-tuple-element.91), channel_id=1, source_target_pairs={{0,4},{1,5},{2,6},{3,7},{4,0},{5,1},{6,2},{7,3},{8,12},{9,13},{10,... | collective-permute-start | bytes 1769480 | tf_op jit(solution)/shard_map/ppermute | solution.py:558
  175.0 40.8 %collective-permute-start.29 = (bf16[4,96,768]{2,1,0:T(8,128)(2,1)}, bf16[4,96,768]{2,1,0:T(8,128)(2,1)S(1)}, u32[]{:S(2)}, u32[]{:S(2)}) collective-permute-start(bf16[4,96,768]{2,1,0:T(8,128)(2,1)} %get-tuple-element.99), channel_id=1, source_target_pairs={{0,4},{1,5},{2,6},{3,7},{4,0},{5,1},{6,2},{7,3},{8,12},{9,13},{10,... | collective-permute-start | bytes 1769480 | tf_op jit(solution)/shard_map/ppermute | solution.py:558
  180.3 35.5 %collective-permute-start.30 = (bf16[4,96,768]{2,1,0:T(8,128)(2,1)}, bf16[4,96,768]{2,1,0:T(8,128)(2,1)S(1)}, u32[]{:S(2)}, u32[]{:S(2)}) collective-permute-start(bf16[4,96,768]{2,1,0:T(8,128)(2,1)} %get-tuple-element.102), channel_id=1, source_target_pairs={{0,4},{1,5},{2,6},{3,7},{4,0},{5,1},{6,2},{7,3},{8,12},{9,13},{10,... | collective-permute-start | bytes 1769480 | tf_op jit(solution)/shard_map/ppermute | solution.py:558
  220.9 21.5 %collective-permute-start.34 = (bf16[2,4,64,768]{3,2,1,0:T(8,128)(2,1)}, bf16[2,4,64,768]{3,2,1,0:T(8,128)(2,1)}, u32[]{:S(2)}, u32[]{:S(2)}) collective-permute-start(bf16[2,4,64,768]{3,2,1,0:T(8,128)(2,1)} %fusion.1), channel_id=1, source_target_pairs={{0,4},{1,5},{2,6},{3,7},{4,0},{5,1},{6,2},{7,3},{8,12},{9,13},{10,... | collective-permute-start | bytes 2359304 | tf_op jit(solution)/shard_map/ppermute | solution.py:558
  223.1 18.4 %collective-permute-start.32 = (bf16[2,4,48,768]{3,2,1,0:T(8,128)(2,1)}, bf16[2,4,48,768]{3,2,1,0:T(8,128)(2,1)}, u32[]{:S(2)}, u32[]{:S(2)}) collective-permute-start(bf16[2,4,48,768]{3,2,1,0:T(8,128)(2,1)} %fusion.3), channel_id=1, source_target_pairs={{0,2},{1,3},{2,0},{3,1},{4,6},{5,7},{6,4},{7,5},{8,10},{9,11},{10,... | collective-permute-start | bytes 1769480 | tf_op jit(solution)/shard_map/ppermute | solution.py:558
  226.2 20.6 %collective-permute-start.37 = (bf16[96,768]{1,0:T(8,128)(2,1)}, bf16[96,768]{1,0:T(8,128)(2,1)S(1)}, u32[]{:S(2)}, u32[]{:S(2)}) collective-permute-start(bf16[96,768]{1,0:T(8,128)(2,1)} %fusion.20), channel_id=1, source_target_pairs={{0,0},{1,8},{2,16},{3,24},{4,1},{5,9},{6,17},{7,25},{8,2},{9,10},{... | collective-permute-start | bytes 442376 | tf_op jit(solution)/shard_map/ppermute | solution.py:558
  228.9 19.5 %collective-permute-start.40 = (bf16[192,768]{1,0:T(8,128)(2,1)}, bf16[192,768]{1,0:T(8,128)(2,1)}, u32[]{:S(2)}, u32[]{:S(2)}) collective-permute-start(bf16[192,768]{1,0:T(8,128)(2,1)} %get-tuple-element.152), channel_id=1, source_target_pairs={{0,24},{1,25},{2,26},{3,27},{4,28},{5,29},{6,30},{7,31},{8,0},{9,1... | collective-permute-start | bytes 884744 | tf_op jit(solution)/shard_map/ppermute | solution.py:558
  233.4 29.2 %collective-permute-start.39 = (bf16[192,768]{1,0:T(8,128)(2,1)}, bf16[192,768]{1,0:T(8,128)(2,1)}, u32[]{:S(2)}, u32[]{:S(2)}) collective-permute-start(bf16[192,768]{1,0:T(8,128)(2,1)} %get-tuple-element.153), channel_id=1, source_target_pairs={{0,16},{1,17},{2,18},{3,19},{4,20},{5,21},{6,22},{7,23},{8,24},{9,... | collective-permute-start | bytes 884744 | tf_op jit(solution)/shard_map/ppermute | solution.py:558
  241.5 21.1 %collective-permute-start.38 = (bf16[192,768]{1,0:T(8,128)(2,1)}, bf16[192,768]{1,0:T(8,128)(2,1)S(1)}, u32[]{:S(2)}, u32[]{:S(2)}) collective-permute-start(bf16[192,768]{1,0:T(8,128)(2,1)} %get-tuple-element.154), channel_id=1, source_target_pairs={{0,8},{1,9},{2,10},{3,11},{4,12},{5,13},{6,14},{7,15},{8,16},{9,17... | collective-permute-start | bytes 884744 | tf_op jit(solution)/shard_map/ppermute | solution.py:558
  244.3 19.7 %collective-permute-start.36 = (bf16[4,64,768]{2,1,0:T(8,128)(2,1)S(1)}, bf16[4,64,768]{2,1,0:T(8,128)(2,1)S(1)}, u32[]{:S(2)}, u32[]{:S(2)}) collective-permute-start(bf16[4,64,768]{2,1,0:T(8,128)(2,1)S(1)} %fusion.8), channel_id=1, source_target_pairs={{0,2},{1,3},{2,0},{3,1},{4,6},{5,7},{6,4},{7,5},{8,10},{9,11},{10,... | collective-permute-start | bytes 1179656 | tf_op jit(solution)/shard_map/ppermute | solution.py:558
  246.8 17.2 %collective-permute-start.35 = (bf16[4,48,768]{2,1,0:T(8,128)(2,1)S(1)}, bf16[4,48,768]{2,1,0:T(8,128)(2,1)S(1)}, u32[]{:S(2)}, u32[]{:S(2)}) collective-permute-start(bf16[4,48,768]{2,1,0:T(8,128)(2,1)S(1)} %fusion.17), channel_id=1, source_target_pairs={{0,4},{1,5},{2,6},{3,7},{4,0},{5,1},{6,2},{7,3},{8,12},{9,13},{10,... | collective-permute-start | bytes 884744 | tf_op jit(solution)/shard_map/ppermute | solution.py:558
  264.0 13.9 %collective-permute-start.44 = (bf16[3,96,768]{2,1,0:T(8,128)(2,1)S(1)}, bf16[3,96,768]{2,1,0:T(8,128)(2,1)S(1)}, u32[]{:S(2)}, u32[]{:S(2)}) collective-permute-start(bf16[3,96,768]{2,1,0:T(8,128)(2,1)S(1)} %bitcast.126), channel_id=1, source_target_pairs={{0,1},{1,0},{2,3},{3,2},{4,5},{5,4},{6,7},{7,6},{8,9},{9,8},{10,11... | collective-permute-start | bytes 1327112 | tf_op jit(solution)/shard_map/ppermute | solution.py:558
  275.8 15.1 %collective-permute-start.42 = (bf16[112,768]{1,0:T(8,128)(2,1)S(1)}, bf16[112,768]{1,0:T(8,128)(2,1)S(1)}, u32[]{:S(2)}, u32[]{:S(2)}) collective-permute-start(bf16[112,768]{1,0:T(8,128)(2,1)S(1)} %get-tuple-element.161), channel_id=1, source_target_pairs={{0,16},{1,17},{2,18},{3,19},{4,20},{5,21},{6,22},{7,23},{8,24},{9,... | collective-permute-start | bytes 516104 | tf_op jit(solution)/shard_map/ppermute | solution.py:558
  275.8 15.1 %collective-permute-start.41 = (bf16[112,768]{1,0:T(8,128)(2,1)S(1)}, bf16[112,768]{1,0:T(8,128)(2,1)S(1)}, u32[]{:S(2)}, u32[]{:S(2)}) collective-permute-start(bf16[112,768]{1,0:T(8,128)(2,1)S(1)} %get-tuple-element.162), channel_id=1, source_target_pairs={{0,8},{1,9},{2,10},{3,11},{4,12},{5,13},{6,14},{7,15},{8,16},{9,17... | collective-permute-start | bytes 516104 | tf_op jit(solution)/shard_map/ppermute | solution.py:558
  (77 other events, 561.0 us)
Sparse Core Ops, SparseCore 0:
  11.5 117.9 all-gather.2

commit v8 on v7

--- a/solution.py
+++ b/solution.py
@@ -398,7 +398,7 @@
     )(dr2, part, came, r1_m, w_attn, norms)
 
 
-def attention_back_kernel(seqs, most, slope_ref, datt_ref, q_ref, qkv_ref, pos_ref, rhs_ref, away_ref, hot_ref):
+def attention_back_kernel(seqs, most, chosen, slope_ref, datt_ref, q_ref, qkv_ref, pos_ref, rhs_ref, away_ref, hot_ref):
     length = qkv_ref.shape[0] // seqs
     listed = seqs * most
     first_m = lax.broadcasted_iota(jnp.int32, (most, 128), 1) < HEAD_DIM
@@ -413,8 +413,9 @@
     @pl.loop(0, HEADS // 2)
     def _(t):
         lane = pl.multiple_of(t * 128, 128)
-        for s in range(seqs):
+        for n, s in enumerate(chosen):
             rows = slice(s * length, (s + 1) * length)
+            placed = slice(n * length, (n + 1) * length)
             mine = slice(s * most, (s + 1) * most)
             away = away_ref[mine, :]
             q = both(q_ref[mine, pl.ds(lane, 128)])
@@ -429,27 +430,27 @@
             ds = (p * (dp - jnp.sum(dp * p, axis=-1, keepdims=True))).astype(LOW)
             dq = mm(ds, k)
             dq = (jnp.where(first_m, dq[:most], dq[most:]) * SCALE).astype(LOW)
-            rhs_ref[rows, pl.ds(lane, 128)] = mm_tn(hot_ref[mine, :], dq).astype(LOW)
-            rhs_ref[rows, pl.ds(D + lane, 128)] = (mm_tn(ds, q) * SCALE).astype(LOW)
-            rhs_ref[rows, pl.ds(2 * D + lane, 128)] = mm_tn(p.astype(LOW), da).astype(LOW)
-
-
-def attention_back(datt, q_m, qkv, pos, slopes, seqs):
+            rhs_ref[placed, pl.ds(lane, 128)] = mm_tn(hot_ref[mine, :], dq).astype(LOW)
+            rhs_ref[placed, pl.ds(D + lane, 128)] = (mm_tn(ds, q) * SCALE).astype(LOW)
+            rhs_ref[placed, pl.ds(2 * D + lane, 128)] = mm_tn(p.astype(LOW), da).astype(LOW)
+
+
+def attention_back(datt, q_m, qkv, pos, slopes, seqs, chosen):
     tokens = qkv.shape[0]
     listed = pos.shape[0]
     return pl.pallas_call(
-        functools.partial(attention_back_kernel, seqs, listed // seqs),
-        out_shape=out((tokens, 3 * D), LOW),
+        functools.partial(attention_back_kernel, seqs, listed // seqs, chosen),
+        out_shape=out((tokens // seqs * len(chosen), 3 * D), LOW),
         in_specs=[SMEM] + [VMEM] * 4,
         out_specs=VMEM,
         scratch_shapes=[pltpu.VMEM((listed, tokens // seqs), F32), pltpu.VMEM((listed, tokens // seqs), LOW)],
         compiler_params=BIG,
-        cost_estimate=cost(15),
+        cost_estimate=cost(8),
         name="attention_back",
     )(slopes, datt, q_m, qkv, pos)
 
 
-def attention_grads_kernel(where_ref, flip_ref, rhs_ref, att_ref, low_ref, small_attn_ref, small_ffn_ref, keep0_ref, keep1_ref, away0_ref, away1_ref, full_ref, tail_ref):
+def attention_grads_kernel(where_ref, flip_ref, rhs0_ref, rhs1_ref, att_ref, low_ref, small_attn_ref, small_ffn_ref, keep0_ref, keep1_ref, away0_ref, away1_ref, full_ref, tail_ref):
     z, y, mine = where_ref[0], where_ref[1], where_ref[4]
     half = ROWS // 2
     step = 256
@@ -474,7 +475,8 @@
                 def _(n):
                     lane = pl.multiple_of(n * step, step)
                     cols = pl.ds(pl.multiple_of(j * D + n * step, step), step)
-                    full_ref[:, pl.ds(lane, step)] = mm(flip_ref[...], rhs_ref[:, cols])
+                    first = rhs0_ref.shape[0]
+                    full_ref[:, pl.ds(lane, step)] = mm(flip_ref[:, :first], rhs0_ref[:, cols]) + mm(flip_ref[:, first:], rhs1_ref[:, cols])
 
             for rz in range(LINE):
                 base = 2 * lax.rem(z + rz, LINE)
@@ -486,47 +488,49 @@
                     cut1_ref[ry, rx, rz, half:] = tail_ref[shard]
 
 
-def attention_grads(where, x_flip, rhs, att_m, low, small_attn, small_ffn):
+def attention_grads(where, x_flip, rhs0, rhs1, att_m, low, small_attn, small_ffn):
     half = ROWS // 2
     return pl.pallas_call(
         attention_grads_kernel,
         out_shape=(out((2, 2, LINE, half, D), LOW), out((2, 2, LINE, half + TAIL, D), LOW)) * 2,
-        in_specs=[SMEM] + [VMEM] * 6,
+        in_specs=[SMEM] + [VMEM] * 7,
         out_specs=(VMEM,) * 4,
         scratch_shapes=[pltpu.VMEM((D, D), F32), pltpu.VMEM((SHARDS, TAIL, D), LOW)],
         compiler_params=BIG,
         cost_estimate=cost(10),
         name="attention_grads",
-    )(where, x_flip, rhs, att_m, low, small_attn, small_ffn)
-
-
-def input_grad_kernel(seqs, rhs_ref, w_ref, dr1_ref, pos_ref, out_ref):
+    )(where, x_flip, rhs0, rhs1, att_m, low, small_attn, small_ffn)
+
+
+def input_grad_kernel(seqs, rhs0_ref, rhs1_ref, w_ref, dr1_ref, pos_ref, out_ref):
     length = out_ref.shape[0] // seqs
     most = dr1_ref.shape[0] // seqs
     for n in range(2):
         lanes = slice(n * D // 2, (n + 1) * D // 2)
         shards = slice(n * SHARDS // 2, (n + 1) * SHARDS // 2)
-        total = mm_nt(rhs_ref[:, 0:D], block(w_ref, shards, 0))
-        total += mm_nt(rhs_ref[:, D : 2 * D], block(w_ref, shards, 1))
-        total += mm_nt(rhs_ref[:, 2 * D : 3 * D], block(w_ref, shards, 2))
-        for s in range(seqs):
-            rows = slice(s * length, (s + 1) * length)
-            hot = (lax.broadcasted_iota(jnp.int32, (length, most), 0) == pos_ref[s : s + 1, :]).astype(F32)
-            spread = jnp.dot(hot, dr1_ref[s * most : (s + 1) * most, lanes], precision=EXACT, preferred_element_type=F32)
-            out_ref[rows, lanes] = total[rows] + spread
-
-
-def input_grad(rhs, w_attn, dr1, positions):
-    tokens = rhs.shape[0]
+        s = 0
+        for rhs_ref in (rhs0_ref, rhs1_ref):
+            total = mm_nt(rhs_ref[:, 0:D], block(w_ref, shards, 0))
+            total += mm_nt(rhs_ref[:, D : 2 * D], block(w_ref, shards, 1))
+            total += mm_nt(rhs_ref[:, 2 * D : 3 * D], block(w_ref, shards, 2))
+            for m in range(rhs_ref.shape[0] // length):
+                hot = (lax.broadcasted_iota(jnp.int32, (length, most), 0) == pos_ref[s : s + 1, :]).astype(F32)
+                spread = jnp.dot(hot, dr1_ref[s * most : (s + 1) * most, lanes], precision=EXACT, preferred_element_type=F32)
+                out_ref[s * length : (s + 1) * length, lanes] = total[m * length : (m + 1) * length] + spread
+                s += 1
+
+
+def input_grad(rhs0, rhs1, w_attn, dr1, positions):
+    tokens = rhs0.shape[0] + rhs1.shape[0]
     return pl.pallas_call(
         functools.partial(input_grad_kernel, positions.shape[0]),
         out_shape=out((tokens, D), F32),
-        in_specs=[VMEM] * 4,
+        in_specs=[VMEM] * 5,
         out_specs=VMEM,
         compiler_params=BIG,
         cost_estimate=cost(8),
         name="input_grad",
-    )(rhs, w_attn, dr1, positions)
+    )(rhs0, rhs1, w_attn, dr1, positions)
 
 
 def place(z, y, x, c):
@@ -689,37 +693,44 @@
     keep_u, away_u = weight_grad(where, after(h_all, (away_g, came)), dup)
     got_u = send(away_u, "y")
     dr1, low, datt, small_attn = norm_back_call(dr2, part, after(came, away_u), r1_m, w_attn, norms)
-    rhs = attention_back(datt, q_m, qkv, pos, slopes, seqs)
-    got_d, rhs = lax.optimization_barrier((got_d, rhs))
+    half = seqs // 2
+    rhs0 = attention_back(datt, q_m, qkv, pos, slopes, seqs, tuple(range(half)))
+    got_d, rhs0 = lax.optimization_barrier((got_d, rhs0))
     parts_d = line_parts(keep_d, got_d)
     line_d = line_send(parts_d)
-    keep0, keep1, away0, away1 = attention_grads(where, x_flip, after(rhs, parts_d), att_m, low, small_attn, small_ffn)
-    away0, away1, line_d, got_g, got_u = lax.optimization_barrier((away0, away1, line_d, got_g, got_u))
+    rhs1 = attention_back(after(datt, (rhs0, parts_d)), q_m, qkv, pos, slopes, seqs, tuple(range(half, seqs)))
+    line_d, got_g, rhs1 = lax.optimization_barrier((line_d, got_g, rhs1))
+    parts_g = line_parts(keep_g, got_g)
+    line_g = line_send(parts_g)
+    keep0, keep1, away0, away1 = attention_grads(where, x_flip, rhs0, after(rhs1, parts_g), att_m, low, small_attn, small_ffn)
+    away0, away1, line_g, got_u = lax.optimization_barrier((away0, away1, line_g, got_u))
     came0, came1 = send(away0, "c"), send(away1, "c")
-    keep_gu, got_gu = jnp.concatenate([keep_g, keep_u], axis=1), jnp.concatenate([got_g, got_u], axis=1)
-    parts_gu = line_parts(keep_gu, got_gu)
-    line_gu = line_send(parts_gu)
+    parts_u = line_parts(keep_u, got_u)
+    line_u = line_send(parts_u)
     g_down = send(line_add(keep_d, got_d, line_d), "down")
     away0, away1 = add(keep0[1], came0[1]).astype(LOW), add(keep1[1], came1[1]).astype(LOW)
     got0, got1 = send(away0, "x"), send(away1, "y")
-    grad_in = input_grad(after(rhs, (away0, away1)), w_attn, dr1, positions)
+    grad_in = input_grad(rhs0, after(rhs1, (away0, away1)), w_attn, dr1, positions)
     got0, got1, grad_in = lax.optimization_barrier((got0, got1, grad_in))
     total0 = add(keep0[0], came0[0]) + got0.astype(F32)
     total1 = add(keep1[0], came1[0]) + got1.astype(F32)
     away0, away1 = total0[1].astype(LOW), total1[1].astype(LOW)
     got0, got1 = send(away0, "y"), send(away1, "x")
-    g_down, line_gu = after((g_down, line_gu), (away0, away1))
-    g_ffn = jnp.concatenate([g_down, line_add(keep_gu, got_gu, line_gu)]).reshape(3, ROWS, D)
-    shared = share_dp(g_ffn)
+    g_down, line_u = after((g_down, line_u), (away0, away1))
+    g_ffn = jnp.stack([g_down, line_add(keep_g, got_g, line_g), line_add(keep_u, got_u, line_u)])
     got0, got1 = after((got0, got1), g_ffn)
     total = jnp.concatenate([add(total0[0], got0), add(total1[0], got1)], axis=1)
     parts = [total[r].astype(LOW) for r in (1, 2, 3)]
     line_a = line_send(parts)
-    grad_down, grad_up = finish_ffn(where, after(shared, parts))
-    line_a = after(line_a, grad_down)
-    g_attn = (total[0] + line_a[0].astype(F32) + line_a[1].astype(F32) + line_a[2].astype(F32))
+    other = send(g_ffn, "x")
+    line_a, other = lax.optimization_barrier((line_a, other))
+    g_attn = total[0] + line_a[0].astype(F32) + line_a[1].astype(F32) + line_a[2].astype(F32)
     small = g_attn[ROWS : ROWS + 4, :ROWS]
-    grad_qkv, grad_out = finish_attention(where, share_dp(g_attn[:ROWS].astype(LOW)))
+    g_attn = g_attn[:ROWS].astype(LOW)
+    shared = (g_ffn, send(g_ffn, "c"), other, send(other, "c"))
+    grad_down, grad_up = finish_ffn(where, after(shared, g_attn))
+    other = after(send(g_attn, "x"), grad_down)
+    grad_qkv, grad_out = finish_attention(where, (g_attn, send(g_attn, "c"), other, send(other, "c")))
     return (
         layer_out.reshape(seqs, length, width),
         grad_in.reshape(seqs, length, width),

time: 308 us -> 299 us (0.971)
  waiting for transfers between devices: 120 us -> 100 us
  starting transfers between devices: 43.9 us -> 49.9 us
  Pallas kernels: 102 us -> 107 us
    ppermute x50 -> x53, waiting for transfers between devices: 89.3 us -> 69.9 us  [send(): return lax.ppermute(value, AXES, MOVES[move])]
    ppermute x50 -> x53, starting transfers between devices: 43.9 us -> 49.8 us  [send(): return lax.ppermute(value, AXES, MOVES[move])]
    pallas_call x1 -> x2, Pallas kernels: 15.7 us -> 19.9 us  [attention_back(): pl.pallas_call(functools.partial(attention_back_kernel, seqs, listed // s...]
    another operation x1 -> x4, other arithmetic: 0.07 us -> 3.26 us  [the longest x3 3.19 us: on_block(): jnp.stack([g_down, line_add(keep_g, got_g, line_g), line_add(keep_u, got_...]
  transfers between devices with their start and end apart: 51 -> 54, of which waited for: 22 -> 26; matrix products, arithmetic and copies ran while one was open for 6% -> 7% of each run, Pallas kernels for 25% -> 27%
where the time goes in v8:
time: 299 us; the launch traced here: 298 us
  Pallas kernels  107 us (36%)
  waiting for transfers between devices  100 us (33%)
  starting transfers between devices  49.9 us (17%)
  other arithmetic  16.7 us (6%)
  between operations  14.8 us (5%)
  local copies, waits for them, and re-layouts  10.2 us (3%)
    ppermute x53, waiting for transfers between devices, send(): return lax.ppermute(value, AXES, MOVES[move])  69.9 us
    ppermute x53, starting transfers between devices, send(): return lax.ppermute(value, AXES, MOVES[move])  49.8 us
    all_gather x1, waiting for transfers between devices, on_block(): lax.all_gather(ffn_piece, AXES, axis=0, tiled=False)  30.3 us
    pallas_call x2, Pallas kernels, attention_back(): pl.pallas_call(functools.partial(attention_back_kernel, seqs, listed // s...  19.9 us
    pallas_call x1, Pallas kernels, attention_forward(): pl.pallas_call(functools.partial(attention_kernel, seqs, listed // seqs),...  18 us
    pallas_call x1, Pallas kernels, ffn_forward(): pl.pallas_call(functools.partial(ffn_kernel, seqs, listed // seqs), out_s...  17 us
    pallas_call x3, Pallas kernels, weight_grad(): pl.pallas_call(weight_grad_kernel, out_shape=(out(shape, LOW), out(shape,...  11.6 us
    pallas_call x1, Pallas kernels, attention_grads(): pl.pallas_call(attention_grads_kernel, out_shape=(out((2, 2, LINE, half,...  8.81 us
  transfers between devices with their start and end apart: 54, of which 26 were waited for; matrix products, arithmetic and copies ran while one was open for 7% of the time, Pallas kernels for 27%

profile of v8, /device:TPU:0, one launch (start us, length us, event | category | flops | bytes accessed | tf_op | source)
XLA Modules:
  0.0 298.4 jit_solution(6852272674880681875)
XLA Ops:
  9.6 4.1 %collective-permute-start.1 = (bf16[104,768]{1,0:T(8,128)(2,1)S(1)}, bf16[104,768]{1,0:T(8,128)(2,1)S(1)}, u32[]{:S(2)}, u32[]{:S(2)}) collective-permute-start(bf16[104,768]{1,0:T(8,128)(2,1)S(1)} %get-tuple-element.185), channel_id=1, source_target_pairs={{0,16},{1,17},{2,18},{3,19},{4,20},{5,21},{6,22},{7,23},{8,24},{9,... | collective-permute-start | bytes 479240 | tf_op jit(solution)/shard_map/ppermute | solution.py:562
  18.7 6.9 %collective-permute-done.1 = bf16[104,768]{1,0:T(8,128)(2,1)S(1)} collective-permute-done((bf16[104,768]{1,0:T(8,128)(2,1)S(1)}, bf16[104,768]{1,0:T(8,128)(2,1)S(1)}, u32[]{:S(2)}, u32[]{:S(2)}) %collective-permute-start.1) | collective-permute-done | bytes 159776 | tf_op jit(solution)/shard_map/ppermute | solution.py:562
  31.4 6.8 %collective-permute-done.6.rest_5_ = bf16[4,56,768]{2,1,0:T(8,128)(2,1)S(1)} collective-permute-done((bf16[4,56,768]{2,1,0:T(8,128)(2,1)S(1)}, bf16[4,56,768]{2,1,0:T(8,128)(2,1)S(1)}, u32[]{:S(2)}, u32[]{:S(2)}) %collective-permute-start.6) | collective-permute-done | bytes 344096 | tf_op jit(solution)/shard_map/ppermute | solution.py:562
  42.5 4.0 %collective-permute-done.4.rest_2_ = bf16[4,48,768]{2,1,0:T(8,128)(2,1)} collective-permute-done((bf16[4,48,768]{2,1,0:T(8,128)(2,1)S(1)}, bf16[4,48,768]{2,1,0:T(8,128)(2,1)}, u32[]{:S(2)}, u32[]{:S(2)}) %collective-permute-start.4) | collective-permute-done | bytes 294944 | tf_op jit(solution)/shard_map/ppermute | solution.py:562
  50.7 5.5 %collective-permute-done.8.rest_7_ = bf16[4,56,768]{2,1,0:T(8,128)(2,1)S(1)} collective-permute-done((bf16[4,56,768]{2,1,0:T(8,128)(2,1)S(1)}, bf16[4,56,768]{2,1,0:T(8,128)(2,1)S(1)}, u32[]{:S(2)}, u32[]{:S(2)}) %collective-permute-start.8) | collective-permute-done | bytes 344096 | tf_op jit(solution)/shard_map/ppermute | solution.py:562
  56.8 6.2 %collective-permute-done.7.rest_6_ = bf16[4,48,768]{2,1,0:T(8,128)(2,1)} collective-permute-done((bf16[4,48,768]{2,1,0:T(8,128)(2,1)}, bf16[4,48,768]{2,1,0:T(8,128)(2,1)}, u32[]{:S(2)}, u32[]{:S(2)}) %collective-permute-start.7) | collective-permute-done | bytes 294944 | tf_op jit(solution)/shard_map/ppermute | solution.py:562
  65.8 18.0 %attention_forward.1 = (bf16[512,2304]{1,0:T(8,128)(2,1)}, f32[512,768]{1,0:T(8,128)}, bf16[128,768]{1,0:T(8,128)(2,1)}, bf16[128,768]{1,0:T(8,128)(2,1)}, bf16[...) custom-call(s32[5]{0:T(128)} %stack.95.where_ref, f32[12]{0:T(128)} %multiply_exponential_fusion.slope_ref, ...), custom_call_target="tpu_custom_call" | custom-call | bytes 60000000 | tf_op jit(solution)/shard_map/attention_forward/pallas_call | solution.py:164
  85.6 10.4 %collective-permute-done.18 = bf16[128,768]{1,0:T(8,128)(2,1)S(1)} collective-permute-done((bf16[128,768]{1,0:T(8,128)(2,1)}, bf16[128,768]{1,0:T(8,128)(2,1)S(1)}, u32[]{:S(2)}, u32[]{:S(2)}) %collective-permute-start.18) | collective-permute-done | bytes 196640 | tf_op jit(solution)/shard_map/ppermute | solution.py:562
  99.3 30.3 %all-gather.3.cloned.1.call-done = bf16[96,96,768]{2,1,0:T(8,128)(2,1)} async-done(((bf16[3,96,768]{2,1,0:T(8,128)(2,1)}), bf16[96,96,768]{2,1,0:T(8,128)(2,1)}) %all-gather.3.cloned.1.call-update) | async-done | bytes 14155792 | tf_op jit(solution)/shard_map/all_gather | solution.py:668
  129.6 17.0 %ffn_forward.1 = (bf16[512,768]{1,0:T(8,128)(2,1)}, f32[128,768]{1,0:T(8,128)}, bf16[128,768]{1,0:T(8,128)(2,1)}, f32[2,768]{1,0:T(2,128)}) custom-call(f32[512,768]{1,0:T(8,128)} %get-tuple-element.91.h1_ref, bf16[8,4,3,96,768]{4,3,2,1,0:T(8,128)(2,1)} %bitcast.136, bf16[8,4,3,96,768]{4,3,2,1,0:T(8,128)(2,1)} %bitcast.137, ...), custom_call_target="tpu_custom_call" | custom-call | bytes 48000000 | tf_op jit(solution)/shard_map/ffn_forward/pallas_call | solution.py:232
  147.2 6.6 %ffn_again.1 = (bf16[512,768]{1,0:T(8,128)(2,1)}, f32[512,768]{1,0:T(8,128)}, f32[512,768]{1,0:T(8,128)}) custom-call(s32[5]{0:T(128)} %stack.95.where_ref, bf16[4,128,768]{2,1,0:T(8,128)(2,1)} %pad_maximum_fusion.1.h_ref.a_ref, bf16[8,4,3,96,768]{4,3,2,1,0:T(8,128)(2,1)} %bitcast.139, bf16[8,4,3,96,768]{4,3,2,1,0:T(8,128)(2,1)} %bitcast.140), custom_call_target="tpu_custom_call" | custom-call | bytes 18000000 | tf_op jit(solution)/shard_map/ffn_again/pallas_call | solution.py:288
  156.4 7.5 %ffn_back.1 = (bf16[512,768]{1,0:T(8,128)(2,1)}, bf16[512,768]{1,0:T(8,128)(2,1)}, f32[2,128,768]{2,1,0:T(8,128)}, bf16[2,128,768]{2,1,0:T(8,128)(2,1)}) custom-call(s32[5]{0:T(128)} %stack.95.where_ref, bf16[4,128,768]{2,1,0:T(8,128)(2,1)} %pad_maximum_fusion.2.b_ref.e_ref, f32[512,768]{1,0:T(8,128)} %get-tuple-element.100.to_gate_ref, ...), custom_call_target="tpu_custom_call" | custom-call | bytes 21000000 | tf_op jit(solution)/shard_map/ffn_back/pallas_call | solution.py:323
  164.2 3.8 %weight_grad.3 = (bf16[4,96,768]{2,1,0:T(8,128)(2,1)}, bf16[4,96,768]{2,1,0:T(8,128)(2,1)}) custom-call(s32[5]{0:T(128)} %stack.95.where_ref, bf16[512,768]{1,0:T(8,128)(2,1)} %get-tuple-element.95.a_ref, bf16[4,128,768]{2,1,0:T(8,128)(2,1)} %pad_maximum_fusion.2.b_ref.e_ref), custom_call_target="tpu_custom_call" | custom-call | bytes 12000000 | tf_op jit(solution)/shard_map/weight_grad/pallas_call | solution.py:359
  171.2 3.8 %weight_grad.4 = (bf16[4,96,768]{2,1,0:T(8,128)(2,1)}, bf16[4,96,768]{2,1,0:T(8,128)(2,1)}) custom-call(s32[5]{0:T(128)} %stack.95.where_ref, bf16[4,128,768]{2,1,0:T(8,128)(2,1)} %pad_maximum_fusion.1.h_ref.a_ref, bf16[512,768]{1,0:T(8,128)(2,1)} %get-tuple-element.105.b_ref), custom_call_target="tpu_custom_call" | custom-call | bytes 12000000 | tf_op jit(solution)/shard_map/weight_grad/pallas_call | solution.py:359
  176.5 3.9 %weight_grad.5 = (bf16[4,96,768]{2,1,0:T(8,128)(2,1)}, bf16[4,96,768]{2,1,0:T(8,128)(2,1)}) custom-call(s32[5]{0:T(128)} %stack.95.where_ref, bf16[4,128,768]{2,1,0:T(8,128)(2,1)} %pad_maximum_fusion.1.h_ref.a_ref, bf16[512,768]{1,0:T(8,128)(2,1)} %get-tuple-element.108.b_ref), custom_call_target="tpu_custom_call" | custom-call | bytes 12000000 | tf_op jit(solution)/shard_map/weight_grad/pallas_call | solution.py:359
  181.7 3.2 %norm_back.1 = (f32[128,768]{1,0:T(8,128)}, bf16[128,768]{1,0:T(8,128)(2,1)}, bf16[128,768]{1,0:T(8,128)(2,1)}, f32[2,768]{1,0:T(2,128)}) custom-call(f32[128,768]{1,0:T(8,128)} %get-tuple-element.99.dr2_ref, f32[128,768]{1,0:T(8,128)} %slice_bitcast_fusion.2.part_ref, bf16[128,768]{1,0:T(8,128)(2,1)} %copy-done.32, f32[128,768]{1,0:T(8,128)} %get-tuple-element.111.r1_ref, ...), custom_call_target="tpu_custom_call" | custom-call | bytes 12000000 | tf_op jit(solution)/shard_map/norm_back/pallas_call | solution.py:389
  184.9 9.8 %attention_back.2.rhs0_ref = bf16[256,2304]{1,0:T(8,128)(2,1)} custom-call(f32[12]{0:T(128)} %multiply_exponential_fusion.slope_ref, bf16[128,768]{1,0:T(8,128)(2,1)} %get-tuple-element.119.datt_ref, bf16[128,768]{1,0:T(8,128)(2,1)} %get-tuple-element.114.q_ref, bf16[512,2304]{1,0:T(8,128)(2,1)} %get-tuple-element.115.qkv_ref, s32[128,1]{1,0:T(8,128)} %reshape.140.pos_ref), custom_call_target="tpu_custom_call" | custom-call | bytes 24000000 | tf_op jit(solution)/shard_map/attention_back/pallas_call | solution.py:441
  198.6 10.0 %attention_back.3.rhs1_ref = bf16[256,2304]{1,0:T(8,128)(2,1)} custom-call(f32[12]{0:T(128)} %multiply_exponential_fusion.slope_ref, bf16[128,768]{1,0:T(8,128)(2,1)} %get-tuple-element.119.datt_ref, bf16[128,768]{1,0:T(8,128)(2,1)} %get-tuple-element.114.q_ref, bf16[512,2304]{1,0:T(8,128)(2,1)} %get-tuple-element.115.qkv_ref, s32[128,1]{1,0:T(8,128)} %reshape.140.pos_ref), custom_call_target="tpu_custom_call" | custom-call | bytes 24000000 | tf_op jit(solution)/shard_map/attention_back/pallas_call | solution.py:441
  214.1 8.8 %attention_grads.1 = (bf16[2,2,4,48,768]{4,3,2,1,0:T(8,128)(2,1)}, bf16[2,2,4,64,768]{4,3,2,1,0:T(8,128)(2,1)}, bf16[2,2,4,48,768]{4,3,2,1,0:T(8,128)(2,1)}, bf16[2,2,4,64,768]{4,3,2,1,0:T(8,128)(2,1)}) custom-call(s32[5]{0:T(128)} %stack.95.where_ref, bf16[768,512]{1,0:T(8,128)(2,1)} %bitcast.144, bf16[256,2304]{1,0:T(8,128)(2,1)} %attention_back.2.rhs0_ref, ...), custom_call_target="tpu_custom_call" | custom-call | bytes 30000000 | tf_op jit(solution)/shard_map/attention_grads/pallas_call | solution.py:493
  239.6 4.0 %collective-permute-start.43 = (bf16[96,768]{1,0:T(8,128)(2,1)}, bf16[96,768]{1,0:T(8,128)(2,1)}, u32[]{:S(2)}, u32[]{:S(2)}) collective-permute-start(bf16[96,768]{1,0:T(8,128)(2,1)} %get-tuple-element.166), channel_id=1, source_target_pairs={{0,24},{1,25},{2,26},{3,27},{4,28},{5,29},{6,30},{7,31},{8,0},{9,1... | collective-permute-start | bytes 442376 | tf_op jit(solution)/shard_map/ppermute | solution.py:562
  244.7 8.3 %input_grad.1 = f32[512,768]{1,0:T(8,128)} custom-call(bf16[256,2304]{1,0:T(8,128)(2,1)} %attention_back.2.rhs0_ref, bf16[256,2304]{1,0:T(8,128)(2,1)} %attention_back.3.rhs1_ref, bf16[8,4,96,768]{3,2,1,0:T(8,128)(2,1)} %get-tuple-element.112.w_ref, f32[128,768]{1,0:T(8,128)} %get-tuple-element.135.dr1_ref, s32[4,32]{1,0:T(4,128)} %pos_ref.1), custom_call_target="tpu_custom_call" | custom-call | bytes 24000000 | tf_op jit(solution)/shard_map/input_grad/pallas_call | solution.py:525
  265.9 4.5 %collective-permute-start.46 = (bf16[112,768]{1,0:T(8,128)(2,1)S(1)}, bf16[112,768]{1,0:T(8,128)(2,1)S(1)}, u32[]{:S(2)}, u32[]{:S(2)}) collective-permute-start(bf16[112,768]{1,0:T(8,128)(2,1)S(1)} %get-tuple-element.177), channel_id=1, source_target_pairs={{0,24},{1,25},{2,26},{3,27},{4,28},{5,29},{6,30},{7,31},{8,0},{9,1... | collective-permute-start | bytes 516104 | tf_op jit(solution)/shard_map/ppermute | solution.py:562
  274.6 6.1 %collective-permute-done.45 = bf16[112,768]{1,0:T(8,128)(2,1)S(1)} collective-permute-done((bf16[112,768]{1,0:T(8,128)(2,1)S(1)}, bf16[112,768]{1,0:T(8,128)(2,1)S(1)}, u32[]{:S(2)}, u32[]{:S(2)}) %collective-permute-start.45) | collective-permute-done | bytes 172064 | tf_op jit(solution)/shard_map/ppermute | solution.py:562
  283.4 3.4 %finish_ffn.1 = (f32[384,768]{1,0:T(8,128)}, f32[96,6144]{1,0:T(8,128)}) custom-call(s32[5]{0:T(128)} %stack.95.where_ref, bf16[3,96,768]{2,1,0:T(8,128)(2,1)} %copy-done.1, bf16[3,96,768]{2,1,0:T(8,128)(2,1)} %copy-done.19, bf16[3,96,768]{2,1,0:T(8,128)(2,1)} %copy-done.18, bf16[3,96,768]{2,1,0:T(8,128)(2,1)} %copy-done.20), custom_call_target="tpu_custom_call" | custom-call | bytes 12000000 | tf_op jit(solution)/shard_map/finish_ffn/pallas_call | solution.py:611
  (258 shorter events, 90.7 us)
Async XLA Ops:
  7.2 122.3 %all-gather.3.cloned.1.call-start = ((), (), s32[]{:S(2)}) async-start(), calls=%async_computation | async-start | bytes 14598144 | tf_op jit(solution)/shard_map/all_gather | solution.py:668
  9.6 16.0 %collective-permute-start.1 = (bf16[104,768]{1,0:T(8,128)(2,1)S(1)}, bf16[104,768]{1,0:T(8,128)(2,1)S(1)}, u32[]{:S(2)}, u32[]{:S(2)}) collective-permute-start(bf16[104,768]{1,0:T(8,128)(2,1)S(1)} %get-tuple-element.185), channel_id=1, source_target_pairs={{0,16},{1,17},{2,18},{3,19},{4,20},{5,21},{6,22},{7,23},{8,24},{9,... | collective-permute-start | bytes 479240 | tf_op jit(solution)/shard_map/ppermute | solution.py:562
  29.0 13.5 %collective-permute-start.5 = (bf16[4,48,768]{2,1,0:T(8,128)(2,1)S(1)}, bf16[4,48,768]{2,1,0:T(8,128)(2,1)}, u32[]{:S(2)}, u32[]{:S(2)}) collective-permute-start(bf16[4,48,768]{2,1,0:T(8,128)(2,1)S(1)} %slice.169.rest_0_), channel_id=1, source_target_pairs={{0,2},{1,3},{2,0},{3,1},{4,6},{5,7},{6,4},{7,5},{8,10},{9,11},{10,... | collective-permute-start | bytes 884744 | tf_op jit(solution)/shard_map/ppermute | solution.py:562
  29.4 17.1 %collective-permute-start.3 = (bf16[4,56,768]{2,1,0:T(8,128)(2,1)S(1)}, bf16[4,56,768]{2,1,0:T(8,128)(2,1)S(1)}, u32[]{:S(2)}, u32[]{:S(2)}) collective-permute-start(bf16[4,56,768]{2,1,0:T(8,128)(2,1)S(1)} %slice.167.rest_1_), channel_id=1, source_target_pairs={{0,4},{1,5},{2,6},{3,7},{4,0},{5,1},{6,2},{7,3},{8,12},{9,13},{10,... | collective-permute-start | bytes 1032200 | tf_op jit(solution)/shard_map/ppermute | solution.py:562
  31.2 15.3 %collective-permute-start.4 = (bf16[4,48,768]{2,1,0:T(8,128)(2,1)S(1)}, bf16[4,48,768]{2,1,0:T(8,128)(2,1)}, u32[]{:S(2)}, u32[]{:S(2)}) collective-permute-start(bf16[4,48,768]{2,1,0:T(8,128)(2,1)S(1)} %slice.169.rest_0_), channel_id=1, source_target_pairs={{0,4},{1,5},{2,6},{3,7},{4,0},{5,1},{6,2},{7,3},{8,12},{9,13},{10,... | collective-permute-start | bytes 884744 | tf_op jit(solution)/shard_map/ppermute | solution.py:562
  31.4 19.1 %collective-permute-start.10 = (bf16[4,56,768]{2,1,0:T(8,128)(2,1)S(1)}, bf16[4,56,768]{2,1,0:T(8,128)(2,1)S(1)}, u32[]{:S(2)}, u32[]{:S(2)}) collective-permute-start(bf16[4,56,768]{2,1,0:T(8,128)(2,1)S(1)} %slice.167.rest_1_), channel_id=1, source_target_pairs={{0,1},{1,0},{2,3},{3,2},{4,5},{5,4},{6,7},{7,6},{8,9},{9,8},{10,11... | collective-permute-start | bytes 1032200 | tf_op jit(solution)/shard_map/ppermute | solution.py:562
  38.2 18.0 %collective-permute-start.8 = (bf16[4,56,768]{2,1,0:T(8,128)(2,1)S(1)}, bf16[4,56,768]{2,1,0:T(8,128)(2,1)S(1)}, u32[]{:S(2)}, u32[]{:S(2)}) collective-permute-start(bf16[4,56,768]{2,1,0:T(8,128)(2,1)S(1)} %collective-permute-done.6.rest_5_), channel_id=1, source_target_pairs={{0,4},{1,5},{2,6},{3,7},{4,0},{5,1},{6,2},{7,3},{8,12},{9,13},{10,... | collective-permute-start | bytes 1032200 | tf_op jit(solution)/shard_map/ppermute | solution.py:562
  46.5 16.4 %collective-permute-start.7 = (bf16[4,48,768]{2,1,0:T(8,128)(2,1)}, bf16[4,48,768]{2,1,0:T(8,128)(2,1)}, u32[]{:S(2)}, u32[]{:S(2)}) collective-permute-start(bf16[4,48,768]{2,1,0:T(8,128)(2,1)} %collective-permute-done.4.rest_2_), channel_id=1, source_target_pairs={{0,2},{1,3},{2,0},{3,1},{4,6},{5,7},{6,4},{7,5},{8,10},{9,11},{10,... | collective-permute-start | bytes 884744 | tf_op jit(solution)/shard_map/ppermute | solution.py:562
  49.8 14.3 %collective-permute-start.14 = (bf16[4,56,768]{2,1,0:T(8,128)(2,1)S(1)}, bf16[4,56,768]{2,1,0:T(8,128)(2,1)S(1)}, u32[]{:S(2)}, u32[]{:S(2)}) collective-permute-start(bf16[4,56,768]{2,1,0:T(8,128)(2,1)S(1)} %collective-permute-done.6.rest_5_), channel_id=1, source_target_pairs={{0,1},{1,0},{2,3},{3,2},{4,5},{5,4},{6,7},{7,6},{8,9},{9,8},{10,11... | collective-permute-start | bytes 1032200 | tf_op jit(solution)/shard_map/ppermute | solution.py:562
  50.6 13.6 %collective-permute-start.12 = (bf16[4,56,768]{2,1,0:T(8,128)(2,1)S(1)}, bf16[4,56,768]{2,1,0:T(8,128)(2,1)S(1)}, u32[]{:S(2)}, u32[]{:S(2)}) collective-permute-start(bf16[4,56,768]{2,1,0:T(8,128)(2,1)S(1)} %collective-permute-done.3.rest_3_), channel_id=1, source_target_pairs={{0,1},{1,0},{2,3},{3,2},{4,5},{5,4},{6,7},{7,6},{8,9},{9,8},{10,11... | collective-permute-start | bytes 1032200 | tf_op jit(solution)/shard_map/ppermute | solution.py:562
  168.1 26.7 %collective-permute-start.23 = (bf16[4,96,768]{2,1,0:T(8,128)(2,1)}, bf16[4,96,768]{2,1,0:T(8,128)(2,1)S(1)}, u32[]{:S(2)}, u32[]{:S(2)}) collective-permute-start(bf16[4,96,768]{2,1,0:T(8,128)(2,1)} %get-tuple-element.98), channel_id=1, source_target_pairs={{0,4},{1,5},{2,6},{3,7},{4,0},{5,1},{6,2},{7,3},{8,12},{9,13},{10,... | collective-permute-start | bytes 1769480 | tf_op jit(solution)/shard_map/ppermute | solution.py:562
  175.0 35.0 %collective-permute-start.29 = (bf16[4,96,768]{2,1,0:T(8,128)(2,1)}, bf16[4,96,768]{2,1,0:T(8,128)(2,1)S(1)}, u32[]{:S(2)}, u32[]{:S(2)}) collective-permute-start(bf16[4,96,768]{2,1,0:T(8,128)(2,1)} %get-tuple-element.106), channel_id=1, source_target_pairs={{0,4},{1,5},{2,6},{3,7},{4,0},{5,1},{6,2},{7,3},{8,12},{9,13},{10,... | collective-permute-start | bytes 1769480 | tf_op jit(solution)/shard_map/ppermute | solution.py:562
  180.4 45.2 %collective-permute-start.33 = (bf16[4,96,768]{2,1,0:T(8,128)(2,1)}, bf16[4,96,768]{2,1,0:T(8,128)(2,1)S(1)}, u32[]{:S(2)}, u32[]{:S(2)}) collective-permute-start(bf16[4,96,768]{2,1,0:T(8,128)(2,1)} %get-tuple-element.109), channel_id=1, source_target_pairs={{0,4},{1,5},{2,6},{3,7},{4,0},{5,1},{6,2},{7,3},{8,12},{9,13},{10,... | collective-permute-start | bytes 1769480 | tf_op jit(solution)/shard_map/ppermute | solution.py:562
  194.9 13.8 %collective-permute-start.28 = (bf16[96,768]{1,0:T(8,128)(2,1)S(1)}, bf16[96,768]{1,0:T(8,128)(2,1)S(1)}, u32[]{:S(2)}, u32[]{:S(2)}) collective-permute-start(bf16[96,768]{1,0:T(8,128)(2,1)S(1)} %get-tuple-element.172), channel_id=1, source_target_pairs={{0,24},{1,25},{2,26},{3,27},{4,28},{5,29},{6,30},{7,31},{8,0},{9,1... | collective-permute-start | bytes 442376 | tf_op jit(solution)/shard_map/ppermute | solution.py:562
  196.7 13.3 %collective-permute-start.27 = (bf16[96,768]{1,0:T(8,128)(2,1)S(1)}, bf16[96,768]{1,0:T(8,128)(2,1)S(1)}, u32[]{:S(2)}, u32[]{:S(2)}) collective-permute-start(bf16[96,768]{1,0:T(8,128)(2,1)S(1)} %get-tuple-element.173), channel_id=1, source_target_pairs={{0,16},{1,17},{2,18},{3,19},{4,20},{5,21},{6,22},{7,23},{8,24},{9,... | collective-permute-start | bytes 442376 | tf_op jit(solution)/shard_map/ppermute | solution.py:562
  197.4 12.6 %collective-permute-start.26 = (bf16[96,768]{1,0:T(8,128)(2,1)S(1)}, bf16[96,768]{1,0:T(8,128)(2,1)S(1)}, u32[]{:S(2)}, u32[]{:S(2)}) collective-permute-start(bf16[96,768]{1,0:T(8,128)(2,1)S(1)} %get-tuple-element.174), channel_id=1, source_target_pairs={{0,8},{1,9},{2,10},{3,11},{4,12},{5,13},{6,14},{7,15},{8,16},{9,17... | collective-permute-start | bytes 442376 | tf_op jit(solution)/shard_map/ppermute | solution.py:562
  210.1 12.8 %collective-permute-start.32 = (bf16[96,768]{1,0:T(8,128)(2,1)S(1)}, bf16[96,768]{1,0:T(8,128)(2,1)S(1)}, u32[]{:S(2)}, u32[]{:S(2)}) collective-permute-start(bf16[96,768]{1,0:T(8,128)(2,1)S(1)} %get-tuple-element.169), channel_id=1, source_target_pairs={{0,24},{1,25},{2,26},{3,27},{4,28},{5,29},{6,30},{7,31},{8,0},{9,1... | collective-permute-start | bytes 442376 | tf_op jit(solution)/shard_map/ppermute | solution.py:562
  211.5 14.1 %collective-permute-start.31 = (bf16[96,768]{1,0:T(8,128)(2,1)S(1)}, bf16[96,768]{1,0:T(8,128)(2,1)S(1)}, u32[]{:S(2)}, u32[]{:S(2)}) collective-permute-start(bf16[96,768]{1,0:T(8,128)(2,1)S(1)} %get-tuple-element.170), channel_id=1, source_target_pairs={{0,16},{1,17},{2,18},{3,19},{4,20},{5,21},{6,22},{7,23},{8,24},{9,... | collective-permute-start | bytes 442376 | tf_op jit(solution)/shard_map/ppermute | solution.py:562
  212.1 13.4 %collective-permute-start.30 = (bf16[96,768]{1,0:T(8,128)(2,1)S(1)}, bf16[96,768]{1,0:T(8,128)(2,1)S(1)}, u32[]{:S(2)}, u32[]{:S(2)}) collective-permute-start(bf16[96,768]{1,0:T(8,128)(2,1)S(1)} %get-tuple-element.171), channel_id=1, source_target_pairs={{0,8},{1,9},{2,10},{3,11},{4,12},{5,13},{6,14},{7,15},{8,16},{9,17... | collective-permute-start | bytes 442376 | tf_op jit(solution)/shard_map/ppermute | solution.py:562
  231.2 22.4 %collective-permute-start.37 = (bf16[2,4,64,768]{3,2,1,0:T(8,128)(2,1)S(1)}, bf16[2,4,64,768]{3,2,1,0:T(8,128)(2,1)}, u32[]{:S(2)}, u32[]{:S(2)}) collective-permute-start(bf16[2,4,64,768]{3,2,1,0:T(8,128)(2,1)S(1)} %fusion.1), channel_id=1, source_target_pairs={{0,4},{1,5},{2,6},{3,7},{4,0},{5,1},{6,2},{7,3},{8,12},{9,13},{10,... | collective-permute-start | bytes 2359304 | tf_op jit(solution)/shard_map/ppermute | solution.py:562
  232.9 20.0 %collective-permute-start.35 = (bf16[2,4,48,768]{3,2,1,0:T(8,128)(2,1)}, bf16[2,4,48,768]{3,2,1,0:T(8,128)(2,1)}, u32[]{:S(2)}, u32[]{:S(2)}) collective-permute-start(bf16[2,4,48,768]{3,2,1,0:T(8,128)(2,1)} %fusion.3), channel_id=1, source_target_pairs={{0,2},{1,3},{2,0},{3,1},{4,6},{5,7},{6,4},{7,5},{8,10},{9,11},{10,... | collective-permute-start | bytes 1769480 | tf_op jit(solution)/shard_map/ppermute | solution.py:562
  236.0 20.6 %collective-permute-start.40 = (bf16[96,768]{1,0:T(8,128)(2,1)}, bf16[96,768]{1,0:T(8,128)(2,1)}, u32[]{:S(2)}, u32[]{:S(2)}) collective-permute-start(bf16[96,768]{1,0:T(8,128)(2,1)} %fusion.20), channel_id=1, source_target_pairs={{0,0},{1,8},{2,16},{3,24},{4,1},{5,9},{6,17},{7,25},{8,2},{9,10},{... | collective-permute-start | bytes 442376 | tf_op jit(solution)/shard_map/ppermute | solution.py:562
  239.6 17.8 %collective-permute-start.43 = (bf16[96,768]{1,0:T(8,128)(2,1)}, bf16[96,768]{1,0:T(8,128)(2,1)}, u32[]{:S(2)}, u32[]{:S(2)}) collective-permute-start(bf16[96,768]{1,0:T(8,128)(2,1)} %get-tuple-element.166), channel_id=1, source_target_pairs={{0,24},{1,25},{2,26},{3,27},{4,28},{5,29},{6,30},{7,31},{8,0},{9,1... | collective-permute-start | bytes 442376 | tf_op jit(solution)/shard_map/ppermute | solution.py:562
  243.6 13.8 %collective-permute-start.42 = (bf16[96,768]{1,0:T(8,128)(2,1)}, bf16[96,768]{1,0:T(8,128)(2,1)}, u32[]{:S(2)}, u32[]{:S(2)}) collective-permute-start(bf16[96,768]{1,0:T(8,128)(2,1)} %get-tuple-element.167), channel_id=1, source_target_pairs={{0,16},{1,17},{2,18},{3,19},{4,20},{5,21},{6,22},{7,23},{8,24},{9,... | collective-permute-start | bytes 442376 | tf_op jit(solution)/shard_map/ppermute | solution.py:562
  (83 other events, 691.3 us)
Sparse Core Ops, SparseCore 0:
  11.5 117.9 all-gather.2

commit v9 on v8

--- a/solution.py
+++ b/solution.py
@@ -181,6 +181,42 @@
     )(where, slopes, x, norms, pos, *lines)
 
 
+def assemble_kernel(where_ref, *rest):
+    pieces, (full_ref, sem) = rest[:4], rest[4:]
+    z, y, mine = where_ref[0], where_ref[1], where_ref[4]
+    size = ROWS // 2
+    copies = []
+    for n, piece in enumerate(pieces):
+        half, rc = n % 2, n // 2
+        for second in (0, 1):
+            for first in (0, 1):
+                ry, rx = (first, second) if half == 0 else (second, first)
+                j = jnp.bitwise_xor(mine, 2 * rx + rc)
+                for r in range(LINE):
+                    shard = 2 * lax.rem(z + LINE - r, LINE) + jnp.bitwise_xor(y, ry)
+                    copies.append(
+                        pltpu.make_async_copy(piece.at[second, first, r], full_ref.at[shard, j, pl.ds(half * size, size)], sem)
+                    )
+    for copy in copies:
+        copy.start()
+    for copy in copies:
+        copy.wait()
+
+
+def assemble(where, pieces):
+    anywhere = pl.BlockSpec(memory_space=pl.ANY)
+    return pl.pallas_call(
+        assemble_kernel,
+        out_shape=out((SHARDS, QUARTERS, ROWS, D), LOW),
+        in_specs=[SMEM] + [anywhere] * 4,
+        out_specs=anywhere,
+        scratch_shapes=[pltpu.SemaphoreType.DMA],
+        compiler_params=BIG,
+        cost_estimate=cost(3),
+        name="assemble",
+    )(where, *pieces)
+
+
 def ffn_kernel(seqs, most, h1_ref, gate_ref, up_ref, down_ref, norm_ref, pos_ref, dy_ref, y_ref, dr2_ref, e2_ref, small_ref, low_ref, act_ref, acc_ref):
     j = pl.program_id(0)
     tokens = h1_ref.shape[0]
@@ -225,7 +261,7 @@
         small_ref[...] = jnp.concatenate(small, axis=0)
 
 
-def ffn_forward(h1, w_ffn, norms, pos, dy, seqs):
+def ffn_forward(h1, w_gu, w_down, norms, pos, dy, seqs):
     tokens = h1.shape[0]
     listed = pos.shape[0]
     whole = lambda shape: pl.BlockSpec(shape, lambda j: (0,) * len(shape), pipeline_mode=pl.Buffered(1))
@@ -237,7 +273,7 @@
             whole((tokens, D)),
             pl.BlockSpec((SHARDS, None, None, ROWS, D), lambda j: (0, j, 0, 0, 0)),
             pl.BlockSpec((SHARDS, None, None, ROWS, D), lambda j: (0, j, 1, 0, 0)),
-            pl.BlockSpec((SHARDS // QUARTERS, QUARTERS, None, ROWS, D), lambda j: (j, 0, 2, 0, 0)),
+            pl.BlockSpec((SHARDS // QUARTERS, QUARTERS, ROWS, D), lambda j: (j, 0, 0, 0)),
             whole(norms.shape),
             whole(pos.shape),
             whole(dy.shape),
@@ -252,7 +288,7 @@
         compiler_params=BIG,
         cost_estimate=cost(16),
         name="ffn_forward",
-    )(h1, w_ffn, w_ffn, w_ffn, norms, pos, dy)
+    )(h1, w_gu, w_gu, w_down, norms, pos, dy)
 
 
 def ffn_again_kernel(where_ref, h_ref, gate_ref, up_ref, act_ref, to_gate_ref, to_up_ref):
@@ -274,7 +310,7 @@
     specs = {
         "gate": pl.BlockSpec((SHARDS, None, None, ROWS, D), lambda g, w: (0, w[4], 0, 0, 0)),
         "up": pl.BlockSpec((SHARDS, None, None, ROWS, D), lambda g, w: (0, w[4], 1, 0, 0)),
-        "down": pl.BlockSpec((SHARDS // QUARTERS, QUARTERS, None, ROWS, D), lambda g, w: (w[4], 0, 2, 0, 0)),
+        "down": pl.BlockSpec((SHARDS // QUARTERS, QUARTERS, ROWS, D), lambda g, w: (w[4], 0, 0, 0)),
     }
     return [specs[name] for name in which]
 
@@ -283,7 +319,7 @@
     return pl.BlockSpec(shape, lambda g, w: (0,) * len(shape))
 
 
-def ffn_again(where, h_all, w_ffn):
+def ffn_again(where, h_all, w_gu):
     rows = h_all.shape[0] * h_all.shape[1]
     return pl.pallas_call(
         ffn_again_kernel,
@@ -297,7 +333,7 @@
         compiler_params=BIG,
         cost_estimate=cost(6),
         name="ffn_again",
-    )(where, h_all, w_ffn, w_ffn)
+    )(where, h_all, w_gu, w_gu)
 
 
 def ffn_back_kernel(where_ref, e_ref, to_gate_ref, to_up_ref, gate_ref, up_ref, down_ref, dgate_ref, dup_ref, keep_ref, send_ref):
@@ -317,7 +353,7 @@
             send_ref[r, :, lanes] = part[(2 * r + 1) * listed : (2 * r + 2) * listed].astype(LOW)
 
 
-def ffn_back(where, e_all, to_gate, to_up, w_ffn):
+def ffn_back(where, e_all, to_gate, to_up, w_gu, w_down):
     count, listed, _ = e_all.shape
     rows = count * listed
     return pl.pallas_call(
@@ -332,7 +368,7 @@
         compiler_params=BIG,
         cost_estimate=cost(7),
         name="ffn_back",
-    )(where, e_all, to_gate, to_up, w_ffn, w_ffn, w_ffn)
+    )(where, e_all, to_gate, to_up, w_gu, w_gu, w_down)
 
 
 def weight_grad_kernel(where_ref, a_ref, b_ref, keep_ref, send_ref, full_ref):
@@ -398,7 +434,7 @@
     )(dr2, part, came, r1_m, w_attn, norms)
 
 
-def attention_back_kernel(seqs, most, chosen, slope_ref, datt_ref, q_ref, qkv_ref, pos_ref, rhs_ref, away_ref, hot_ref):
+def attention_back_kernel(seqs, most, slope_ref, datt_ref, q_ref, qkv_ref, pos_ref, rhs_ref, away_ref, hot_ref):
     length = qkv_ref.shape[0] // seqs
     listed = seqs * most
     first_m = lax.broadcasted_iota(jnp.int32, (most, 128), 1) < HEAD_DIM
@@ -413,9 +449,8 @@
     @pl.loop(0, HEADS // 2)
     def _(t):
         lane = pl.multiple_of(t * 128, 128)
-        for n, s in enumerate(chosen):
+        for s in range(seqs):
             rows = slice(s * length, (s + 1) * length)
-            placed = slice(n * length, (n + 1) * length)
             mine = slice(s * most, (s + 1) * most)
             away = away_ref[mine, :]
             q = both(q_ref[mine, pl.ds(lane, 128)])
@@ -430,20 +465,22 @@
             ds = (p * (dp - jnp.sum(dp * p, axis=-1, keepdims=True))).astype(LOW)
             dq = mm(ds, k)
             dq = (jnp.where(first_m, dq[:most], dq[most:]) * SCALE).astype(LOW)
-            rhs_ref[placed, pl.ds(lane, 128)] = mm_tn(hot_ref[mine, :], dq).astype(LOW)
-            rhs_ref[placed, pl.ds(D + lane, 128)] = (mm_tn(ds, q) * SCALE).astype(LOW)
-            rhs_ref[placed, pl.ds(2 * D + lane, 128)] = mm_tn(p.astype(LOW), da).astype(LOW)
-
-
-def attention_back(datt, q_m, qkv, pos, slopes, seqs, chosen):
-    tokens = qkv.shape[0]
-    listed = pos.shape[0]
-    return pl.pallas_call(
-        functools.partial(attention_back_kernel, seqs, listed // seqs, chosen),
-        out_shape=out((tokens // seqs * len(chosen), 3 * D), LOW),
-        in_specs=[SMEM] + [VMEM] * 4,
-        out_specs=VMEM,
-        scratch_shapes=[pltpu.VMEM((listed, tokens // seqs), F32), pltpu.VMEM((listed, tokens // seqs), LOW)],
+            rhs_ref[rows, pl.ds(lane, 128)] = mm_tn(hot_ref[mine, :], dq).astype(LOW)
+            rhs_ref[rows, pl.ds(D + lane, 128)] = (mm_tn(ds, q) * SCALE).astype(LOW)
+            rhs_ref[rows, pl.ds(2 * D + lane, 128)] = mm_tn(p.astype(LOW), da).astype(LOW)
+
+
+def attention_back(datt, q_m, qkv, pos, slopes, seqs, part):
+    tokens, listed = qkv.shape[0] // 2, pos.shape[0] // 2
+    length = tokens * 2 // seqs
+    mine = lambda shape: pl.BlockSpec(shape, lambda g: (part, 0))
+    return pl.pallas_call(
+        functools.partial(attention_back_kernel, seqs // 2, listed * 2 // seqs),
+        out_shape=out((tokens, 3 * D), LOW),
+        grid=(1,),
+        in_specs=[SMEM, mine((listed, D)), mine((listed, D)), mine((tokens, 3 * D)), mine((listed, 1))],
+        out_specs=pl.BlockSpec((tokens, 3 * D), lambda g: (0, 0)),
+        scratch_shapes=[pltpu.VMEM((listed, length), F32), pltpu.VMEM((listed, length), LOW)],
         compiler_params=BIG,
         cost_estimate=cost(8),
         name="attention_back",
@@ -632,14 +669,6 @@
     )(where, *pieces)
 
 
-def spread(piece, order):
-    got = {frozenset(): piece}
-    for step in (*order, "c"):
-        for key in list(got):
-            got[key | {step}] = send(got[key], step)
-    return [got[frozenset(n for n, b in zip("yxc", key) if b)] for key in KEYS]
-
-
 def on_block(hidden_in, w_qkv, w_out, w_up, w_down, gain_attn, shift_attn, gain_ffn, shift_ffn, grad_listed, positions, counts):
     seqs, length, width = hidden_in.shape
     tokens = seqs * length
@@ -653,19 +682,28 @@
     line = jnp.stack([attn_piece] + [send(attn_piece, r) for r in (1, 2, 3)])
     x = hidden_in.reshape(tokens, width)
     line, x_flip = lax.optimization_barrier((line, x.T))
-    halves = [
-        spread(line[:, start : start + size], order)
-        for (start, size), order in zip(HALVES, (("y", "x"), ("x", "y")))
-    ]
+    down_piece = after(lax.dynamic_slice_in_dim(w_down, j * ROWS, ROWS, axis=0), line)
+    down_line = jnp.stack([down_piece] + [send(down_piece, r) for r in (1, 2, 3)])
+    cuts = [line[:, start : start + size] for start, size in HALVES]
+    orders = (("y", "x"), ("x", "y"))
+    got = [{(): cut, (order[0],): send(cut, order[0])} for cut, order in zip(cuts, orders)]
+    got, down_line = lax.optimization_barrier((got, down_line))
+    for have, order in zip(got, orders):
+        for key in list(have):
+            have[(*key, order[1])] = send(have[key], order[1])
+    got, down_line = lax.optimization_barrier((got, down_line))
+    downs = [down_line[:, : ROWS // 2], down_line[:, ROWS // 2 :]]
+    downs = [jnp.stack([cut, send(cut, order[0])]) for cut, order in zip(downs, orders)]
+    for have in got:
+        for key in list(have):
+            have[(*key, "c")] = send(have[key], "c")
+    halves = []
+    for have, order in zip(got, orders):
+        flags = [dict(zip("yxc", key)) for key in KEYS]
+        halves.append([have[tuple(step for step in (*order, "c") if flag[step])] for flag in flags])
     lines = [half[n] for n in range(len(KEYS)) for half in halves]
-    ffn_piece = jnp.stack(
-        [
-            lax.dynamic_slice_in_dim(w_up, j * D, D, axis=1),
-            lax.dynamic_slice_in_dim(w_up, ff + j * D, D, axis=1),
-            lax.dynamic_slice_in_dim(w_down, j * ROWS, ROWS, axis=0),
-        ]
-    )
-    w_ffn = lax.all_gather(ffn_piece, AXES, axis=0, tiled=False).reshape(SHARDS, QUARTERS, 3, ROWS, D)
+    gu_piece = jnp.stack([lax.dynamic_slice_in_dim(w_up, start + j * D, D, axis=1) for start in (0, ff)])
+    w_gu = lax.all_gather(gu_piece, AXES, axis=0, tiled=False).reshape(SHARDS, QUARTERS, 2, ROWS, D)
     tails = jnp.stack([halves[1][n][:, 48, : 4 * ROWS] for n in range(2)])
     tails = jnp.where(i % 2 == 0, tails, tails[::-1])
     tails = jnp.roll(tails[:, ::-1], i // 2 + 1, axis=1)
@@ -675,14 +713,17 @@
     live = jnp.arange(most, dtype=jnp.int32)[None, :] < counts[:, None]
     dy = jnp.where(live[:, :, None], grad_listed, jnp.zeros_like(grad_listed)).reshape(seqs * most, width)
 
-    qkv, h1, att_m, h1_m, q_m, r1_m, w_attn = attention_forward(where, x, lines, norms, pos, slopes, seqs)
+    qkv, h1, att_m, h1_m, q_m, r1_m, w_attn = attention_forward(where, after(x, downs), lines, norms, pos, slopes, seqs)
+    downs_far, h1 = lax.optimization_barrier(([send(cut, order[1]) for cut, order in zip(downs, orders)], h1))
+    downs = [jnp.stack(pair) for pair in zip(downs, downs_far)]
+    down_all = assemble(where, (*downs, *[send(cut, "c") for cut in downs]))
     h_all = jnp.stack(share_dp(h1_m))
     h1, h_all = lax.optimization_barrier((h1, h_all))
-    layer_out, dr2, e2, small_ffn = ffn_forward(h1, w_ffn, norms, pos, dy, seqs)
-    act, to_gate, to_up = ffn_again(where, h_all, w_ffn)
+    layer_out, dr2, e2, small_ffn = ffn_forward(h1, w_gu, down_all, norms, pos, dy, seqs)
+    act, to_gate, to_up = ffn_again(where, h_all, w_gu)
     other = after(send(e2, "x"), act)
     e_all = jnp.stack([e2, send(e2, "c"), other, send(other, "c")])
-    dgate, dup, keep, away = ffn_back(where, e_all, to_gate, to_up, w_ffn)
+    dgate, dup, keep, away = ffn_back(where, e_all, to_gate, to_up, w_gu, down_all)
     part = add(keep, send(away, "c"))
     part, part_away = part[0], part[1].astype(LOW)
     keep_d, away_d = weight_grad(where, act, e_all)
@@ -693,12 +734,11 @@
     keep_u, away_u = weight_grad(where, after(h_all, (away_g, came)), dup)
     got_u = send(away_u, "y")
     dr1, low, datt, small_attn = norm_back_call(dr2, part, after(came, away_u), r1_m, w_attn, norms)
-    half = seqs // 2
-    rhs0 = attention_back(datt, q_m, qkv, pos, slopes, seqs, tuple(range(half)))
+    rhs0 = attention_back(datt, q_m, qkv, pos, slopes, seqs, 0)
     got_d, rhs0 = lax.optimization_barrier((got_d, rhs0))
     parts_d = line_parts(keep_d, got_d)
     line_d = line_send(parts_d)
-    rhs1 = attention_back(after(datt, (rhs0, parts_d)), q_m, qkv, pos, slopes, seqs, tuple(range(half, seqs)))
+    rhs1 = attention_back(after(datt, (rhs0, parts_d)), q_m, qkv, pos, slopes, seqs, 1)
     line_d, got_g, rhs1 = lax.optimization_barrier((line_d, got_g, rhs1))
     parts_g = line_parts(keep_g, got_g)
     line_g = line_send(parts_g)

time: 299 us -> 456 us (1.53)
  Pallas kernels: 107 us -> 250 us
  starting transfers between devices: 49.9 us -> 67.7 us
  waiting for transfers between devices: 100 us -> 92.2 us
    pallas_call x2 -> x3, Pallas kernels: 19.9 us -> 164 us  [the longest x1 145 us: assemble(): pl.pallas_call(assemble_kernel, out_shape=out((SHARDS, QUARTERS, ROWS, D)...]
    all_gather x1, waiting for transfers between devices: 30.3 us -> 0.02 us  [on_block(): lax.all_gather(gu_piece, AXES, axis=0, tiled=False)]
    ppermute x53 -> x62, waiting for transfers between devices: 69.9 us -> 92.1 us  [send(): return lax.ppermute(value, AXES, MOVES[move])]
    ppermute x53 -> x62, starting transfers between devices: 49.8 us -> 67.7 us  [send(): return lax.ppermute(value, AXES, MOVES[move])]
  transfers between devices with their start and end apart: 54 -> 63, of which waited for: 26 -> 23; matrix products, arithmetic and copies ran while one was open for 7% -> 5% of each run, Pallas kernels for 27% -> 49%
where the time goes in v9:
time: 456 us; the launch traced here: 455 us
  Pallas kernels  250 us (55%)
  waiting for transfers between devices  92.2 us (20%)
  starting transfers between devices  67.7 us (15%)
  other arithmetic  18.4 us (4%)
  between operations  14.9 us (3%)
  local copies, waits for them, and re-layouts  11.9 us (3%)
    pallas_call x1, Pallas kernels, assemble(): pl.pallas_call(assemble_kernel, out_shape=out((SHARDS, QUARTERS, ROWS, D)...  145 us
    ppermute x62, waiting for transfers between devices, send(): return lax.ppermute(value, AXES, MOVES[move])  92.1 us
    ppermute x62, starting transfers between devices, send(): return lax.ppermute(value, AXES, MOVES[move])  67.7 us
    pallas_call x2, Pallas kernels, attention_back(): pl.pallas_call(functools.partial(attention_back_kernel, seqs // 2, listed...  18.8 us
    pallas_call x1, Pallas kernels, attention_forward(): pl.pallas_call(functools.partial(attention_kernel, seqs, listed // seqs),...  17.8 us
    pallas_call x1, Pallas kernels, ffn_forward(): pl.pallas_call(functools.partial(ffn_kernel, seqs, listed // seqs), out_s...  17 us
    pallas_call x3, Pallas kernels, weight_grad(): pl.pallas_call(weight_grad_kernel, out_shape=(out(shape, LOW), out(shape,...  11.6 us
  transfers between devices with their start and end apart: 63, of which 23 were waited for; matrix products, arithmetic and copies ran while one was open for 5% of the time, Pallas kernels for 49%

profile of v9, /device:TPU:0, one launch (start us, length us, event | category | flops | bytes accessed | tf_op | source)
XLA Modules:
  0.0 455.2 jit_solution(16769920899237488807)
XLA Ops:
  9.5 4.1 collective-permute-start.1
  17.8 7.7 %collective-permute-done.1 = bf16[104,768]{1,0:T(8,128)(2,1)S(1)} collective-permute-done((bf16[104,768]{1,0:T(8,128)(2,1)S(1)}, bf16[104,768]{1,0:T(8,128)(2,1)S(1)}, u32[]{:S(2)}, u32[]{:S(2)}) %collective-permute-start.1) | collective-permute-done | bytes 159776 | tf_op jit(solution)/shard_map/ppermute | solution.py:599
  33.1 10.4 %collective-permute-start.6 = (bf16[96,768]{1,0:T(8,128)(2,1)S(1)}, bf16[96,768]{1,0:T(8,128)(2,1)S(1)}, u32[]{:S(2)}, u32[]{:S(2)}) collective-permute-start(bf16[96,768]{1,0:T(8,128)(2,1)S(1)} %constant_dynamic-slice_fusion), channel_id=1, source_target_pairs={{0,16},{1,17},{2,18},{3,19},{4,20},{5,21},{6,22},{7,23},{8,24},{9,... | collective-permute-start | bytes 442376 | tf_op jit(solution)/shard_map/ppermute | solution.py:599
  45.5 21.1 %collective-permute-done.6 = bf16[96,768]{1,0:T(8,128)(2,1)S(1)} collective-permute-done((bf16[96,768]{1,0:T(8,128)(2,1)S(1)}, bf16[96,768]{1,0:T(8,128)(2,1)S(1)}, u32[]{:S(2)}, u32[]{:S(2)}) %collective-permute-start.6) | collective-permute-done | bytes 147488 | tf_op jit(solution)/shard_map/ppermute | solution.py:599
  70.9 10.1 %collective-permute-done.8.rest_4_ = bf16[4,48,768]{2,1,0:T(8,128)(2,1)} collective-permute-done((bf16[4,48,768]{2,1,0:T(8,128)(2,1)S(1)}, bf16[4,48,768]{2,1,0:T(8,128)(2,1)}, u32[]{:S(2)}, u32[]{:S(2)}) %collective-permute-start.8) | collective-permute-done | bytes 294944 | tf_op jit(solution)/shard_map/ppermute | solution.py:599
  81.0 9.5 %collective-permute-done.9.rest_6_ = bf16[4,48,768]{2,1,0:T(8,128)(2,1)} collective-permute-done((bf16[4,48,768]{2,1,0:T(8,128)(2,1)S(1)}, bf16[4,48,768]{2,1,0:T(8,128)(2,1)}, u32[]{:S(2)}, u32[]{:S(2)}) %collective-permute-start.9) | collective-permute-done | bytes 294944 | tf_op jit(solution)/shard_map/ppermute | solution.py:599
  91.5 8.9 %collective-permute-done.14 = bf16[4,48,768]{2,1,0:T(8,128)(2,1)S(1)} collective-permute-done((bf16[4,48,768]{2,1,0:T(8,128)(2,1)S(1)}, bf16[4,48,768]{2,1,0:T(8,128)(2,1)S(1)}, u32[]{:S(2)}, u32[]{:S(2)}) %collective-permute-start.14) | collective-permute-done | bytes 294944 | tf_op jit(solution)/shard_map/ppermute | solution.py:599
  109.5 17.8 %attention_forward.1 = (bf16[512,2304]{1,0:T(8,128)(2,1)}, f32[512,768]{1,0:T(8,128)}, bf16[128,768]{1,0:T(8,128)(2,1)}, bf16[128,768]{1,0:T(8,128)(2,1)}, bf16[...) custom-call(s32[5]{0:T(128)} %stack.159.where_ref, ...), custom_call_target="tpu_custom_call" | custom-call | bytes 60000000 | tf_op jit(solution)/shard_map/attention_forward/pallas_call | solution.py:164
  131.1 5.3 %collective-permute-done.25 = bf16[128,768]{1,0:T(8,128)(2,1)S(1)} collective-permute-done((bf16[128,768]{1,0:T(8,128)(2,1)S(1)}, bf16[128,768]{1,0:T(8,128)(2,1)S(1)}, u32[]{:S(2)}, u32[]{:S(2)}) %collective-permute-start.25) | collective-permute-done | bytes 196640 | tf_op jit(solution)/shard_map/ppermute | solution.py:599
  139.9 144.7 %assemble.1.down_ref = bf16[8,4,96,768]{3,2,1,0:T(8,128)(2,1)} custom-call(s32[5]{0:T(128)} %stack.159.where_ref, bf16[2,2,4,48,768]{4,3,2,1,0:T(8,128)(2,1)} %copy-done.4, bf16[2,2,4,48,768]{4,3,2,1,0:T(8,128)(2,1)} %copy-done.3, bf16[2,2,4,48,768]{4,3,2,1,0:T(8,128)(2,1)} %collective-permute-done.27.rest_2_, bf16[2,2,4,48,768]{4,3,2,1,0:T(8,128)(2,1)} %copy-done.8), custom_call_target="tpu_custom_call" | custom-call | bytes 9000000 | tf_op jit(solution)/shard_map/assemble/pallas_call | solution.py:208
  284.7 17.0 %ffn_forward.1 = (bf16[512,768]{1,0:T(8,128)(2,1)}, f32[128,768]{1,0:T(8,128)}, bf16[128,768]{1,0:T(8,128)(2,1)}, f32[2,768]{1,0:T(2,128)}) custom-call(f32[512,768]{1,0:T(8,128)} %get-tuple-element.127.h1_ref, bf16[8,4,2,96,768]{4,3,2,1,0:T(8,128)(2,1)} %bitcast.150, bf16[8,4,2,96,768]{4,3,2,1,0:T(8,128)(2,1)} %bitcast.151, ...), custom_call_target="tpu_custom_call" | custom-call | bytes 48000000 | tf_op jit(solution)/shard_map/ffn_forward/pallas_call | solution.py:268
  303.5 6.6 %ffn_again.1 = (bf16[512,768]{1,0:T(8,128)(2,1)}, f32[512,768]{1,0:T(8,128)}, f32[512,768]{1,0:T(8,128)}) custom-call(s32[5]{0:T(128)} %stack.159.where_ref, bf16[4,128,768]{2,1,0:T(8,128)(2,1)} %pad_maximum_fusion.3.h_ref.a_ref, bf16[8,4,2,96,768]{4,3,2,1,0:T(8,128)(2,1)} %bitcast.152, bf16[8,4,2,96,768]{4,3,2,1,0:T(8,128)(2,1)} %bitcast.153), custom_call_target="tpu_custom_call" | custom-call | bytes 18000000 | tf_op jit(solution)/shard_map/ffn_again/pallas_call | solution.py:324
  312.7 7.4 %ffn_back.1 = (bf16[512,768]{1,0:T(8,128)(2,1)}, bf16[512,768]{1,0:T(8,128)(2,1)}, f32[2,128,768]{2,1,0:T(8,128)}, bf16[2,128,768]{2,1,0:T(8,128)(2,1)}) custom-call(s32[5]{0:T(128)} %stack.159.where_ref, bf16[4,128,768]{2,1,0:T(8,128)(2,1)} %pad_maximum_fusion.4.b_ref.e_ref, f32[512,768]{1,0:T(8,128)} %get-tuple-element.138.to_gate_ref, ...), custom_call_target="tpu_custom_call" | custom-call | bytes 21000000 | tf_op jit(solution)/shard_map/ffn_back/pallas_call | solution.py:359
  320.5 3.9 weight_grad.3
  326.6 3.8 weight_grad.4
  333.0 3.9 weight_grad.5
  340.4 9.5 %attention_back.2.rhs0_ref = bf16[256,2304]{1,0:T(8,128)(2,1)} custom-call(f32[12]{0:T(128)} %multiply_exponential_fusion.slope_ref, bf16[128,768]{1,0:T(8,128)(2,1)} %get-tuple-element.157.datt_ref, bf16[128,768]{1,0:T(8,128)(2,1)} %get-tuple-element.152.q_ref, bf16[512,2304]{1,0:T(8,128)(2,1)} %get-tuple-element.153.qkv_ref, s32[128,1]{1,0:T(8,128)} %reshape.140.pos_ref), custom_call_target="tpu_custom_call" | custom-call | bytes 24000000 | tf_op jit(solution)/shard_map/attention_back/pallas_call | solution.py:477
  350.1 5.7 %collective-permute-start.36 = (bf16[96,768]{1,0:T(8,128)(2,1)S(1)}, bf16[96,768]{1,0:T(8,128)(2,1)S(1)}, u32[]{:S(2)}, u32[]{:S(2)}) collective-permute-start(bf16[96,768]{1,0:T(8,128)(2,1)S(1)} %get-tuple-element.211), channel_id=1, source_target_pairs={{0,16},{1,17},{2,18},{3,19},{4,20},{5,21},{6,22},{7,23},{8,24},{9,... | collective-permute-start | bytes 442376 | tf_op jit(solution)/shard_map/ppermute | solution.py:599
  357.8 9.3 %attention_back.3.rhs1_ref = bf16[256,2304]{1,0:T(8,128)(2,1)} custom-call(f32[12]{0:T(128)} %multiply_exponential_fusion.slope_ref, bf16[128,768]{1,0:T(8,128)(2,1)} %get-tuple-element.157.datt_ref, bf16[128,768]{1,0:T(8,128)(2,1)} %get-tuple-element.152.q_ref, bf16[512,2304]{1,0:T(8,128)(2,1)} %get-tuple-element.153.qkv_ref, s32[128,1]{1,0:T(8,128)} %reshape.140.pos_ref), custom_call_target="tpu_custom_call" | custom-call | bytes 24000000 | tf_op jit(solution)/shard_map/attention_back/pallas_call | solution.py:477
  370.5 8.8 %attention_grads.1 = (bf16[2,2,4,48,768]{4,3,2,1,0:T(8,128)(2,1)}, bf16[2,2,4,64,768]{4,3,2,1,0:T(8,128)(2,1)}, bf16[2,2,4,48,768]{4,3,2,1,0:T(8,128)(2,1)}, bf16[2,2,4,64,768]{4,3,2,1,0:T(8,128)(2,1)}) custom-call(s32[5]{0:T(128)} %stack.159.where_ref, bf16[768,512]{1,0:T(8,128)(2,1)} %bitcast.156, bf16[256,2304]{1,0:T(8,128)(2,1)} %attention_back.2.rhs0_ref, ...), custom_call_target="tpu_custom_call" | custom-call | bytes 30000000 | tf_op jit(solution)/shard_map/attention_grads/pallas_call | solution.py:530
  395.8 3.9 collective-permute-start.52
  400.7 8.3 %input_grad.1 = f32[512,768]{1,0:T(8,128)} custom-call(bf16[256,2304]{1,0:T(8,128)(2,1)} %attention_back.2.rhs0_ref, bf16[256,2304]{1,0:T(8,128)(2,1)} %attention_back.3.rhs1_ref, bf16[8,4,96,768]{3,2,1,0:T(8,128)(2,1)} %get-tuple-element.150.w_ref, f32[128,768]{1,0:T(8,128)} %get-tuple-element.173.dr1_ref, s32[4,32]{1,0:T(4,128)} %pos_ref.1), custom_call_target="tpu_custom_call" | custom-call | bytes 24000000 | tf_op jit(solution)/shard_map/input_grad/pallas_call | solution.py:562
  422.8 4.0 collective-permute-start.55
  431.9 5.7 %collective-permute-done.54 = bf16[112,768]{1,0:T(8,128)(2,1)S(1)} collective-permute-done((bf16[112,768]{1,0:T(8,128)(2,1)S(1)}, bf16[112,768]{1,0:T(8,128)(2,1)S(1)}, u32[]{:S(2)}, u32[]{:S(2)}) %collective-permute-start.54) | collective-permute-done | bytes 172064 | tf_op jit(solution)/shard_map/ppermute | solution.py:599
  (289 shorter events, 102.6 us)
Async XLA Ops:
  7.3 277.4 %all-gather.3.cloned.1.call-start = ((), (), s32[]{:S(2)}) async-start(), calls=%async_computation | async-start | bytes 9732096 | tf_op jit(solution)/shard_map/all_gather | solution.py:706
  9.5 16.0 %collective-permute-start.1 = (bf16[104,768]{1,0:T(8,128)(2,1)S(1)}, bf16[104,768]{1,0:T(8,128)(2,1)S(1)}, u32[]{:S(2)}, u32[]{:S(2)}) collective-permute-start(bf16[104,768]{1,0:T(8,128)(2,1)S(1)} %get-tuple-element.231), channel_id=1, source_target_pairs={{0,16},{1,17},{2,18},{3,19},{4,20},{5,21},{6,22},{7,23},{8,24},{9,... | collective-permute-start | bytes 479240 | tf_op jit(solution)/shard_map/ppermute | solution.py:599
  15.3 12.6 %collective-permute-start.2 = (bf16[104,768]{1,0:T(8,128)(2,1)S(1)}, bf16[104,768]{1,0:T(8,128)(2,1)S(1)}, u32[]{:S(2)}, u32[]{:S(2)}) collective-permute-start(bf16[104,768]{1,0:T(8,128)(2,1)S(1)} %get-tuple-element.231), channel_id=1, source_target_pairs={{0,24},{1,25},{2,26},{3,27},{4,28},{5,29},{6,30},{7,31},{8,0},{9,1... | collective-permute-start | bytes 479240 | tf_op jit(solution)/shard_map/ppermute | solution.py:599
  28.1 38.7 %collective-permute-start.3 = (bf16[4,48,768]{2,1,0:T(8,128)(2,1)S(1)}, bf16[4,48,768]{2,1,0:T(8,128)(2,1)S(1)}, u32[]{:S(2)}, u32[]{:S(2)}) collective-permute-start(bf16[4,48,768]{2,1,0:T(8,128)(2,1)S(1)} %slice.171.rest_0_), channel_id=1, source_target_pairs={{0,4},{1,5},{2,6},{3,7},{4,0},{5,1},{6,2},{7,3},{8,12},{9,13},{10,... | collective-permute-start | bytes 884744 | tf_op jit(solution)/shard_map/ppermute | solution.py:599
  29.7 37.0 %collective-permute-start.4 = (bf16[4,56,768]{2,1,0:T(8,128)(2,1)S(1)}, bf16[4,56,768]{2,1,0:T(8,128)(2,1)}, u32[]{:S(2)}, u32[]{:S(2)}) collective-permute-start(bf16[4,56,768]{2,1,0:T(8,128)(2,1)S(1)} %slice.172.rest_1_), channel_id=1, source_target_pairs={{0,2},{1,3},{2,0},{3,1},{4,6},{5,7},{6,4},{7,5},{8,10},{9,11},{10,... | collective-permute-start | bytes 1032200 | tf_op jit(solution)/shard_map/ppermute | solution.py:599
  31.2 14.3 %collective-permute-start.7 = (bf16[96,768]{1,0:T(8,128)(2,1)S(1)}, bf16[96,768]{1,0:T(8,128)(2,1)S(1)}, u32[]{:S(2)}, u32[]{:S(2)}) collective-permute-start(bf16[96,768]{1,0:T(8,128)(2,1)S(1)} %constant_dynamic-slice_fusion), channel_id=1, source_target_pairs={{0,24},{1,25},{2,26},{3,27},{4,28},{5,29},{6,30},{7,31},{8,0},{9,1... | collective-permute-start | bytes 442376 | tf_op jit(solution)/shard_map/ppermute | solution.py:599
  33.1 33.5 %collective-permute-start.6 = (bf16[96,768]{1,0:T(8,128)(2,1)S(1)}, bf16[96,768]{1,0:T(8,128)(2,1)S(1)}, u32[]{:S(2)}, u32[]{:S(2)}) collective-permute-start(bf16[96,768]{1,0:T(8,128)(2,1)S(1)} %constant_dynamic-slice_fusion), channel_id=1, source_target_pairs={{0,16},{1,17},{2,18},{3,19},{4,20},{5,21},{6,22},{7,23},{8,24},{9,... | collective-permute-start | bytes 442376 | tf_op jit(solution)/shard_map/ppermute | solution.py:599
  43.6 23.1 %collective-permute-start.5 = (bf16[96,768]{1,0:T(8,128)(2,1)S(1)}, bf16[96,768]{1,0:T(8,128)(2,1)S(1)}, u32[]{:S(2)}, u32[]{:S(2)}) collective-permute-start(bf16[96,768]{1,0:T(8,128)(2,1)S(1)} %constant_dynamic-slice_fusion), channel_id=1, source_target_pairs={{0,8},{1,9},{2,10},{3,11},{4,12},{5,13},{6,14},{7,15},{8,16},{9,17... | collective-permute-start | bytes 442376 | tf_op jit(solution)/shard_map/ppermute | solution.py:599
  66.8 23.7 %collective-permute-start.11 = (bf16[4,56,768]{2,1,0:T(8,128)(2,1)S(1)}, bf16[4,56,768]{2,1,0:T(8,128)(2,1)S(1)}, u32[]{:S(2)}, u32[]{:S(2)}) collective-permute-start(bf16[4,56,768]{2,1,0:T(8,128)(2,1)S(1)} %slice.172.rest_1_), channel_id=1, source_target_pairs={{0,4},{1,5},{2,6},{3,7},{4,0},{5,1},{6,2},{7,3},{8,12},{9,13},{10,... | collective-permute-start | bytes 1032200 | tf_op jit(solution)/shard_map/ppermute | solution.py:599
  66.8 23.7 %collective-permute-start.10 = (bf16[4,56,768]{2,1,0:T(8,128)(2,1)}, bf16[4,56,768]{2,1,0:T(8,128)(2,1)}, u32[]{:S(2)}, u32[]{:S(2)}) collective-permute-start(bf16[4,56,768]{2,1,0:T(8,128)(2,1)} %collective-permute-done.4.rest_5_), channel_id=1, source_target_pairs={{0,4},{1,5},{2,6},{3,7},{4,0},{5,1},{6,2},{7,3},{8,12},{9,13},{10,... | collective-permute-start | bytes 1032200 | tf_op jit(solution)/shard_map/ppermute | solution.py:599
  68.8 21.6 %collective-permute-start.9 = (bf16[4,48,768]{2,1,0:T(8,128)(2,1)S(1)}, bf16[4,48,768]{2,1,0:T(8,128)(2,1)}, u32[]{:S(2)}, u32[]{:S(2)}) collective-permute-start(bf16[4,48,768]{2,1,0:T(8,128)(2,1)S(1)} %collective-permute-done.3.rest_2_), channel_id=1, source_target_pairs={{0,2},{1,3},{2,0},{3,1},{4,6},{5,7},{6,4},{7,5},{8,10},{9,11},{10,... | collective-permute-start | bytes 884744 | tf_op jit(solution)/shard_map/ppermute | solution.py:599
  91.4 14.9 %collective-permute-start.20 = (bf16[4,48,768]{2,1,0:T(8,128)(2,1)}, bf16[4,48,768]{2,1,0:T(8,128)(2,1)}, u32[]{:S(2)}, u32[]{:S(2)}) collective-permute-start(bf16[4,48,768]{2,1,0:T(8,128)(2,1)} %collective-permute-done.8.rest_4_), channel_id=1, source_target_pairs={{0,1},{1,0},{2,3},{3,2},{4,5},{5,4},{6,7},{7,6},{8,9},{9,8},{10,11... | collective-permute-start | bytes 884744 | tf_op jit(solution)/shard_map/ppermute | solution.py:599
  101.9 25.3 %collective-permute-start.15 = (bf16[2,4,48,768]{3,2,1,0:T(8,128)(2,1)}, bf16[2,4,48,768]{3,2,1,0:T(8,128)(2,1)S(1)}, u32[]{:S(2)}, u32[]{:S(2)}) collective-permute-start(bf16[2,4,48,768]{3,2,1,0:T(8,128)(2,1)} %get-tuple-element.219), channel_id=1, source_target_pairs={{0,4},{1,5},{2,6},{3,7},{4,0},{5,1},{6,2},{7,3},{8,12},{9,13},{10,... | collective-permute-start | bytes 1769480 | tf_op jit(solution)/shard_map/ppermute | solution.py:599
  103.4 23.9 %collective-permute-start.13 = (bf16[2,4,48,768]{3,2,1,0:T(8,128)(2,1)S(1)}, bf16[2,4,48,768]{3,2,1,0:T(8,128)(2,1)}, u32[]{:S(2)}, u32[]{:S(2)}) collective-permute-start(bf16[2,4,48,768]{3,2,1,0:T(8,128)(2,1)S(1)} %get-tuple-element.221), channel_id=1, source_target_pairs={{0,2},{1,3},{2,0},{3,1},{4,6},{5,7},{6,4},{7,5},{8,10},{9,11},{10,... | collective-permute-start | bytes 1769480 | tf_op jit(solution)/shard_map/ppermute | solution.py:599
  324.4 25.6 %collective-permute-start.32 = (bf16[4,96,768]{2,1,0:T(8,128)(2,1)}, bf16[4,96,768]{2,1,0:T(8,128)(2,1)S(1)}, u32[]{:S(2)}, u32[]{:S(2)}) collective-permute-start(bf16[4,96,768]{2,1,0:T(8,128)(2,1)} %get-tuple-element.136), channel_id=1, source_target_pairs={{0,4},{1,5},{2,6},{3,7},{4,0},{5,1},{6,2},{7,3},{8,12},{9,13},{10,... | collective-permute-start | bytes 1769480 | tf_op jit(solution)/shard_map/ppermute | solution.py:599
  330.4 37.9 %collective-permute-start.38 = (bf16[4,96,768]{2,1,0:T(8,128)(2,1)}, bf16[4,96,768]{2,1,0:T(8,128)(2,1)S(1)}, u32[]{:S(2)}, u32[]{:S(2)}) collective-permute-start(bf16[4,96,768]{2,1,0:T(8,128)(2,1)} %get-tuple-element.144), channel_id=1, source_target_pairs={{0,4},{1,5},{2,6},{3,7},{4,0},{5,1},{6,2},{7,3},{8,12},{9,13},{10,... | collective-permute-start | bytes 1769480 | tf_op jit(solution)/shard_map/ppermute | solution.py:599
  336.9 44.7 %collective-permute-start.42 = (bf16[4,96,768]{2,1,0:T(8,128)(2,1)}, bf16[4,96,768]{2,1,0:T(8,128)(2,1)S(1)}, u32[]{:S(2)}, u32[]{:S(2)}) collective-permute-start(bf16[4,96,768]{2,1,0:T(8,128)(2,1)} %get-tuple-element.147), channel_id=1, source_target_pairs={{0,4},{1,5},{2,6},{3,7},{4,0},{5,1},{6,2},{7,3},{8,12},{9,13},{10,... | collective-permute-start | bytes 1769480 | tf_op jit(solution)/shard_map/ppermute | solution.py:599
  350.0 17.0 %collective-permute-start.37 = (bf16[96,768]{1,0:T(8,128)(2,1)S(1)}, bf16[96,768]{1,0:T(8,128)(2,1)S(1)}, u32[]{:S(2)}, u32[]{:S(2)}) collective-permute-start(bf16[96,768]{1,0:T(8,128)(2,1)S(1)} %get-tuple-element.210), channel_id=1, source_target_pairs={{0,24},{1,25},{2,26},{3,27},{4,28},{5,29},{6,30},{7,31},{8,0},{9,1... | collective-permute-start | bytes 442376 | tf_op jit(solution)/shard_map/ppermute | solution.py:599
  350.1 18.2 %collective-permute-start.36 = (bf16[96,768]{1,0:T(8,128)(2,1)S(1)}, bf16[96,768]{1,0:T(8,128)(2,1)S(1)}, u32[]{:S(2)}, u32[]{:S(2)}) collective-permute-start(bf16[96,768]{1,0:T(8,128)(2,1)S(1)} %get-tuple-element.211), channel_id=1, source_target_pairs={{0,16},{1,17},{2,18},{3,19},{4,20},{5,21},{6,22},{7,23},{8,24},{9,... | collective-permute-start | bytes 442376 | tf_op jit(solution)/shard_map/ppermute | solution.py:599
  387.4 23.0 %collective-permute-start.46 = (bf16[2,4,64,768]{3,2,1,0:T(8,128)(2,1)S(1)}, bf16[2,4,64,768]{3,2,1,0:T(8,128)(2,1)}, u32[]{:S(2)}, u32[]{:S(2)}) collective-permute-start(bf16[2,4,64,768]{3,2,1,0:T(8,128)(2,1)S(1)} %fusion.1), channel_id=1, source_target_pairs={{0,4},{1,5},{2,6},{3,7},{4,0},{5,1},{6,2},{7,3},{8,12},{9,13},{10,... | collective-permute-start | bytes 2359304 | tf_op jit(solution)/shard_map/ppermute | solution.py:599
  390.0 19.0 %collective-permute-start.44 = (bf16[2,4,48,768]{3,2,1,0:T(8,128)(2,1)}, bf16[2,4,48,768]{3,2,1,0:T(8,128)(2,1)}, u32[]{:S(2)}, u32[]{:S(2)}) collective-permute-start(bf16[2,4,48,768]{3,2,1,0:T(8,128)(2,1)} %fusion.3), channel_id=1, source_target_pairs={{0,2},{1,3},{2,0},{3,1},{4,6},{5,7},{6,4},{7,5},{8,10},{9,11},{10,... | collective-permute-start | bytes 1769480 | tf_op jit(solution)/shard_map/ppermute | solution.py:599
  392.1 22.5 %collective-permute-start.49 = (bf16[96,768]{1,0:T(8,128)(2,1)}, bf16[96,768]{1,0:T(8,128)(2,1)}, u32[]{:S(2)}, u32[]{:S(2)}) collective-permute-start(bf16[96,768]{1,0:T(8,128)(2,1)} %fusion.20), channel_id=1, source_target_pairs={{0,0},{1,8},{2,16},{3,24},{4,1},{5,9},{6,17},{7,25},{8,2},{9,10},{... | collective-permute-start | bytes 442376 | tf_op jit(solution)/shard_map/ppermute | solution.py:599
  395.8 18.9 %collective-permute-start.52 = (bf16[96,768]{1,0:T(8,128)(2,1)}, bf16[96,768]{1,0:T(8,128)(2,1)}, u32[]{:S(2)}, u32[]{:S(2)}) collective-permute-start(bf16[96,768]{1,0:T(8,128)(2,1)} %get-tuple-element.204), channel_id=1, source_target_pairs={{0,24},{1,25},{2,26},{3,27},{4,28},{5,29},{6,30},{7,31},{8,0},{9,1... | collective-permute-start | bytes 442376 | tf_op jit(solution)/shard_map/ppermute | solution.py:599
  399.6 17.5 %collective-permute-start.51 = (bf16[96,768]{1,0:T(8,128)(2,1)}, bf16[96,768]{1,0:T(8,128)(2,1)}, u32[]{:S(2)}, u32[]{:S(2)}) collective-permute-start(bf16[96,768]{1,0:T(8,128)(2,1)} %get-tuple-element.205), channel_id=1, source_target_pairs={{0,16},{1,17},{2,18},{3,19},{4,20},{5,21},{6,22},{7,23},{8,24},{9,... | collective-permute-start | bytes 442376 | tf_op jit(solution)/shard_map/ppermute | solution.py:599
  (94 other events, 867.5 us)
Sparse Core Ops, SparseCore 0:
  11.0 106.0 all-gather.2

commit v10 on v8

--- a/solution.py
+++ b/solution.py
@@ -81,7 +81,7 @@
 
 
 EXTRA = 8
-TAIL = 16
+TAIL = 8
 HALVES = ((0, 48), (48, 56))
 KEYS = [(ry, rx, rc) for rc in (0, 1) for rx in (0, 1) for ry in (0, 1)]
 
@@ -398,7 +398,7 @@
     )(dr2, part, came, r1_m, w_attn, norms)
 
 
-def attention_back_kernel(seqs, most, chosen, slope_ref, datt_ref, q_ref, qkv_ref, pos_ref, rhs_ref, away_ref, hot_ref):
+def attention_back_kernel(seqs, most, slope_ref, datt_ref, q_ref, qkv_ref, pos_ref, rhs_ref, away_ref, hot_ref):
     length = qkv_ref.shape[0] // seqs
     listed = seqs * most
     first_m = lax.broadcasted_iota(jnp.int32, (most, 128), 1) < HEAD_DIM
@@ -413,9 +413,8 @@
     @pl.loop(0, HEADS // 2)
     def _(t):
         lane = pl.multiple_of(t * 128, 128)
-        for n, s in enumerate(chosen):
+        for s in range(seqs):
             rows = slice(s * length, (s + 1) * length)
-            placed = slice(n * length, (n + 1) * length)
             mine = slice(s * most, (s + 1) * most)
             away = away_ref[mine, :]
             q = both(q_ref[mine, pl.ds(lane, 128)])
@@ -430,20 +429,22 @@
             ds = (p * (dp - jnp.sum(dp * p, axis=-1, keepdims=True))).astype(LOW)
             dq = mm(ds, k)
             dq = (jnp.where(first_m, dq[:most], dq[most:]) * SCALE).astype(LOW)
-            rhs_ref[placed, pl.ds(lane, 128)] = mm_tn(hot_ref[mine, :], dq).astype(LOW)
-            rhs_ref[placed, pl.ds(D + lane, 128)] = (mm_tn(ds, q) * SCALE).astype(LOW)
-            rhs_ref[placed, pl.ds(2 * D + lane, 128)] = mm_tn(p.astype(LOW), da).astype(LOW)
-
-
-def attention_back(datt, q_m, qkv, pos, slopes, seqs, chosen):
-    tokens = qkv.shape[0]
-    listed = pos.shape[0]
-    return pl.pallas_call(
-        functools.partial(attention_back_kernel, seqs, listed // seqs, chosen),
-        out_shape=out((tokens // seqs * len(chosen), 3 * D), LOW),
-        in_specs=[SMEM] + [VMEM] * 4,
-        out_specs=VMEM,
-        scratch_shapes=[pltpu.VMEM((listed, tokens // seqs), F32), pltpu.VMEM((listed, tokens // seqs), LOW)],
+            rhs_ref[rows, pl.ds(lane, 128)] = mm_tn(hot_ref[mine, :], dq).astype(LOW)
+            rhs_ref[rows, pl.ds(D + lane, 128)] = (mm_tn(ds, q) * SCALE).astype(LOW)
+            rhs_ref[rows, pl.ds(2 * D + lane, 128)] = mm_tn(p.astype(LOW), da).astype(LOW)
+
+
+def attention_back(datt, q_m, qkv, pos, slopes, seqs, part):
+    tokens, listed = qkv.shape[0] // 2, pos.shape[0] // 2
+    length = tokens * 2 // seqs
+    mine = lambda shape: pl.BlockSpec(shape, lambda g: (part, 0))
+    return pl.pallas_call(
+        functools.partial(attention_back_kernel, seqs // 2, listed * 2 // seqs),
+        out_shape=out((tokens, 3 * D), LOW),
+        grid=(1,),
+        in_specs=[SMEM, mine((listed, D)), mine((listed, D)), mine((tokens, 3 * D)), mine((listed, 1))],
+        out_specs=pl.BlockSpec((tokens, 3 * D), lambda g: (0, 0)),
+        scratch_shapes=[pltpu.VMEM((listed, length), F32), pltpu.VMEM((listed, length), LOW)],
         compiler_params=BIG,
         cost_estimate=cost(8),
         name="attention_back",
@@ -693,12 +694,11 @@
     keep_u, away_u = weight_grad(where, after(h_all, (away_g, came)), dup)
     got_u = send(away_u, "y")
     dr1, low, datt, small_attn = norm_back_call(dr2, part, after(came, away_u), r1_m, w_attn, norms)
-    half = seqs // 2
-    rhs0 = attention_back(datt, q_m, qkv, pos, slopes, seqs, tuple(range(half)))
+    rhs0 = attention_back(datt, q_m, qkv, pos, slopes, seqs, 0)
     got_d, rhs0 = lax.optimization_barrier((got_d, rhs0))
     parts_d = line_parts(keep_d, got_d)
     line_d = line_send(parts_d)
-    rhs1 = attention_back(after(datt, (rhs0, parts_d)), q_m, qkv, pos, slopes, seqs, tuple(range(half, seqs)))
+    rhs1 = attention_back(after(datt, (rhs0, parts_d)), q_m, qkv, pos, slopes, seqs, 1)
     line_d, got_g, rhs1 = lax.optimization_barrier((line_d, got_g, rhs1))
     parts_g = line_parts(keep_g, got_g)
     line_g = line_send(parts_g)
@@ -710,8 +710,6 @@
     g_down = send(line_add(keep_d, got_d, line_d), "down")
     away0, away1 = add(keep0[1], came0[1]).astype(LOW), add(keep1[1], came1[1]).astype(LOW)
     got0, got1 = send(away0, "x"), send(away1, "y")
-    grad_in = input_grad(rhs0, after(rhs1, (away0, away1)), w_attn, dr1, positions)
-    got0, got1, grad_in = lax.optimization_barrier((got0, got1, grad_in))
     total0 = add(keep0[0], came0[0]) + got0.astype(F32)
     total1 = add(keep1[0], came1[0]) + got1.astype(F32)
     away0, away1 = total0[1].astype(LOW), total1[1].astype(LOW)
@@ -723,7 +721,8 @@
     parts = [total[r].astype(LOW) for r in (1, 2, 3)]
     line_a = line_send(parts)
     other = send(g_ffn, "x")
-    line_a, other = lax.optimization_barrier((line_a, other))
+    grad_in = input_grad(rhs0, after(rhs1, parts), w_attn, dr1, positions)
+    line_a, other, grad_in = lax.optimization_barrier((line_a, other, grad_in))
     g_attn = total[0] + line_a[0].astype(F32) + line_a[1].astype(F32) + line_a[2].astype(F32)
     small = g_attn[ROWS : ROWS + 4, :ROWS]
     g_attn = g_attn[:ROWS].astype(LOW)

time: 299 us -> 294 us (0.983)
  other arithmetic: 16.7 us -> 8.86 us
  waiting for transfers between devices: 100 us -> 104 us
    ppermute x53, waiting for transfers between devices: 69.9 us -> 74 us  [send(): return lax.ppermute(value, AXES, MOVES[move])]
  transfers between devices with their start and end apart: 54 -> 54, of which waited for: 26 -> 22; matrix products, arithmetic and copies ran while one was open for 7% -> 4% of each run, Pallas kernels for 27% -> 27%
where the time goes in v10:
time: 294 us
  Pallas kernels  105 us (36%)
  waiting for transfers between devices  104 us (35%)
  starting transfers between devices  50.3 us (17%)
  between operations  14.7 us (5%)
  local copies, waits for them, and re-layouts  10.3 us (4%)
  other arithmetic  8.86 us (3%)
    ppermute x53, waiting for transfers between devices, send(): return lax.ppermute(value, AXES, MOVES[move])  74 us
    ppermute x53, starting transfers between devices, send(): return lax.ppermute(value, AXES, MOVES[move])  50.2 us
    all_gather x1, waiting for transfers between devices, on_block(): lax.all_gather(ffn_piece, AXES, axis=0, tiled=False)  30.3 us
    pallas_call x2, Pallas kernels, attention_back(): pl.pallas_call(functools.partial(attention_back_kernel, seqs // 2, listed...  18.8 us
    pallas_call x1, Pallas kernels, attention_forward(): pl.pallas_call(functools.partial(attention_kernel, seqs, listed // seqs),...  18 us
    pallas_call x1, Pallas kernels, ffn_forward(): pl.pallas_call(functools.partial(ffn_kernel, seqs, listed // seqs), out_s...  17 us
    pallas_call x3, Pallas kernels, weight_grad(): pl.pallas_call(weight_grad_kernel, out_shape=(out(shape, LOW), out(shape,...  11.6 us
    pallas_call x1, Pallas kernels, attention_grads(): pl.pallas_call(attention_grads_kernel, out_shape=(out((2, 2, LINE, half,...  8.65 us
  transfers between devices with their start and end apart: 54, of which 22 were waited for; matrix products, arithmetic and copies ran while one was open for 4% of the time, Pallas kernels for 27%

profile of v10, /device:TPU:0, one launch (start us, length us, event | category | flops | bytes accessed | tf_op | source)
XLA Modules:
  0.0 293.6 jit_solution(14781136794613632816)
XLA Ops:
  9.6 4.1 %collective-permute-start.1 = (bf16[104,768]{1,0:T(8,128)(2,1)S(1)}, bf16[104,768]{1,0:T(8,128)(2,1)S(1)}, u32[]{:S(2)}, u32[]{:S(2)}) collective-permute-start(bf16[104,768]{1,0:T(8,128)(2,1)S(1)} %get-tuple-element.181), channel_id=1, source_target_pairs={{0,16},{1,17},{2,18},{3,19},{4,20},{5,21},{6,22},{7,23},{8,24},{9,... | collective-permute-start | bytes 479240 | tf_op jit(solution)/shard_map/ppermute | solution.py:563
  18.8 6.8 %collective-permute-done.1 = bf16[104,768]{1,0:T(8,128)(2,1)S(1)} collective-permute-done((bf16[104,768]{1,0:T(8,128)(2,1)S(1)}, bf16[104,768]{1,0:T(8,128)(2,1)S(1)}, u32[]{:S(2)}, u32[]{:S(2)}) %collective-permute-start.1) | collective-permute-done | bytes 159776 | tf_op jit(solution)/shard_map/ppermute | solution.py:563
  31.4 6.8 %collective-permute-done.6.rest_5_ = bf16[4,56,768]{2,1,0:T(8,128)(2,1)S(1)} collective-permute-done((bf16[4,56,768]{2,1,0:T(8,128)(2,1)S(1)}, bf16[4,56,768]{2,1,0:T(8,128)(2,1)S(1)}, u32[]{:S(2)}, u32[]{:S(2)}) %collective-permute-start.6) | collective-permute-done | bytes 344096 | tf_op jit(solution)/shard_map/ppermute | solution.py:563
  42.5 4.0 %collective-permute-done.4.rest_2_ = bf16[4,48,768]{2,1,0:T(8,128)(2,1)} collective-permute-done((bf16[4,48,768]{2,1,0:T(8,128)(2,1)S(1)}, bf16[4,48,768]{2,1,0:T(8,128)(2,1)}, u32[]{:S(2)}, u32[]{:S(2)}) %collective-permute-start.4) | collective-permute-done | bytes 294944 | tf_op jit(solution)/shard_map/ppermute | solution.py:563
  50.7 5.5 %collective-permute-done.8.rest_7_ = bf16[4,56,768]{2,1,0:T(8,128)(2,1)S(1)} collective-permute-done((bf16[4,56,768]{2,1,0:T(8,128)(2,1)S(1)}, bf16[4,56,768]{2,1,0:T(8,128)(2,1)S(1)}, u32[]{:S(2)}, u32[]{:S(2)}) %collective-permute-start.8) | collective-permute-done | bytes 344096 | tf_op jit(solution)/shard_map/ppermute | solution.py:563
  56.8 6.1 %collective-permute-done.7.rest_6_ = bf16[4,48,768]{2,1,0:T(8,128)(2,1)} collective-permute-done((bf16[4,48,768]{2,1,0:T(8,128)(2,1)}, bf16[4,48,768]{2,1,0:T(8,128)(2,1)}, u32[]{:S(2)}, u32[]{:S(2)}) %collective-permute-start.7) | collective-permute-done | bytes 294944 | tf_op jit(solution)/shard_map/ppermute | solution.py:563
  65.8 18.0 %attention_forward.1 = (bf16[512,2304]{1,0:T(8,128)(2,1)}, f32[512,768]{1,0:T(8,128)}, bf16[128,768]{1,0:T(8,128)(2,1)}, bf16[128,768]{1,0:T(8,128)(2,1)}, bf16[...) custom-call(s32[5]{0:T(128)} %stack.95.where_ref, f32[12]{0:T(128)} %multiply_exponential_fusion.slope_ref, ...), custom_call_target="tpu_custom_call" | custom-call | bytes 60000000 | tf_op jit(solution)/shard_map/attention_forward/pallas_call | solution.py:164
  85.6 10.4 %collective-permute-done.18 = bf16[128,768]{1,0:T(8,128)(2,1)S(1)} collective-permute-done((bf16[128,768]{1,0:T(8,128)(2,1)}, bf16[128,768]{1,0:T(8,128)(2,1)S(1)}, u32[]{:S(2)}, u32[]{:S(2)}) %collective-permute-start.18) | collective-permute-done | bytes 196640 | tf_op jit(solution)/shard_map/ppermute | solution.py:563
  99.3 30.3 %all-gather.3.cloned.1.call-done = bf16[96,96,768]{2,1,0:T(8,128)(2,1)} async-done(((bf16[3,96,768]{2,1,0:T(8,128)(2,1)}), bf16[96,96,768]{2,1,0:T(8,128)(2,1)}) %all-gather.3.cloned.1.call-update) | async-done | bytes 14155792 | tf_op jit(solution)/shard_map/all_gather | solution.py:669
  129.6 17.0 %ffn_forward.1 = (bf16[512,768]{1,0:T(8,128)(2,1)}, f32[128,768]{1,0:T(8,128)}, bf16[128,768]{1,0:T(8,128)(2,1)}, f32[2,768]{1,0:T(2,128)}) custom-call(f32[512,768]{1,0:T(8,128)} %get-tuple-element.89.h1_ref, bf16[8,4,3,96,768]{4,3,2,1,0:T(8,128)(2,1)} %bitcast.136, bf16[8,4,3,96,768]{4,3,2,1,0:T(8,128)(2,1)} %bitcast.137, ...), custom_call_target="tpu_custom_call" | custom-call | bytes 48000000 | tf_op jit(solution)/shard_map/ffn_forward/pallas_call | solution.py:232
  147.2 6.6 %ffn_again.1 = (bf16[512,768]{1,0:T(8,128)(2,1)}, f32[512,768]{1,0:T(8,128)}, f32[512,768]{1,0:T(8,128)}) custom-call(s32[5]{0:T(128)} %stack.95.where_ref, bf16[4,128,768]{2,1,0:T(8,128)(2,1)} %pad_maximum_fusion.1.h_ref.a_ref, bf16[8,4,3,96,768]{4,3,2,1,0:T(8,128)(2,1)} %bitcast.139, bf16[8,4,3,96,768]{4,3,2,1,0:T(8,128)(2,1)} %bitcast.140), custom_call_target="tpu_custom_call" | custom-call | bytes 18000000 | tf_op jit(solution)/shard_map/ffn_again/pallas_call | solution.py:288
  156.3 7.5 %ffn_back.1 = (bf16[512,768]{1,0:T(8,128)(2,1)}, bf16[512,768]{1,0:T(8,128)(2,1)}, f32[2,128,768]{2,1,0:T(8,128)}, bf16[2,128,768]{2,1,0:T(8,128)(2,1)}) custom-call(s32[5]{0:T(128)} %stack.95.where_ref, bf16[4,128,768]{2,1,0:T(8,128)(2,1)} %pad_maximum_fusion.2.b_ref.e_ref, f32[512,768]{1,0:T(8,128)} %get-tuple-element.98.to_gate_ref, ...), custom_call_target="tpu_custom_call" | custom-call | bytes 21000000 | tf_op jit(solution)/shard_map/ffn_back/pallas_call | solution.py:323
  164.2 3.8 %weight_grad.3 = (bf16[4,96,768]{2,1,0:T(8,128)(2,1)}, bf16[4,96,768]{2,1,0:T(8,128)(2,1)}) custom-call(s32[5]{0:T(128)} %stack.95.where_ref, bf16[512,768]{1,0:T(8,128)(2,1)} %get-tuple-element.93.a_ref, bf16[4,128,768]{2,1,0:T(8,128)(2,1)} %pad_maximum_fusion.2.b_ref.e_ref), custom_call_target="tpu_custom_call" | custom-call | bytes 12000000 | tf_op jit(solution)/shard_map/weight_grad/pallas_call | solution.py:359
  171.1 3.8 %weight_grad.4 = (bf16[4,96,768]{2,1,0:T(8,128)(2,1)}, bf16[4,96,768]{2,1,0:T(8,128)(2,1)}) custom-call(s32[5]{0:T(128)} %stack.95.where_ref, bf16[4,128,768]{2,1,0:T(8,128)(2,1)} %pad_maximum_fusion.1.h_ref.a_ref, bf16[512,768]{1,0:T(8,128)(2,1)} %get-tuple-element.103.b_ref), custom_call_target="tpu_custom_call" | custom-call | bytes 12000000 | tf_op jit(solution)/shard_map/weight_grad/pallas_call | solution.py:359
  176.4 3.9 %weight_grad.5 = (bf16[4,96,768]{2,1,0:T(8,128)(2,1)}, bf16[4,96,768]{2,1,0:T(8,128)(2,1)}) custom-call(s32[5]{0:T(128)} %stack.95.where_ref, bf16[4,128,768]{2,1,0:T(8,128)(2,1)} %pad_maximum_fusion.1.h_ref.a_ref, bf16[512,768]{1,0:T(8,128)(2,1)} %get-tuple-element.106.b_ref), custom_call_target="tpu_custom_call" | custom-call | bytes 12000000 | tf_op jit(solution)/shard_map/weight_grad/pallas_call | solution.py:359
  181.7 3.2 %norm_back.1 = (f32[128,768]{1,0:T(8,128)}, bf16[128,768]{1,0:T(8,128)(2,1)}, bf16[128,768]{1,0:T(8,128)(2,1)}, f32[2,768]{1,0:T(2,128)}) custom-call(f32[128,768]{1,0:T(8,128)} %get-tuple-element.97.dr2_ref, f32[128,768]{1,0:T(8,128)} %slice_bitcast_fusion.2.part_ref, bf16[128,768]{1,0:T(8,128)(2,1)} %copy-done.26, f32[128,768]{1,0:T(8,128)} %get-tuple-element.109.r1_ref, ...), custom_call_target="tpu_custom_call" | custom-call | bytes 12000000 | tf_op jit(solution)/shard_map/norm_back/pallas_call | solution.py:389
  184.9 9.3 %attention_back.2.rhs0_ref = bf16[256,2304]{1,0:T(8,128)(2,1)} custom-call(f32[12]{0:T(128)} %multiply_exponential_fusion.slope_ref, bf16[128,768]{1,0:T(8,128)(2,1)} %get-tuple-element.117.datt_ref, bf16[128,768]{1,0:T(8,128)(2,1)} %get-tuple-element.112.q_ref, bf16[512,2304]{1,0:T(8,128)(2,1)} %get-tuple-element.113.qkv_ref, s32[128,1]{1,0:T(8,128)} %reshape.140.pos_ref), custom_call_target="tpu_custom_call" | custom-call | bytes 24000000 | tf_op jit(solution)/shard_map/attention_back/pallas_call | solution.py:441
  198.0 9.5 %attention_back.3.rhs1_ref = bf16[256,2304]{1,0:T(8,128)(2,1)} custom-call(f32[12]{0:T(128)} %multiply_exponential_fusion.slope_ref, bf16[128,768]{1,0:T(8,128)(2,1)} %get-tuple-element.117.datt_ref, bf16[128,768]{1,0:T(8,128)(2,1)} %get-tuple-element.112.q_ref, bf16[512,2304]{1,0:T(8,128)(2,1)} %get-tuple-element.113.qkv_ref, s32[128,1]{1,0:T(8,128)} %reshape.140.pos_ref), custom_call_target="tpu_custom_call" | custom-call | bytes 24000000 | tf_op jit(solution)/shard_map/attention_back/pallas_call | solution.py:441
  214.1 8.6 %attention_grads.1 = (bf16[2,2,4,48,768]{4,3,2,1,0:T(8,128)(2,1)}, bf16[2,2,4,56,768]{4,3,2,1,0:T(8,128)(2,1)}, bf16[2,2,4,48,768]{4,3,2,1,0:T(8,128)(2,1)}, bf16[2,2,4,56,768]{4,3,2,1,0:T(8,128)(2,1)}) custom-call(s32[5]{0:T(128)} %stack.95.where_ref, bf16[768,512]{1,0:T(8,128)(2,1)} %bitcast.144, bf16[256,2304]{1,0:T(8,128)(2,1)} %attention_back.2.rhs0_ref, ...), custom_call_target="tpu_custom_call" | custom-call | bytes 30000000 | tf_op jit(solution)/shard_map/attention_grads/pallas_call | solution.py:494
  222.8 3.0 %collective-permute-done.31 = bf16[96,768]{1,0:T(8,128)(2,1)S(1)} collective-permute-done((bf16[96,768]{1,0:T(8,128)(2,1)S(1)}, bf16[96,768]{1,0:T(8,128)(2,1)S(1)}, u32[]{:S(2)}, u32[]{:S(2)}) %collective-permute-start.31) | collective-permute-done | bytes 147488 | tf_op jit(solution)/shard_map/ppermute | solution.py:563
  235.2 11.6 %collective-permute-done.35 = bf16[2,4,48,768]{3,2,1,0:T(8,128)(2,1)S(1)} collective-permute-done((bf16[2,4,48,768]{3,2,1,0:T(8,128)(2,1)S(1)}, bf16[2,4,48,768]{3,2,1,0:T(8,128)(2,1)S(1)}, u32[]{:S(2)}, u32[]{:S(2)}) %collective-permute-start.35) | collective-permute-done | bytes 589856 | tf_op jit(solution)/shard_map/ppermute | solution.py:563
  256.4 6.3 %collective-permute-done.39 = bf16[4,56,768]{2,1,0:T(8,128)(2,1)S(1)} collective-permute-done((bf16[4,56,768]{2,1,0:T(8,128)(2,1)S(1)}, bf16[4,56,768]{2,1,0:T(8,128)(2,1)S(1)}, u32[]{:S(2)}, u32[]{:S(2)}) %collective-permute-start.39) | collective-permute-done | bytes 344096 | tf_op jit(solution)/shard_map/ppermute | solution.py:563
  266.4 8.2 %input_grad.1 = f32[512,768]{1,0:T(8,128)} custom-call(bf16[256,2304]{1,0:T(8,128)(2,1)} %attention_back.2.rhs0_ref, bf16[256,2304]{1,0:T(8,128)(2,1)} %attention_back.3.rhs1_ref, bf16[8,4,96,768]{3,2,1,0:T(8,128)(2,1)} %get-tuple-element.110.w_ref, f32[128,768]{1,0:T(8,128)} %get-tuple-element.147.dr1_ref, s32[4,32]{1,0:T(4,128)} %pos_ref.1), custom_call_target="tpu_custom_call" | custom-call | bytes 24000000 | tf_op jit(solution)/shard_map/input_grad/pallas_call | solution.py:526
  278.7 3.4 %finish_ffn.1 = (f32[384,768]{1,0:T(8,128)}, f32[96,6144]{1,0:T(8,128)}) custom-call(s32[5]{0:T(128)} %stack.95.where_ref, bf16[3,96,768]{2,1,0:T(8,128)(2,1)} %copy-done.1, bf16[3,96,768]{2,1,0:T(8,128)(2,1)} %copy-done.13, bf16[3,96,768]{2,1,0:T(8,128)(2,1)} %copy-done.12, bf16[3,96,768]{2,1,0:T(8,128)(2,1)} %copy-done.14), custom_call_target="tpu_custom_call" | custom-call | bytes 12000000 | tf_op jit(solution)/shard_map/finish_ffn/pallas_call | solution.py:612
  (226 shorter events, 81.2 us)
Async XLA Ops:
  7.2 122.3 %all-gather.3.cloned.1.call-start = ((), (), s32[]{:S(2)}) async-start(), calls=%async_computation | async-start | bytes 14598144 | tf_op jit(solution)/shard_map/all_gather | solution.py:669
  9.6 16.0 %collective-permute-start.1 = (bf16[104,768]{1,0:T(8,128)(2,1)S(1)}, bf16[104,768]{1,0:T(8,128)(2,1)S(1)}, u32[]{:S(2)}, u32[]{:S(2)}) collective-permute-start(bf16[104,768]{1,0:T(8,128)(2,1)S(1)} %get-tuple-element.181), channel_id=1, source_target_pairs={{0,16},{1,17},{2,18},{3,19},{4,20},{5,21},{6,22},{7,23},{8,24},{9,... | collective-permute-start | bytes 479240 | tf_op jit(solution)/shard_map/ppermute | solution.py:563
  29.0 13.5 %collective-permute-start.5 = (bf16[4,48,768]{2,1,0:T(8,128)(2,1)S(1)}, bf16[4,48,768]{2,1,0:T(8,128)(2,1)}, u32[]{:S(2)}, u32[]{:S(2)}) collective-permute-start(bf16[4,48,768]{2,1,0:T(8,128)(2,1)S(1)} %slice.169.rest_0_), channel_id=1, source_target_pairs={{0,2},{1,3},{2,0},{3,1},{4,6},{5,7},{6,4},{7,5},{8,10},{9,11},{10,... | collective-permute-start | bytes 884744 | tf_op jit(solution)/shard_map/ppermute | solution.py:563
  29.4 17.1 %collective-permute-start.3 = (bf16[4,56,768]{2,1,0:T(8,128)(2,1)S(1)}, bf16[4,56,768]{2,1,0:T(8,128)(2,1)S(1)}, u32[]{:S(2)}, u32[]{:S(2)}) collective-permute-start(bf16[4,56,768]{2,1,0:T(8,128)(2,1)S(1)} %slice.167.rest_1_), channel_id=1, source_target_pairs={{0,4},{1,5},{2,6},{3,7},{4,0},{5,1},{6,2},{7,3},{8,12},{9,13},{10,... | collective-permute-start | bytes 1032200 | tf_op jit(solution)/shard_map/ppermute | solution.py:563
  31.2 15.3 %collective-permute-start.4 = (bf16[4,48,768]{2,1,0:T(8,128)(2,1)S(1)}, bf16[4,48,768]{2,1,0:T(8,128)(2,1)}, u32[]{:S(2)}, u32[]{:S(2)}) collective-permute-start(bf16[4,48,768]{2,1,0:T(8,128)(2,1)S(1)} %slice.169.rest_0_), channel_id=1, source_target_pairs={{0,4},{1,5},{2,6},{3,7},{4,0},{5,1},{6,2},{7,3},{8,12},{9,13},{10,... | collective-permute-start | bytes 884744 | tf_op jit(solution)/shard_map/ppermute | solution.py:563
  31.4 19.1 %collective-permute-start.10 = (bf16[4,56,768]{2,1,0:T(8,128)(2,1)S(1)}, bf16[4,56,768]{2,1,0:T(8,128)(2,1)S(1)}, u32[]{:S(2)}, u32[]{:S(2)}) collective-permute-start(bf16[4,56,768]{2,1,0:T(8,128)(2,1)S(1)} %slice.167.rest_1_), channel_id=1, source_target_pairs={{0,1},{1,0},{2,3},{3,2},{4,5},{5,4},{6,7},{7,6},{8,9},{9,8},{10,11... | collective-permute-start | bytes 1032200 | tf_op jit(solution)/shard_map/ppermute | solution.py:563
  38.2 18.0 %collective-permute-start.8 = (bf16[4,56,768]{2,1,0:T(8,128)(2,1)S(1)}, bf16[4,56,768]{2,1,0:T(8,128)(2,1)S(1)}, u32[]{:S(2)}, u32[]{:S(2)}) collective-permute-start(bf16[4,56,768]{2,1,0:T(8,128)(2,1)S(1)} %collective-permute-done.6.rest_5_), channel_id=1, source_target_pairs={{0,4},{1,5},{2,6},{3,7},{4,0},{5,1},{6,2},{7,3},{8,12},{9,13},{10,... | collective-permute-start | bytes 1032200 | tf_op jit(solution)/shard_map/ppermute | solution.py:563
  46.5 16.4 %collective-permute-start.7 = (bf16[4,48,768]{2,1,0:T(8,128)(2,1)}, bf16[4,48,768]{2,1,0:T(8,128)(2,1)}, u32[]{:S(2)}, u32[]{:S(2)}) collective-permute-start(bf16[4,48,768]{2,1,0:T(8,128)(2,1)} %collective-permute-done.4.rest_2_), channel_id=1, source_target_pairs={{0,2},{1,3},{2,0},{3,1},{4,6},{5,7},{6,4},{7,5},{8,10},{9,11},{10,... | collective-permute-start | bytes 884744 | tf_op jit(solution)/shard_map/ppermute | solution.py:563
  49.8 14.3 %collective-permute-start.14 = (bf16[4,56,768]{2,1,0:T(8,128)(2,1)S(1)}, bf16[4,56,768]{2,1,0:T(8,128)(2,1)S(1)}, u32[]{:S(2)}, u32[]{:S(2)}) collective-permute-start(bf16[4,56,768]{2,1,0:T(8,128)(2,1)S(1)} %collective-permute-done.6.rest_5_), channel_id=1, source_target_pairs={{0,1},{1,0},{2,3},{3,2},{4,5},{5,4},{6,7},{7,6},{8,9},{9,8},{10,11... | collective-permute-start | bytes 1032200 | tf_op jit(solution)/shard_map/ppermute | solution.py:563
  50.6 13.6 %collective-permute-start.12 = (bf16[4,56,768]{2,1,0:T(8,128)(2,1)S(1)}, bf16[4,56,768]{2,1,0:T(8,128)(2,1)S(1)}, u32[]{:S(2)}, u32[]{:S(2)}) collective-permute-start(bf16[4,56,768]{2,1,0:T(8,128)(2,1)S(1)} %collective-permute-done.3.rest_3_), channel_id=1, source_target_pairs={{0,1},{1,0},{2,3},{3,2},{4,5},{5,4},{6,7},{7,6},{8,9},{9,8},{10,11... | collective-permute-start | bytes 1032200 | tf_op jit(solution)/shard_map/ppermute | solution.py:563
  168.0 26.2 %collective-permute-start.23 = (bf16[4,96,768]{2,1,0:T(8,128)(2,1)}, bf16[4,96,768]{2,1,0:T(8,128)(2,1)S(1)}, u32[]{:S(2)}, u32[]{:S(2)}) collective-permute-start(bf16[4,96,768]{2,1,0:T(8,128)(2,1)} %get-tuple-element.96), channel_id=1, source_target_pairs={{0,4},{1,5},{2,6},{3,7},{4,0},{5,1},{6,2},{7,3},{8,12},{9,13},{10,... | collective-permute-start | bytes 1769480 | tf_op jit(solution)/shard_map/ppermute | solution.py:563
  175.0 34.4 %collective-permute-start.29 = (bf16[4,96,768]{2,1,0:T(8,128)(2,1)}, bf16[4,96,768]{2,1,0:T(8,128)(2,1)S(1)}, u32[]{:S(2)}, u32[]{:S(2)}) collective-permute-start(bf16[4,96,768]{2,1,0:T(8,128)(2,1)} %get-tuple-element.104), channel_id=1, source_target_pairs={{0,4},{1,5},{2,6},{3,7},{4,0},{5,1},{6,2},{7,3},{8,12},{9,13},{10,... | collective-permute-start | bytes 1769480 | tf_op jit(solution)/shard_map/ppermute | solution.py:563
  180.3 45.5 %collective-permute-start.33 = (bf16[4,96,768]{2,1,0:T(8,128)(2,1)}, bf16[4,96,768]{2,1,0:T(8,128)(2,1)S(1)}, u32[]{:S(2)}, u32[]{:S(2)}) collective-permute-start(bf16[4,96,768]{2,1,0:T(8,128)(2,1)} %get-tuple-element.107), channel_id=1, source_target_pairs={{0,4},{1,5},{2,6},{3,7},{4,0},{5,1},{6,2},{7,3},{8,12},{9,13},{10,... | collective-permute-start | bytes 1769480 | tf_op jit(solution)/shard_map/ppermute | solution.py:563
  194.3 13.2 %collective-permute-start.28 = (bf16[96,768]{1,0:T(8,128)(2,1)S(1)}, bf16[96,768]{1,0:T(8,128)(2,1)S(1)}, u32[]{:S(2)}, u32[]{:S(2)}) collective-permute-start(bf16[96,768]{1,0:T(8,128)(2,1)S(1)} %get-tuple-element.168), channel_id=1, source_target_pairs={{0,24},{1,25},{2,26},{3,27},{4,28},{5,29},{6,30},{7,31},{8,0},{9,1... | collective-permute-start | bytes 442376 | tf_op jit(solution)/shard_map/ppermute | solution.py:563
  196.1 13.3 %collective-permute-start.27 = (bf16[96,768]{1,0:T(8,128)(2,1)S(1)}, bf16[96,768]{1,0:T(8,128)(2,1)S(1)}, u32[]{:S(2)}, u32[]{:S(2)}) collective-permute-start(bf16[96,768]{1,0:T(8,128)(2,1)S(1)} %get-tuple-element.169), channel_id=1, source_target_pairs={{0,16},{1,17},{2,18},{3,19},{4,20},{5,21},{6,22},{7,23},{8,24},{9,... | collective-permute-start | bytes 442376 | tf_op jit(solution)/shard_map/ppermute | solution.py:563
  210.2 12.6 %collective-permute-start.32 = (bf16[96,768]{1,0:T(8,128)(2,1)}, bf16[96,768]{1,0:T(8,128)(2,1)S(1)}, u32[]{:S(2)}, u32[]{:S(2)}) collective-permute-start(bf16[96,768]{1,0:T(8,128)(2,1)} %get-tuple-element.165), channel_id=1, source_target_pairs={{0,24},{1,25},{2,26},{3,27},{4,28},{5,29},{6,30},{7,31},{8,0},{9,1... | collective-permute-start | bytes 442376 | tf_op jit(solution)/shard_map/ppermute | solution.py:563
  210.9 14.9 %collective-permute-start.31 = (bf16[96,768]{1,0:T(8,128)(2,1)S(1)}, bf16[96,768]{1,0:T(8,128)(2,1)S(1)}, u32[]{:S(2)}, u32[]{:S(2)}) collective-permute-start(bf16[96,768]{1,0:T(8,128)(2,1)S(1)} %get-tuple-element.166), channel_id=1, source_target_pairs={{0,16},{1,17},{2,18},{3,19},{4,20},{5,21},{6,22},{7,23},{8,24},{9,... | collective-permute-start | bytes 442376 | tf_op jit(solution)/shard_map/ppermute | solution.py:563
  212.1 13.7 %collective-permute-start.30 = (bf16[96,768]{1,0:T(8,128)(2,1)S(1)}, bf16[96,768]{1,0:T(8,128)(2,1)S(1)}, u32[]{:S(2)}, u32[]{:S(2)}) collective-permute-start(bf16[96,768]{1,0:T(8,128)(2,1)S(1)} %get-tuple-element.167), channel_id=1, source_target_pairs={{0,8},{1,9},{2,10},{3,11},{4,12},{5,13},{6,14},{7,15},{8,16},{9,17... | collective-permute-start | bytes 442376 | tf_op jit(solution)/shard_map/ppermute | solution.py:563
  226.5 25.1 %collective-permute-start.40 = (bf16[96,768]{1,0:T(8,128)(2,1)S(1)}, bf16[96,768]{1,0:T(8,128)(2,1)S(1)}, u32[]{:S(2)}, u32[]{:S(2)}) collective-permute-start(bf16[96,768]{1,0:T(8,128)(2,1)S(1)} %fusion.20), channel_id=1, source_target_pairs={{0,0},{1,8},{2,16},{3,24},{4,1},{5,9},{6,17},{7,25},{8,2},{9,10},{... | collective-permute-start | bytes 442376 | tf_op jit(solution)/shard_map/ppermute | solution.py:563
  230.3 16.5 %collective-permute-start.35 = (bf16[2,4,48,768]{3,2,1,0:T(8,128)(2,1)S(1)}, bf16[2,4,48,768]{3,2,1,0:T(8,128)(2,1)S(1)}, u32[]{:S(2)}, u32[]{:S(2)}) collective-permute-start(bf16[2,4,48,768]{3,2,1,0:T(8,128)(2,1)S(1)} %fusion.3), channel_id=1, source_target_pairs={{0,2},{1,3},{2,0},{3,1},{4,6},{5,7},{6,4},{7,5},{8,10},{9,11},{10,... | collective-permute-start | bytes 1769480 | tf_op jit(solution)/shard_map/ppermute | solution.py:563
  232.2 21.2 %collective-permute-start.43 = (bf16[96,768]{1,0:T(8,128)(2,1)S(1)}, bf16[96,768]{1,0:T(8,128)(2,1)S(1)}, u32[]{:S(2)}, u32[]{:S(2)}) collective-permute-start(bf16[96,768]{1,0:T(8,128)(2,1)S(1)} %get-tuple-element.162), channel_id=1, source_target_pairs={{0,24},{1,25},{2,26},{3,27},{4,28},{5,29},{6,30},{7,31},{8,0},{9,1... | collective-permute-start | bytes 442376 | tf_op jit(solution)/shard_map/ppermute | solution.py:563
  234.6 18.8 %collective-permute-start.42 = (bf16[96,768]{1,0:T(8,128)(2,1)S(1)}, bf16[96,768]{1,0:T(8,128)(2,1)S(1)}, u32[]{:S(2)}, u32[]{:S(2)}) collective-permute-start(bf16[96,768]{1,0:T(8,128)(2,1)S(1)} %get-tuple-element.163), channel_id=1, source_target_pairs={{0,16},{1,17},{2,18},{3,19},{4,20},{5,21},{6,22},{7,23},{8,24},{9,... | collective-permute-start | bytes 442376 | tf_op jit(solution)/shard_map/ppermute | solution.py:563
  234.8 14.6 %collective-permute-start.38 = (bf16[2,4,56,768]{3,2,1,0:T(8,128)(2,1)S(1)}, bf16[2,4,56,768]{3,2,1,0:T(8,128)(2,1)S(1)}, u32[]{:S(2)}, u32[]{:S(2)}) collective-permute-start(bf16[2,4,56,768]{3,2,1,0:T(8,128)(2,1)S(1)} %fusion.1), channel_id=1, source_target_pairs={{0,4},{1,5},{2,6},{3,7},{4,0},{5,1},{6,2},{7,3},{8,12},{9,13},{10,... | collective-permute-start | bytes 2064392 | tf_op jit(solution)/shard_map/ppermute | solution.py:563
  253.8 20.8 %collective-permute-start.47 = (bf16[3,96,768]{2,1,0:T(8,128)(2,1)S(1)}, bf16[3,96,768]{2,1,0:T(8,128)(2,1)S(1)}, u32[]{:S(2)}, u32[]{:S(2)}) collective-permute-start(bf16[3,96,768]{2,1,0:T(8,128)(2,1)S(1)} %pad_maximum_fusion.5.rest_0_), channel_id=1, source_target_pairs={{0,2},{1,3},{2,0},{3,1},{4,6},{5,7},{6,4},{7,5},{8,10},{9,11},{10,... | collective-permute-start | bytes 1327112 | tf_op jit(solution)/shard_map/ppermute | solution.py:563
  (67 other events, 566.3 us)
Sparse Core Ops, SparseCore 0:
  11.5 117.9 all-gather.2

commit v11 on v10

--- a/solution.py
+++ b/solution.py
@@ -192,18 +192,19 @@
         low_ref[...] = h1_ref[...].astype(LOW)
         acc_ref[...] = h1_ref[...]
 
-    @pl.loop(0, D // step)
-    def _(n):
-        lane = pl.multiple_of(n * step, step)
-        gate = mm(low_ref[...], gate_ref[:, :, pl.ds(lane, step)].reshape(D, step))
-        up = mm(low_ref[...], up_ref[:, :, pl.ds(lane, step)].reshape(D, step))
+    def products(n):
+        lanes = slice(n * step, (n + 1) * step)
+        return mm(low_ref[...], gate_ref[:, :, lanes].reshape(D, step)), mm(low_ref[...], up_ref[:, :, lanes].reshape(D, step))
+
+    gate, up = products(0)
+    for n in range(D // step):
+        following = products(n + 1) if (n + 1) * step < D else (None, None)
         cdf = 0.5 * (1.0 + lax.erf(gate * (0.5**0.5)))
-        act_ref[:, pl.ds(lane, step)] = (gate * cdf * up).astype(LOW)
-
-    @pl.loop(0, D // step)
-    def _(n):
-        lane = pl.multiple_of(n * step, step)
-        acc_ref[:, pl.ds(lane, step)] += mm(act_ref[...], down_ref[:, :, :, pl.ds(lane, step)].reshape(D, step))
+        act_ref[:, n * step : (n + 1) * step] = (gate * cdf * up).astype(LOW)
+        gate, up = following
+    for n in range(D // step):
+        lanes = slice(n * step, (n + 1) * step)
+        acc_ref[:, lanes] += mm(act_ref[...], down_ref[:, :, :, lanes].reshape(D, step))
 
     @pl.when(j == QUARTERS - 1)
     def _():
@@ -258,16 +259,21 @@
 def ffn_again_kernel(where_ref, h_ref, gate_ref, up_ref, act_ref, to_gate_ref, to_up_ref):
     step = 256
 
-    @pl.loop(0, D // step)
-    def _(n):
-        lane = pl.multiple_of(n * step, step)
-        rows = block(h_ref)
-        gate = mm(rows, gate_ref[:, :, pl.ds(lane, step)].reshape(D, step))
-        up = mm(rows, up_ref[:, :, pl.ds(lane, step)].reshape(D, step))
+    rows = block(h_ref)
+
+    def products(n):
+        lanes = slice(n * step, (n + 1) * step)
+        return mm(rows, gate_ref[:, :, lanes].reshape(D, step)), mm(rows, up_ref[:, :, lanes].reshape(D, step))
+
+    gate, up = products(0)
+    for n in range(D // step):
+        following = products(n + 1) if (n + 1) * step < D else (None, None)
+        lanes = slice(n * step, (n + 1) * step)
         value, slope = gelu_parts(gate)
-        act_ref[:, pl.ds(lane, step)] = (value * up).astype(LOW)
-        to_gate_ref[:, pl.ds(lane, step)] = slope * up
-        to_up_ref[:, pl.ds(lane, step)] = value
+        act_ref[:, lanes] = (value * up).astype(LOW)
+        to_gate_ref[:, lanes] = slope * up
+        to_up_ref[:, lanes] = value
+        gate, up = following
 
 
 def quarter_specs(which):
@@ -340,11 +346,9 @@
     b = block(b_ref)
     step = 256
 
-    @pl.loop(0, D // step)
-    def _(n):
-        lane = pl.multiple_of(n * step, step)
-        a = block(a_ref, *([slice(None)] * (len(a_ref.shape) - 1)), pl.ds(lane, step))
-        full_ref[pl.ds(lane, step), :] = mm_tn(a, b)
+    for n in range(D // step):
+        rows = slice(n * step, (n + 1) * step)
+        full_ref[rows, :] = mm_tn(block(a_ref, *([slice(None)] * (len(a_ref.shape) - 1)), rows), b)
 
     for r in range(LINE):
         base = 2 * lax.rem(z + r, LINE)
@@ -410,10 +414,11 @@
         zero = jnp.zeros_like(value)
         return jnp.concatenate([jnp.where(first_m, value, zero), jnp.where(first_m, zero, value)], axis=0)
 
-    @pl.loop(0, HEADS // 2)
-    def _(t):
-        lane = pl.multiple_of(t * 128, 128)
-        for s in range(seqs):
+    @pl.loop(0, HEADS // 4)
+    def _(step):
+        for n, s in ((n, s) for n in (0, 1) for s in range(seqs)):
+            t = 2 * step + n
+            lane = pl.multiple_of(t * 128, 128)
             rows = slice(s * length, (s + 1) * length)
             mine = slice(s * most, (s + 1) * most)
             away = away_ref[mine, :]

time: 294 us -> 289 us (0.983)
  Pallas kernels: 105 us -> 98.9 us
    pallas_call x1, Pallas kernels: 17 us -> 13.9 us  [ffn_forward(): pl.pallas_call(functools.partial(ffn_kernel, seqs, listed // seqs), out_s...]
  transfers between devices with their start and end apart: 54 -> 54, of which waited for: 22 -> 22; matrix products, arithmetic and copies ran while one was open for 4% -> 4% of each run, Pallas kernels for 27% -> 26%
where the time goes in v11:
time: 289 us; the launch traced here: 288 us
  waiting for transfers between devices  105 us (36%)
  Pallas kernels  98.9 us (34%)
  starting transfers between devices  50.4 us (17%)
  between operations  14.7 us (5%)
  local copies, waits for them, and re-layouts  9.92 us (3%)
  other arithmetic  8.86 us (3%)
    ppermute x53, waiting for transfers between devices, send(): return lax.ppermute(value, AXES, MOVES[move])  75.2 us
    ppermute x53, starting transfers between devices, send(): return lax.ppermute(value, AXES, MOVES[move])  50.4 us
    all_gather x1, waiting for transfers between devices, on_block(): lax.all_gather(ffn_piece, AXES, axis=0, tiled=False)  30.3 us
    pallas_call x1, Pallas kernels, attention_forward(): pl.pallas_call(functools.partial(attention_kernel, seqs, listed // seqs),...  18.1 us
    pallas_call x2, Pallas kernels, attention_back(): pl.pallas_call(functools.partial(attention_back_kernel, seqs // 2, listed...  17.3 us
    pallas_call x1, Pallas kernels, ffn_forward(): pl.pallas_call(functools.partial(ffn_kernel, seqs, listed // seqs), out_s...  13.9 us
    pallas_call x3, Pallas kernels, weight_grad(): pl.pallas_call(weight_grad_kernel, out_shape=(out(shape, LOW), out(shape,...  9.96 us
    pallas_call x1, Pallas kernels, attention_grads(): pl.pallas_call(attention_grads_kernel, out_shape=(out((2, 2, LINE, half,...  8.84 us
  transfers between devices with their start and end apart: 54, of which 22 were waited for; matrix products, arithmetic and copies ran while one was open for 4% of the time, Pallas kernels for 26%

profile of v11, /device:TPU:0, one launch (start us, length us, event | category | flops | bytes accessed | tf_op | source)
XLA Modules:
  0.0 288.2 jit_solution(3056757324216577281)
XLA Ops:
  9.6 4.1 %collective-permute-start.1 = (bf16[104,768]{1,0:T(8,128)(2,1)S(1)}, bf16[104,768]{1,0:T(8,128)(2,1)S(1)}, u32[]{:S(2)}, u32[]{:S(2)}) collective-permute-start(bf16[104,768]{1,0:T(8,128)(2,1)S(1)} %get-tuple-element.181), channel_id=1, source_target_pairs={{0,16},{1,17},{2,18},{3,19},{4,20},{5,21},{6,22},{7,23},{8,24},{9,... | collective-permute-start | bytes 479240 | tf_op jit(solution)/shard_map/ppermute | solution.py:568
  18.8 6.8 %collective-permute-done.1 = bf16[104,768]{1,0:T(8,128)(2,1)S(1)} collective-permute-done((bf16[104,768]{1,0:T(8,128)(2,1)S(1)}, bf16[104,768]{1,0:T(8,128)(2,1)S(1)}, u32[]{:S(2)}, u32[]{:S(2)}) %collective-permute-start.1) | collective-permute-done | bytes 159776 | tf_op jit(solution)/shard_map/ppermute | solution.py:568
  31.4 6.8 %collective-permute-done.6.rest_5_ = bf16[4,56,768]{2,1,0:T(8,128)(2,1)S(1)} collective-permute-done((bf16[4,56,768]{2,1,0:T(8,128)(2,1)S(1)}, bf16[4,56,768]{2,1,0:T(8,128)(2,1)S(1)}, u32[]{:S(2)}, u32[]{:S(2)}) %collective-permute-start.6) | collective-permute-done | bytes 344096 | tf_op jit(solution)/shard_map/ppermute | solution.py:568
  42.5 4.0 %collective-permute-done.4.rest_2_ = bf16[4,48,768]{2,1,0:T(8,128)(2,1)} collective-permute-done((bf16[4,48,768]{2,1,0:T(8,128)(2,1)S(1)}, bf16[4,48,768]{2,1,0:T(8,128)(2,1)}, u32[]{:S(2)}, u32[]{:S(2)}) %collective-permute-start.4) | collective-permute-done | bytes 294944 | tf_op jit(solution)/shard_map/ppermute | solution.py:568
  50.7 5.5 %collective-permute-done.8.rest_7_ = bf16[4,56,768]{2,1,0:T(8,128)(2,1)S(1)} collective-permute-done((bf16[4,56,768]{2,1,0:T(8,128)(2,1)S(1)}, bf16[4,56,768]{2,1,0:T(8,128)(2,1)S(1)}, u32[]{:S(2)}, u32[]{:S(2)}) %collective-permute-start.8) | collective-permute-done | bytes 344096 | tf_op jit(solution)/shard_map/ppermute | solution.py:568
  56.8 6.1 %collective-permute-done.7.rest_6_ = bf16[4,48,768]{2,1,0:T(8,128)(2,1)} collective-permute-done((bf16[4,48,768]{2,1,0:T(8,128)(2,1)}, bf16[4,48,768]{2,1,0:T(8,128)(2,1)}, u32[]{:S(2)}, u32[]{:S(2)}) %collective-permute-start.7) | collective-permute-done | bytes 294944 | tf_op jit(solution)/shard_map/ppermute | solution.py:568
  65.7 18.1 %attention_forward.1 = (bf16[512,2304]{1,0:T(8,128)(2,1)}, f32[512,768]{1,0:T(8,128)}, bf16[128,768]{1,0:T(8,128)(2,1)}, bf16[128,768]{1,0:T(8,128)(2,1)}, bf16[...) custom-call(s32[5]{0:T(128)} %stack.95.where_ref, f32[12]{0:T(128)} %multiply_exponential_fusion.slope_ref, ...), custom_call_target="tpu_custom_call" | custom-call | bytes 60000000 | tf_op jit(solution)/shard_map/attention_forward/pallas_call | solution.py:164
  85.6 10.4 %collective-permute-done.18 = bf16[128,768]{1,0:T(8,128)(2,1)S(1)} collective-permute-done((bf16[128,768]{1,0:T(8,128)(2,1)}, bf16[128,768]{1,0:T(8,128)(2,1)S(1)}, u32[]{:S(2)}, u32[]{:S(2)}) %collective-permute-start.18) | collective-permute-done | bytes 196640 | tf_op jit(solution)/shard_map/ppermute | solution.py:568
  99.3 30.3 %all-gather.3.cloned.1.call-done = bf16[96,96,768]{2,1,0:T(8,128)(2,1)} async-done(((bf16[3,96,768]{2,1,0:T(8,128)(2,1)}), bf16[96,96,768]{2,1,0:T(8,128)(2,1)}) %all-gather.3.cloned.1.call-update) | async-done | bytes 14155792 | tf_op jit(solution)/shard_map/all_gather | solution.py:674
  129.6 13.9 %ffn_forward.1 = (bf16[512,768]{1,0:T(8,128)(2,1)}, f32[128,768]{1,0:T(8,128)}, bf16[128,768]{1,0:T(8,128)(2,1)}, f32[2,768]{1,0:T(2,128)}) custom-call(f32[512,768]{1,0:T(8,128)} %get-tuple-element.89.h1_ref, bf16[8,4,3,96,768]{4,3,2,1,0:T(8,128)(2,1)} %bitcast.136, bf16[8,4,3,96,768]{4,3,2,1,0:T(8,128)(2,1)} %bitcast.137, ...), custom_call_target="tpu_custom_call" | custom-call | bytes 48000000 | tf_op jit(solution)/shard_map/ffn_forward/pallas_call | solution.py:233
  144.1 6.1 %ffn_again.1 = (bf16[512,768]{1,0:T(8,128)(2,1)}, f32[512,768]{1,0:T(8,128)}, f32[512,768]{1,0:T(8,128)}) custom-call(s32[5]{0:T(128)} %stack.95.where_ref, bf16[4,128,768]{2,1,0:T(8,128)(2,1)} %pad_maximum_fusion.1.h_ref.a_ref, bf16[8,4,3,96,768]{4,3,2,1,0:T(8,128)(2,1)} %bitcast.139, bf16[8,4,3,96,768]{4,3,2,1,0:T(8,128)(2,1)} %bitcast.140), custom_call_target="tpu_custom_call" | custom-call | bytes 18000000 | tf_op jit(solution)/shard_map/ffn_again/pallas_call | solution.py:294
  153.3 7.5 %ffn_back.1 = (bf16[512,768]{1,0:T(8,128)(2,1)}, bf16[512,768]{1,0:T(8,128)(2,1)}, f32[2,128,768]{2,1,0:T(8,128)}, bf16[2,128,768]{2,1,0:T(8,128)(2,1)}) custom-call(s32[5]{0:T(128)} %stack.95.where_ref, bf16[4,128,768]{2,1,0:T(8,128)(2,1)} %pad_maximum_fusion.2.b_ref.e_ref, f32[512,768]{1,0:T(8,128)} %get-tuple-element.98.to_gate_ref, ...), custom_call_target="tpu_custom_call" | custom-call | bytes 21000000 | tf_op jit(solution)/shard_map/ffn_back/pallas_call | solution.py:329
  160.9 3.3 %weight_grad.3 = (bf16[4,96,768]{2,1,0:T(8,128)(2,1)}, bf16[4,96,768]{2,1,0:T(8,128)(2,1)}) custom-call(s32[5]{0:T(128)} %stack.95.where_ref, bf16[512,768]{1,0:T(8,128)(2,1)} %get-tuple-element.93.a_ref, bf16[4,128,768]{2,1,0:T(8,128)(2,1)} %pad_maximum_fusion.2.b_ref.e_ref), custom_call_target="tpu_custom_call" | custom-call | bytes 12000000 | tf_op jit(solution)/shard_map/weight_grad/pallas_call | solution.py:363
  167.0 3.3 %weight_grad.4 = (bf16[4,96,768]{2,1,0:T(8,128)(2,1)}, bf16[4,96,768]{2,1,0:T(8,128)(2,1)}) custom-call(s32[5]{0:T(128)} %stack.95.where_ref, bf16[4,128,768]{2,1,0:T(8,128)(2,1)} %pad_maximum_fusion.1.h_ref.a_ref, bf16[512,768]{1,0:T(8,128)(2,1)} %get-tuple-element.103.b_ref), custom_call_target="tpu_custom_call" | custom-call | bytes 12000000 | tf_op jit(solution)/shard_map/weight_grad/pallas_call | solution.py:363
  172.7 3.3 %weight_grad.5 = (bf16[4,96,768]{2,1,0:T(8,128)(2,1)}, bf16[4,96,768]{2,1,0:T(8,128)(2,1)}) custom-call(s32[5]{0:T(128)} %stack.95.where_ref, bf16[4,128,768]{2,1,0:T(8,128)(2,1)} %pad_maximum_fusion.1.h_ref.a_ref, bf16[512,768]{1,0:T(8,128)(2,1)} %get-tuple-element.106.b_ref), custom_call_target="tpu_custom_call" | custom-call | bytes 12000000 | tf_op jit(solution)/shard_map/weight_grad/pallas_call | solution.py:363
  179.7 8.7 %attention_back.2.rhs0_ref = bf16[256,2304]{1,0:T(8,128)(2,1)} custom-call(f32[12]{0:T(128)} %multiply_exponential_fusion.slope_ref, bf16[128,768]{1,0:T(8,128)(2,1)} %get-tuple-element.117.datt_ref, bf16[128,768]{1,0:T(8,128)(2,1)} %get-tuple-element.112.q_ref, bf16[512,2304]{1,0:T(8,128)(2,1)} %get-tuple-element.113.qkv_ref, s32[128,1]{1,0:T(8,128)} %reshape.140.pos_ref), custom_call_target="tpu_custom_call" | custom-call | bytes 24000000 | tf_op jit(solution)/shard_map/attention_back/pallas_call | solution.py:446
  192.3 8.6 %attention_back.3.rhs1_ref = bf16[256,2304]{1,0:T(8,128)(2,1)} custom-call(f32[12]{0:T(128)} %multiply_exponential_fusion.slope_ref, bf16[128,768]{1,0:T(8,128)(2,1)} %get-tuple-element.117.datt_ref, bf16[128,768]{1,0:T(8,128)(2,1)} %get-tuple-element.112.q_ref, bf16[512,2304]{1,0:T(8,128)(2,1)} %get-tuple-element.113.qkv_ref, s32[128,1]{1,0:T(8,128)} %reshape.140.pos_ref), custom_call_target="tpu_custom_call" | custom-call | bytes 24000000 | tf_op jit(solution)/shard_map/attention_back/pallas_call | solution.py:446
  208.2 8.8 %attention_grads.1 = (bf16[2,2,4,48,768]{4,3,2,1,0:T(8,128)(2,1)}, bf16[2,2,4,56,768]{4,3,2,1,0:T(8,128)(2,1)}, bf16[2,2,4,48,768]{4,3,2,1,0:T(8,128)(2,1)}, bf16[2,2,4,56,768]{4,3,2,1,0:T(8,128)(2,1)}) custom-call(s32[5]{0:T(128)} %stack.95.where_ref, bf16[768,512]{1,0:T(8,128)(2,1)} %bitcast.144, bf16[256,2304]{1,0:T(8,128)(2,1)} %attention_back.2.rhs0_ref, ...), custom_call_target="tpu_custom_call" | custom-call | bytes 30000000 | tf_op jit(solution)/shard_map/attention_grads/pallas_call | solution.py:499
  225.8 3.4 %collective-permute-start.43 = (bf16[96,768]{1,0:T(8,128)(2,1)S(1)}, bf16[96,768]{1,0:T(8,128)(2,1)S(1)}, u32[]{:S(2)}, u32[]{:S(2)}) collective-permute-start(bf16[96,768]{1,0:T(8,128)(2,1)S(1)} %get-tuple-element.162), channel_id=1, source_target_pairs={{0,24},{1,25},{2,26},{3,27},{4,28},{5,29},{6,30},{7,31},{8,0},{9,1... | collective-permute-start | bytes 442376 | tf_op jit(solution)/shard_map/ppermute | solution.py:568
  229.8 11.4 %collective-permute-done.35 = bf16[2,4,48,768]{3,2,1,0:T(8,128)(2,1)S(1)} collective-permute-done((bf16[2,4,48,768]{3,2,1,0:T(8,128)(2,1)S(1)}, bf16[2,4,48,768]{3,2,1,0:T(8,128)(2,1)S(1)}, u32[]{:S(2)}, u32[]{:S(2)}) %collective-permute-start.35) | collective-permute-done | bytes 589856 | tf_op jit(solution)/shard_map/ppermute | solution.py:568
  251.5 4.3 %collective-permute-done.39 = bf16[4,56,768]{2,1,0:T(8,128)(2,1)S(1)} collective-permute-done((bf16[4,56,768]{2,1,0:T(8,128)(2,1)S(1)}, bf16[4,56,768]{2,1,0:T(8,128)(2,1)S(1)}, u32[]{:S(2)}, u32[]{:S(2)}) %collective-permute-start.39) | collective-permute-done | bytes 344096 | tf_op jit(solution)/shard_map/ppermute | solution.py:568
  256.1 3.8 %collective-permute-start.46 = (bf16[104,768]{1,0:T(8,128)(2,1)S(1)}, bf16[104,768]{1,0:T(8,128)(2,1)S(1)}, u32[]{:S(2)}, u32[]{:S(2)}) collective-permute-start(bf16[104,768]{1,0:T(8,128)(2,1)S(1)} %get-tuple-element.173), channel_id=1, source_target_pairs={{0,24},{1,25},{2,26},{3,27},{4,28},{5,29},{6,30},{7,31},{8,0},{9,1... | collective-permute-start | bytes 479240 | tf_op jit(solution)/shard_map/ppermute | solution.py:568
  261.3 8.2 %input_grad.1 = f32[512,768]{1,0:T(8,128)} custom-call(bf16[256,2304]{1,0:T(8,128)(2,1)} %attention_back.2.rhs0_ref, bf16[256,2304]{1,0:T(8,128)(2,1)} %attention_back.3.rhs1_ref, bf16[8,4,96,768]{3,2,1,0:T(8,128)(2,1)} %get-tuple-element.110.w_ref, f32[128,768]{1,0:T(8,128)} %get-tuple-element.147.dr1_ref, s32[4,32]{1,0:T(4,128)} %pos_ref.1), custom_call_target="tpu_custom_call" | custom-call | bytes 24000000 | tf_op jit(solution)/shard_map/input_grad/pallas_call | solution.py:531
  273.5 3.4 %finish_ffn.1 = (f32[384,768]{1,0:T(8,128)}, f32[96,6144]{1,0:T(8,128)}) custom-call(s32[5]{0:T(128)} %stack.95.where_ref, bf16[3,96,768]{2,1,0:T(8,128)(2,1)} %copy-done.1, bf16[3,96,768]{2,1,0:T(8,128)(2,1)} %copy-done.13, bf16[3,96,768]{2,1,0:T(8,128)(2,1)} %copy-done.12, bf16[3,96,768]{2,1,0:T(8,128)(2,1)} %copy-done.14), custom_call_target="tpu_custom_call" | custom-call | bytes 12000000 | tf_op jit(solution)/shard_map/finish_ffn/pallas_call | solution.py:617
  (226 shorter events, 83.2 us)
Async XLA Ops:
  7.2 122.3 %all-gather.3.cloned.1.call-start = ((), (), s32[]{:S(2)}) async-start(), calls=%async_computation | async-start | bytes 14598144 | tf_op jit(solution)/shard_map/all_gather | solution.py:674
  9.6 16.0 %collective-permute-start.1 = (bf16[104,768]{1,0:T(8,128)(2,1)S(1)}, bf16[104,768]{1,0:T(8,128)(2,1)S(1)}, u32[]{:S(2)}, u32[]{:S(2)}) collective-permute-start(bf16[104,768]{1,0:T(8,128)(2,1)S(1)} %get-tuple-element.181), channel_id=1, source_target_pairs={{0,16},{1,17},{2,18},{3,19},{4,20},{5,21},{6,22},{7,23},{8,24},{9,... | collective-permute-start | bytes 479240 | tf_op jit(solution)/shard_map/ppermute | solution.py:568
  29.0 13.5 %collective-permute-start.5 = (bf16[4,48,768]{2,1,0:T(8,128)(2,1)S(1)}, bf16[4,48,768]{2,1,0:T(8,128)(2,1)}, u32[]{:S(2)}, u32[]{:S(2)}) collective-permute-start(bf16[4,48,768]{2,1,0:T(8,128)(2,1)S(1)} %slice.169.rest_0_), channel_id=1, source_target_pairs={{0,2},{1,3},{2,0},{3,1},{4,6},{5,7},{6,4},{7,5},{8,10},{9,11},{10,... | collective-permute-start | bytes 884744 | tf_op jit(solution)/shard_map/ppermute | solution.py:568
  29.4 17.1 %collective-permute-start.3 = (bf16[4,56,768]{2,1,0:T(8,128)(2,1)S(1)}, bf16[4,56,768]{2,1,0:T(8,128)(2,1)S(1)}, u32[]{:S(2)}, u32[]{:S(2)}) collective-permute-start(bf16[4,56,768]{2,1,0:T(8,128)(2,1)S(1)} %slice.167.rest_1_), channel_id=1, source_target_pairs={{0,4},{1,5},{2,6},{3,7},{4,0},{5,1},{6,2},{7,3},{8,12},{9,13},{10,... | collective-permute-start | bytes 1032200 | tf_op jit(solution)/shard_map/ppermute | solution.py:568
  31.2 15.3 %collective-permute-start.4 = (bf16[4,48,768]{2,1,0:T(8,128)(2,1)S(1)}, bf16[4,48,768]{2,1,0:T(8,128)(2,1)}, u32[]{:S(2)}, u32[]{:S(2)}) collective-permute-start(bf16[4,48,768]{2,1,0:T(8,128)(2,1)S(1)} %slice.169.rest_0_), channel_id=1, source_target_pairs={{0,4},{1,5},{2,6},{3,7},{4,0},{5,1},{6,2},{7,3},{8,12},{9,13},{10,... | collective-permute-start | bytes 884744 | tf_op jit(solution)/shard_map/ppermute | solution.py:568
  31.4 19.1 %collective-permute-start.10 = (bf16[4,56,768]{2,1,0:T(8,128)(2,1)S(1)}, bf16[4,56,768]{2,1,0:T(8,128)(2,1)S(1)}, u32[]{:S(2)}, u32[]{:S(2)}) collective-permute-start(bf16[4,56,768]{2,1,0:T(8,128)(2,1)S(1)} %slice.167.rest_1_), channel_id=1, source_target_pairs={{0,1},{1,0},{2,3},{3,2},{4,5},{5,4},{6,7},{7,6},{8,9},{9,8},{10,11... | collective-permute-start | bytes 1032200 | tf_op jit(solution)/shard_map/ppermute | solution.py:568
  38.2 18.0 %collective-permute-start.8 = (bf16[4,56,768]{2,1,0:T(8,128)(2,1)S(1)}, bf16[4,56,768]{2,1,0:T(8,128)(2,1)S(1)}, u32[]{:S(2)}, u32[]{:S(2)}) collective-permute-start(bf16[4,56,768]{2,1,0:T(8,128)(2,1)S(1)} %collective-permute-done.6.rest_5_), channel_id=1, source_target_pairs={{0,4},{1,5},{2,6},{3,7},{4,0},{5,1},{6,2},{7,3},{8,12},{9,13},{10,... | collective-permute-start | bytes 1032200 | tf_op jit(solution)/shard_map/ppermute | solution.py:568
  46.5 16.4 %collective-permute-start.7 = (bf16[4,48,768]{2,1,0:T(8,128)(2,1)}, bf16[4,48,768]{2,1,0:T(8,128)(2,1)}, u32[]{:S(2)}, u32[]{:S(2)}) collective-permute-start(bf16[4,48,768]{2,1,0:T(8,128)(2,1)} %collective-permute-done.4.rest_2_), channel_id=1, source_target_pairs={{0,2},{1,3},{2,0},{3,1},{4,6},{5,7},{6,4},{7,5},{8,10},{9,11},{10,... | collective-permute-start | bytes 884744 | tf_op jit(solution)/shard_map/ppermute | solution.py:568
  49.8 14.1 %collective-permute-start.14 = (bf16[4,56,768]{2,1,0:T(8,128)(2,1)S(1)}, bf16[4,56,768]{2,1,0:T(8,128)(2,1)S(1)}, u32[]{:S(2)}, u32[]{:S(2)}) collective-permute-start(bf16[4,56,768]{2,1,0:T(8,128)(2,1)S(1)} %collective-permute-done.6.rest_5_), channel_id=1, source_target_pairs={{0,1},{1,0},{2,3},{3,2},{4,5},{5,4},{6,7},{7,6},{8,9},{9,8},{10,11... | collective-permute-start | bytes 1032200 | tf_op jit(solution)/shard_map/ppermute | solution.py:568
  50.6 13.4 %collective-permute-start.12 = (bf16[4,56,768]{2,1,0:T(8,128)(2,1)S(1)}, bf16[4,56,768]{2,1,0:T(8,128)(2,1)S(1)}, u32[]{:S(2)}, u32[]{:S(2)}) collective-permute-start(bf16[4,56,768]{2,1,0:T(8,128)(2,1)S(1)} %collective-permute-done.3.rest_3_), channel_id=1, source_target_pairs={{0,1},{1,0},{2,3},{3,2},{4,5},{5,4},{6,7},{7,6},{8,9},{9,8},{10,11... | collective-permute-start | bytes 1032200 | tf_op jit(solution)/shard_map/ppermute | solution.py:568
  164.2 24.2 %collective-permute-start.23 = (bf16[4,96,768]{2,1,0:T(8,128)(2,1)}, bf16[4,96,768]{2,1,0:T(8,128)(2,1)S(1)}, u32[]{:S(2)}, u32[]{:S(2)}) collective-permute-start(bf16[4,96,768]{2,1,0:T(8,128)(2,1)} %get-tuple-element.96), channel_id=1, source_target_pairs={{0,4},{1,5},{2,6},{3,7},{4,0},{5,1},{6,2},{7,3},{8,12},{9,13},{10,... | collective-permute-start | bytes 1769480 | tf_op jit(solution)/shard_map/ppermute | solution.py:568
  170.3 33.3 %collective-permute-start.29 = (bf16[4,96,768]{2,1,0:T(8,128)(2,1)}, bf16[4,96,768]{2,1,0:T(8,128)(2,1)S(1)}, u32[]{:S(2)}, u32[]{:S(2)}) collective-permute-start(bf16[4,96,768]{2,1,0:T(8,128)(2,1)} %get-tuple-element.104), channel_id=1, source_target_pairs={{0,4},{1,5},{2,6},{3,7},{4,0},{5,1},{6,2},{7,3},{8,12},{9,13},{10,... | collective-permute-start | bytes 1769480 | tf_op jit(solution)/shard_map/ppermute | solution.py:568
  176.0 43.9 %collective-permute-start.33 = (bf16[4,96,768]{2,1,0:T(8,128)(2,1)}, bf16[4,96,768]{2,1,0:T(8,128)(2,1)S(1)}, u32[]{:S(2)}, u32[]{:S(2)}) collective-permute-start(bf16[4,96,768]{2,1,0:T(8,128)(2,1)} %get-tuple-element.107), channel_id=1, source_target_pairs={{0,4},{1,5},{2,6},{3,7},{4,0},{5,1},{6,2},{7,3},{8,12},{9,13},{10,... | collective-permute-start | bytes 1769480 | tf_op jit(solution)/shard_map/ppermute | solution.py:568
  190.3 13.3 %collective-permute-start.27 = (bf16[96,768]{1,0:T(8,128)(2,1)S(1)}, bf16[96,768]{1,0:T(8,128)(2,1)S(1)}, u32[]{:S(2)}, u32[]{:S(2)}) collective-permute-start(bf16[96,768]{1,0:T(8,128)(2,1)S(1)} %get-tuple-element.169), channel_id=1, source_target_pairs={{0,16},{1,17},{2,18},{3,19},{4,20},{5,21},{6,22},{7,23},{8,24},{9,... | collective-permute-start | bytes 442376 | tf_op jit(solution)/shard_map/ppermute | solution.py:568
  204.4 12.7 %collective-permute-start.32 = (bf16[96,768]{1,0:T(8,128)(2,1)}, bf16[96,768]{1,0:T(8,128)(2,1)S(1)}, u32[]{:S(2)}, u32[]{:S(2)}) collective-permute-start(bf16[96,768]{1,0:T(8,128)(2,1)} %get-tuple-element.165), channel_id=1, source_target_pairs={{0,24},{1,25},{2,26},{3,27},{4,28},{5,29},{6,30},{7,31},{8,0},{9,1... | collective-permute-start | bytes 442376 | tf_op jit(solution)/shard_map/ppermute | solution.py:568
  204.4 15.6 %collective-permute-start.31 = (bf16[96,768]{1,0:T(8,128)(2,1)S(1)}, bf16[96,768]{1,0:T(8,128)(2,1)S(1)}, u32[]{:S(2)}, u32[]{:S(2)}) collective-permute-start(bf16[96,768]{1,0:T(8,128)(2,1)S(1)} %get-tuple-element.166), channel_id=1, source_target_pairs={{0,16},{1,17},{2,18},{3,19},{4,20},{5,21},{6,22},{7,23},{8,24},{9,... | collective-permute-start | bytes 442376 | tf_op jit(solution)/shard_map/ppermute | solution.py:568
  206.2 13.7 %collective-permute-start.30 = (bf16[96,768]{1,0:T(8,128)(2,1)S(1)}, bf16[96,768]{1,0:T(8,128)(2,1)S(1)}, u32[]{:S(2)}, u32[]{:S(2)}) collective-permute-start(bf16[96,768]{1,0:T(8,128)(2,1)S(1)} %get-tuple-element.167), channel_id=1, source_target_pairs={{0,8},{1,9},{2,10},{3,11},{4,12},{5,13},{6,14},{7,15},{8,16},{9,17... | collective-permute-start | bytes 442376 | tf_op jit(solution)/shard_map/ppermute | solution.py:568
  220.6 25.7 %collective-permute-start.40 = (bf16[96,768]{1,0:T(8,128)(2,1)S(1)}, bf16[96,768]{1,0:T(8,128)(2,1)S(1)}, u32[]{:S(2)}, u32[]{:S(2)}) collective-permute-start(bf16[96,768]{1,0:T(8,128)(2,1)S(1)} %fusion.20), channel_id=1, source_target_pairs={{0,0},{1,8},{2,16},{3,24},{4,1},{5,9},{6,17},{7,25},{8,2},{9,10},{... | collective-permute-start | bytes 442376 | tf_op jit(solution)/shard_map/ppermute | solution.py:568
  224.4 16.8 %collective-permute-start.35 = (bf16[2,4,48,768]{3,2,1,0:T(8,128)(2,1)S(1)}, bf16[2,4,48,768]{3,2,1,0:T(8,128)(2,1)S(1)}, u32[]{:S(2)}, u32[]{:S(2)}) collective-permute-start(bf16[2,4,48,768]{3,2,1,0:T(8,128)(2,1)S(1)} %fusion.3), channel_id=1, source_target_pairs={{0,2},{1,3},{2,0},{3,1},{4,6},{5,7},{6,4},{7,5},{8,10},{9,11},{10,... | collective-permute-start | bytes 1769480 | tf_op jit(solution)/shard_map/ppermute | solution.py:568
  225.8 21.7 %collective-permute-start.43 = (bf16[96,768]{1,0:T(8,128)(2,1)S(1)}, bf16[96,768]{1,0:T(8,128)(2,1)S(1)}, u32[]{:S(2)}, u32[]{:S(2)}) collective-permute-start(bf16[96,768]{1,0:T(8,128)(2,1)S(1)} %get-tuple-element.162), channel_id=1, source_target_pairs={{0,24},{1,25},{2,26},{3,27},{4,28},{5,29},{6,30},{7,31},{8,0},{9,1... | collective-permute-start | bytes 442376 | tf_op jit(solution)/shard_map/ppermute | solution.py:568
  229.2 18.3 %collective-permute-start.42 = (bf16[96,768]{1,0:T(8,128)(2,1)S(1)}, bf16[96,768]{1,0:T(8,128)(2,1)S(1)}, u32[]{:S(2)}, u32[]{:S(2)}) collective-permute-start(bf16[96,768]{1,0:T(8,128)(2,1)S(1)} %get-tuple-element.163), channel_id=1, source_target_pairs={{0,16},{1,17},{2,18},{3,19},{4,20},{5,21},{6,22},{7,23},{8,24},{9,... | collective-permute-start | bytes 442376 | tf_op jit(solution)/shard_map/ppermute | solution.py:568
  229.4 14.2 %collective-permute-start.38 = (bf16[2,4,56,768]{3,2,1,0:T(8,128)(2,1)S(1)}, bf16[2,4,56,768]{3,2,1,0:T(8,128)(2,1)S(1)}, u32[]{:S(2)}, u32[]{:S(2)}) collective-permute-start(bf16[2,4,56,768]{3,2,1,0:T(8,128)(2,1)S(1)} %fusion.1), channel_id=1, source_target_pairs={{0,4},{1,5},{2,6},{3,7},{4,0},{5,1},{6,2},{7,3},{8,12},{9,13},{10,... | collective-permute-start | bytes 2064392 | tf_op jit(solution)/shard_map/ppermute | solution.py:568
  249.0 20.6 %collective-permute-start.47 = (bf16[3,96,768]{2,1,0:T(8,128)(2,1)S(1)}, bf16[3,96,768]{2,1,0:T(8,128)(2,1)S(1)}, u32[]{:S(2)}, u32[]{:S(2)}) collective-permute-start(bf16[3,96,768]{2,1,0:T(8,128)(2,1)S(1)} %pad_maximum_fusion.5.rest_0_), channel_id=1, source_target_pairs={{0,2},{1,3},{2,0},{3,1},{4,6},{5,7},{6,4},{7,5},{8,10},{9,11},{10,... | collective-permute-start | bytes 1327112 | tf_op jit(solution)/shard_map/ppermute | solution.py:568
  256.1 13.5 %collective-permute-start.46 = (bf16[104,768]{1,0:T(8,128)(2,1)S(1)}, bf16[104,768]{1,0:T(8,128)(2,1)S(1)}, u32[]{:S(2)}, u32[]{:S(2)}) collective-permute-start(bf16[104,768]{1,0:T(8,128)(2,1)S(1)} %get-tuple-element.173), channel_id=1, source_target_pairs={{0,24},{1,25},{2,26},{3,27},{4,28},{5,29},{6,30},{7,31},{8,0},{9,1... | collective-permute-start | bytes 479240 | tf_op jit(solution)/shard_map/ppermute | solution.py:568
  (67 other events, 563.3 us)
Sparse Core Ops, SparseCore 0:
  11.5 117.9 all-gather.2

commit v12 on v11

--- a/solution.py
+++ b/solution.py
@@ -402,17 +402,50 @@
     )(dr2, part, came, r1_m, w_attn, norms)
 
 
-def attention_back_kernel(seqs, most, slope_ref, datt_ref, q_ref, qkv_ref, pos_ref, rhs_ref, away_ref, hot_ref):
-    length = qkv_ref.shape[0] // seqs
-    listed = seqs * most
+def both_heads(value):
+    first = lax.broadcasted_iota(jnp.int32, value.shape, 1) < HEAD_DIM
+    zero = jnp.zeros_like(value)
+    return jnp.concatenate([jnp.where(first, value, zero), jnp.where(first, zero, value)], axis=0)
+
+
+def attention_again_kernel(seqs, slope_ref, q_ref, k_ref, pos_ref, p_ref):
+    length, most = k_ref.shape[0] // seqs, q_ref.shape[0] // seqs
+    spots = lax.broadcasted_iota(jnp.int32, (most, length), 1)
+
+    @pl.loop(0, HEADS // 2)
+    def _(t):
+        lane = pl.multiple_of(t * 128, 128)
+        for s in range(seqs):
+            rows = slice(s * length, (s + 1) * length)
+            mine = slice(s * most, (s + 1) * most)
+            away = jnp.abs(pos_ref[mine, :] - spots).astype(F32)
+            bias = jnp.concatenate([slope_ref[2 * t] * away, slope_ref[2 * t + 1] * away], axis=0)
+            score = mm_nt(both_heads(q_ref[mine, pl.ds(lane, 128)]), k_ref[rows, pl.ds(lane, 128)]) * SCALE - bias
+            e = jnp.exp(score - jnp.max(score, axis=-1, keepdims=True))
+            p = e * (1.0 / jnp.sum(e, axis=-1, keepdims=True))
+            p_ref[2 * t, mine, :] = p[:most]
+            p_ref[2 * t + 1, mine, :] = p[most:]
+
+
+def attention_again(q_m, qkv, pos, slopes, seqs):
+    tokens, listed = qkv.shape[0], pos.shape[0]
+    shape = (HEADS, listed, tokens // seqs)
+    return pl.pallas_call(
+        functools.partial(attention_again_kernel, seqs),
+        out_shape=out(shape, F32),
+        grid=(1,),
+        in_specs=[SMEM, pl.BlockSpec((listed, D), lambda g: (0, 0)), pl.BlockSpec((tokens, D), lambda g: (0, 1)), pl.BlockSpec((listed, 1), lambda g: (0, 0))],
+        out_specs=pl.BlockSpec(shape, lambda g: (0, 0, 0)),
+        compiler_params=BIG,
+        cost_estimate=cost(8),
+        name="attention_again",
+    )(slopes, q_m, qkv, pos)
+
+
+def attention_back_kernel(seqs, datt_ref, q_ref, k_ref, v_ref, p_ref, pos_ref, rhs_ref, hot_ref):
+    length, most = k_ref.shape[0] // seqs, q_ref.shape[0] // seqs
     first_m = lax.broadcasted_iota(jnp.int32, (most, 128), 1) < HEAD_DIM
-    spots = lax.broadcasted_iota(jnp.int32, (listed, length), 1)
-    away_ref[...] = jnp.abs(pos_ref[...] - spots).astype(F32)
-    hot_ref[...] = (spots == pos_ref[...]).astype(LOW)
-
-    def both(value):
-        zero = jnp.zeros_like(value)
-        return jnp.concatenate([jnp.where(first_m, value, zero), jnp.where(first_m, zero, value)], axis=0)
+    hot_ref[...] = (lax.broadcasted_iota(jnp.int32, hot_ref.shape, 1) == pos_ref[...]).astype(LOW)
 
     @pl.loop(0, HEADS // 4)
     def _(step):
@@ -421,15 +454,11 @@
             lane = pl.multiple_of(t * 128, 128)
             rows = slice(s * length, (s + 1) * length)
             mine = slice(s * most, (s + 1) * most)
-            away = away_ref[mine, :]
-            q = both(q_ref[mine, pl.ds(lane, 128)])
-            da = both(datt_ref[mine, pl.ds(lane, 128)])
-            k = qkv_ref[rows, pl.ds(D + lane, 128)]
-            v = qkv_ref[rows, pl.ds(2 * D + lane, 128)]
-            bias = jnp.concatenate([slope_ref[2 * t] * away, slope_ref[2 * t + 1] * away], axis=0)
-            score = mm_nt(q, k) * SCALE - bias
-            e = jnp.exp(score - jnp.max(score, axis=-1, keepdims=True))
-            p = e * (1.0 / jnp.sum(e, axis=-1, keepdims=True))
+            q = both_heads(q_ref[mine, pl.ds(lane, 128)])
+            da = both_heads(datt_ref[mine, pl.ds(lane, 128)])
+            k = k_ref[rows, pl.ds(lane, 128)]
+            v = v_ref[rows, pl.ds(lane, 128)]
+            p = jnp.concatenate([p_ref[2 * t, mine, :], p_ref[2 * t + 1, mine, :]], axis=0)
             dp = mm_nt(da, v)
             ds = (p * (dp - jnp.sum(dp * p, axis=-1, keepdims=True))).astype(LOW)
             dq = mm(ds, k)
@@ -439,21 +468,28 @@
             rhs_ref[rows, pl.ds(2 * D + lane, 128)] = mm_tn(p.astype(LOW), da).astype(LOW)
 
 
-def attention_back(datt, q_m, qkv, pos, slopes, seqs, part):
+def attention_back(datt, q_m, qkv, p_m, pos, seqs, part):
     tokens, listed = qkv.shape[0] // 2, pos.shape[0] // 2
     length = tokens * 2 // seqs
-    mine = lambda shape: pl.BlockSpec(shape, lambda g: (part, 0))
-    return pl.pallas_call(
-        functools.partial(attention_back_kernel, seqs // 2, listed * 2 // seqs),
+    mine = lambda shape, lane=0: pl.BlockSpec(shape, lambda g: (part, lane))
+    return pl.pallas_call(
+        functools.partial(attention_back_kernel, seqs // 2),
         out_shape=out((tokens, 3 * D), LOW),
         grid=(1,),
-        in_specs=[SMEM, mine((listed, D)), mine((listed, D)), mine((tokens, 3 * D)), mine((listed, 1))],
+        in_specs=[
+            mine((listed, D)),
+            mine((listed, D)),
+            mine((tokens, D), 1),
+            mine((tokens, D), 2),
+            pl.BlockSpec((HEADS, listed, length), lambda g: (0, part, 0)),
+            mine((listed, 1)),
+        ],
         out_specs=pl.BlockSpec((tokens, 3 * D), lambda g: (0, 0)),
-        scratch_shapes=[pltpu.VMEM((listed, length), F32), pltpu.VMEM((listed, length), LOW)],
+        scratch_shapes=[pltpu.VMEM((listed, length), LOW)],
         compiler_params=BIG,
         cost_estimate=cost(8),
         name="attention_back",
-    )(slopes, datt, q_m, qkv, pos)
+    )(datt, q_m, qkv, qkv, p_m, pos)
 
 
 def attention_grads_kernel(where_ref, flip_ref, rhs0_ref, rhs1_ref, att_ref, low_ref, small_attn_ref, small_ffn_ref, keep0_ref, keep1_ref, away0_ref, away1_ref, full_ref, tail_ref):
@@ -683,7 +719,8 @@
 
     qkv, h1, att_m, h1_m, q_m, r1_m, w_attn = attention_forward(where, x, lines, norms, pos, slopes, seqs)
     h_all = jnp.stack(share_dp(h1_m))
-    h1, h_all = lax.optimization_barrier((h1, h_all))
+    p_m = attention_again(q_m, qkv, pos, slopes, seqs)
+    h1, h_all, p_m = lax.optimization_barrier((h1, h_all, p_m))
     layer_out, dr2, e2, small_ffn = ffn_forward(h1, w_ffn, norms, pos, dy, seqs)
     act, to_gate, to_up = ffn_again(where, h_all, w_ffn)
     other = after(send(e2, "x"), act)
@@ -699,18 +736,20 @@
     keep_u, away_u = weight_grad(where, after(h_all, (away_g, came)), dup)
     got_u = send(away_u, "y")
     dr1, low, datt, small_attn = norm_back_call(dr2, part, after(came, away_u), r1_m, w_attn, norms)
-    rhs0 = attention_back(datt, q_m, qkv, pos, slopes, seqs, 0)
+    rhs0 = attention_back(datt, q_m, qkv, p_m, pos, seqs, 0)
     got_d, rhs0 = lax.optimization_barrier((got_d, rhs0))
     parts_d = line_parts(keep_d, got_d)
     line_d = line_send(parts_d)
-    rhs1 = attention_back(after(datt, (rhs0, parts_d)), q_m, qkv, pos, slopes, seqs, 1)
+    rhs1 = attention_back(after(datt, (rhs0, parts_d)), q_m, qkv, p_m, pos, seqs, 1)
     line_d, got_g, rhs1 = lax.optimization_barrier((line_d, got_g, rhs1))
-    parts_g = line_parts(keep_g, got_g)
+    half = ROWS // 2
+    parts_g = line_parts(keep_g[:, :half], got_g[:, :half])
     line_g = line_send(parts_g)
     keep0, keep1, away0, away1 = attention_grads(where, x_flip, rhs0, after(rhs1, parts_g), att_m, low, small_attn, small_ffn)
     away0, away1, line_g, got_u = lax.optimization_barrier((away0, away1, line_g, got_u))
     came0, came1 = send(away0, "c"), send(away1, "c")
-    parts_u = line_parts(keep_u, got_u)
+    rest_g = line_parts(keep_g[:, half:], got_g[:, half:])
+    parts_u = [jnp.concatenate(pair) for pair in zip(rest_g, line_parts(keep_u, got_u))]
     line_u = line_send(parts_u)
     g_down = send(line_add(keep_d, got_d, line_d), "down")
     away0, away1 = add(keep0[1], came0[1]).astype(LOW), add(keep1[1], came1[1]).astype(LOW)
@@ -720,7 +759,14 @@
     away0, away1 = total0[1].astype(LOW), total1[1].astype(LOW)
     got0, got1 = send(away0, "y"), send(away1, "x")
     g_down, line_u = after((g_down, line_u), (away0, away1))
-    g_ffn = jnp.stack([g_down, line_add(keep_g, got_g, line_g), line_add(keep_u, got_u, line_u)])
+    g_ffn = jnp.concatenate(
+        [
+            g_down,
+            line_add(keep_g[:, :half], got_g[:, :half], line_g),
+            line_add(keep_g[:, half:], got_g[:, half:], [value[:half] for value in line_u]),
+            line_add(keep_u, got_u, [value[half:] for value in line_u]),
+        ]
+    ).reshape(3, ROWS, D)
     got0, got1 = after((got0, got1), g_ffn)
     total = jnp.concatenate([add(total0[0], got0), add(total1[0], got1)], axis=1)
     parts = [total[r].astype(LOW) for r in (1, 2, 3)]

time: 289 us -> 286 us (0.990)
    ppermute x53, waiting for transfers between devices: 75.2 us -> 78.1 us  [send(): return lax.ppermute(value, AXES, MOVES[move])]
    pallas_call x2 -> x3, Pallas kernels: 17.3 us -> 17.7 us  [the longest x2 13.3 us: attention_back(): pl.pallas_call(functools.partial(attention_back_kernel, seqs // 2), out_s...]
  transfers between devices with their start and end apart: 54 -> 54, of which waited for: 22 -> 23; matrix products, arithmetic and copies ran while one was open for 4% -> 4% of each run, Pallas kernels for 26% -> 26%
where the time goes in v12:
time: 286 us; the launch traced here: 285 us
  waiting for transfers between devices  106 us (37%)
  Pallas kernels  99.2 us (35%)
  starting transfers between devices  47.9 us (17%)
  between operations  14.7 us (5%)
  local copies, waits for them, and re-layouts  9.13 us (3%)
  other arithmetic  8.66 us (3%)
    ppermute x53, waiting for transfers between devices, send(): return lax.ppermute(value, AXES, MOVES[move])  78.1 us
    ppermute x53, starting transfers between devices, send(): return lax.ppermute(value, AXES, MOVES[move])  47.9 us
    all_gather x1, waiting for transfers between devices, on_block(): lax.all_gather(ffn_piece, AXES, axis=0, tiled=False)  27.5 us
    pallas_call x1, Pallas kernels, attention_forward(): pl.pallas_call(functools.partial(attention_kernel, seqs, listed // seqs),...  18.1 us
    pallas_call x1, Pallas kernels, ffn_forward(): pl.pallas_call(functools.partial(ffn_kernel, seqs, listed // seqs), out_s...  13.9 us
    pallas_call x2, Pallas kernels, attention_back(): pl.pallas_call(functools.partial(attention_back_kernel, seqs // 2), out_s...  13.3 us
    pallas_call x3, Pallas kernels, weight_grad(): pl.pallas_call(weight_grad_kernel, out_shape=(out(shape, LOW), out(shape,...  9.94 us
    pallas_call x1, Pallas kernels, attention_grads(): pl.pallas_call(attention_grads_kernel, out_shape=(out((2, 2, LINE, half,...  8.89 us
  transfers between devices with their start and end apart: 54, of which 23 were waited for; matrix products, arithmetic and copies ran while one was open for 4% of the time, Pallas kernels for 26%

profile of v12, /device:TPU:0, one launch (start us, length us, event | category | flops | bytes accessed | tf_op | source)
XLA Modules:
  0.0 285.2 jit_solution(17996267467899820097)
XLA Ops:
  9.6 4.1 %collective-permute-start.1 = (bf16[104,768]{1,0:T(8,128)(2,1)S(1)}, bf16[104,768]{1,0:T(8,128)(2,1)S(1)}, u32[]{:S(2)}, u32[]{:S(2)}) collective-permute-start(bf16[104,768]{1,0:T(8,128)(2,1)S(1)} %get-tuple-element.188), channel_id=1, source_target_pairs={{0,16},{1,17},{2,18},{3,19},{4,20},{5,21},{6,22},{7,23},{8,24},{9,... | collective-permute-start | bytes 479240 | tf_op jit(solution)/shard_map/ppermute | solution.py:604
  18.8 6.8 %collective-permute-done.1 = bf16[104,768]{1,0:T(8,128)(2,1)S(1)} collective-permute-done((bf16[104,768]{1,0:T(8,128)(2,1)S(1)}, bf16[104,768]{1,0:T(8,128)(2,1)S(1)}, u32[]{:S(2)}, u32[]{:S(2)}) %collective-permute-start.1) | collective-permute-done | bytes 159776 | tf_op jit(solution)/shard_map/ppermute | solution.py:604
  31.4 6.8 %collective-permute-done.6.rest_5_ = bf16[4,56,768]{2,1,0:T(8,128)(2,1)S(1)} collective-permute-done((bf16[4,56,768]{2,1,0:T(8,128)(2,1)S(1)}, bf16[4,56,768]{2,1,0:T(8,128)(2,1)S(1)}, u32[]{:S(2)}, u32[]{:S(2)}) %collective-permute-start.6) | collective-permute-done | bytes 344096 | tf_op jit(solution)/shard_map/ppermute | solution.py:604
  42.5 4.0 %collective-permute-done.4.rest_2_ = bf16[4,48,768]{2,1,0:T(8,128)(2,1)} collective-permute-done((bf16[4,48,768]{2,1,0:T(8,128)(2,1)S(1)}, bf16[4,48,768]{2,1,0:T(8,128)(2,1)}, u32[]{:S(2)}, u32[]{:S(2)}) %collective-permute-start.4) | collective-permute-done | bytes 294944 | tf_op jit(solution)/shard_map/ppermute | solution.py:604
  50.7 5.5 %collective-permute-done.8.rest_7_ = bf16[4,56,768]{2,1,0:T(8,128)(2,1)S(1)} collective-permute-done((bf16[4,56,768]{2,1,0:T(8,128)(2,1)S(1)}, bf16[4,56,768]{2,1,0:T(8,128)(2,1)S(1)}, u32[]{:S(2)}, u32[]{:S(2)}) %collective-permute-start.8) | collective-permute-done | bytes 344096 | tf_op jit(solution)/shard_map/ppermute | solution.py:604
  56.8 6.1 %collective-permute-done.7.rest_6_ = bf16[4,48,768]{2,1,0:T(8,128)(2,1)} collective-permute-done((bf16[4,48,768]{2,1,0:T(8,128)(2,1)}, bf16[4,48,768]{2,1,0:T(8,128)(2,1)}, u32[]{:S(2)}, u32[]{:S(2)}) %collective-permute-start.7) | collective-permute-done | bytes 294944 | tf_op jit(solution)/shard_map/ppermute | solution.py:604
  65.7 18.1 %attention_forward.1 = (bf16[512,2304]{1,0:T(8,128)(2,1)}, f32[512,768]{1,0:T(8,128)}, bf16[128,768]{1,0:T(8,128)(2,1)}, bf16[128,768]{1,0:T(8,128)(2,1)}, bf16[...) custom-call(s32[5]{0:T(128)} %stack.83.where_ref, f32[12]{0:T(128)} %multiply_exponential_fusion.slope_ref, ...), custom_call_target="tpu_custom_call" | custom-call | bytes 60000000 | tf_op jit(solution)/shard_map/attention_forward/pallas_call | solution.py:164
  85.5 10.4 %collective-permute-done.18 = bf16[128,768]{1,0:T(8,128)(2,1)S(1)} collective-permute-done((bf16[128,768]{1,0:T(8,128)(2,1)}, bf16[128,768]{1,0:T(8,128)(2,1)S(1)}, u32[]{:S(2)}, u32[]{:S(2)}) %collective-permute-start.18) | collective-permute-done | bytes 196640 | tf_op jit(solution)/shard_map/ppermute | solution.py:604
  96.7 4.3 %attention_again.1.p_ref = f32[12,128,128]{2,1,0:T(8,128)} custom-call(f32[12]{0:T(128)} %multiply_exponential_fusion.slope_ref, bf16[128,768]{1,0:T(8,128)(2,1)} %get-tuple-element.90.q_ref, bf16[512,2304]{1,0:T(8,128)(2,1)} %get-tuple-element.91.k_ref.v_ref, s32[128,1]{1,0:T(8,128)} %reshape.159.pos_ref), custom_call_target="tpu_custom_call" | custom-call | bytes 24000000 | tf_op jit(solution)/shard_map/attention_again/pallas_call | solution.py:433
  102.0 27.5 %all-gather.3.cloned.1.call-done = bf16[96,96,768]{2,1,0:T(8,128)(2,1)} async-done(((bf16[3,96,768]{2,1,0:T(8,128)(2,1)}), bf16[96,96,768]{2,1,0:T(8,128)(2,1)}) %all-gather.3.cloned.1.call-update) | async-done | bytes 14155792 | tf_op jit(solution)/shard_map/all_gather | solution.py:710
  129.6 13.9 %ffn_forward.1 = (bf16[512,768]{1,0:T(8,128)(2,1)}, f32[128,768]{1,0:T(8,128)}, bf16[128,768]{1,0:T(8,128)(2,1)}, f32[2,768]{1,0:T(2,128)}) custom-call(f32[512,768]{1,0:T(8,128)} %get-tuple-element.92.h1_ref, bf16[8,4,3,96,768]{4,3,2,1,0:T(8,128)(2,1)} %bitcast.142, bf16[8,4,3,96,768]{4,3,2,1,0:T(8,128)(2,1)} %bitcast.143, ...), custom_call_target="tpu_custom_call" | custom-call | bytes 48000000 | tf_op jit(solution)/shard_map/ffn_forward/pallas_call | solution.py:233
  144.1 6.1 %ffn_again.1 = (bf16[512,768]{1,0:T(8,128)(2,1)}, f32[512,768]{1,0:T(8,128)}, f32[512,768]{1,0:T(8,128)}) custom-call(s32[5]{0:T(128)} %stack.83.where_ref, bf16[4,128,768]{2,1,0:T(8,128)(2,1)} %pad_maximum_fusion.1.h_ref.a_ref, bf16[8,4,3,96,768]{4,3,2,1,0:T(8,128)(2,1)} %bitcast.145, bf16[8,4,3,96,768]{4,3,2,1,0:T(8,128)(2,1)} %bitcast.146), custom_call_target="tpu_custom_call" | custom-call | bytes 18000000 | tf_op jit(solution)/shard_map/ffn_again/pallas_call | solution.py:294
  153.3 7.4 %ffn_back.1 = (bf16[512,768]{1,0:T(8,128)(2,1)}, bf16[512,768]{1,0:T(8,128)(2,1)}, f32[2,128,768]{2,1,0:T(8,128)}, bf16[2,128,768]{2,1,0:T(8,128)(2,1)}) custom-call(s32[5]{0:T(128)} %stack.83.where_ref, bf16[4,128,768]{2,1,0:T(8,128)(2,1)} %pad_maximum_fusion.2.b_ref.e_ref, f32[512,768]{1,0:T(8,128)} %get-tuple-element.101.to_gate_ref, ...), custom_call_target="tpu_custom_call" | custom-call | bytes 21000000 | tf_op jit(solution)/shard_map/ffn_back/pallas_call | solution.py:329
  160.8 3.3 %weight_grad.3 = (bf16[4,96,768]{2,1,0:T(8,128)(2,1)}, bf16[4,96,768]{2,1,0:T(8,128)(2,1)}) custom-call(s32[5]{0:T(128)} %stack.83.where_ref, bf16[512,768]{1,0:T(8,128)(2,1)} %get-tuple-element.96.a_ref, bf16[4,128,768]{2,1,0:T(8,128)(2,1)} %pad_maximum_fusion.2.b_ref.e_ref), custom_call_target="tpu_custom_call" | custom-call | bytes 12000000 | tf_op jit(solution)/shard_map/weight_grad/pallas_call | solution.py:363
  172.6 3.3 %weight_grad.5 = (bf16[4,96,768]{2,1,0:T(8,128)(2,1)}, bf16[4,96,768]{2,1,0:T(8,128)(2,1)}) custom-call(s32[5]{0:T(128)} %stack.83.where_ref, bf16[4,128,768]{2,1,0:T(8,128)(2,1)} %pad_maximum_fusion.1.h_ref.a_ref, bf16[512,768]{1,0:T(8,128)(2,1)} %get-tuple-element.109.b_ref), custom_call_target="tpu_custom_call" | custom-call | bytes 12000000 | tf_op jit(solution)/shard_map/weight_grad/pallas_call | solution.py:363
  179.7 6.7 %attention_back.2.rhs0_ref = bf16[256,2304]{1,0:T(8,128)(2,1)} custom-call(bf16[128,768]{1,0:T(8,128)(2,1)} %get-tuple-element.119.datt_ref, bf16[128,768]{1,0:T(8,128)(2,1)} %get-tuple-element.90.q_ref, bf16[512,2304]{1,0:T(8,128)(2,1)} %get-tuple-element.91.k_ref.v_ref, bf16[512,2304]{1,0:T(8,128)(2,1)} %get-tuple-element.91.k_ref.v_ref, ...), custom_call_target="tpu_custom_call" | custom-call | bytes 24000000 | tf_op jit(solution)/shard_map/attention_back/pallas_call | solution.py:475
  190.2 6.6 %attention_back.3.rhs1_ref = bf16[256,2304]{1,0:T(8,128)(2,1)} custom-call(bf16[128,768]{1,0:T(8,128)(2,1)} %get-tuple-element.119.datt_ref, bf16[128,768]{1,0:T(8,128)(2,1)} %get-tuple-element.90.q_ref, bf16[512,2304]{1,0:T(8,128)(2,1)} %get-tuple-element.91.k_ref.v_ref, bf16[512,2304]{1,0:T(8,128)(2,1)} %get-tuple-element.91.k_ref.v_ref, ...), custom_call_target="tpu_custom_call" | custom-call | bytes 24000000 | tf_op jit(solution)/shard_map/attention_back/pallas_call | solution.py:475
  196.9 4.6 %collective-permute-done.27 = bf16[96,768]{1,0:T(8,128)(2,1)S(1)} collective-permute-done((bf16[96,768]{1,0:T(8,128)(2,1)S(1)}, bf16[96,768]{1,0:T(8,128)(2,1)S(1)}, u32[]{:S(2)}, u32[]{:S(2)}) %collective-permute-start.27) | collective-permute-done | bytes 147488 | tf_op jit(solution)/shard_map/ppermute | solution.py:604
  206.2 8.9 %attention_grads.1 = (bf16[2,2,4,48,768]{4,3,2,1,0:T(8,128)(2,1)}, bf16[2,2,4,56,768]{4,3,2,1,0:T(8,128)(2,1)}, bf16[2,2,4,48,768]{4,3,2,1,0:T(8,128)(2,1)}, bf16[2,2,4,56,768]{4,3,2,1,0:T(8,128)(2,1)}) custom-call(s32[5]{0:T(128)} %stack.83.where_ref, bf16[768,512]{1,0:T(8,128)(2,1)} %bitcast.150, bf16[256,2304]{1,0:T(8,128)(2,1)} %attention_back.2.rhs0_ref, ...), custom_call_target="tpu_custom_call" | custom-call | bytes 30000000 | tf_op jit(solution)/shard_map/attention_grads/pallas_call | solution.py:535
  225.3 12.0 %collective-permute-done.35 = bf16[2,4,48,768]{3,2,1,0:T(8,128)(2,1)S(1)} collective-permute-done((bf16[2,4,48,768]{3,2,1,0:T(8,128)(2,1)S(1)}, bf16[2,4,48,768]{3,2,1,0:T(8,128)(2,1)S(1)}, u32[]{:S(2)}, u32[]{:S(2)}) %collective-permute-start.35) | collective-permute-done | bytes 589856 | tf_op jit(solution)/shard_map/ppermute | solution.py:604
  237.3 3.7 %collective-permute-start.43 = (bf16[144,768]{1,0:T(8,128)(2,1)S(1)}, bf16[144,768]{1,0:T(8,128)(2,1)S(1)}, u32[]{:S(2)}, u32[]{:S(2)}) collective-permute-start(bf16[144,768]{1,0:T(8,128)(2,1)S(1)} %pad_maximum_fusion.8), channel_id=1, source_target_pairs={{0,24},{1,25},{2,26},{3,27},{4,28},{5,29},{6,30},{7,31},{8,0},{9,1... | collective-permute-start | bytes 663560 | tf_op jit(solution)/shard_map/ppermute | solution.py:604
  249.7 3.9 %collective-permute-done.39 = bf16[4,56,768]{2,1,0:T(8,128)(2,1)S(1)} collective-permute-done((bf16[4,56,768]{2,1,0:T(8,128)(2,1)S(1)}, bf16[4,56,768]{2,1,0:T(8,128)(2,1)S(1)}, u32[]{:S(2)}, u32[]{:S(2)}) %collective-permute-start.39) | collective-permute-done | bytes 344096 | tf_op jit(solution)/shard_map/ppermute | solution.py:604
  256.5 8.2 %input_grad.1 = f32[512,768]{1,0:T(8,128)} custom-call(bf16[256,2304]{1,0:T(8,128)(2,1)} %attention_back.2.rhs0_ref, bf16[256,2304]{1,0:T(8,128)(2,1)} %attention_back.3.rhs1_ref, bf16[8,4,96,768]{3,2,1,0:T(8,128)(2,1)} %get-tuple-element.113.w_ref, f32[128,768]{1,0:T(8,128)} %get-tuple-element.149.dr1_ref, s32[4,32]{1,0:T(4,128)} %pos_ref.1), custom_call_target="tpu_custom_call" | custom-call | bytes 24000000 | tf_op jit(solution)/shard_map/input_grad/pallas_call | solution.py:567
  270.2 3.4 %finish_ffn.1 = (f32[384,768]{1,0:T(8,128)}, f32[96,6144]{1,0:T(8,128)}) custom-call(s32[5]{0:T(128)} %stack.83.where_ref, bf16[3,96,768]{2,1,0:T(8,128)(2,1)} %bitcast.155, bf16[3,96,768]{2,1,0:T(8,128)(2,1)} %copy-done.13, bf16[3,96,768]{2,1,0:T(8,128)(2,1)} %copy-done.12, bf16[3,96,768]{2,1,0:T(8,128)(2,1)} %copy-done.14), custom_call_target="tpu_custom_call" | custom-call | bytes 12000000 | tf_op jit(solution)/shard_map/finish_ffn/pallas_call | solution.py:653
  (234 shorter events, 84.5 us)
Async XLA Ops:
  7.2 122.3 %all-gather.3.cloned.1.call-start = ((), (), s32[]{:S(2)}) async-start(), calls=%async_computation | async-start | bytes 14598144 | tf_op jit(solution)/shard_map/all_gather | solution.py:710
  9.6 16.0 %collective-permute-start.1 = (bf16[104,768]{1,0:T(8,128)(2,1)S(1)}, bf16[104,768]{1,0:T(8,128)(2,1)S(1)}, u32[]{:S(2)}, u32[]{:S(2)}) collective-permute-start(bf16[104,768]{1,0:T(8,128)(2,1)S(1)} %get-tuple-element.188), channel_id=1, source_target_pairs={{0,16},{1,17},{2,18},{3,19},{4,20},{5,21},{6,22},{7,23},{8,24},{9,... | collective-permute-start | bytes 479240 | tf_op jit(solution)/shard_map/ppermute | solution.py:604
  29.0 13.5 %collective-permute-start.5 = (bf16[4,48,768]{2,1,0:T(8,128)(2,1)S(1)}, bf16[4,48,768]{2,1,0:T(8,128)(2,1)}, u32[]{:S(2)}, u32[]{:S(2)}) collective-permute-start(bf16[4,48,768]{2,1,0:T(8,128)(2,1)S(1)} %slice.235.rest_0_), channel_id=1, source_target_pairs={{0,2},{1,3},{2,0},{3,1},{4,6},{5,7},{6,4},{7,5},{8,10},{9,11},{10,... | collective-permute-start | bytes 884744 | tf_op jit(solution)/shard_map/ppermute | solution.py:604
  29.4 17.1 %collective-permute-start.3 = (bf16[4,56,768]{2,1,0:T(8,128)(2,1)S(1)}, bf16[4,56,768]{2,1,0:T(8,128)(2,1)S(1)}, u32[]{:S(2)}, u32[]{:S(2)}) collective-permute-start(bf16[4,56,768]{2,1,0:T(8,128)(2,1)S(1)} %slice.233.rest_1_), channel_id=1, source_target_pairs={{0,4},{1,5},{2,6},{3,7},{4,0},{5,1},{6,2},{7,3},{8,12},{9,13},{10,... | collective-permute-start | bytes 1032200 | tf_op jit(solution)/shard_map/ppermute | solution.py:604
  31.2 15.3 %collective-permute-start.4 = (bf16[4,48,768]{2,1,0:T(8,128)(2,1)S(1)}, bf16[4,48,768]{2,1,0:T(8,128)(2,1)}, u32[]{:S(2)}, u32[]{:S(2)}) collective-permute-start(bf16[4,48,768]{2,1,0:T(8,128)(2,1)S(1)} %slice.235.rest_0_), channel_id=1, source_target_pairs={{0,4},{1,5},{2,6},{3,7},{4,0},{5,1},{6,2},{7,3},{8,12},{9,13},{10,... | collective-permute-start | bytes 884744 | tf_op jit(solution)/shard_map/ppermute | solution.py:604
  31.4 19.1 %collective-permute-start.10 = (bf16[4,56,768]{2,1,0:T(8,128)(2,1)S(1)}, bf16[4,56,768]{2,1,0:T(8,128)(2,1)S(1)}, u32[]{:S(2)}, u32[]{:S(2)}) collective-permute-start(bf16[4,56,768]{2,1,0:T(8,128)(2,1)S(1)} %slice.233.rest_1_), channel_id=1, source_target_pairs={{0,1},{1,0},{2,3},{3,2},{4,5},{5,4},{6,7},{7,6},{8,9},{9,8},{10,11... | collective-permute-start | bytes 1032200 | tf_op jit(solution)/shard_map/ppermute | solution.py:604
  38.2 18.0 %collective-permute-start.8 = (bf16[4,56,768]{2,1,0:T(8,128)(2,1)S(1)}, bf16[4,56,768]{2,1,0:T(8,128)(2,1)S(1)}, u32[]{:S(2)}, u32[]{:S(2)}) collective-permute-start(bf16[4,56,768]{2,1,0:T(8,128)(2,1)S(1)} %collective-permute-done.6.rest_5_), channel_id=1, source_target_pairs={{0,4},{1,5},{2,6},{3,7},{4,0},{5,1},{6,2},{7,3},{8,12},{9,13},{10,... | collective-permute-start | bytes 1032200 | tf_op jit(solution)/shard_map/ppermute | solution.py:604
  46.5 16.4 %collective-permute-start.7 = (bf16[4,48,768]{2,1,0:T(8,128)(2,1)}, bf16[4,48,768]{2,1,0:T(8,128)(2,1)}, u32[]{:S(2)}, u32[]{:S(2)}) collective-permute-start(bf16[4,48,768]{2,1,0:T(8,128)(2,1)} %collective-permute-done.4.rest_2_), channel_id=1, source_target_pairs={{0,2},{1,3},{2,0},{3,1},{4,6},{5,7},{6,4},{7,5},{8,10},{9,11},{10,... | collective-permute-start | bytes 884744 | tf_op jit(solution)/shard_map/ppermute | solution.py:604
  49.8 14.1 %collective-permute-start.14 = (bf16[4,56,768]{2,1,0:T(8,128)(2,1)S(1)}, bf16[4,56,768]{2,1,0:T(8,128)(2,1)S(1)}, u32[]{:S(2)}, u32[]{:S(2)}) collective-permute-start(bf16[4,56,768]{2,1,0:T(8,128)(2,1)S(1)} %collective-permute-done.6.rest_5_), channel_id=1, source_target_pairs={{0,1},{1,0},{2,3},{3,2},{4,5},{5,4},{6,7},{7,6},{8,9},{9,8},{10,11... | collective-permute-start | bytes 1032200 | tf_op jit(solution)/shard_map/ppermute | solution.py:604
  50.6 13.4 %collective-permute-start.12 = (bf16[4,56,768]{2,1,0:T(8,128)(2,1)S(1)}, bf16[4,56,768]{2,1,0:T(8,128)(2,1)S(1)}, u32[]{:S(2)}, u32[]{:S(2)}) collective-permute-start(bf16[4,56,768]{2,1,0:T(8,128)(2,1)S(1)} %collective-permute-done.3.rest_3_), channel_id=1, source_target_pairs={{0,1},{1,0},{2,3},{3,2},{4,5},{5,4},{6,7},{7,6},{8,9},{9,8},{10,11... | collective-permute-start | bytes 1032200 | tf_op jit(solution)/shard_map/ppermute | solution.py:604
  85.5 15.6 %collective-permute-start.17 = (bf16[128,768]{1,0:T(8,128)(2,1)}, bf16[128,768]{1,0:T(8,128)(2,1)S(1)}, u32[]{:S(2)}, u32[]{:S(2)}) collective-permute-start(bf16[128,768]{1,0:T(8,128)(2,1)} %get-tuple-element.89), channel_id=1, source_target_pairs={{0,1},{1,0},{2,3},{3,2},{4,5},{5,4},{6,7},{7,6},{8,9},{9,8},{10,11... | collective-permute-start | bytes 589832 | tf_op jit(solution)/shard_map/ppermute | solution.py:604
  164.2 22.2 %collective-permute-start.23 = (bf16[4,96,768]{2,1,0:T(8,128)(2,1)}, bf16[4,96,768]{2,1,0:T(8,128)(2,1)S(1)}, u32[]{:S(2)}, u32[]{:S(2)}) collective-permute-start(bf16[4,96,768]{2,1,0:T(8,128)(2,1)} %get-tuple-element.99), channel_id=1, source_target_pairs={{0,4},{1,5},{2,6},{3,7},{4,0},{5,1},{6,2},{7,3},{8,12},{9,13},{10,... | collective-permute-start | bytes 1769480 | tf_op jit(solution)/shard_map/ppermute | solution.py:604
  170.2 31.3 %collective-permute-start.29 = (bf16[4,96,768]{2,1,0:T(8,128)(2,1)}, bf16[4,96,768]{2,1,0:T(8,128)(2,1)S(1)}, u32[]{:S(2)}, u32[]{:S(2)}) collective-permute-start(bf16[4,96,768]{2,1,0:T(8,128)(2,1)} %get-tuple-element.107), channel_id=1, source_target_pairs={{0,4},{1,5},{2,6},{3,7},{4,0},{5,1},{6,2},{7,3},{8,12},{9,13},{10,... | collective-permute-start | bytes 1769480 | tf_op jit(solution)/shard_map/ppermute | solution.py:604
  175.9 39.1 %collective-permute-start.33 = (bf16[4,96,768]{2,1,0:T(8,128)(2,1)}, bf16[4,96,768]{2,1,0:T(8,128)(2,1)S(1)}, u32[]{:S(2)}, u32[]{:S(2)}) collective-permute-start(bf16[4,96,768]{2,1,0:T(8,128)(2,1)} %get-tuple-element.110), channel_id=1, source_target_pairs={{0,4},{1,5},{2,6},{3,7},{4,0},{5,1},{6,2},{7,3},{8,12},{9,13},{10,... | collective-permute-start | bytes 1769480 | tf_op jit(solution)/shard_map/ppermute | solution.py:604
  188.3 13.2 %collective-permute-start.27 = (bf16[96,768]{1,0:T(8,128)(2,1)S(1)}, bf16[96,768]{1,0:T(8,128)(2,1)S(1)}, u32[]{:S(2)}, u32[]{:S(2)}) collective-permute-start(bf16[96,768]{1,0:T(8,128)(2,1)S(1)} %get-tuple-element.176), channel_id=1, source_target_pairs={{0,16},{1,17},{2,18},{3,19},{4,20},{5,21},{6,22},{7,23},{8,24},{9,... | collective-permute-start | bytes 442376 | tf_op jit(solution)/shard_map/ppermute | solution.py:604
  189.0 12.5 %collective-permute-start.26 = (bf16[96,768]{1,0:T(8,128)(2,1)S(1)}, bf16[96,768]{1,0:T(8,128)(2,1)S(1)}, u32[]{:S(2)}, u32[]{:S(2)}) collective-permute-start(bf16[96,768]{1,0:T(8,128)(2,1)S(1)} %get-tuple-element.177), channel_id=1, source_target_pairs={{0,8},{1,9},{2,10},{3,11},{4,12},{5,13},{6,14},{7,15},{8,16},{9,17... | collective-permute-start | bytes 442376 | tf_op jit(solution)/shard_map/ppermute | solution.py:604
  202.3 12.8 %collective-permute-start.32 = (bf16[48,768]{1,0:T(8,128)(2,1)}, bf16[48,768]{1,0:T(8,128)(2,1)S(1)}, u32[]{:S(2)}, u32[]{:S(2)}) collective-permute-start(bf16[48,768]{1,0:T(8,128)(2,1)} %get-tuple-element.169), channel_id=1, source_target_pairs={{0,24},{1,25},{2,26},{3,27},{4,28},{5,29},{6,30},{7,31},{8,0},{9,1... | collective-permute-start | bytes 221192 | tf_op jit(solution)/shard_map/ppermute | solution.py:604
  202.3 12.8 %collective-permute-start.31 = (bf16[48,768]{1,0:T(8,128)(2,1)}, bf16[48,768]{1,0:T(8,128)(2,1)}, u32[]{:S(2)}, u32[]{:S(2)}) collective-permute-start(bf16[48,768]{1,0:T(8,128)(2,1)} %get-tuple-element.170), channel_id=1, source_target_pairs={{0,16},{1,17},{2,18},{3,19},{4,20},{5,21},{6,22},{7,23},{8,24},{9,... | collective-permute-start | bytes 221192 | tf_op jit(solution)/shard_map/ppermute | solution.py:604
  216.7 26.1 %collective-permute-start.40 = (bf16[96,768]{1,0:T(8,128)(2,1)S(1)}, bf16[96,768]{1,0:T(8,128)(2,1)S(1)}, u32[]{:S(2)}, u32[]{:S(2)}) collective-permute-start(bf16[96,768]{1,0:T(8,128)(2,1)S(1)} %fusion.17), channel_id=1, source_target_pairs={{0,0},{1,8},{2,16},{3,24},{4,1},{5,9},{6,17},{7,25},{8,2},{9,10},{... | collective-permute-start | bytes 442376 | tf_op jit(solution)/shard_map/ppermute | solution.py:604
  218.4 18.9 %collective-permute-start.35 = (bf16[2,4,48,768]{3,2,1,0:T(8,128)(2,1)S(1)}, bf16[2,4,48,768]{3,2,1,0:T(8,128)(2,1)S(1)}, u32[]{:S(2)}, u32[]{:S(2)}) collective-permute-start(bf16[2,4,48,768]{3,2,1,0:T(8,128)(2,1)S(1)} %fusion.3), channel_id=1, source_target_pairs={{0,2},{1,3},{2,0},{3,1},{4,6},{5,7},{6,4},{7,5},{8,10},{9,11},{10,... | collective-permute-start | bytes 1769480 | tf_op jit(solution)/shard_map/ppermute | solution.py:604
  221.5 22.6 %collective-permute-start.41 = (bf16[144,768]{1,0:T(8,128)(2,1)S(1)}, bf16[144,768]{1,0:T(8,128)(2,1)S(1)}, u32[]{:S(2)}, u32[]{:S(2)}) collective-permute-start(bf16[144,768]{1,0:T(8,128)(2,1)S(1)} %pad_maximum_fusion.6), channel_id=1, source_target_pairs={{0,8},{1,9},{2,10},{3,11},{4,12},{5,13},{6,14},{7,15},{8,16},{9,17... | collective-permute-start | bytes 663560 | tf_op jit(solution)/shard_map/ppermute | solution.py:604
  221.8 19.5 %collective-permute-start.38 = (bf16[2,4,56,768]{3,2,1,0:T(8,128)(2,1)S(1)}, bf16[2,4,56,768]{3,2,1,0:T(8,128)(2,1)S(1)}, u32[]{:S(2)}, u32[]{:S(2)}) collective-permute-start(bf16[2,4,56,768]{3,2,1,0:T(8,128)(2,1)S(1)} %fusion.1), channel_id=1, source_target_pairs={{0,4},{1,5},{2,6},{3,7},{4,0},{5,1},{6,2},{7,3},{8,12},{9,13},{10,... | collective-permute-start | bytes 2064392 | tf_op jit(solution)/shard_map/ppermute | solution.py:604
  223.0 21.1 %collective-permute-start.42 = (bf16[144,768]{1,0:T(8,128)(2,1)S(1)}, bf16[144,768]{1,0:T(8,128)(2,1)S(1)}, u32[]{:S(2)}, u32[]{:S(2)}) collective-permute-start(bf16[144,768]{1,0:T(8,128)(2,1)S(1)} %pad_maximum_fusion.7), channel_id=1, source_target_pairs={{0,16},{1,17},{2,18},{3,19},{4,20},{5,21},{6,22},{7,23},{8,24},{9,... | collective-permute-start | bytes 663560 | tf_op jit(solution)/shard_map/ppermute | solution.py:604
  248.3 16.4 %collective-permute-start.47 = (bf16[3,96,768]{2,1,0:T(8,128)(2,1)S(1)}, bf16[3,96,768]{2,1,0:T(8,128)(2,1)S(1)}, u32[]{:S(2)}, u32[]{:S(2)}) collective-permute-start(bf16[3,96,768]{2,1,0:T(8,128)(2,1)S(1)} %bitcast.153), channel_id=1, source_target_pairs={{0,2},{1,3},{2,0},{3,1},{4,6},{5,7},{6,4},{7,5},{8,10},{9,11},{10,... | collective-permute-start | bytes 1327112 | tf_op jit(solution)/shard_map/ppermute | solution.py:604
  (69 other events, 568.7 us)
Sparse Core Ops, SparseCore 0:
  11.5 117.9 all-gather.2

commit v13 on v12

--- a/solution.py
+++ b/solution.py
@@ -468,31 +468,31 @@
             rhs_ref[rows, pl.ds(2 * D + lane, 128)] = mm_tn(p.astype(LOW), da).astype(LOW)
 
 
-def attention_back(datt, q_m, qkv, p_m, pos, seqs, part):
-    tokens, listed = qkv.shape[0] // 2, pos.shape[0] // 2
-    length = tokens * 2 // seqs
-    mine = lambda shape, lane=0: pl.BlockSpec(shape, lambda g: (part, lane))
-    return pl.pallas_call(
-        functools.partial(attention_back_kernel, seqs // 2),
+def attention_back(datt, q_m, qkv, p_m, pos, seqs):
+    tokens, listed = qkv.shape[0], pos.shape[0]
+    length = tokens // seqs
+    whole = lambda shape, lane=0: pl.BlockSpec(shape, lambda g: (0, lane))
+    return pl.pallas_call(
+        functools.partial(attention_back_kernel, seqs),
         out_shape=out((tokens, 3 * D), LOW),
         grid=(1,),
         in_specs=[
-            mine((listed, D)),
-            mine((listed, D)),
-            mine((tokens, D), 1),
-            mine((tokens, D), 2),
-            pl.BlockSpec((HEADS, listed, length), lambda g: (0, part, 0)),
-            mine((listed, 1)),
+            whole((listed, D)),
+            whole((listed, D)),
+            whole((tokens, D), 1),
+            whole((tokens, D), 2),
+            pl.BlockSpec((HEADS, listed, length), lambda g: (0, 0, 0)),
+            whole((listed, 1)),
         ],
         out_specs=pl.BlockSpec((tokens, 3 * D), lambda g: (0, 0)),
         scratch_shapes=[pltpu.VMEM((listed, length), LOW)],
         compiler_params=BIG,
-        cost_estimate=cost(8),
+        cost_estimate=cost(12),
         name="attention_back",
     )(datt, q_m, qkv, qkv, p_m, pos)
 
 
-def attention_grads_kernel(where_ref, flip_ref, rhs0_ref, rhs1_ref, att_ref, low_ref, small_attn_ref, small_ffn_ref, keep0_ref, keep1_ref, away0_ref, away1_ref, full_ref, tail_ref):
+def attention_grads_kernel(where_ref, flip_ref, rhs_ref, att_ref, low_ref, small_attn_ref, small_ffn_ref, keep0_ref, keep1_ref, away0_ref, away1_ref, full_ref, tail_ref):
     z, y, mine = where_ref[0], where_ref[1], where_ref[4]
     half = ROWS // 2
     step = 256
@@ -517,8 +517,7 @@
                 def _(n):
                     lane = pl.multiple_of(n * step, step)
                     cols = pl.ds(pl.multiple_of(j * D + n * step, step), step)
-                    first = rhs0_ref.shape[0]
-                    full_ref[:, pl.ds(lane, step)] = mm(flip_ref[:, :first], rhs0_ref[:, cols]) + mm(flip_ref[:, first:], rhs1_ref[:, cols])
+                    full_ref[:, pl.ds(lane, step)] = mm(flip_ref[...], rhs_ref[:, cols])
 
             for rz in range(LINE):
                 base = 2 * lax.rem(z + rz, LINE)
@@ -530,49 +529,47 @@
                     cut1_ref[ry, rx, rz, half:] = tail_ref[shard]
 
 
-def attention_grads(where, x_flip, rhs0, rhs1, att_m, low, small_attn, small_ffn):
+def attention_grads(where, x_flip, rhs, att_m, low, small_attn, small_ffn):
     half = ROWS // 2
     return pl.pallas_call(
         attention_grads_kernel,
         out_shape=(out((2, 2, LINE, half, D), LOW), out((2, 2, LINE, half + TAIL, D), LOW)) * 2,
-        in_specs=[SMEM] + [VMEM] * 7,
+        in_specs=[SMEM] + [VMEM] * 6,
         out_specs=(VMEM,) * 4,
         scratch_shapes=[pltpu.VMEM((D, D), F32), pltpu.VMEM((SHARDS, TAIL, D), LOW)],
         compiler_params=BIG,
         cost_estimate=cost(10),
         name="attention_grads",
-    )(where, x_flip, rhs0, rhs1, att_m, low, small_attn, small_ffn)
-
-
-def input_grad_kernel(seqs, rhs0_ref, rhs1_ref, w_ref, dr1_ref, pos_ref, out_ref):
+    )(where, x_flip, rhs, att_m, low, small_attn, small_ffn)
+
+
+def input_grad_kernel(seqs, rhs_ref, w_ref, dr1_ref, pos_ref, out_ref):
     length = out_ref.shape[0] // seqs
     most = dr1_ref.shape[0] // seqs
     for n in range(2):
         lanes = slice(n * D // 2, (n + 1) * D // 2)
         shards = slice(n * SHARDS // 2, (n + 1) * SHARDS // 2)
-        s = 0
-        for rhs_ref in (rhs0_ref, rhs1_ref):
-            total = mm_nt(rhs_ref[:, 0:D], block(w_ref, shards, 0))
-            total += mm_nt(rhs_ref[:, D : 2 * D], block(w_ref, shards, 1))
-            total += mm_nt(rhs_ref[:, 2 * D : 3 * D], block(w_ref, shards, 2))
-            for m in range(rhs_ref.shape[0] // length):
-                hot = (lax.broadcasted_iota(jnp.int32, (length, most), 0) == pos_ref[s : s + 1, :]).astype(F32)
-                spread = jnp.dot(hot, dr1_ref[s * most : (s + 1) * most, lanes], precision=EXACT, preferred_element_type=F32)
-                out_ref[s * length : (s + 1) * length, lanes] = total[m * length : (m + 1) * length] + spread
-                s += 1
-
-
-def input_grad(rhs0, rhs1, w_attn, dr1, positions):
-    tokens = rhs0.shape[0] + rhs1.shape[0]
+        total = mm_nt(rhs_ref[:, 0:D], block(w_ref, shards, 0))
+        total += mm_nt(rhs_ref[:, D : 2 * D], block(w_ref, shards, 1))
+        total += mm_nt(rhs_ref[:, 2 * D : 3 * D], block(w_ref, shards, 2))
+        for s in range(seqs):
+            rows = slice(s * length, (s + 1) * length)
+            hot = (lax.broadcasted_iota(jnp.int32, (length, most), 0) == pos_ref[s : s + 1, :]).astype(F32)
+            spread = jnp.dot(hot, dr1_ref[s * most : (s + 1) * most, lanes], precision=EXACT, preferred_element_type=F32)
+            out_ref[rows, lanes] = total[rows] + spread
+
+
+def input_grad(rhs, w_attn, dr1, positions):
+    tokens = rhs.shape[0]
     return pl.pallas_call(
         functools.partial(input_grad_kernel, positions.shape[0]),
         out_shape=out((tokens, D), F32),
-        in_specs=[VMEM] * 5,
+        in_specs=[VMEM] * 4,
         out_specs=VMEM,
         compiler_params=BIG,
         cost_estimate=cost(8),
         name="input_grad",
-    )(rhs0, rhs1, w_attn, dr1, positions)
+    )(rhs, w_attn, dr1, positions)
 
 
 def place(z, y, x, c):
@@ -736,21 +733,15 @@
     keep_u, away_u = weight_grad(where, after(h_all, (away_g, came)), dup)
     got_u = send(away_u, "y")
     dr1, low, datt, small_attn = norm_back_call(dr2, part, after(came, away_u), r1_m, w_attn, norms)
-    rhs0 = attention_back(datt, q_m, qkv, p_m, pos, seqs, 0)
-    got_d, rhs0 = lax.optimization_barrier((got_d, rhs0))
+    rhs = attention_back(datt, q_m, qkv, p_m, pos, seqs)
+    got_d, rhs = lax.optimization_barrier((got_d, rhs))
     parts_d = line_parts(keep_d, got_d)
     line_d = line_send(parts_d)
-    rhs1 = attention_back(after(datt, (rhs0, parts_d)), q_m, qkv, p_m, pos, seqs, 1)
-    line_d, got_g, rhs1 = lax.optimization_barrier((line_d, got_g, rhs1))
-    half = ROWS // 2
-    parts_g = line_parts(keep_g[:, :half], got_g[:, :half])
-    line_g = line_send(parts_g)
-    keep0, keep1, away0, away1 = attention_grads(where, x_flip, rhs0, after(rhs1, parts_g), att_m, low, small_attn, small_ffn)
-    away0, away1, line_g, got_u = lax.optimization_barrier((away0, away1, line_g, got_u))
+    keep0, keep1, away0, away1 = attention_grads(where, x_flip, after(rhs, parts_d), att_m, low, small_attn, small_ffn)
+    away0, away1, line_d, got_g, got_u = lax.optimization_barrier((away0, away1, line_d, got_g, got_u))
     came0, came1 = send(away0, "c"), send(away1, "c")
-    rest_g = line_parts(keep_g[:, half:], got_g[:, half:])
-    parts_u = [jnp.concatenate(pair) for pair in zip(rest_g, line_parts(keep_u, got_u))]
-    line_u = line_send(parts_u)
+    parts_gu = [jnp.concatenate(pair) for pair in zip(line_parts(keep_g, got_g), line_parts(keep_u, got_u))]
+    line_gu = line_send(parts_gu)
     g_down = send(line_add(keep_d, got_d, line_d), "down")
     away0, away1 = add(keep0[1], came0[1]).astype(LOW), add(keep1[1], came1[1]).astype(LOW)
     got0, got1 = send(away0, "x"), send(away1, "y")
@@ -758,21 +749,20 @@
     total1 = add(keep1[0], came1[0]) + got1.astype(F32)
     away0, away1 = total0[1].astype(LOW), total1[1].astype(LOW)
     got0, got1 = send(away0, "y"), send(away1, "x")
-    g_down, line_u = after((g_down, line_u), (away0, away1))
-    g_ffn = jnp.concatenate(
+    g_down, line_gu = after((g_down, line_gu), (away0, away1))
+    g_ffn = jnp.stack(
         [
             g_down,
-            line_add(keep_g[:, :half], got_g[:, :half], line_g),
-            line_add(keep_g[:, half:], got_g[:, half:], [value[:half] for value in line_u]),
-            line_add(keep_u, got_u, [value[half:] for value in line_u]),
+            line_add(keep_g, got_g, [value[:ROWS] for value in line_gu]),
+            line_add(keep_u, got_u, [value[ROWS:] for value in line_gu]),
         ]
-    ).reshape(3, ROWS, D)
+    )
     got0, got1 = after((got0, got1), g_ffn)
     total = jnp.concatenate([add(total0[0], got0), add(total1[0], got1)], axis=1)
     parts = [total[r].astype(LOW) for r in (1, 2, 3)]
     line_a = line_send(parts)
     other = send(g_ffn, "x")
-    grad_in = input_grad(rhs0, after(rhs1, parts), w_attn, dr1, positions)
+    grad_in = input_grad(after(rhs, parts), w_attn, dr1, positions)
     line_a, other, grad_in = lax.optimization_barrier((line_a, other, grad_in))
     g_attn = total[0] + line_a[0].astype(F32) + line_a[1].astype(F32) + line_a[2].astype(F32)
     small = g_attn[ROWS : ROWS + 4, :ROWS]

time: 286 us -> 279 us (0.976)
  starting transfers between devices: 47.9 us -> 45 us
    ppermute x53 -> x50, starting transfers between devices: 47.9 us -> 45 us  [send(): return lax.ppermute(value, AXES, MOVES[move])]
    pallas_call x2 -> x1, Pallas kernels: 13.3 us -> 11 us  [attention_back(): pl.pallas_call(functools.partial(attention_back_kernel, seqs), out_shape=...]
    ppermute x53 -> x50, waiting for transfers between devices: 78.1 us -> 78.5 us  [send(): return lax.ppermute(value, AXES, MOVES[move])]
  transfers between devices with their start and end apart: 54 -> 51, of which waited for: 23 -> 20; matrix products, arithmetic and copies ran while one was open for 4% -> 3% of each run, Pallas kernels for 26% -> 26%
where the time goes in v13:
time: 279 us; the launch traced here: 278 us
  waiting for transfers between devices  106 us (38%)
  Pallas kernels  96.6 us (35%)
  starting transfers between devices  45 us (16%)
  between operations  14.7 us (5%)
  local copies, waits for them, and re-layouts  9.86 us (4%)
  other arithmetic  6.18 us (2%)
    ppermute x50, waiting for transfers between devices, send(): return lax.ppermute(value, AXES, MOVES[move])  78.5 us
    ppermute x50, starting transfers between devices, send(): return lax.ppermute(value, AXES, MOVES[move])  45 us
    all_gather x1, waiting for transfers between devices, on_block(): lax.all_gather(ffn_piece, AXES, axis=0, tiled=False)  27.5 us
    pallas_call x1, Pallas kernels, attention_forward(): pl.pallas_call(functools.partial(attention_kernel, seqs, listed // seqs),...  18.1 us
    pallas_call x1, Pallas kernels, ffn_forward(): pl.pallas_call(functools.partial(ffn_kernel, seqs, listed // seqs), out_s...  13.9 us
    pallas_call x1, Pallas kernels, attention_back(): pl.pallas_call(functools.partial(attention_back_kernel, seqs), out_shape=...  11 us
    pallas_call x3, Pallas kernels, weight_grad(): pl.pallas_call(weight_grad_kernel, out_shape=(out(shape, LOW), out(shape,...  9.99 us
    pallas_call x1, Pallas kernels, attention_grads(): pl.pallas_call(attention_grads_kernel, out_shape=(out((2, 2, LINE, half,...  8.68 us
  transfers between devices with their start and end apart: 51, of which 20 were waited for; matrix products, arithmetic and copies ran while one was open for 3% of the time, Pallas kernels for 26%

profile of v13, /device:TPU:0, one launch (start us, length us, event | category | flops | bytes accessed | tf_op | source)
XLA Modules:
  0.0 278.4 jit_solution(8398726272257453538)
XLA Ops:
  9.6 4.1 %collective-permute-start.1 = (bf16[104,768]{1,0:T(8,128)(2,1)S(1)}, bf16[104,768]{1,0:T(8,128)(2,1)S(1)}, u32[]{:S(2)}, u32[]{:S(2)}) collective-permute-start(bf16[104,768]{1,0:T(8,128)(2,1)S(1)} %get-tuple-element.175), channel_id=1, source_target_pairs={{0,16},{1,17},{2,18},{3,19},{4,20},{5,21},{6,22},{7,23},{8,24},{9,... | collective-permute-start | bytes 479240 | tf_op jit(solution)/shard_map/ppermute | solution.py:601
  18.8 6.8 %collective-permute-done.1 = bf16[104,768]{1,0:T(8,128)(2,1)S(1)} collective-permute-done((bf16[104,768]{1,0:T(8,128)(2,1)S(1)}, bf16[104,768]{1,0:T(8,128)(2,1)S(1)}, u32[]{:S(2)}, u32[]{:S(2)}) %collective-permute-start.1) | collective-permute-done | bytes 159776 | tf_op jit(solution)/shard_map/ppermute | solution.py:601
  31.4 6.8 %collective-permute-done.6.rest_5_ = bf16[4,56,768]{2,1,0:T(8,128)(2,1)S(1)} collective-permute-done((bf16[4,56,768]{2,1,0:T(8,128)(2,1)S(1)}, bf16[4,56,768]{2,1,0:T(8,128)(2,1)S(1)}, u32[]{:S(2)}, u32[]{:S(2)}) %collective-permute-start.6) | collective-permute-done | bytes 344096 | tf_op jit(solution)/shard_map/ppermute | solution.py:601
  42.5 4.0 %collective-permute-done.4.rest_2_ = bf16[4,48,768]{2,1,0:T(8,128)(2,1)} collective-permute-done((bf16[4,48,768]{2,1,0:T(8,128)(2,1)S(1)}, bf16[4,48,768]{2,1,0:T(8,128)(2,1)}, u32[]{:S(2)}, u32[]{:S(2)}) %collective-permute-start.4) | collective-permute-done | bytes 294944 | tf_op jit(solution)/shard_map/ppermute | solution.py:601
  50.7 5.5 %collective-permute-done.8.rest_7_ = bf16[4,56,768]{2,1,0:T(8,128)(2,1)S(1)} collective-permute-done((bf16[4,56,768]{2,1,0:T(8,128)(2,1)S(1)}, bf16[4,56,768]{2,1,0:T(8,128)(2,1)S(1)}, u32[]{:S(2)}, u32[]{:S(2)}) %collective-permute-start.8) | collective-permute-done | bytes 344096 | tf_op jit(solution)/shard_map/ppermute | solution.py:601
  56.8 6.2 %collective-permute-done.7.rest_6_ = bf16[4,48,768]{2,1,0:T(8,128)(2,1)} collective-permute-done((bf16[4,48,768]{2,1,0:T(8,128)(2,1)}, bf16[4,48,768]{2,1,0:T(8,128)(2,1)}, u32[]{:S(2)}, u32[]{:S(2)}) %collective-permute-start.7) | collective-permute-done | bytes 294944 | tf_op jit(solution)/shard_map/ppermute | solution.py:601
  65.7 18.1 %attention_forward.1 = (bf16[512,2304]{1,0:T(8,128)(2,1)}, f32[512,768]{1,0:T(8,128)}, bf16[128,768]{1,0:T(8,128)(2,1)}, bf16[128,768]{1,0:T(8,128)(2,1)}, bf16[...) custom-call(s32[5]{0:T(128)} %stack.95.where_ref, f32[12]{0:T(128)} %multiply_exponential_fusion.slope_ref, ...), custom_call_target="tpu_custom_call" | custom-call | bytes 60000000 | tf_op jit(solution)/shard_map/attention_forward/pallas_call | solution.py:164
  85.6 10.4 %collective-permute-done.18 = bf16[128,768]{1,0:T(8,128)(2,1)S(1)} collective-permute-done((bf16[128,768]{1,0:T(8,128)(2,1)}, bf16[128,768]{1,0:T(8,128)(2,1)S(1)}, u32[]{:S(2)}, u32[]{:S(2)}) %collective-permute-start.18) | collective-permute-done | bytes 196640 | tf_op jit(solution)/shard_map/ppermute | solution.py:601
  96.7 4.3 %attention_again.1.p_ref = f32[12,128,128]{2,1,0:T(8,128)} custom-call(f32[12]{0:T(128)} %multiply_exponential_fusion.slope_ref, bf16[128,768]{1,0:T(8,128)(2,1)} %get-tuple-element.85.q_ref, bf16[512,2304]{1,0:T(8,128)(2,1)} %get-tuple-element.86.k_ref.v_ref, s32[128,1]{1,0:T(8,128)} %reshape.140.pos_ref), custom_call_target="tpu_custom_call" | custom-call | bytes 24000000 | tf_op jit(solution)/shard_map/attention_again/pallas_call | solution.py:433
  102.0 27.5 %all-gather.3.cloned.1.call-done = bf16[96,96,768]{2,1,0:T(8,128)(2,1)} async-done(((bf16[3,96,768]{2,1,0:T(8,128)(2,1)}), bf16[96,96,768]{2,1,0:T(8,128)(2,1)}) %all-gather.3.cloned.1.call-update) | async-done | bytes 14155792 | tf_op jit(solution)/shard_map/all_gather | solution.py:707
  129.6 13.9 %ffn_forward.1 = (bf16[512,768]{1,0:T(8,128)(2,1)}, f32[128,768]{1,0:T(8,128)}, bf16[128,768]{1,0:T(8,128)(2,1)}, f32[2,768]{1,0:T(2,128)}) custom-call(f32[512,768]{1,0:T(8,128)} %get-tuple-element.87.h1_ref, bf16[8,4,3,96,768]{4,3,2,1,0:T(8,128)(2,1)} %bitcast.136, bf16[8,4,3,96,768]{4,3,2,1,0:T(8,128)(2,1)} %bitcast.137, ...), custom_call_target="tpu_custom_call" | custom-call | bytes 48000000 | tf_op jit(solution)/shard_map/ffn_forward/pallas_call | solution.py:233
  144.1 6.1 %ffn_again.1 = (bf16[512,768]{1,0:T(8,128)(2,1)}, f32[512,768]{1,0:T(8,128)}, f32[512,768]{1,0:T(8,128)}) custom-call(s32[5]{0:T(128)} %stack.95.where_ref, bf16[4,128,768]{2,1,0:T(8,128)(2,1)} %pad_maximum_fusion.1.h_ref.a_ref, bf16[8,4,3,96,768]{4,3,2,1,0:T(8,128)(2,1)} %bitcast.139, bf16[8,4,3,96,768]{4,3,2,1,0:T(8,128)(2,1)} %bitcast.140), custom_call_target="tpu_custom_call" | custom-call | bytes 18000000 | tf_op jit(solution)/shard_map/ffn_again/pallas_call | solution.py:294
  153.3 7.4 %ffn_back.1 = (bf16[512,768]{1,0:T(8,128)(2,1)}, bf16[512,768]{1,0:T(8,128)(2,1)}, f32[2,128,768]{2,1,0:T(8,128)}, bf16[2,128,768]{2,1,0:T(8,128)(2,1)}) custom-call(s32[5]{0:T(128)} %stack.95.where_ref, bf16[4,128,768]{2,1,0:T(8,128)(2,1)} %pad_maximum_fusion.2.b_ref.e_ref, f32[512,768]{1,0:T(8,128)} %get-tuple-element.96.to_gate_ref, ...), custom_call_target="tpu_custom_call" | custom-call | bytes 21000000 | tf_op jit(solution)/shard_map/ffn_back/pallas_call | solution.py:329
  172.6 3.4 %weight_grad.5 = (bf16[4,96,768]{2,1,0:T(8,128)(2,1)}, bf16[4,96,768]{2,1,0:T(8,128)(2,1)}) custom-call(s32[5]{0:T(128)} %stack.95.where_ref, bf16[4,128,768]{2,1,0:T(8,128)(2,1)} %pad_maximum_fusion.1.h_ref.a_ref, bf16[512,768]{1,0:T(8,128)(2,1)} %get-tuple-element.104.b_ref), custom_call_target="tpu_custom_call" | custom-call | bytes 12000000 | tf_op jit(solution)/shard_map/weight_grad/pallas_call | solution.py:363
  180.5 11.0 %attention_back.1.rhs_ref = bf16[512,2304]{1,0:T(8,128)(2,1)} custom-call(bf16[128,768]{1,0:T(8,128)(2,1)} %get-tuple-element.109.datt_ref, bf16[128,768]{1,0:T(8,128)(2,1)} %get-tuple-element.85.q_ref, bf16[512,2304]{1,0:T(8,128)(2,1)} %get-tuple-element.86.k_ref.v_ref, bf16[512,2304]{1,0:T(8,128)(2,1)} %get-tuple-element.86.k_ref.v_ref, ...), custom_call_target="tpu_custom_call" | custom-call | bytes 36000000 | tf_op jit(solution)/shard_map/attention_back/pallas_call | solution.py:475
  195.3 8.7 %attention_grads.1 = (bf16[2,2,4,48,768]{4,3,2,1,0:T(8,128)(2,1)}, bf16[2,2,4,56,768]{4,3,2,1,0:T(8,128)(2,1)}, bf16[2,2,4,48,768]{4,3,2,1,0:T(8,128)(2,1)}, bf16[2,2,4,56,768]{4,3,2,1,0:T(8,128)(2,1)}) custom-call(s32[5]{0:T(128)} %stack.95.where_ref, bf16[768,512]{1,0:T(8,128)(2,1)} %bitcast.144, bf16[512,2304]{1,0:T(8,128)(2,1)} %attention_back.1.rhs_ref, ...), custom_call_target="tpu_custom_call" | custom-call | bytes 30000000 | tf_op jit(solution)/shard_map/attention_grads/pallas_call | solution.py:534
  209.8 3.4 %collective-permute-start.32 = (bf16[2,4,48,768]{3,2,1,0:T(8,128)(2,1)S(1)}, bf16[2,4,48,768]{3,2,1,0:T(8,128)(2,1)S(1)}, u32[]{:S(2)}, u32[]{:S(2)}) collective-permute-start(bf16[2,4,48,768]{3,2,1,0:T(8,128)(2,1)S(1)} %fusion.3), channel_id=1, source_target_pairs={{0,2},{1,3},{2,0},{3,1},{4,6},{5,7},{6,4},{7,5},{8,10},{9,11},{10,... | collective-permute-start | bytes 1769480 | tf_op jit(solution)/shard_map/ppermute | solution.py:601
  216.5 11.3 %collective-permute-done.32 = bf16[2,4,48,768]{3,2,1,0:T(8,128)(2,1)S(1)} collective-permute-done((bf16[2,4,48,768]{3,2,1,0:T(8,128)(2,1)S(1)}, bf16[2,4,48,768]{3,2,1,0:T(8,128)(2,1)S(1)}, u32[]{:S(2)}, u32[]{:S(2)}) %collective-permute-start.32) | collective-permute-done | bytes 589856 | tf_op jit(solution)/shard_map/ppermute | solution.py:601
  227.8 3.4 %collective-permute-start.40 = (bf16[192,768]{1,0:T(8,128)(2,1)S(1)}, bf16[192,768]{1,0:T(8,128)(2,1)S(1)}, u32[]{:S(2)}, u32[]{:S(2)}) collective-permute-start(bf16[192,768]{1,0:T(8,128)(2,1)S(1)} %pad_maximum_fusion.8), channel_id=1, source_target_pairs={{0,24},{1,25},{2,26},{3,27},{4,28},{5,29},{6,30},{7,31},{8,0},{9,1... | collective-permute-start | bytes 884744 | tf_op jit(solution)/shard_map/ppermute | solution.py:601
  233.8 5.2 %collective-permute-done.39 = bf16[192,768]{1,0:T(8,128)(2,1)S(1)} collective-permute-done((bf16[192,768]{1,0:T(8,128)(2,1)S(1)}, bf16[192,768]{1,0:T(8,128)(2,1)S(1)}, u32[]{:S(2)}, u32[]{:S(2)}) %collective-permute-start.39) | collective-permute-done | bytes 294944 | tf_op jit(solution)/shard_map/ppermute | solution.py:601
  239.0 4.5 %collective-permute-done.40 = bf16[192,768]{1,0:T(8,128)(2,1)S(1)} collective-permute-done((bf16[192,768]{1,0:T(8,128)(2,1)S(1)}, bf16[192,768]{1,0:T(8,128)(2,1)S(1)}, u32[]{:S(2)}, u32[]{:S(2)}) %collective-permute-start.40) | collective-permute-done | bytes 294944 | tf_op jit(solution)/shard_map/ppermute | solution.py:601
  247.5 8.1 %input_grad.1 = f32[512,768]{1,0:T(8,128)} custom-call(bf16[512,2304]{1,0:T(8,128)(2,1)} %attention_back.1.rhs_ref, bf16[8,4,96,768]{3,2,1,0:T(8,128)(2,1)} %get-tuple-element.108.w_ref, f32[128,768]{1,0:T(8,128)} %get-tuple-element.139.dr1_ref, s32[4,32]{1,0:T(4,128)} %pos_ref.1), custom_call_target="tpu_custom_call" | custom-call | bytes 24000000 | tf_op jit(solution)/shard_map/input_grad/pallas_call | solution.py:564
  255.6 4.8 %collective-permute-done.42 = bf16[104,768]{1,0:T(8,128)(2,1)S(1)} collective-permute-done((bf16[104,768]{1,0:T(8,128)(2,1)S(1)}, bf16[104,768]{1,0:T(8,128)(2,1)S(1)}, u32[]{:S(2)}, u32[]{:S(2)}) %collective-permute-start.42) | collective-permute-done | bytes 159776 | tf_op jit(solution)/shard_map/ppermute | solution.py:601
  263.7 3.4 %finish_ffn.1 = (f32[384,768]{1,0:T(8,128)}, f32[96,6144]{1,0:T(8,128)}) custom-call(s32[5]{0:T(128)} %stack.95.where_ref, bf16[3,96,768]{2,1,0:T(8,128)(2,1)} %copy-done.1, bf16[3,96,768]{2,1,0:T(8,128)(2,1)} %copy-done.13, bf16[3,96,768]{2,1,0:T(8,128)(2,1)} %copy-done.12, bf16[3,96,768]{2,1,0:T(8,128)(2,1)} %copy-done.14), custom_call_target="tpu_custom_call" | custom-call | bytes 12000000 | tf_op jit(solution)/shard_map/finish_ffn/pallas_call | solution.py:650
  (224 shorter events, 75.3 us)
Async XLA Ops:
  7.2 122.3 %all-gather.3.cloned.1.call-start = ((), (), s32[]{:S(2)}) async-start(), calls=%async_computation | async-start | bytes 14598144 | tf_op jit(solution)/shard_map/all_gather | solution.py:707
  9.6 16.0 %collective-permute-start.1 = (bf16[104,768]{1,0:T(8,128)(2,1)S(1)}, bf16[104,768]{1,0:T(8,128)(2,1)S(1)}, u32[]{:S(2)}, u32[]{:S(2)}) collective-permute-start(bf16[104,768]{1,0:T(8,128)(2,1)S(1)} %get-tuple-element.175), channel_id=1, source_target_pairs={{0,16},{1,17},{2,18},{3,19},{4,20},{5,21},{6,22},{7,23},{8,24},{9,... | collective-permute-start | bytes 479240 | tf_op jit(solution)/shard_map/ppermute | solution.py:601
  29.0 13.5 %collective-permute-start.5 = (bf16[4,48,768]{2,1,0:T(8,128)(2,1)S(1)}, bf16[4,48,768]{2,1,0:T(8,128)(2,1)}, u32[]{:S(2)}, u32[]{:S(2)}) collective-permute-start(bf16[4,48,768]{2,1,0:T(8,128)(2,1)S(1)} %slice.187.rest_0_), channel_id=1, source_target_pairs={{0,2},{1,3},{2,0},{3,1},{4,6},{5,7},{6,4},{7,5},{8,10},{9,11},{10,... | collective-permute-start | bytes 884744 | tf_op jit(solution)/shard_map/ppermute | solution.py:601
  29.4 17.1 %collective-permute-start.3 = (bf16[4,56,768]{2,1,0:T(8,128)(2,1)S(1)}, bf16[4,56,768]{2,1,0:T(8,128)(2,1)S(1)}, u32[]{:S(2)}, u32[]{:S(2)}) collective-permute-start(bf16[4,56,768]{2,1,0:T(8,128)(2,1)S(1)} %slice.185.rest_1_), channel_id=1, source_target_pairs={{0,4},{1,5},{2,6},{3,7},{4,0},{5,1},{6,2},{7,3},{8,12},{9,13},{10,... | collective-permute-start | bytes 1032200 | tf_op jit(solution)/shard_map/ppermute | solution.py:601
  31.2 15.3 %collective-permute-start.4 = (bf16[4,48,768]{2,1,0:T(8,128)(2,1)S(1)}, bf16[4,48,768]{2,1,0:T(8,128)(2,1)}, u32[]{:S(2)}, u32[]{:S(2)}) collective-permute-start(bf16[4,48,768]{2,1,0:T(8,128)(2,1)S(1)} %slice.187.rest_0_), channel_id=1, source_target_pairs={{0,4},{1,5},{2,6},{3,7},{4,0},{5,1},{6,2},{7,3},{8,12},{9,13},{10,... | collective-permute-start | bytes 884744 | tf_op jit(solution)/shard_map/ppermute | solution.py:601
  31.4 19.1 %collective-permute-start.10 = (bf16[4,56,768]{2,1,0:T(8,128)(2,1)S(1)}, bf16[4,56,768]{2,1,0:T(8,128)(2,1)S(1)}, u32[]{:S(2)}, u32[]{:S(2)}) collective-permute-start(bf16[4,56,768]{2,1,0:T(8,128)(2,1)S(1)} %slice.185.rest_1_), channel_id=1, source_target_pairs={{0,1},{1,0},{2,3},{3,2},{4,5},{5,4},{6,7},{7,6},{8,9},{9,8},{10,11... | collective-permute-start | bytes 1032200 | tf_op jit(solution)/shard_map/ppermute | solution.py:601
  38.2 18.0 %collective-permute-start.8 = (bf16[4,56,768]{2,1,0:T(8,128)(2,1)S(1)}, bf16[4,56,768]{2,1,0:T(8,128)(2,1)S(1)}, u32[]{:S(2)}, u32[]{:S(2)}) collective-permute-start(bf16[4,56,768]{2,1,0:T(8,128)(2,1)S(1)} %collective-permute-done.6.rest_5_), channel_id=1, source_target_pairs={{0,4},{1,5},{2,6},{3,7},{4,0},{5,1},{6,2},{7,3},{8,12},{9,13},{10,... | collective-permute-start | bytes 1032200 | tf_op jit(solution)/shard_map/ppermute | solution.py:601
  46.5 16.4 %collective-permute-start.7 = (bf16[4,48,768]{2,1,0:T(8,128)(2,1)}, bf16[4,48,768]{2,1,0:T(8,128)(2,1)}, u32[]{:S(2)}, u32[]{:S(2)}) collective-permute-start(bf16[4,48,768]{2,1,0:T(8,128)(2,1)} %collective-permute-done.4.rest_2_), channel_id=1, source_target_pairs={{0,2},{1,3},{2,0},{3,1},{4,6},{5,7},{6,4},{7,5},{8,10},{9,11},{10,... | collective-permute-start | bytes 884744 | tf_op jit(solution)/shard_map/ppermute | solution.py:601
  49.8 14.2 %collective-permute-start.14 = (bf16[4,56,768]{2,1,0:T(8,128)(2,1)S(1)}, bf16[4,56,768]{2,1,0:T(8,128)(2,1)S(1)}, u32[]{:S(2)}, u32[]{:S(2)}) collective-permute-start(bf16[4,56,768]{2,1,0:T(8,128)(2,1)S(1)} %collective-permute-done.6.rest_5_), channel_id=1, source_target_pairs={{0,1},{1,0},{2,3},{3,2},{4,5},{5,4},{6,7},{7,6},{8,9},{9,8},{10,11... | collective-permute-start | bytes 1032200 | tf_op jit(solution)/shard_map/ppermute | solution.py:601
  50.5 13.4 %collective-permute-start.12 = (bf16[4,56,768]{2,1,0:T(8,128)(2,1)S(1)}, bf16[4,56,768]{2,1,0:T(8,128)(2,1)S(1)}, u32[]{:S(2)}, u32[]{:S(2)}) collective-permute-start(bf16[4,56,768]{2,1,0:T(8,128)(2,1)S(1)} %collective-permute-done.3.rest_3_), channel_id=1, source_target_pairs={{0,1},{1,0},{2,3},{3,2},{4,5},{5,4},{6,7},{7,6},{8,9},{9,8},{10,11... | collective-permute-start | bytes 1032200 | tf_op jit(solution)/shard_map/ppermute | solution.py:601
  85.5 15.6 %collective-permute-start.17 = (bf16[128,768]{1,0:T(8,128)(2,1)}, bf16[128,768]{1,0:T(8,128)(2,1)S(1)}, u32[]{:S(2)}, u32[]{:S(2)}) collective-permute-start(bf16[128,768]{1,0:T(8,128)(2,1)} %get-tuple-element.84), channel_id=1, source_target_pairs={{0,1},{1,0},{2,3},{3,2},{4,5},{5,4},{6,7},{7,6},{8,9},{9,8},{10,11... | collective-permute-start | bytes 589832 | tf_op jit(solution)/shard_map/ppermute | solution.py:601
  164.1 27.4 %collective-permute-start.23 = (bf16[4,96,768]{2,1,0:T(8,128)(2,1)}, bf16[4,96,768]{2,1,0:T(8,128)(2,1)S(1)}, u32[]{:S(2)}, u32[]{:S(2)}) collective-permute-start(bf16[4,96,768]{2,1,0:T(8,128)(2,1)} %get-tuple-element.94), channel_id=1, source_target_pairs={{0,4},{1,5},{2,6},{3,7},{4,0},{5,1},{6,2},{7,3},{8,12},{9,13},{10,... | collective-permute-start | bytes 1769480 | tf_op jit(solution)/shard_map/ppermute | solution.py:601
  170.3 36.3 %collective-permute-start.29 = (bf16[4,96,768]{2,1,0:T(8,128)(2,1)}, bf16[4,96,768]{2,1,0:T(8,128)(2,1)S(1)}, u32[]{:S(2)}, u32[]{:S(2)}) collective-permute-start(bf16[4,96,768]{2,1,0:T(8,128)(2,1)} %get-tuple-element.102), channel_id=1, source_target_pairs={{0,4},{1,5},{2,6},{3,7},{4,0},{5,1},{6,2},{7,3},{8,12},{9,13},{10,... | collective-permute-start | bytes 1769480 | tf_op jit(solution)/shard_map/ppermute | solution.py:601
  176.0 30.6 %collective-permute-start.30 = (bf16[4,96,768]{2,1,0:T(8,128)(2,1)}, bf16[4,96,768]{2,1,0:T(8,128)(2,1)S(1)}, u32[]{:S(2)}, u32[]{:S(2)}) collective-permute-start(bf16[4,96,768]{2,1,0:T(8,128)(2,1)} %get-tuple-element.105), channel_id=1, source_target_pairs={{0,4},{1,5},{2,6},{3,7},{4,0},{5,1},{6,2},{7,3},{8,12},{9,13},{10,... | collective-permute-start | bytes 1769480 | tf_op jit(solution)/shard_map/ppermute | solution.py:601
  193.4 13.1 %collective-permute-start.27 = (bf16[96,768]{1,0:T(8,128)(2,1)S(1)}, bf16[96,768]{1,0:T(8,128)(2,1)S(1)}, u32[]{:S(2)}, u32[]{:S(2)}) collective-permute-start(bf16[96,768]{1,0:T(8,128)(2,1)S(1)} %get-tuple-element.161), channel_id=1, source_target_pairs={{0,16},{1,17},{2,18},{3,19},{4,20},{5,21},{6,22},{7,23},{8,24},{9,... | collective-permute-start | bytes 442376 | tf_op jit(solution)/shard_map/ppermute | solution.py:601
  207.2 25.6 %collective-permute-start.37 = (bf16[96,768]{1,0:T(8,128)(2,1)S(1)}, bf16[96,768]{1,0:T(8,128)(2,1)S(1)}, u32[]{:S(2)}, u32[]{:S(2)}) collective-permute-start(bf16[96,768]{1,0:T(8,128)(2,1)S(1)} %fusion.20), channel_id=1, source_target_pairs={{0,0},{1,8},{2,16},{3,24},{4,1},{5,9},{6,17},{7,25},{8,2},{9,10},{... | collective-permute-start | bytes 442376 | tf_op jit(solution)/shard_map/ppermute | solution.py:601
  209.8 17.9 %collective-permute-start.32 = (bf16[2,4,48,768]{3,2,1,0:T(8,128)(2,1)S(1)}, bf16[2,4,48,768]{3,2,1,0:T(8,128)(2,1)S(1)}, u32[]{:S(2)}, u32[]{:S(2)}) collective-permute-start(bf16[2,4,48,768]{3,2,1,0:T(8,128)(2,1)S(1)} %fusion.3), channel_id=1, source_target_pairs={{0,2},{1,3},{2,0},{3,1},{4,6},{5,7},{6,4},{7,5},{8,10},{9,11},{10,... | collective-permute-start | bytes 1769480 | tf_op jit(solution)/shard_map/ppermute | solution.py:601
  213.3 20.5 %collective-permute-start.38 = (bf16[192,768]{1,0:T(8,128)(2,1)S(1)}, bf16[192,768]{1,0:T(8,128)(2,1)S(1)}, u32[]{:S(2)}, u32[]{:S(2)}) collective-permute-start(bf16[192,768]{1,0:T(8,128)(2,1)S(1)} %pad_maximum_fusion.6), channel_id=1, source_target_pairs={{0,8},{1,9},{2,10},{3,11},{4,12},{5,13},{6,14},{7,15},{8,16},{9,17... | collective-permute-start | bytes 884744 | tf_op jit(solution)/shard_map/ppermute | solution.py:601
  213.7 17.7 %collective-permute-start.35 = (bf16[2,4,56,768]{3,2,1,0:T(8,128)(2,1)S(1)}, bf16[2,4,56,768]{3,2,1,0:T(8,128)(2,1)S(1)}, u32[]{:S(2)}, u32[]{:S(2)}) collective-permute-start(bf16[2,4,56,768]{3,2,1,0:T(8,128)(2,1)S(1)} %fusion.1), channel_id=1, source_target_pairs={{0,4},{1,5},{2,6},{3,7},{4,0},{5,1},{6,2},{7,3},{8,12},{9,13},{10,... | collective-permute-start | bytes 2064392 | tf_op jit(solution)/shard_map/ppermute | solution.py:601
  214.9 24.1 %collective-permute-start.39 = (bf16[192,768]{1,0:T(8,128)(2,1)S(1)}, bf16[192,768]{1,0:T(8,128)(2,1)S(1)}, u32[]{:S(2)}, u32[]{:S(2)}) collective-permute-start(bf16[192,768]{1,0:T(8,128)(2,1)S(1)} %pad_maximum_fusion.7), channel_id=1, source_target_pairs={{0,16},{1,17},{2,18},{3,19},{4,20},{5,21},{6,22},{7,23},{8,24},{9,... | collective-permute-start | bytes 884744 | tf_op jit(solution)/shard_map/ppermute | solution.py:601
  227.8 15.8 %collective-permute-start.40 = (bf16[192,768]{1,0:T(8,128)(2,1)S(1)}, bf16[192,768]{1,0:T(8,128)(2,1)S(1)}, u32[]{:S(2)}, u32[]{:S(2)}) collective-permute-start(bf16[192,768]{1,0:T(8,128)(2,1)S(1)} %pad_maximum_fusion.8), channel_id=1, source_target_pairs={{0,24},{1,25},{2,26},{3,27},{4,28},{5,29},{6,30},{7,31},{8,0},{9,1... | collective-permute-start | bytes 884744 | tf_op jit(solution)/shard_map/ppermute | solution.py:601
  246.8 13.5 %collective-permute-start.42 = (bf16[104,768]{1,0:T(8,128)(2,1)S(1)}, bf16[104,768]{1,0:T(8,128)(2,1)S(1)}, u32[]{:S(2)}, u32[]{:S(2)}) collective-permute-start(bf16[104,768]{1,0:T(8,128)(2,1)S(1)} %get-tuple-element.168), channel_id=1, source_target_pairs={{0,16},{1,17},{2,18},{3,19},{4,20},{5,21},{6,22},{7,23},{8,24},{9,... | collective-permute-start | bytes 479240 | tf_op jit(solution)/shard_map/ppermute | solution.py:601
  246.8 13.5 %collective-permute-start.41 = (bf16[104,768]{1,0:T(8,128)(2,1)S(1)}, bf16[104,768]{1,0:T(8,128)(2,1)S(1)}, u32[]{:S(2)}, u32[]{:S(2)}) collective-permute-start(bf16[104,768]{1,0:T(8,128)(2,1)S(1)} %get-tuple-element.169), channel_id=1, source_target_pairs={{0,8},{1,9},{2,10},{3,11},{4,12},{5,13},{6,14},{7,15},{8,16},{9,17... | collective-permute-start | bytes 479240 | tf_op jit(solution)/shard_map/ppermute | solution.py:601
  247.5 14.7 %collective-permute-start.47 = (bf16[3,96,768]{2,1,0:T(8,128)(2,1)S(1)}, bf16[3,96,768]{2,1,0:T(8,128)(2,1)S(1)}, u32[]{:S(2)}, u32[]{:S(2)}) collective-permute-start(bf16[3,96,768]{2,1,0:T(8,128)(2,1)S(1)} %pad_maximum_fusion.5.rest_0_), channel_id=1, source_target_pairs={{0,1},{1,0},{2,3},{3,2},{4,5},{5,4},{6,7},{7,6},{8,9},{9,8},{10,11... | collective-permute-start | bytes 1327112 | tf_op jit(solution)/shard_map/ppermute | solution.py:601
  (65 other events, 544.2 us)
Sparse Core Ops, SparseCore 0:
  11.5 118.0 all-gather.2

commit v14 on v13

--- a/solution.py
+++ b/solution.py
@@ -271,8 +271,8 @@
         lanes = slice(n * step, (n + 1) * step)
         value, slope = gelu_parts(gate)
         act_ref[:, lanes] = (value * up).astype(LOW)
-        to_gate_ref[:, lanes] = slope * up
-        to_up_ref[:, lanes] = value
+        to_gate_ref[:, lanes] = (slope * up).astype(LOW)
+        to_up_ref[:, lanes] = value.astype(LOW)
         gate, up = following
 
 
@@ -293,7 +293,7 @@
     rows = h_all.shape[0] * h_all.shape[1]
     return pl.pallas_call(
         ffn_again_kernel,
-        out_shape=(out((rows, D), LOW), out((rows, D), F32), out((rows, D), F32)),
+        out_shape=(out((rows, D), LOW),) * 3,
         grid_spec=pltpu.PrefetchScalarGridSpec(
             num_scalar_prefetch=1,
             grid=(1,),
@@ -306,14 +306,18 @@
     )(where, h_all, w_ffn, w_ffn)
 
 
-def ffn_back_kernel(where_ref, e_ref, to_gate_ref, to_up_ref, gate_ref, up_ref, down_ref, dgate_ref, dup_ref, keep_ref, send_ref):
-    listed = e_ref.shape[1]
+def ffn_back_kernel(where_ref, *rest):
+    pieces, rest = rest[:QUARTERS], rest[QUARTERS:]
+    to_gate_ref, to_up_ref, gate_ref, up_ref, down_ref, dgate_ref, dup_ref, keep_ref, send_ref, e_ref = rest
+    listed = pieces[0].shape[0]
+    for n, piece in enumerate(pieces):
+        e_ref[n * listed : (n + 1) * listed, :] = piece[...]
     half = QUARTERS // 2
     for n in range(SHARDS // QUARTERS):
         lanes = slice(n * QUARTERS * ROWS, (n + 1) * QUARTERS * ROWS)
-        dact = mm_nt(block(e_ref), block(down_ref, n))
-        dgate_ref[:, lanes] = (dact * to_gate_ref[:, lanes]).astype(LOW)
-        dup_ref[:, lanes] = (dact * to_up_ref[:, lanes]).astype(LOW)
+        dact = mm_nt(e_ref[...], block(down_ref, n))
+        dgate_ref[:, lanes] = (dact * to_gate_ref[:, lanes].astype(F32)).astype(LOW)
+        dup_ref[:, lanes] = (dact * to_up_ref[:, lanes].astype(F32)).astype(LOW)
     for n in range(2):
         shards = slice(n * SHARDS // 2, (n + 1) * SHARDS // 2)
         lanes = slice(n * D // 2, (n + 1) * D // 2)
@@ -323,22 +327,22 @@
             send_ref[r, :, lanes] = part[(2 * r + 1) * listed : (2 * r + 2) * listed].astype(LOW)
 
 
-def ffn_back(where, e_all, to_gate, to_up, w_ffn):
-    count, listed, _ = e_all.shape
+def ffn_back(where, pieces, to_gate, to_up, w_ffn):
+    count, listed = len(pieces), pieces[0].shape[0]
     rows = count * listed
     return pl.pallas_call(
         ffn_back_kernel,
-        out_shape=(out((rows, D), LOW), out((rows, D), LOW), out((count // 2, listed, D), F32), out((count // 2, listed, D), LOW)),
+        out_shape=(out((rows, D), LOW), out((rows, D), LOW), out((count // 2, listed, D), F32), out((count // 2, listed, D), LOW), out((rows, D), LOW)),
         grid_spec=pltpu.PrefetchScalarGridSpec(
             num_scalar_prefetch=1,
             grid=(1,),
-            in_specs=[at_once(e_all.shape), at_once((rows, D)), at_once((rows, D)), *quarter_specs(["gate", "up", "down"])],
-            out_specs=(at_once((rows, D)), at_once((rows, D)), at_once((count // 2, listed, D)), at_once((count // 2, listed, D))),
+            in_specs=[*[at_once((listed, D))] * count, at_once((rows, D)), at_once((rows, D)), *quarter_specs(["gate", "up", "down"])],
+            out_specs=(at_once((rows, D)), at_once((rows, D)), at_once((count // 2, listed, D)), at_once((count // 2, listed, D)), at_once((rows, D))),
         ),
         compiler_params=BIG,
         cost_estimate=cost(7),
         name="ffn_back",
-    )(where, e_all, to_gate, to_up, w_ffn, w_ffn, w_ffn)
+    )(where, *pieces, to_gate, to_up, w_ffn, w_ffn, w_ffn)
 
 
 def weight_grad_kernel(where_ref, a_ref, b_ref, keep_ref, send_ref, full_ref):
@@ -721,8 +725,8 @@
     layer_out, dr2, e2, small_ffn = ffn_forward(h1, w_ffn, norms, pos, dy, seqs)
     act, to_gate, to_up = ffn_again(where, h_all, w_ffn)
     other = after(send(e2, "x"), act)
-    e_all = jnp.stack([e2, send(e2, "c"), other, send(other, "c")])
-    dgate, dup, keep, away = ffn_back(where, e_all, to_gate, to_up, w_ffn)
+    pieces = (e2, send(e2, "c"), other, send(other, "c"))
+    dgate, dup, keep, away, e_all = ffn_back(where, pieces, to_gate, to_up, w_ffn)
     part = add(keep, send(away, "c"))
     part, part_away = part[0], part[1].astype(LOW)
     keep_d, away_d = weight_grad(where, act, e_all)

time: 279 us -> 278 us (level)
  no operation moved by 1% of the time
where the time goes in v14:
time: 278 us
  waiting for transfers between devices  106 us (38%)
  Pallas kernels  96.2 us (35%)
  starting transfers between devices  45.5 us (16%)
  between operations  14.8 us (5%)
  local copies, waits for them, and re-layouts  10.5 us (4%)
  other arithmetic  5.2 us (2%)
    ppermute x50, waiting for transfers between devices, send(): return lax.ppermute(value, AXES, MOVES[move])  78.3 us
    ppermute x50, starting transfers between devices, send(): return lax.ppermute(value, AXES, MOVES[move])  45.5 us
    all_gather x1, waiting for transfers between devices, on_block(): lax.all_gather(ffn_piece, AXES, axis=0, tiled=False)  27.5 us
    pallas_call x1, Pallas kernels, attention_forward(): pl.pallas_call(functools.partial(attention_kernel, seqs, listed // seqs),...  18.1 us
    pallas_call x1, Pallas kernels, ffn_forward(): pl.pallas_call(functools.partial(ffn_kernel, seqs, listed // seqs), out_s...  13.9 us
    pallas_call x1, Pallas kernels, attention_back(): pl.pallas_call(functools.partial(attention_back_kernel, seqs), out_shape=...  11 us
    pallas_call x3, Pallas kernels, weight_grad(): pl.pallas_call(weight_grad_kernel, out_shape=(out(shape, LOW), out(shape,...  10 us
    pallas_call x1, Pallas kernels, attention_grads(): pl.pallas_call(attention_grads_kernel, out_shape=(out((2, 2, LINE, half,...  8.7 us
  transfers between devices with their start and end apart: 51, of which 20 were waited for; matrix products, arithmetic and copies ran while one was open for 3% of the time, Pallas kernels for 26%

profile of v14, /device:TPU:0, one launch (start us, length us, event | category | flops | bytes accessed | tf_op | source)
XLA Modules:
  0.0 278.0 jit_solution(14136395710437236595)
XLA Ops:
  9.6 4.1 %collective-permute-start.1 = (bf16[104,768]{1,0:T(8,128)(2,1)S(1)}, bf16[104,768]{1,0:T(8,128)(2,1)S(1)}, u32[]{:S(2)}, u32[]{:S(2)}) collective-permute-start(bf16[104,768]{1,0:T(8,128)(2,1)S(1)} %get-tuple-element.177), channel_id=1, source_target_pairs={{0,16},{1,17},{2,18},{3,19},{4,20},{5,21},{6,22},{7,23},{8,24},{9,... | collective-permute-start | bytes 479240 | tf_op jit(solution)/shard_map/ppermute | solution.py:605
  18.7 6.9 %collective-permute-done.1 = bf16[104,768]{1,0:T(8,128)(2,1)S(1)} collective-permute-done((bf16[104,768]{1,0:T(8,128)(2,1)S(1)}, bf16[104,768]{1,0:T(8,128)(2,1)S(1)}, u32[]{:S(2)}, u32[]{:S(2)}) %collective-permute-start.1) | collective-permute-done | bytes 159776 | tf_op jit(solution)/shard_map/ppermute | solution.py:605
  31.4 6.8 %collective-permute-done.6.rest_5_ = bf16[4,56,768]{2,1,0:T(8,128)(2,1)S(1)} collective-permute-done((bf16[4,56,768]{2,1,0:T(8,128)(2,1)S(1)}, bf16[4,56,768]{2,1,0:T(8,128)(2,1)S(1)}, u32[]{:S(2)}, u32[]{:S(2)}) %collective-permute-start.6) | collective-permute-done | bytes 344096 | tf_op jit(solution)/shard_map/ppermute | solution.py:605
  42.5 4.0 %collective-permute-done.4.rest_2_ = bf16[4,48,768]{2,1,0:T(8,128)(2,1)} collective-permute-done((bf16[4,48,768]{2,1,0:T(8,128)(2,1)S(1)}, bf16[4,48,768]{2,1,0:T(8,128)(2,1)}, u32[]{:S(2)}, u32[]{:S(2)}) %collective-permute-start.4) | collective-permute-done | bytes 294944 | tf_op jit(solution)/shard_map/ppermute | solution.py:605
  50.7 5.5 %collective-permute-done.8.rest_7_ = bf16[4,56,768]{2,1,0:T(8,128)(2,1)S(1)} collective-permute-done((bf16[4,56,768]{2,1,0:T(8,128)(2,1)S(1)}, bf16[4,56,768]{2,1,0:T(8,128)(2,1)S(1)}, u32[]{:S(2)}, u32[]{:S(2)}) %collective-permute-start.8) | collective-permute-done | bytes 344096 | tf_op jit(solution)/shard_map/ppermute | solution.py:605
  56.8 6.1 %collective-permute-done.7.rest_6_ = bf16[4,48,768]{2,1,0:T(8,128)(2,1)} collective-permute-done((bf16[4,48,768]{2,1,0:T(8,128)(2,1)}, bf16[4,48,768]{2,1,0:T(8,128)(2,1)}, u32[]{:S(2)}, u32[]{:S(2)}) %collective-permute-start.7) | collective-permute-done | bytes 294944 | tf_op jit(solution)/shard_map/ppermute | solution.py:605
  65.7 18.1 %attention_forward.1 = (bf16[512,2304]{1,0:T(8,128)(2,1)}, f32[512,768]{1,0:T(8,128)}, bf16[128,768]{1,0:T(8,128)(2,1)}, bf16[128,768]{1,0:T(8,128)(2,1)}, bf16[...) custom-call(s32[5]{0:T(128)} %stack.80.where_ref, f32[12]{0:T(128)} %multiply_exponential_fusion.slope_ref, ...), custom_call_target="tpu_custom_call" | custom-call | bytes 60000000 | tf_op jit(solution)/shard_map/attention_forward/pallas_call | solution.py:164
  85.5 10.4 %collective-permute-done.18 = bf16[128,768]{1,0:T(8,128)(2,1)S(1)} collective-permute-done((bf16[128,768]{1,0:T(8,128)(2,1)}, bf16[128,768]{1,0:T(8,128)(2,1)S(1)}, u32[]{:S(2)}, u32[]{:S(2)}) %collective-permute-start.18) | collective-permute-done | bytes 196640 | tf_op jit(solution)/shard_map/ppermute | solution.py:605
  96.7 4.4 %attention_again.1.p_ref = f32[12,128,128]{2,1,0:T(8,128)} custom-call(f32[12]{0:T(128)} %multiply_exponential_fusion.slope_ref, bf16[128,768]{1,0:T(8,128)(2,1)} %get-tuple-element.86.q_ref, bf16[512,2304]{1,0:T(8,128)(2,1)} %get-tuple-element.87.k_ref.v_ref, s32[128,1]{1,0:T(8,128)} %reshape.140.pos_ref), custom_call_target="tpu_custom_call" | custom-call | bytes 24000000 | tf_op jit(solution)/shard_map/attention_again/pallas_call | solution.py:437
  102.0 27.5 %all-gather.3.cloned.1.call-done = bf16[96,96,768]{2,1,0:T(8,128)(2,1)} async-done(((bf16[3,96,768]{2,1,0:T(8,128)(2,1)}), bf16[96,96,768]{2,1,0:T(8,128)(2,1)}) %all-gather.3.cloned.1.call-update) | async-done | bytes 14155792 | tf_op jit(solution)/shard_map/all_gather | solution.py:711
  129.6 13.9 %ffn_forward.1 = (bf16[512,768]{1,0:T(8,128)(2,1)}, f32[128,768]{1,0:T(8,128)}, bf16[128,768]{1,0:T(8,128)(2,1)}, f32[2,768]{1,0:T(2,128)}) custom-call(f32[512,768]{1,0:T(8,128)} %get-tuple-element.88.h1_ref, bf16[8,4,3,96,768]{4,3,2,1,0:T(8,128)(2,1)} %bitcast.132, bf16[8,4,3,96,768]{4,3,2,1,0:T(8,128)(2,1)} %bitcast.133, ...), custom_call_target="tpu_custom_call" | custom-call | bytes 48000000 | tf_op jit(solution)/shard_map/ffn_forward/pallas_call | solution.py:233
  144.1 5.7 %ffn_again.1 = (bf16[512,768]{1,0:T(8,128)(2,1)}, bf16[512,768]{1,0:T(8,128)(2,1)}, bf16[512,768]{1,0:T(8,128)(2,1)}) custom-call(s32[5]{0:T(128)} %stack.80.where_ref, bf16[4,128,768]{2,1,0:T(8,128)(2,1)} %pad_maximum_fusion.1.h_ref.a_ref, bf16[8,4,3,96,768]{4,3,2,1,0:T(8,128)(2,1)} %bitcast.135, bf16[8,4,3,96,768]{4,3,2,1,0:T(8,128)(2,1)} %bitcast.136), custom_call_target="tpu_custom_call" | custom-call | bytes 18000000 | tf_op jit(solution)/shard_map/ffn_again/pallas_call | solution.py:294
  152.9 7.4 %ffn_back.1 = (bf16[512,768]{1,0:T(8,128)(2,1)}, bf16[512,768]{1,0:T(8,128)(2,1)}, f32[2,128,768]{2,1,0:T(8,128)}, bf16[2,128,768]{2,1,0:T(8,128)(2,1)}, bf16[512,768]{1,0:T(8,128)(2,1)}) custom-call(s32[5]{0:T(128)} %stack.80.where_ref, bf16[128,768]{1,0:T(8,128)(2,1)} %get-tuple-element.93.rest_0_, bf16[128,768]{1,0:T(8,128)(2,1)} %copy-done.25, ...), custom_call_target="tpu_custom_call" | custom-call | bytes 21000000 | tf_op jit(solution)/shard_map/ffn_back/pallas_call | solution.py:333
  160.4 3.3 %weight_grad.3 = (bf16[4,96,768]{2,1,0:T(8,128)(2,1)}, bf16[4,96,768]{2,1,0:T(8,128)(2,1)}) custom-call(s32[5]{0:T(128)} %stack.80.where_ref, bf16[512,768]{1,0:T(8,128)(2,1)} %get-tuple-element.92.a_ref, bf16[512,768]{1,0:T(8,128)(2,1)} %get-tuple-element.97.b_ref), custom_call_target="tpu_custom_call" | custom-call | bytes 12000000 | tf_op jit(solution)/shard_map/weight_grad/pallas_call | solution.py:367
  172.2 3.3 %weight_grad.5 = (bf16[4,96,768]{2,1,0:T(8,128)(2,1)}, bf16[4,96,768]{2,1,0:T(8,128)(2,1)}) custom-call(s32[5]{0:T(128)} %stack.80.where_ref, bf16[4,128,768]{2,1,0:T(8,128)(2,1)} %pad_maximum_fusion.1.h_ref.a_ref, bf16[512,768]{1,0:T(8,128)(2,1)} %get-tuple-element.106.b_ref), custom_call_target="tpu_custom_call" | custom-call | bytes 12000000 | tf_op jit(solution)/shard_map/weight_grad/pallas_call | solution.py:367
  180.1 11.0 %attention_back.1.rhs_ref = bf16[512,2304]{1,0:T(8,128)(2,1)} custom-call(bf16[128,768]{1,0:T(8,128)(2,1)} %get-tuple-element.111.datt_ref, bf16[128,768]{1,0:T(8,128)(2,1)} %get-tuple-element.86.q_ref, bf16[512,2304]{1,0:T(8,128)(2,1)} %get-tuple-element.87.k_ref.v_ref, bf16[512,2304]{1,0:T(8,128)(2,1)} %get-tuple-element.87.k_ref.v_ref, ...), custom_call_target="tpu_custom_call" | custom-call | bytes 36000000 | tf_op jit(solution)/shard_map/attention_back/pallas_call | solution.py:479
  194.9 8.7 %attention_grads.1 = (bf16[2,2,4,48,768]{4,3,2,1,0:T(8,128)(2,1)}, bf16[2,2,4,56,768]{4,3,2,1,0:T(8,128)(2,1)}, bf16[2,2,4,48,768]{4,3,2,1,0:T(8,128)(2,1)}, bf16[2,2,4,56,768]{4,3,2,1,0:T(8,128)(2,1)}) custom-call(s32[5]{0:T(128)} %stack.80.where_ref, bf16[768,512]{1,0:T(8,128)(2,1)} %bitcast.140, bf16[512,2304]{1,0:T(8,128)(2,1)} %attention_back.1.rhs_ref, ...), custom_call_target="tpu_custom_call" | custom-call | bytes 30000000 | tf_op jit(solution)/shard_map/attention_grads/pallas_call | solution.py:538
  209.4 4.3 %collective-permute-start.32 = (bf16[2,4,48,768]{3,2,1,0:T(8,128)(2,1)S(1)}, bf16[2,4,48,768]{3,2,1,0:T(8,128)(2,1)S(1)}, u32[]{:S(2)}, u32[]{:S(2)}) collective-permute-start(bf16[2,4,48,768]{3,2,1,0:T(8,128)(2,1)S(1)} %fusion.3), channel_id=1, source_target_pairs={{0,2},{1,3},{2,0},{3,1},{4,6},{5,7},{6,4},{7,5},{8,10},{9,11},{10,... | collective-permute-start | bytes 1769480 | tf_op jit(solution)/shard_map/ppermute | solution.py:605
  216.5 10.6 %collective-permute-done.32 = bf16[2,4,48,768]{3,2,1,0:T(8,128)(2,1)S(1)} collective-permute-done((bf16[2,4,48,768]{3,2,1,0:T(8,128)(2,1)S(1)}, bf16[2,4,48,768]{3,2,1,0:T(8,128)(2,1)S(1)}, u32[]{:S(2)}, u32[]{:S(2)}) %collective-permute-start.32) | collective-permute-done | bytes 589856 | tf_op jit(solution)/shard_map/ppermute | solution.py:605
  233.4 4.9 %collective-permute-done.39 = bf16[192,768]{1,0:T(8,128)(2,1)S(1)} collective-permute-done((bf16[192,768]{1,0:T(8,128)(2,1)S(1)}, bf16[192,768]{1,0:T(8,128)(2,1)S(1)}, u32[]{:S(2)}, u32[]{:S(2)}) %collective-permute-start.39) | collective-permute-done | bytes 294944 | tf_op jit(solution)/shard_map/ppermute | solution.py:605
  238.3 4.3 %collective-permute-done.40 = bf16[192,768]{1,0:T(8,128)(2,1)S(1)} collective-permute-done((bf16[192,768]{1,0:T(8,128)(2,1)S(1)}, bf16[192,768]{1,0:T(8,128)(2,1)S(1)}, u32[]{:S(2)}, u32[]{:S(2)}) %collective-permute-start.40) | collective-permute-done | bytes 294944 | tf_op jit(solution)/shard_map/ppermute | solution.py:605
  246.6 8.1 %input_grad.1 = f32[512,768]{1,0:T(8,128)} custom-call(bf16[512,2304]{1,0:T(8,128)(2,1)} %attention_back.1.rhs_ref, bf16[8,4,96,768]{3,2,1,0:T(8,128)(2,1)} %get-tuple-element.110.w_ref, f32[128,768]{1,0:T(8,128)} %get-tuple-element.141.dr1_ref, s32[4,32]{1,0:T(4,128)} %pos_ref.1), custom_call_target="tpu_custom_call" | custom-call | bytes 24000000 | tf_op jit(solution)/shard_map/input_grad/pallas_call | solution.py:568
  254.7 4.9 %collective-permute-done.42 = bf16[104,768]{1,0:T(8,128)(2,1)S(1)} collective-permute-done((bf16[104,768]{1,0:T(8,128)(2,1)S(1)}, bf16[104,768]{1,0:T(8,128)(2,1)S(1)}, u32[]{:S(2)}, u32[]{:S(2)}) %collective-permute-start.42) | collective-permute-done | bytes 159776 | tf_op jit(solution)/shard_map/ppermute | solution.py:605
  263.3 3.4 %finish_ffn.1 = (f32[384,768]{1,0:T(8,128)}, f32[96,6144]{1,0:T(8,128)}) custom-call(s32[5]{0:T(128)} %stack.80.where_ref, bf16[3,96,768]{2,1,0:T(8,128)(2,1)} %copy-done.1, bf16[3,96,768]{2,1,0:T(8,128)(2,1)} %copy-done.13, bf16[3,96,768]{2,1,0:T(8,128)(2,1)} %copy-done.12, bf16[3,96,768]{2,1,0:T(8,128)(2,1)} %copy-done.14), custom_call_target="tpu_custom_call" | custom-call | bytes 12000000 | tf_op jit(solution)/shard_map/finish_ffn/pallas_call | solution.py:654
  (227 shorter events, 75.5 us)
Async XLA Ops:
  7.2 122.3 %all-gather.3.cloned.1.call-start = ((), (), s32[]{:S(2)}) async-start(), calls=%async_computation | async-start | bytes 14598144 | tf_op jit(solution)/shard_map/all_gather | solution.py:711
  9.6 16.0 %collective-permute-start.1 = (bf16[104,768]{1,0:T(8,128)(2,1)S(1)}, bf16[104,768]{1,0:T(8,128)(2,1)S(1)}, u32[]{:S(2)}, u32[]{:S(2)}) collective-permute-start(bf16[104,768]{1,0:T(8,128)(2,1)S(1)} %get-tuple-element.177), channel_id=1, source_target_pairs={{0,16},{1,17},{2,18},{3,19},{4,20},{5,21},{6,22},{7,23},{8,24},{9,... | collective-permute-start | bytes 479240 | tf_op jit(solution)/shard_map/ppermute | solution.py:605
  29.0 13.5 %collective-permute-start.5 = (bf16[4,48,768]{2,1,0:T(8,128)(2,1)S(1)}, bf16[4,48,768]{2,1,0:T(8,128)(2,1)}, u32[]{:S(2)}, u32[]{:S(2)}) collective-permute-start(bf16[4,48,768]{2,1,0:T(8,128)(2,1)S(1)} %slice.187.rest_0_), channel_id=1, source_target_pairs={{0,2},{1,3},{2,0},{3,1},{4,6},{5,7},{6,4},{7,5},{8,10},{9,11},{10,... | collective-permute-start | bytes 884744 | tf_op jit(solution)/shard_map/ppermute | solution.py:605
  29.4 17.1 %collective-permute-start.3 = (bf16[4,56,768]{2,1,0:T(8,128)(2,1)S(1)}, bf16[4,56,768]{2,1,0:T(8,128)(2,1)S(1)}, u32[]{:S(2)}, u32[]{:S(2)}) collective-permute-start(bf16[4,56,768]{2,1,0:T(8,128)(2,1)S(1)} %slice.185.rest_1_), channel_id=1, source_target_pairs={{0,4},{1,5},{2,6},{3,7},{4,0},{5,1},{6,2},{7,3},{8,12},{9,13},{10,... | collective-permute-start | bytes 1032200 | tf_op jit(solution)/shard_map/ppermute | solution.py:605
  31.2 15.3 %collective-permute-start.4 = (bf16[4,48,768]{2,1,0:T(8,128)(2,1)S(1)}, bf16[4,48,768]{2,1,0:T(8,128)(2,1)}, u32[]{:S(2)}, u32[]{:S(2)}) collective-permute-start(bf16[4,48,768]{2,1,0:T(8,128)(2,1)S(1)} %slice.187.rest_0_), channel_id=1, source_target_pairs={{0,4},{1,5},{2,6},{3,7},{4,0},{5,1},{6,2},{7,3},{8,12},{9,13},{10,... | collective-permute-start | bytes 884744 | tf_op jit(solution)/shard_map/ppermute | solution.py:605
  31.4 19.1 %collective-permute-start.10 = (bf16[4,56,768]{2,1,0:T(8,128)(2,1)S(1)}, bf16[4,56,768]{2,1,0:T(8,128)(2,1)S(1)}, u32[]{:S(2)}, u32[]{:S(2)}) collective-permute-start(bf16[4,56,768]{2,1,0:T(8,128)(2,1)S(1)} %slice.185.rest_1_), channel_id=1, source_target_pairs={{0,1},{1,0},{2,3},{3,2},{4,5},{5,4},{6,7},{7,6},{8,9},{9,8},{10,11... | collective-permute-start | bytes 1032200 | tf_op jit(solution)/shard_map/ppermute | solution.py:605
  38.2 18.0 %collective-permute-start.8 = (bf16[4,56,768]{2,1,0:T(8,128)(2,1)S(1)}, bf16[4,56,768]{2,1,0:T(8,128)(2,1)S(1)}, u32[]{:S(2)}, u32[]{:S(2)}) collective-permute-start(bf16[4,56,768]{2,1,0:T(8,128)(2,1)S(1)} %collective-permute-done.6.rest_5_), channel_id=1, source_target_pairs={{0,4},{1,5},{2,6},{3,7},{4,0},{5,1},{6,2},{7,3},{8,12},{9,13},{10,... | collective-permute-start | bytes 1032200 | tf_op jit(solution)/shard_map/ppermute | solution.py:605
  46.5 16.4 %collective-permute-start.7 = (bf16[4,48,768]{2,1,0:T(8,128)(2,1)}, bf16[4,48,768]{2,1,0:T(8,128)(2,1)}, u32[]{:S(2)}, u32[]{:S(2)}) collective-permute-start(bf16[4,48,768]{2,1,0:T(8,128)(2,1)} %collective-permute-done.4.rest_2_), channel_id=1, source_target_pairs={{0,2},{1,3},{2,0},{3,1},{4,6},{5,7},{6,4},{7,5},{8,10},{9,11},{10,... | collective-permute-start | bytes 884744 | tf_op jit(solution)/shard_map/ppermute | solution.py:605
  49.8 14.1 %collective-permute-start.14 = (bf16[4,56,768]{2,1,0:T(8,128)(2,1)S(1)}, bf16[4,56,768]{2,1,0:T(8,128)(2,1)S(1)}, u32[]{:S(2)}, u32[]{:S(2)}) collective-permute-start(bf16[4,56,768]{2,1,0:T(8,128)(2,1)S(1)} %collective-permute-done.6.rest_5_), channel_id=1, source_target_pairs={{0,1},{1,0},{2,3},{3,2},{4,5},{5,4},{6,7},{7,6},{8,9},{9,8},{10,11... | collective-permute-start | bytes 1032200 | tf_op jit(solution)/shard_map/ppermute | solution.py:605
  50.5 13.4 %collective-permute-start.12 = (bf16[4,56,768]{2,1,0:T(8,128)(2,1)S(1)}, bf16[4,56,768]{2,1,0:T(8,128)(2,1)S(1)}, u32[]{:S(2)}, u32[]{:S(2)}) collective-permute-start(bf16[4,56,768]{2,1,0:T(8,128)(2,1)S(1)} %collective-permute-done.3.rest_3_), channel_id=1, source_target_pairs={{0,1},{1,0},{2,3},{3,2},{4,5},{5,4},{6,7},{7,6},{8,9},{9,8},{10,11... | collective-permute-start | bytes 1032200 | tf_op jit(solution)/shard_map/ppermute | solution.py:605
  85.4 15.6 %collective-permute-start.17 = (bf16[128,768]{1,0:T(8,128)(2,1)}, bf16[128,768]{1,0:T(8,128)(2,1)S(1)}, u32[]{:S(2)}, u32[]{:S(2)}) collective-permute-start(bf16[128,768]{1,0:T(8,128)(2,1)} %get-tuple-element.85), channel_id=1, source_target_pairs={{0,1},{1,0},{2,3},{3,2},{4,5},{5,4},{6,7},{7,6},{8,9},{9,8},{10,11... | collective-permute-start | bytes 589832 | tf_op jit(solution)/shard_map/ppermute | solution.py:605
  163.8 27.3 %collective-permute-start.23 = (bf16[4,96,768]{2,1,0:T(8,128)(2,1)}, bf16[4,96,768]{2,1,0:T(8,128)(2,1)S(1)}, u32[]{:S(2)}, u32[]{:S(2)}) collective-permute-start(bf16[4,96,768]{2,1,0:T(8,128)(2,1)} %get-tuple-element.98), channel_id=1, source_target_pairs={{0,4},{1,5},{2,6},{3,7},{4,0},{5,1},{6,2},{7,3},{8,12},{9,13},{10,... | collective-permute-start | bytes 1769480 | tf_op jit(solution)/shard_map/ppermute | solution.py:605
  169.5 36.7 %collective-permute-start.29 = (bf16[4,96,768]{2,1,0:T(8,128)(2,1)}, bf16[4,96,768]{2,1,0:T(8,128)(2,1)S(1)}, u32[]{:S(2)}, u32[]{:S(2)}) collective-permute-start(bf16[4,96,768]{2,1,0:T(8,128)(2,1)} %get-tuple-element.104), channel_id=1, source_target_pairs={{0,4},{1,5},{2,6},{3,7},{4,0},{5,1},{6,2},{7,3},{8,12},{9,13},{10,... | collective-permute-start | bytes 1769480 | tf_op jit(solution)/shard_map/ppermute | solution.py:605
  175.6 30.6 %collective-permute-start.30 = (bf16[4,96,768]{2,1,0:T(8,128)(2,1)}, bf16[4,96,768]{2,1,0:T(8,128)(2,1)S(1)}, u32[]{:S(2)}, u32[]{:S(2)}) collective-permute-start(bf16[4,96,768]{2,1,0:T(8,128)(2,1)} %get-tuple-element.107), channel_id=1, source_target_pairs={{0,4},{1,5},{2,6},{3,7},{4,0},{5,1},{6,2},{7,3},{8,12},{9,13},{10,... | collective-permute-start | bytes 1769480 | tf_op jit(solution)/shard_map/ppermute | solution.py:605
  193.0 13.2 %collective-permute-start.27 = (bf16[96,768]{1,0:T(8,128)(2,1)S(1)}, bf16[96,768]{1,0:T(8,128)(2,1)S(1)}, u32[]{:S(2)}, u32[]{:S(2)}) collective-permute-start(bf16[96,768]{1,0:T(8,128)(2,1)S(1)} %get-tuple-element.163), channel_id=1, source_target_pairs={{0,16},{1,17},{2,18},{3,19},{4,20},{5,21},{6,22},{7,23},{8,24},{9,... | collective-permute-start | bytes 442376 | tf_op jit(solution)/shard_map/ppermute | solution.py:605
  206.8 25.3 %collective-permute-start.37 = (bf16[96,768]{1,0:T(8,128)(2,1)S(1)}, bf16[96,768]{1,0:T(8,128)(2,1)S(1)}, u32[]{:S(2)}, u32[]{:S(2)}) collective-permute-start(bf16[96,768]{1,0:T(8,128)(2,1)S(1)} %fusion.20), channel_id=1, source_target_pairs={{0,0},{1,8},{2,16},{3,24},{4,1},{5,9},{6,17},{7,25},{8,2},{9,10},{... | collective-permute-start | bytes 442376 | tf_op jit(solution)/shard_map/ppermute | solution.py:605
  209.4 17.7 %collective-permute-start.32 = (bf16[2,4,48,768]{3,2,1,0:T(8,128)(2,1)S(1)}, bf16[2,4,48,768]{3,2,1,0:T(8,128)(2,1)S(1)}, u32[]{:S(2)}, u32[]{:S(2)}) collective-permute-start(bf16[2,4,48,768]{3,2,1,0:T(8,128)(2,1)S(1)} %fusion.3), channel_id=1, source_target_pairs={{0,2},{1,3},{2,0},{3,1},{4,6},{5,7},{6,4},{7,5},{8,10},{9,11},{10,... | collective-permute-start | bytes 1769480 | tf_op jit(solution)/shard_map/ppermute | solution.py:605
  213.7 19.7 %collective-permute-start.38 = (bf16[192,768]{1,0:T(8,128)(2,1)S(1)}, bf16[192,768]{1,0:T(8,128)(2,1)S(1)}, u32[]{:S(2)}, u32[]{:S(2)}) collective-permute-start(bf16[192,768]{1,0:T(8,128)(2,1)S(1)} %pad_maximum_fusion.5), channel_id=1, source_target_pairs={{0,8},{1,9},{2,10},{3,11},{4,12},{5,13},{6,14},{7,15},{8,16},{9,17... | collective-permute-start | bytes 884744 | tf_op jit(solution)/shard_map/ppermute | solution.py:605
  214.0 16.7 %collective-permute-start.35 = (bf16[2,4,56,768]{3,2,1,0:T(8,128)(2,1)S(1)}, bf16[2,4,56,768]{3,2,1,0:T(8,128)(2,1)S(1)}, u32[]{:S(2)}, u32[]{:S(2)}) collective-permute-start(bf16[2,4,56,768]{3,2,1,0:T(8,128)(2,1)S(1)} %fusion.1), channel_id=1, source_target_pairs={{0,4},{1,5},{2,6},{3,7},{4,0},{5,1},{6,2},{7,3},{8,12},{9,13},{10,... | collective-permute-start | bytes 2064392 | tf_op jit(solution)/shard_map/ppermute | solution.py:605
  215.2 23.1 %collective-permute-start.39 = (bf16[192,768]{1,0:T(8,128)(2,1)S(1)}, bf16[192,768]{1,0:T(8,128)(2,1)S(1)}, u32[]{:S(2)}, u32[]{:S(2)}) collective-permute-start(bf16[192,768]{1,0:T(8,128)(2,1)S(1)} %pad_maximum_fusion.6), channel_id=1, source_target_pairs={{0,16},{1,17},{2,18},{3,19},{4,20},{5,21},{6,22},{7,23},{8,24},{9,... | collective-permute-start | bytes 884744 | tf_op jit(solution)/shard_map/ppermute | solution.py:605
  227.1 15.5 %collective-permute-start.40 = (bf16[192,768]{1,0:T(8,128)(2,1)S(1)}, bf16[192,768]{1,0:T(8,128)(2,1)S(1)}, u32[]{:S(2)}, u32[]{:S(2)}) collective-permute-start(bf16[192,768]{1,0:T(8,128)(2,1)S(1)} %pad_maximum_fusion.7), channel_id=1, source_target_pairs={{0,24},{1,25},{2,26},{3,27},{4,28},{5,29},{6,30},{7,31},{8,0},{9,1... | collective-permute-start | bytes 884744 | tf_op jit(solution)/shard_map/ppermute | solution.py:605
  245.9 13.7 %collective-permute-start.42 = (bf16[104,768]{1,0:T(8,128)(2,1)S(1)}, bf16[104,768]{1,0:T(8,128)(2,1)S(1)}, u32[]{:S(2)}, u32[]{:S(2)}) collective-permute-start(bf16[104,768]{1,0:T(8,128)(2,1)S(1)} %get-tuple-element.170), channel_id=1, source_target_pairs={{0,16},{1,17},{2,18},{3,19},{4,20},{5,21},{6,22},{7,23},{8,24},{9,... | collective-permute-start | bytes 479240 | tf_op jit(solution)/shard_map/ppermute | solution.py:605
  246.3 13.3 %collective-permute-start.41 = (bf16[104,768]{1,0:T(8,128)(2,1)S(1)}, bf16[104,768]{1,0:T(8,128)(2,1)S(1)}, u32[]{:S(2)}, u32[]{:S(2)}) collective-permute-start(bf16[104,768]{1,0:T(8,128)(2,1)S(1)} %get-tuple-element.171), channel_id=1, source_target_pairs={{0,8},{1,9},{2,10},{3,11},{4,12},{5,13},{6,14},{7,15},{8,16},{9,17... | collective-permute-start | bytes 479240 | tf_op jit(solution)/shard_map/ppermute | solution.py:605
  246.6 15.1 %collective-permute-start.47 = (bf16[3,96,768]{2,1,0:T(8,128)(2,1)S(1)}, bf16[3,96,768]{2,1,0:T(8,128)(2,1)S(1)}, u32[]{:S(2)}, u32[]{:S(2)}) collective-permute-start(bf16[3,96,768]{2,1,0:T(8,128)(2,1)S(1)} %pad_maximum_fusion.4.rest_0_), channel_id=1, source_target_pairs={{0,1},{1,0},{2,3},{3,2},{4,5},{5,4},{6,7},{7,6},{8,9},{9,8},{10,11... | collective-permute-start | bytes 1327112 | tf_op jit(solution)/shard_map/ppermute | solution.py:605
  (67 other events, 532.0 us)
Sparse Core Ops, SparseCore 0:
  11.5 117.9 all-gather.2
